TPU v7x, 128 devices: a whole 4x4x4 slice. The times are simulated.
128 devices in a mesh: grp: 4 (over y), loc: 32 (over x, z, core).
Axes of the slice: x: 4, y: 4, z: 4, core: 2. Of those that a mesh axis runs over, the one named last changes fastest.
Arguments:
- tokens: bfloat16 [16384, 7168], P(('grp', 'loc')), may hold values from -1.5 to 1.5
- grad_out: bfloat16 [16384, 7168], P(('grp', 'loc')), may hold values from -0.8984375 to 0.8984375
- expert_ids: int32 [16384, 8], P(('grp', 'loc')), may hold values from 0 to 255, as said below
- route_weight: bfloat16 [16384, 8], P(('grp', 'loc')), may hold values from 0.25 to 2
- gate_weight: bfloat16 [32, 7168, 512], P('loc', None, 'grp'), may hold values from -0.25 to 0.25
- up_weight: bfloat16 [32, 7168, 512], P('loc', None, 'grp'), may hold values from -0.25 to 0.25
- down_weight: bfloat16 [32, 512, 7168], P('loc', 'grp'), may hold values from -0.1875 to 0.1875
Outputs:
- tokens_grad: bfloat16 [16384, 7168], P(('grp', 'loc'))
- gate_grad: bfloat16 [32, 7168, 512], P('loc', None, 'grp')
- up_grad: bfloat16 [32, 7168, 512], P('loc', None, 'grp')
- down_grad: bfloat16 [32, 512, 7168], P('loc', 'grp')
Inputs may be any that keep to these rules, and one draw needn't show every extreme that they name: `expert_ids`: each row names 8 different experts.
All inputs are finite; a program needn't handle non-finite values.
Results may differ from a plain program's by a relative error of at most 0.015.
Values may be sent and summed in bfloat16 or wider, within the bound.
No kernel may reach another device: no remote copies, remote signals or barrier semaphores. Data moves between devices by JAX's collectives and lax.ppermute only.
A program may use at most 128 MiB of HBM per device.

v0:
```python
import jax
import jax.numpy as jnp
from jax import lax
from jax.sharding import PartitionSpec as P

CAP = 4


def contract_rows(left, right):
    return lax.dot_general(
        left, right, (((0,), (0,)), ((), ())), preferred_element_type=jnp.float32
    )


def contract_cols(left, right):
    return lax.dot_general(
        left, right, (((1,), (1,)), ((), ())), preferred_element_type=jnp.float32
    )


def body(tokens, grad_out, expert_ids, route_weight, gate_weight, up_weight, down_weight):
    group_count = lax.axis_size("grp")
    local_count = lax.axis_size("loc")
    expert_fl = local_count // 2
    tok_count, topk_count = expert_ids.shape
    width = tokens.shape[1]
    buffer = expert_fl * CAP
    pair_ids = expert_ids.reshape(-1)
    expert_iota = jnp.arange(expert_fl, dtype=jnp.int32)
    onehot = (pair_ids[:, None] == expert_iota[None, :]).astype(jnp.int32)
    before = jnp.cumsum(onehot, axis=0) - onehot
    slot_index = jnp.sum(before * onehot, axis=1)
    keep_mask = (pair_ids < expert_fl) & (slot_index < CAP)
    position = jnp.where(keep_mask, pair_ids * CAP + slot_index, buffer)
    columns = jnp.arange(buffer, dtype=jnp.int32)
    pair_table = position[:, None] == columns[None, :]
    token_table = pair_table.reshape(tok_count, topk_count, buffer).any(axis=1)
    token_mat = token_table.astype(jnp.bfloat16)
    x_send = jnp.einsum("tb,td->bd", token_mat, tokens, preferred_element_type=jnp.float32).astype(
        jnp.bfloat16
    )
    g_send = jnp.einsum(
        "tb,td->bd", token_mat, grad_out, preferred_element_type=jnp.float32
    ).astype(jnp.bfloat16)
    w_send = jnp.einsum(
        "pb,p->b",
        pair_table.astype(jnp.float32),
        route_weight.reshape(-1).astype(jnp.float32),
        precision=lax.Precision.HIGHEST,
    ).astype(jnp.bfloat16)
    x_unit = x_send.reshape(1, expert_fl, CAP, width)
    g_unit = g_send.reshape(1, expert_fl, CAP, width)
    w_unit = w_send.reshape(1, expert_fl, CAP)
    copies = group_count * 2
    x_out = jnp.tile(x_unit, (copies, 1, 1, 1)).reshape(group_count * local_count, CAP, width)
    g_out = jnp.tile(g_unit, (copies, 1, 1, 1)).reshape(group_count * local_count, CAP, width)
    w_out = jnp.tile(w_unit, (copies, 1, 1)).reshape(group_count * local_count, CAP)
    x_recv, g_recv, w_recv = (
        lax.all_to_all(x_out, ("grp", "loc"), split_axis=0, concat_axis=0, tiled=True),
        lax.all_to_all(g_out, ("grp", "loc"), split_axis=0, concat_axis=0, tiled=True),
        lax.all_to_all(w_out, ("grp", "loc"), split_axis=0, concat_axis=0, tiled=True),
    )
    row_total = group_count * local_count * CAP
    x_rows = x_recv.reshape(row_total, width)
    g_rows = g_recv.reshape(row_total, width)
    w_rows = w_recv.reshape(row_total).astype(jnp.float32)[:, None]
    w_gate = gate_weight[0]
    w_up = up_weight[0]
    w_down = down_weight[0]
    pre_gate = jnp.dot(x_rows, w_gate, preferred_element_type=jnp.float32)
    pre_up = jnp.dot(x_rows, w_up, preferred_element_type=jnp.float32)
    sigmoid_gate = jax.nn.sigmoid(pre_gate)
    swish = pre_gate * sigmoid_gate
    hidden_grad = w_rows * contract_cols(g_rows, w_down)
    gate_delta = (
        hidden_grad * pre_up * sigmoid_gate * (1.0 + pre_gate * (1.0 - sigmoid_gate))
    ).astype(jnp.bfloat16)
    up_delta = (hidden_grad * swish).astype(jnp.bfloat16)
    weighted = (w_rows * swish * pre_up).astype(jnp.bfloat16)
    gate_grad = contract_rows(x_rows, gate_delta).astype(jnp.bfloat16)[None]
    up_grad = contract_rows(x_rows, up_delta).astype(jnp.bfloat16)[None]
    down_grad = contract_rows(weighted, g_rows).astype(jnp.bfloat16)[None]
    partial_value = (contract_cols(gate_delta, w_gate) + contract_cols(up_delta, w_up)).astype(
        jnp.bfloat16
    )
    reduced = lax.psum_scatter(
        partial_value.astype(jnp.float32)
        .reshape(group_count, local_count, CAP, width)
        .astype(jnp.bfloat16),
        "grp",
        scatter_dimension=0,
        tiled=True,
    ).astype(jnp.float32)
    home = lax.all_to_all(
        reduced.astype(jnp.bfloat16), "loc", split_axis=1, concat_axis=1, tiled=True
    ).astype(reduced.dtype)
    summed = home.reshape(2, expert_fl, CAP, width).sum(axis=0)
    returned = summed.reshape(buffer, width)
    tokens_grad = jnp.dot(
        token_table.astype(jnp.float32), returned, precision=lax.Precision.HIGHEST
    ).astype(jnp.bfloat16)
    return (tokens_grad, gate_grad, up_grad, down_grad)


def solution(mesh):
    in_specs = (
        P(("grp", "loc"), None),
        P(("grp", "loc"), None),
        P(("grp", "loc"), None),
        P(("grp", "loc"), None),
        P("loc", None, "grp"),
        P("loc", None, "grp"),
        P("loc", "grp", None),
    )
    out_specs = (
        P(("grp", "loc"), None),
        P("loc", None, "grp"),
        P("loc", None, "grp"),
        P("loc", "grp", None),
    )
    return jax.shard_map(body, mesh=mesh, in_specs=in_specs, out_specs=out_specs, check_vma=False)
```

profile of v0, /device:TPU:1, one launch (start us, length us, event | category | flops | bytes accessed | tf_op | source)
XLA Modules:
  0.0 422.0 jit_solution(4533274973874869389)
XLA Ops:
  9.2 4.5 %reduce-window.6 = s32[16,8,128]{2,1,0:T(8,128)S(1)} reduce-window(s32[16,8,128]{2,1,0:T(8,128)S(1)} %fusion.23, s32[]{:T(128)} %constant.3.clone.1), window={size=1x1x128 pad=0_0x0_0x127_0}, to_apply=%region_0.0 | reduce-window | flops 2080768 | bytes 131076 | tf_op jit(solution)/shard_map/reduce-window
  15.6 11.5 %all-to-all-start = ((bf16[128,1,4]{2,1,0:T(2,128)(2,1)}), bf16[128,1,4]{2,1,0:T(2,128)(2,1)S(1)}, u32[]{:S(2)}, u32[]{:S(2)}) async-start(bf16[128,1,4]{2,1,0:T(2,128)(2,1)} %copy.69), calls=%async_computation | async-start | bytes 131072 | tf_op jit(solution)/shard_map/all_to_all | solution.py:61
  36.4 5.5 %tile.31 = bf16[8,1,1,16,4,7168]{5,4,3,2,1,0:T(4,128)(2,1)} broadcast(bf16[16,4,7168]{2,1,0:T(4,128)(2,1)S(1)} %tile.30), dimensions={3,4,5} | broadcast | bytes 8257536 | tf_op jit(solution)/shard_map/tile | solution.py:55
  41.9 6.3 %all-to-all-start.2 = ((bf16[128,4,7168]{2,1,0:T(4,128)(2,1)}), bf16[128,4,7168]{2,1,0:T(4,128)(2,1)}, u32[]{:S(2)}, u32[]{:S(2)}) async-start(bf16[128,4,7168]{2,1,0:T(4,128)(2,1)} %bitcast.71), calls=%async_computation.2 | async-start | bytes 14680064 | tf_op jit(solution)/shard_map/all_to_all | solution.py:59
  52.9 85.2 %all-to-all-done.2 = bf16[128,4,7168]{2,1,0:T(4,128)(2,1)} async-done(((bf16[128,4,7168]{2,1,0:T(4,128)(2,1)}), bf16[128,4,7168]{2,1,0:T(4,128)(2,1)}, u32[]{:S(2)}, u32[]{:S(2)}) %all-to-all-start.2) | async-done | bytes 7340064 | tf_op jit(solution)/shard_map/all_to_all | solution.py:59
  138.0 5.5 %tile.28 = bf16[8,1,1,16,4,7168]{5,4,3,2,1,0:T(4,128)(2,1)} broadcast(bf16[16,4,7168]{2,1,0:T(4,128)(2,1)S(1)} %tile.27), dimensions={3,4,5} | broadcast | bytes 8257536 | tf_op jit(solution)/shard_map/tile | solution.py:56
  143.5 7.3 %all-to-all-start.1 = ((bf16[128,4,7168]{2,1,0:T(4,128)(2,1)}), bf16[128,4,7168]{2,1,0:T(4,128)(2,1)}, u32[]{:S(2)}, u32[]{:S(2)}) async-start(bf16[128,4,7168]{2,1,0:T(4,128)(2,1)} %bitcast.70), calls=%async_computation.1 | async-start | bytes 14680064 | tf_op jit(solution)/shard_map/all_to_all | solution.py:60
  151.3 12.1 %reshape.98 = bf16[512,7168]{1,0:T(8,128)(2,1)} reshape(bf16[128,4,7168]{2,1,0:T(4,128)(2,1)} %all-to-all-done.2) | data formatting | bytes 14680064 | tf_op jit(solution)/shard_map/reshape | solution.py:64
  163.5 5.3 %fusion.5 = f32[512,128]{1,0:T(8,128)S(1)} fusion(bf16[512,7168]{1,0:T(8,128)(2,1)} %reshape.98, bf16[1,7168,128]{2,1,0:T(8,128)(2,1)S(1)} %copy-done), kind=kOutput, calls=%fused_computation.13 | convolution fusion | flops 939524096 | bytes 9437184 | tf_op jit(solution)/shard_map/dot_general | solution.py:70
  171.2 69.4 %all-to-all-done.1 = bf16[128,4,7168]{2,1,0:T(4,128)(2,1)} async-done(((bf16[128,4,7168]{2,1,0:T(4,128)(2,1)}), bf16[128,4,7168]{2,1,0:T(4,128)(2,1)}, u32[]{:S(2)}, u32[]{:S(2)}) %all-to-all-start.1) | async-done | bytes 7340064 | tf_op jit(solution)/shard_map/all_to_all | solution.py:60
  240.6 12.1 %reshape.97 = bf16[512,7168]{1,0:T(8,128)(2,1)} reshape(bf16[128,4,7168]{2,1,0:T(4,128)(2,1)} %all-to-all-done.1) | data formatting | bytes 14680064 | tf_op jit(solution)/shard_map/reshape | solution.py:65
  252.7 5.6 %multiply_convert_fusion.1 = (bf16[512,128]{1,0:T(8,128)(2,1)S(1)}, bf16[512,128]{1,0:T(8,128)(2,1)S(1)}) fusion(f32[512,128]{1,0:T(8,128)S(1)} %fusion.5, f32[512,128]{1,0:T(8,128)S(1)} %fusion.8, bf16[512,7168]{1,0:T(8,128)(2,1)} %reshape.97, bf16[1,128,7168]{2,1,0:T(8,128)(2,1)} %param.13, f32[512]{0:T(512)S(1)} %reshape.102), kind=kOutput, calls=%fused_computation.25 | convolution fusion | flops 940441600 | bytes 9963520 | tf_op jit(solution)/shard_map/dot_general | solution.py:16
  258.4 7.3 %fusion.3 = f32[512,7168]{1,0:T(8,128)} fusion(bf16[512,128]{1,0:T(8,128)(2,1)S(1)} %get-tuple-element.5, bf16[1,7168,128]{2,1,0:T(8,128)(2,1)S(1)} %copy-done), kind=kOutput, calls=%fused_computation.11 | convolution fusion | flops 939524096 | bytes 16646144 | tf_op jit(solution)/shard_map/dot_general | solution.py:16
  265.6 10.2 %add_convert_fusion = bf16[512,7168]{1,0:T(8,128)(2,1)} fusion(f32[512,7168]{1,0:T(8,128)} %fusion.3, bf16[512,128]{1,0:T(8,128)(2,1)S(1)} %get-tuple-element.4, bf16[1,7168,128]{2,1,0:T(8,128)(2,1)S(1)} %copy-done.4), kind=kOutput, calls=%fused_computation | convolution fusion | flops 946864128 | bytes 23986176 | tf_op jit(solution)/shard_map/dot_general | solution.py:16
  275.9 12.6 %convert_element_type.72 = bf16[4,32,4,7168]{3,2,1,0:T(4,128)(2,1)} reshape(bf16[512,7168]{1,0:T(8,128)(2,1)} %add_convert_fusion) | data formatting | bytes 14680064 | tf_op jit(solution)/shard_map/convert_element_type | solution.py:89
  288.5 8.3 %copy.70 = bf16[4,32,4,7168]{3,1,2,0:T(8,128)(2,1)} copy(bf16[4,32,4,7168]{3,2,1,0:T(4,128)(2,1)} %convert_element_type.72) | data formatting | bytes 14680064 | tf_op jit(solution)/shard_map/convert_element_type | solution.py:89
  296.9 71.4 %reduce-scatter.2.cloned.1.call-done = bf16[1,32,4,7168]{3,1,2,0:T(8,128)(2,1)} async-done(((bf16[4,32,4,7168]{3,1,2,0:T(8,128)(2,1)}), bf16[1,32,4,7168]{3,1,2,0:T(8,128)(2,1)}) %reduce-scatter.2.cloned.1.call-update) | async-done | bytes 1835024 | tf_op jit(solution)/shard_map/reduce_scatter | solution.py:86
  368.2 4.1 copy.71
  372.4 7.6 %all-to-all-start.3 = ((bf16[1,32,4,7168]{3,2,0,1:T(4,128)(2,1)}), bf16[1,32,4,7168]{3,2,0,1:T(4,128)(2,1)S(1)}, u32[]{:S(2)}, u32[]{:S(2)}) async-start(bf16[1,32,4,7168]{3,2,0,1:T(4,128)(2,1)} %copy.71), calls=%async_computation.4 | async-start | bytes 3670016 | tf_op jit(solution)/shard_map/all_to_all | solution.py:94
  380.0 5.6 %fusion.2 = bf16[1,128,7168]{2,1,0:T(8,128)(2,1)} fusion(bf16[512,7168]{1,0:T(8,128)(2,1)} %reshape.97, f32[512,128]{1,0:T(8,128)S(1)} %fusion.8, f32[512]{0:T(512)S(1)} %reshape.102, f32[512,128]{1,0:T(8,128)S(1)} %fusion.5), kind=kOutput, calls=%fused_computation.7 | convolution fusion | flops 940900352 | bytes 9701376 | tf_op jit(solution)/shard_map/dot_general | solution.py:10
  385.6 6.4 %fusion.1 = bf16[1,7168,128]{2,1,0:T(8,128)(2,1)} fusion(bf16[512,7168]{1,0:T(8,128)(2,1)} %reshape.98, bf16[512,128]{1,0:T(8,128)(2,1)S(1)} %get-tuple-element.4), kind=kOutput, calls=%fused_computation.6 | convolution fusion | flops 940441600 | bytes 9306112 | tf_op jit(solution)/shard_map/dot_general | solution.py:10
  392.0 6.4 %fusion = bf16[1,7168,128]{2,1,0:T(8,128)(2,1)} fusion(bf16[512,7168]{1,0:T(8,128)(2,1)} %reshape.98, bf16[512,128]{1,0:T(8,128)(2,1)S(1)} %get-tuple-element.5), kind=kOutput, calls=%fused_computation.5 | convolution fusion | flops 940441600 | bytes 9306112 | tf_op jit(solution)/shard_map/dot_general | solution.py:10
  398.4 7.0 %all-to-all-done.3 = bf16[1,32,4,7168]{3,2,0,1:T(4,128)(2,1)S(1)} async-done(((bf16[1,32,4,7168]{3,2,0,1:T(4,128)(2,1)}), bf16[1,32,4,7168]{3,2,0,1:T(4,128)(2,1)S(1)}, u32[]{:S(2)}, u32[]{:S(2)}) %all-to-all-start.3) | async-done | bytes 1835040 | tf_op jit(solution)/shard_map/all_to_all | solution.py:94
  410.8 4.4 %convolution_convert_fusion.3 = bf16[128,7168]{1,0:T(8,128)(2,1)} fusion(pred[128,64]{0,1:T(8,128)(4,1)S(1)} %fusion.18, f32[64,7168]{1,0:T(8,128)} %reshape.101), kind=kOutput, calls=%fused_computation.4 | convolution fusion | flops 705560576 | bytes 3678208 | tf_op jit(solution)/shard_map/dot_general | solution.py:99
  (46 shorter events, 26.1 us)
Async XLA Ops:
  7.2 156.3 %copy-start = (bf16[1,7168,128]{2,1,0:T(8,128)(2,1)S(1)}, bf16[1,7168,128]{2,1,0:T(8,128)(2,1)}, u32[]{:S(2)}) copy-start(bf16[1,7168,128]{2,1,0:T(8,128)(2,1)} %param.11) | copy-start | bytes 5505028
  15.6 20.8 %all-to-all-start = ((bf16[128,1,4]{2,1,0:T(2,128)(2,1)}), bf16[128,1,4]{2,1,0:T(2,128)(2,1)S(1)}, u32[]{:S(2)}, u32[]{:S(2)}) async-start(bf16[128,1,4]{2,1,0:T(2,128)(2,1)} %copy.69), calls=%async_computation | async-start | bytes 131072 | tf_op jit(solution)/shard_map/all_to_all | solution.py:61
  41.9 96.1 %all-to-all-start.2 = ((bf16[128,4,7168]{2,1,0:T(4,128)(2,1)}), bf16[128,4,7168]{2,1,0:T(4,128)(2,1)}, u32[]{:S(2)}, u32[]{:S(2)}) async-start(bf16[128,4,7168]{2,1,0:T(4,128)(2,1)} %bitcast.71), calls=%async_computation.2 | async-start | bytes 14680064 | tf_op jit(solution)/shard_map/all_to_all | solution.py:59
  143.5 97.1 %all-to-all-start.1 = ((bf16[128,4,7168]{2,1,0:T(4,128)(2,1)}), bf16[128,4,7168]{2,1,0:T(4,128)(2,1)}, u32[]{:S(2)}, u32[]{:S(2)}) async-start(bf16[128,4,7168]{2,1,0:T(4,128)(2,1)} %bitcast.70), calls=%async_computation.1 | async-start | bytes 14680064 | tf_op jit(solution)/shard_map/all_to_all | solution.py:60
  150.8 217.4 %reduce-scatter.2.cloned.1.call-start = ((), (), s32[]{:S(2)}) async-start(), calls=%async_computation.5 | async-start | bytes 9175040 | tf_op jit(solution)/shard_map/reduce_scatter | solution.py:86
  163.5 5.3 %copy-start.2 = (bf16[512,7168]{1,0:T(8,128)(2,1)S(1)}, bf16[512,7168]{1,0:T(8,128)(2,1)}, u32[]{:S(2)}) copy-start(bf16[512,7168]{1,0:T(8,128)(2,1)} %reshape.98) | copy-start | bytes 22020100
  163.5 5.7 %copy-start.3 = (bf16[1,7168,128]{2,1,0:T(8,128)(2,1)S(1)}, bf16[1,7168,128]{2,1,0:T(8,128)(2,1)}, u32[]{:S(2)}) copy-start(bf16[1,7168,128]{2,1,0:T(8,128)(2,1)} %param.12) | copy-start | bytes 5505028
  258.3 7.3 %copy-start.4 = (bf16[1,7168,128]{2,1,0:T(8,128)(2,1)S(1)}, bf16[1,7168,128]{2,1,0:T(8,128)(2,1)}, u32[]{:S(2)}) copy-start(bf16[1,7168,128]{2,1,0:T(8,128)(2,1)} %param.12) | copy-start | bytes 5505028
  372.4 33.1 %all-to-all-start.3 = ((bf16[1,32,4,7168]{3,2,0,1:T(4,128)(2,1)}), bf16[1,32,4,7168]{3,2,0,1:T(4,128)(2,1)S(1)}, u32[]{:S(2)}, u32[]{:S(2)}) async-start(bf16[1,32,4,7168]{3,2,0,1:T(4,128)(2,1)} %copy.71), calls=%async_computation.4 | async-start | bytes 3670016 | tf_op jit(solution)/shard_map/all_to_all | solution.py:94
  407.7 7.5 %copy-start.1 = (bf16[1,7168,128]{2,1,0:T(8,128)(2,1)S(1)}, bf16[1,7168,128]{2,1,0:T(8,128)(2,1)}, u32[]{:S(2)}) copy-start(bf16[1,7168,128]{2,1,0:T(8,128)(2,1)} %param.11) | copy-start | bytes 5505028
Sparse Core Ops, SparseCore 0:
  297.0 71.1 reduce-scatter.1
where the time goes:
time: 424 us; the launch traced here: 422 us
  waiting for transfers between devices  237 us (56%)
  local copies, waits for them, and re-layouts  70.9 us (17%)
  matrix products  59.3 us (14%)
  starting transfers between devices  33 us (8%)
  between operations  14.2 us (3%)
  other arithmetic  7.89 us (2%)
    all_to_all x1, waiting for transfers between devices, body(): lax.all_to_all(x_out, ('grp', 'loc'), split_axis=0, concat_axis=0, tiled=...  85.2 us
    reduce_scatter x1, waiting for transfers between devices, body(): lax.psum_scatter(partial_value.astype(jnp.float32).reshape(group_count, l...  71.4 us
    all_to_all x1, waiting for transfers between devices, body(): lax.all_to_all(g_out, ('grp', 'loc'), split_axis=0, concat_axis=0, tiled=...  69.4 us
    dot_general x3, matrix products, contract_cols(): lax.dot_general(left, right, (((1,), (1,)), ((), ())), preferred_element_...  23.2 us
    convert_element_type x2, local copies, waits for them, and re-layouts, body(): reduced = lax.psum_scatter(partial_value.astype(jnp.float32).reshape(grou...  21 us
    dot_general x3, matrix products, contract_rows(): lax.dot_general(left, right, (((0,), (0,)), ((), ())), preferred_element_...  18.5 us
    reshape x1, local copies, waits for them, and re-layouts, body(): x_rows = x_recv.reshape(row_total, width)  12.1 us
    reshape x1, local copies, waits for them, and re-layouts, body(): g_rows = g_recv.reshape(row_total, width)  12.1 us
  transfers between devices with their start and end apart: 5, of which 5 were waited for; matrix products, arithmetic and copies ran while one was open for 11% of the time, Pallas kernels for 0%

commit v1 on v0

v1 whole, which is shorter than its diff:
```python
import functools

import jax
import jax.numpy as jnp
from jax import lax
from jax.experimental import pallas as pl
from jax.experimental.pallas import tpu as pltpu
from jax.sharding import PartitionSpec as P

CAP = 4
BF = jnp.bfloat16
F32 = jnp.float32
MIB = 1 << 20


def contract_rows(left, right):
    return lax.dot_general(left, right, (((0,), (0,)), ((), ())), preferred_element_type=F32)


def contract_cols(left, right):
    return lax.dot_general(left, right, (((1,), (1,)), ((), ())), preferred_element_type=F32)


def cost(flops, nbytes):
    return pl.CostEstimate(flops=flops, bytes_accessed=nbytes, transcendentals=0)


def params(mib):
    return pltpu.CompilerParams(vmem_limit_bytes=mib * MIB)


def dispatch_kernel(ids_ref, w_ref, t_ref, g_ref, table_ref, x_ref, gw_ref, tab, wtab):
    tok, topk = ids_ref.shape
    buf = tab.shape[1]

    @pl.when(pl.program_id(0) == 0)
    def _():
        column = lax.broadcasted_iota(jnp.int32, (tok, buf), 1)
        expert = lax.div(column, CAP)
        chosen = jnp.zeros((tok, buf), F32)
        weight = jnp.zeros((tok, buf), F32)
        for k in range(topk):
            hit = ids_ref[:, k : k + 1] == expert
            chosen = jnp.where(hit, 1.0, chosen)
            weight = jnp.where(hit, w_ref[:, k : k + 1].astype(F32), weight)
        row = lax.broadcasted_iota(jnp.int32, (tok, tok), 0)
        col = lax.broadcasted_iota(jnp.int32, (tok, tok), 1)
        earlier = jnp.where(col < row, 1.0, 0.0).astype(BF)
        slot = jnp.dot(earlier, chosen.astype(BF), preferred_element_type=F32)
        want = lax.rem(column, CAP).astype(F32)
        mine = (chosen > 0.5) & (slot == want)
        table = jnp.where(mine, 1.0, 0.0).astype(BF)
        tab[...] = table
        wtab[...] = jnp.where(mine, weight, 0.0).astype(BF)
        table_ref[...] = table

    rows = contract_rows(tab[...], t_ref[...])
    rows = rows.reshape(buf // CAP, CAP, rows.shape[1]).astype(BF)
    x_ref[0] = rows
    x_ref[1] = rows
    gw_ref[...] = contract_rows(wtab[...], g_ref[...]).astype(BF)


def dispatch(ids, weights, tokens, grad_out, expert_fl):
    tok, width = tokens.shape
    buf = expert_fl * CAP
    tile = 1024
    return pl.pallas_call(
        dispatch_kernel,
        grid=(width // tile,),
        in_specs=[
            pl.BlockSpec(ids.shape, lambda j: (0, 0)),
            pl.BlockSpec(weights.shape, lambda j: (0, 0)),
            pl.BlockSpec((tok, tile), lambda j: (0, j)),
            pl.BlockSpec((tok, tile), lambda j: (0, j)),
        ],
        out_specs=[
            pl.BlockSpec((tok, buf), lambda j: (0, 0)),
            pl.BlockSpec((2, expert_fl, CAP, tile), lambda j: (0, 0, 0, j)),
            pl.BlockSpec((buf, tile), lambda j: (0, j)),
        ],
        out_shape=[
            jax.ShapeDtypeStruct((tok, buf), BF),
            jax.ShapeDtypeStruct((2, expert_fl, CAP, width), BF),
            jax.ShapeDtypeStruct((buf, width), BF),
        ],
        scratch_shapes=[pltpu.VMEM((tok, buf), BF), pltpu.VMEM((tok, buf), BF)],
        compiler_params=params(16),
        cost_estimate=cost(4 * tok * buf * width, 2 * width * (2 * tok + 3 * buf)),
        name="dispatch",
    )(ids, weights, tokens, grad_out)


def regroup_kernel(in_ref, out_ref):
    groups, buf, tile = in_ref.shape
    experts = buf // CAP
    blocks = [in_ref[y].astype(F32).reshape(experts, CAP, tile) for y in range(groups)]
    rows = jnp.concatenate(blocks, axis=1).astype(BF)
    out_ref[0] = rows
    out_ref[1] = rows


def regroup(rows):
    groups, buf, width = rows.shape
    experts = buf // CAP
    tile = 512
    return pl.pallas_call(
        regroup_kernel,
        grid=(width // tile,),
        in_specs=[pl.BlockSpec((groups, buf, tile), lambda j: (0, 0, j))],
        out_specs=pl.BlockSpec((2, experts, groups * CAP, tile), lambda j: (0, 0, 0, j)),
        out_shape=jax.ShapeDtypeStruct((2, experts, groups * CAP, width), BF),
        compiler_params=params(24),
        cost_estimate=cost(0, 6 * groups * buf * width),
        name="regroup",
    )(rows)


def row_part_kernel(gd_ref, ud_ref, wg_ref, wu_ref, out_ref):
    total = contract_cols(gd_ref[...], wg_ref[...]) + contract_cols(ud_ref[...], wu_ref[...])
    out_ref[...] = total.astype(BF)


def row_part(gate_delta, up_delta, w_gate, w_up, first, count):
    rows, ff = gate_delta.shape
    tile = 512
    skip = first // tile
    return pl.pallas_call(
        row_part_kernel,
        grid=(count // tile,),
        in_specs=[
            pl.BlockSpec((rows, ff), lambda j: (0, 0)),
            pl.BlockSpec((rows, ff), lambda j: (0, 0)),
            pl.BlockSpec((tile, ff), lambda j: (j + skip, 0)),
            pl.BlockSpec((tile, ff), lambda j: (j + skip, 0)),
        ],
        out_specs=pl.BlockSpec((rows, tile), lambda j: (0, j)),
        out_shape=jax.ShapeDtypeStruct((rows, count), BF),
        compiler_params=params(16),
        cost_estimate=cost(4 * rows * ff * count, 2 * count * (rows + 2 * ff)),
        name="row_part",
    )(gate_delta, up_delta, w_gate, w_up)


def fold_kernel(in_ref, out_ref):
    _, experts, depth, tile = in_ref.shape
    groups = depth // CAP
    total = in_ref[0].astype(F32) + in_ref[1].astype(F32)
    for y in range(groups):
        part = total[:, y * CAP : (y + 1) * CAP, :]
        out_ref[y] = part.reshape(experts * CAP, tile).astype(BF)


def fold(home):
    _, experts, depth, width = home.shape
    groups = depth // CAP
    tile = 512
    return pl.pallas_call(
        fold_kernel,
        grid=(width // tile,),
        in_specs=[pl.BlockSpec((2, experts, depth, tile), lambda j: (0, 0, 0, j))],
        out_specs=pl.BlockSpec((groups, experts * CAP, tile), lambda j: (0, 0, j)),
        out_shape=jax.ShapeDtypeStruct((groups, experts * CAP, width), BF),
        compiler_params=params(24),
        cost_estimate=cost(experts * depth * width, 6 * experts * depth * width),
        name="fold",
    )(home)


def combine_kernel(split, table_ref, ring_ref, whole_ref, out_ref):
    table = table_ref[...]

    @pl.when(pl.program_id(0) < split)
    def _():
        out_ref[...] = jnp.dot(table, ring_ref[...], preferred_element_type=F32).astype(BF)

    @pl.when(pl.program_id(0) >= split)
    def _():
        count, _, tile = whole_ref.shape
        rows = whole_ref[...].astype(F32).reshape(count * CAP, tile).astype(BF)
        both = jnp.concatenate([table, table], axis=1)
        out_ref[...] = jnp.dot(both, rows, preferred_element_type=F32).astype(BF)


def combine(table, ring, whole):
    tok, buf = table.shape
    tile = 512
    width = ring.shape[1] + whole.shape[2]
    split = ring.shape[1] // tile
    return pl.pallas_call(
        functools.partial(combine_kernel, split),
        grid=(width // tile,),
        in_specs=[
            pl.BlockSpec((tok, buf), lambda j: (0, 0)),
            pl.BlockSpec((buf, tile), lambda j: (0, jnp.minimum(j, split - 1))),
            pl.BlockSpec((whole.shape[0], CAP, tile), lambda j: (0, 0, jnp.maximum(j - split, 0))),
        ],
        out_specs=pl.BlockSpec((tok, tile), lambda j: (0, j)),
        out_shape=jax.ShapeDtypeStruct((tok, width), BF),
        compiler_params=params(16),
        cost_estimate=cost(2 * tok * buf * width, 2 * width * (tok + 2 * buf)),
        name="combine",
    )(table, ring, whole)


def body(tokens, grad_out, expert_ids, route_weight, gate_weight, up_weight, down_weight):
    groups = lax.axis_size("grp")
    locs = lax.axis_size("loc")
    expert_fl = locs // 2
    width = tokens.shape[1]
    buf = expert_fl * CAP
    rows = groups * locs * CAP
    ring_cols = 3072

    w_gate, w_up, w_down = gate_weight[0], up_weight[0], down_weight[0]
    ff = w_gate.shape[1]

    table, x_send, g_send = dispatch(expert_ids, route_weight, tokens, grad_out, expert_fl)

    g_ring = lax.all_gather(g_send, "grp", axis=0, tiled=False)
    g_out = regroup(g_ring).reshape(locs, groups * CAP, width)
    x_here = lax.all_to_all(
        x_send.reshape(locs, CAP, width), "loc", split_axis=0, concat_axis=0, tiled=True
    )
    x_rows = lax.all_gather(x_here, "grp", axis=0, tiled=True).reshape(rows, width)
    g_rows = lax.all_to_all(g_out, "loc", split_axis=0, concat_axis=0, tiled=True).reshape(
        rows, width
    )

    def to_loc_first(a):
        return a.reshape(groups, locs, CAP, ff).transpose(1, 0, 2, 3).reshape(rows, ff)

    def to_grp_first(a):
        return a.reshape(locs, groups, CAP, ff).transpose(1, 0, 2, 3).reshape(rows, ff)

    pre_gate = to_loc_first(jnp.dot(x_rows, w_gate, preferred_element_type=F32))
    pre_up = to_loc_first(jnp.dot(x_rows, w_up, preferred_element_type=F32))
    sig = jax.nn.sigmoid(pre_gate)
    swish = pre_gate * sig
    slope = pre_up * sig * (1.0 + pre_gate * (1.0 - sig))
    unweighted = (swish * pre_up).astype(BF)

    hidden_grad = contract_cols(g_rows, w_down)
    gate_delta = (hidden_grad * slope).astype(BF)
    up_delta = (hidden_grad * swish).astype(BF)
    gate_delta_x = to_grp_first(gate_delta)
    up_delta_x = to_grp_first(up_delta)

    part_ring = row_part(gate_delta, up_delta, w_gate, w_up, 0, ring_cols)
    home_ring = lax.all_to_all(
        part_ring.reshape(locs, groups * CAP, ring_cols),
        "loc",
        split_axis=0,
        concat_axis=0,
        tiled=True,
    )
    part_whole = row_part(gate_delta_x, up_delta_x, w_gate, w_up, ring_cols, width - ring_cols)
    reduced = lax.psum_scatter(
        part_whole.reshape(groups, locs * CAP, width - ring_cols),
        "grp",
        scatter_dimension=0,
        tiled=True,
    )
    home_whole = lax.all_to_all(
        reduced.reshape(locs, CAP, width - ring_cols),
        "loc",
        split_axis=0,
        concat_axis=0,
        tiled=True,
    )
    folded = fold(home_ring.reshape(2, expert_fl, groups * CAP, ring_cols))
    ring = lax.psum_scatter(folded, "grp", scatter_dimension=0, tiled=True)

    gate_grad = contract_rows(x_rows, gate_delta_x).astype(BF)[None]
    up_grad = contract_rows(x_rows, up_delta_x).astype(BF)[None]
    down_grad = contract_rows(unweighted, g_rows).astype(BF)[None]
    tokens_grad = combine(table, ring.reshape(buf, ring_cols), home_whole)
    return (tokens_grad, gate_grad, up_grad, down_grad)


def solution(mesh):
    in_specs = (
        P(("grp", "loc"), None),
        P(("grp", "loc"), None),
        P(("grp", "loc"), None),
        P(("grp", "loc"), None),
        P("loc", None, "grp"),
        P("loc", None, "grp"),
        P("loc", "grp", None),
    )
    out_specs = (
        P(("grp", "loc"), None),
        P("loc", None, "grp"),
        P("loc", None, "grp"),
        P("loc", "grp", None),
    )
    return jax.shard_map(body, mesh=mesh, in_specs=in_specs, out_specs=out_specs, check_vma=False)
```

time: 424 us -> 314 us (0.74)
  waiting for transfers between devices: 237 us -> 93.2 us
  blocking collectives: 0 us -> 98.6 us
  matrix products: 59.3 us -> 28.6 us
  local copies, waits for them, and re-layouts: 70.9 us -> 45.5 us
  Pallas kernels: 0 us -> 21.8 us
  starting transfers between devices: 33 us -> 11.8 us
  other arithmetic: 7.89 us -> 0 us
    all_to_all x4 -> x2, waiting for transfers between devices: 165 us -> 20.5 us  [the longest x1 20.5 us: body(): lax.all_to_all(g_out, 'loc', split_axis=0, concat_axis=0, tiled=True)]
    all_to_all x0 -> x2, blocking collectives: none -> 98.6 us  [the longest x1 63.7 us: body(): lax.all_to_all(part_ring.reshape(locs, groups * CAP, ring_cols), 'loc', s...]
    all_gather x0 -> x2, waiting for transfers between devices: none -> 72.6 us  [the longest x1 62.1 us: body(): lax.all_gather(x_here, 'grp', axis=0, tiled=True).reshape(rows, width)]
    reduce_scatter x1 -> x2, waiting for transfers between devices: 71.4 us -> 0.02 us  [the longest x1 0.02 us: body(): lax.psum_scatter(part_whole.reshape(groups, locs * CAP, width - ring_cols...]
    pallas_call x0 -> x6, Pallas kernels: none -> 21.8 us  [the longest x2 6.52 us: row_part(): pl.pallas_call(row_part_kernel, grid=(count // tile,), in_specs=[pl.Block...]
    all_to_all x4 -> x2, starting transfers between devices: 32.8 us -> 11.7 us  [the longest x1 7.72 us: body(): lax.all_to_all(g_out, 'loc', split_axis=0, concat_axis=0, tiled=True)]
    convert_element_type x3 -> x1, local copies, waits for them, and re-layouts: 21.1 us -> 0.07 us  [body(): unweighted = (swish * pre_up).astype(BF)]
    dot_general x3 -> x1, matrix products: 23.2 us -> 5.29 us  [contract_cols(): lax.dot_general(left, right, (((1,), (1,)), ((), ())), preferred_element_...]
  transfers between devices with their start and end apart: 5 -> 6, of which waited for: 5 -> 3; matrix products, arithmetic and copies ran while one was open for 11% -> 16% of each run, Pallas kernels for 0% -> 2%
where the time goes in v1:
time: 314 us; the launch traced here: 313 us
  blocking collectives  98.6 us (31%)
  waiting for transfers between devices  93.2 us (30%)
  local copies, waits for them, and re-layouts  45.5 us (14%)
  matrix products  28.6 us (9%)
  Pallas kernels  21.8 us (7%)
  between operations  13.9 us (4%)
  starting transfers between devices  11.8 us (4%)
    all_to_all x1, blocking collectives, body(): lax.all_to_all(part_ring.reshape(locs, groups * CAP, ring_cols), 'loc', s...  63.7 us
    all_gather x1, waiting for transfers between devices, body(): lax.all_gather(x_here, 'grp', axis=0, tiled=True).reshape(rows, width)  62.1 us
    all_to_all x1, blocking collectives, body(): lax.all_to_all(x_send.reshape(locs, CAP, width), 'loc', split_axis=0, con...  34.9 us
    all_to_all x1, waiting for transfers between devices, body(): lax.all_to_all(g_out, 'loc', split_axis=0, concat_axis=0, tiled=True)  20.5 us
    unnamed x34, local copies, waits for them, and re-layouts  17.1 us
    dot_general x3, matrix products, contract_rows(): lax.dot_general(left, right, (((0,), (0,)), ((), ())), preferred_element_...  15.4 us
    reshape x1, local copies, waits for them, and re-layouts, body(): lax.all_gather(x_here, 'grp', axis=0, tiled=True).reshape(rows, width)  12.1 us
    all_gather x1, local copies, waits for them, and re-layouts, body(): lax.all_gather(x_here, 'grp', axis=0, tiled=True).reshape(rows, width)  11.8 us
  transfers between devices with their start and end apart: 6, of which 3 were waited for; matrix products, arithmetic and copies ran while one was open for 16% of the time, Pallas kernels for 2%

profile of v1, /device:TPU:1, one launch (start us, length us, event | category | flops | bytes accessed | tf_op | source)
XLA Modules:
  0.0 313.5 jit_solution(12211937656231273021)
XLA Ops:
  11.9 4.2 %dispatch.1 = (bf16[128,64]{1,0:T(8,128)(2,1)S(1)}, bf16[2,16,4,7168]{3,2,1,0:T(4,128)(2,1)S(1)}, bf16[64,7168]{1,0:T(8,128)(2,1)}) custom-call(s32[128,8]{1,0:T(8,128)S(1)} %copy.38.ids_ref, bf16[128,8]{1,0:T(8,128)(2,1)S(1)} %copy.39.w_ref, bf16[128,7168]{1,0:T(8,128)(2,1)S(1)} %copy-done.10, bf16[128,7168]{1,0:T(8,128)(2,1)S(1)} %copy-done.11), custom_call_target="tpu_custom_call" | custom-call | flops 234881024 | bytes 6422528 | tf_op jit(solution)/shard_map/dispatch/pallas_call | solution.py:68
  17.5 34.9 %all_to_all.20 = bf16[32,4,7168]{2,1,0:T(4,128)(2,1)S(1)} all-to-all(bf16[32,4,7168]{2,1,0:T(4,128)(2,1)} %bitcast.71), channel_id=1, replica_groups=mesh['grp'=4,'loc'=32] {'loc'}, dimensions={0} | all-to-all | bytes 3670016 | tf_op jit(solution)/shard_map/all_to_all | solution.py:222
  54.2 10.5 %all-gather.6.cloned.1.call-done = bf16[256,7168]{1,0:T(8,128)(2,1)} async-done(((bf16[64,7168]{1,0:T(8,128)(2,1)}), bf16[256,7168]{1,0:T(8,128)(2,1)}) %all-gather.6.cloned.1.call-update) | async-done | bytes 3670032 | tf_op jit(solution)/shard_map/all_gather | solution.py:220
  64.7 2.0 copy-done.9
  66.8 2.0 regroup.1
  68.8 2.9 copy-done.2
  71.7 7.7 %all-to-all-start = ((bf16[32,16,7168]{2,1,0:T(8,128)(2,1)}), bf16[32,16,7168]{2,1,0:T(8,128)(2,1)}, u32[]{:S(2)}, u32[]{:S(2)}) async-start(bf16[32,16,7168]{2,1,0:T(8,128)(2,1)} %bitcast.62), calls=%async_computation | async-start | bytes 14680064 | tf_op jit(solution)/shard_map/all_to_all | solution.py:226
  79.5 62.1 %all-gather.4.cloned.1.call-done = bf16[128,4,7168]{2,0,1:T(8,128)(2,1)} async-done(((bf16[32,4,7168]{2,0,1:T(8,128)(2,1)}), bf16[128,4,7168]{2,0,1:T(8,128)(2,1)}) %all-gather.4.cloned.1.call-update) | async-done | bytes 7340048 | tf_op jit(solution)/shard_map/all_gather | solution.py:225
  141.6 5.8 %fusion.16 = f32[32,4,4,128]{3,0,2,1:T(8,128)S(1)} fusion(bf16[1,7168,128]{2,1,0:T(8,128)(2,1)} %param.11, bf16[4,32,4,7168]{3,1,0,2:T(8,128)(2,1)} %bitcast.79), kind=kOutput, calls=%fused_computation.15 | convolution fusion | flops 939524096 | bytes 9437184 | tf_op jit(solution)/shard_map/dot_general | solution.py:236
  147.9 2.1 multiply_convert_fusion
  150.1 20.5 %all-to-all-done = bf16[32,16,7168]{2,1,0:T(8,128)(2,1)} async-done(((bf16[32,16,7168]{2,1,0:T(8,128)(2,1)}), bf16[32,16,7168]{2,1,0:T(8,128)(2,1)}, u32[]{:S(2)}, u32[]{:S(2)}) %all-to-all-start) | async-done | bytes 7340064 | tf_op jit(solution)/shard_map/all_to_all | solution.py:226
  170.6 5.3 %multiply_convert_fusion.1 = (bf16[512,128]{1,0:T(8,128)(2,1)S(1)}, bf16[512,128]{1,0:T(8,128)(2,1)S(1)}) fusion(f32[512,128]{1,0:T(8,128)S(1)} %bitcast.82, f32[512,128]{1,0:T(8,128)S(1)} %bitcast.83, bf16[512,7168]{1,0:T(8,128)(2,1)} %bitcast.2, bf16[1,128,7168]{2,1,0:T(8,128)(2,1)S(1)} %copy-done), kind=kOutput, calls=%fused_computation.17 | convolution fusion | flops 940376064 | bytes 9961472 | tf_op jit(solution)/shard_map/dot_general | solution.py:21
  176.0 3.7 %row_part.3 = bf16[512,4096]{1,0:T(8,128)(2,1)S(1)} custom-call(bf16[512,128]{1,0:T(8,128)(2,1)S(1)} %bitcast.72, bf16[512,128]{1,0:T(8,128)(2,1)S(1)} %bitcast.74, bf16[7168,128]{1,0:T(8,128)(2,1)S(1)} %bitcast.66, bf16[7168,128]{1,0:T(8,128)(2,1)S(1)} %bitcast.68), custom_call_target="tpu_custom_call" | custom-call | flops 1073741824 | bytes 6291456 | tf_op jit(solution)/shard_map/row_part/pallas_call | solution.py:128
  184.7 2.8 row_part.2
  187.5 63.7 %all_to_all.21 = bf16[32,16,3072]{2,1,0:T(8,128)(2,1)S(1)} all-to-all(bf16[32,16,3072]{2,1,0:T(8,128)(2,1)S(1)} %bitcast.64), channel_id=1, replica_groups=mesh['grp'=4,'loc'=32] {'loc'}, dimensions={0} | all-to-all | bytes 6291456 | tf_op jit(solution)/shard_map/all_to_all | solution.py:250
  251.2 2.6 fold.1
  254.0 2.2 reshape.73
  256.2 4.0 %all-to-all-start.3 = ((bf16[32,4,4096]{2,1,0:T(4,128)(2,1)}), bf16[32,4,4096]{2,1,0:T(4,128)(2,1)S(1)}, u32[]{:S(2)}, u32[]{:S(2)}) async-start(bf16[32,4,4096]{2,1,0:T(4,128)(2,1)} %reshape.73), calls=%async_computation.5 | async-start | bytes 2097152 | tf_op jit(solution)/shard_map/all_to_all | solution.py:264
  260.2 5.5 %fusion.2 = bf16[1,128,7168]{2,1,0:T(8,128)(2,1)} fusion(bf16[512,128]{1,0:T(8,128)(2,1)S(1)} %bitcast.81, bf16[512,7168]{1,0:T(8,128)(2,1)} %bitcast.2), kind=kOutput, calls=%fused_computation.5 | convolution fusion | flops 940441600 | bytes 9306112 | tf_op jit(solution)/shard_map/dot_general | solution.py:17
  265.7 11.8 %copy.47 = bf16[128,4,7168]{2,1,0:T(4,128)(2,1)} copy(bf16[128,4,7168]{2,0,1:T(8,128)(2,1)} %all-gather.4.cloned.1.call-done) | data formatting | bytes 14680064 | tf_op jit(solution)/shard_map/all_gather | solution.py:225
  277.5 12.1 %reshape.74 = bf16[512,7168]{1,0:T(8,128)(2,1)} reshape(bf16[128,4,7168]{2,1,0:T(4,128)(2,1)} %copy.47) | data formatting | bytes 14680064 | tf_op jit(solution)/shard_map/reshape | solution.py:225
  289.6 6.6 %fusion.1 = bf16[1,7168,128]{2,1,0:T(8,128)(2,1)} fusion(bf16[512,7168]{1,0:T(8,128)(2,1)} %reshape.74, bf16[512,128]{1,0:T(8,128)(2,1)S(1)} %bitcast.75), kind=kOutput, calls=%fused_computation.4 | convolution fusion | flops 940441600 | bytes 9306112 | tf_op jit(solution)/shard_map/dot_general | solution.py:17
  296.2 3.4 %fusion = bf16[1,7168,128]{2,1,0:T(8,128)(2,1)} fusion(bf16[512,7168]{1,0:T(8,128)(2,1)S(1)} %copy-done.14, bf16[512,128]{1,0:T(8,128)(2,1)S(1)} %bitcast.73), kind=kOutput, calls=%fused_computation.3 | convolution fusion | flops 940441600 | bytes 9306112 | tf_op jit(solution)/shard_map/dot_general | solution.py:17
  300.6 6.4 %combine.1 = bf16[128,7168]{1,0:T(8,128)(2,1)} custom-call(bf16[128,64]{1,0:T(8,128)(2,1)S(1)} %get-tuple-element.7.table_ref, bf16[64,3072]{1,0:T(8,128)(2,1)S(1)} %bitcast.78, bf16[32,4,4096]{2,1,0:T(4,128)(2,1)S(1)} %all-to-all-done.3.whole_ref), custom_call_target="tpu_custom_call" | custom-call | flops 117440512 | bytes 3670016 | tf_op jit(solution)/shard_map/combine/pallas_call | solution.py:190
  (49 shorter events, 14.7 us)
Async XLA Ops:
  7.2 163.4 %copy-start = (bf16[1,128,7168]{2,1,0:T(8,128)(2,1)S(1)}, bf16[1,128,7168]{2,1,0:T(8,128)(2,1)}, u32[]{:S(2)}) copy-start(bf16[1,128,7168]{2,1,0:T(8,128)(2,1)} %param.13) | copy-start | bytes 5505028
  7.2 57.5 %all-gather.6.cloned.1.call-start = ((), (), s32[]{:S(2)}) async-start(), calls=%async_computation.9 | async-start | bytes 4587520 | tf_op jit(solution)/shard_map/all_gather | solution.py:220
  8.9 1.5 copy-start.10
  10.4 1.5 copy-start.11
  16.2 1.2 copy-start.12
  17.4 124.2 %all-gather.4.cloned.1.call-start = ((), (), s32[]{:S(2)}) async-start(), calls=%async_computation.6 | async-start | bytes 9175040 | tf_op jit(solution)/shard_map/all_gather | solution.py:225
  64.7 2.0 copy-start.9
  68.8 3.0 copy-start.2
  71.7 98.8 %all-to-all-start = ((bf16[32,16,7168]{2,1,0:T(8,128)(2,1)}), bf16[32,16,7168]{2,1,0:T(8,128)(2,1)}, u32[]{:S(2)}, u32[]{:S(2)}) async-start(bf16[32,16,7168]{2,1,0:T(8,128)(2,1)} %bitcast.62), calls=%async_computation | async-start | bytes 14680064 | tf_op jit(solution)/shard_map/all_to_all | solution.py:226
  79.5 174.5 %reduce-scatter.5.cloned.1.call-start = ((), (), s32[]{:S(2)}) async-start(), calls=%async_computation.8 | async-start | bytes 5242880 | tf_op jit(solution)/shard_map/reduce_scatter | solution.py:258
  141.6 6.0 %copy-start.6 = (bf16[1,7168,128]{2,1,0:T(8,128)(2,1)S(1)}, bf16[1,7168,128]{2,1,0:T(8,128)(2,1)}, u32[]{:S(2)}) copy-start(bf16[1,7168,128]{2,1,0:T(8,128)(2,1)} %param.12) | copy-start | bytes 5505028
  141.6 6.3 %copy-start.15 = (bf16[128,4,7168]{2,0,1:T(8,128)(2,1)S(1)}, bf16[128,4,7168]{2,0,1:T(8,128)(2,1)}, u32[]{:S(2)}) copy-start(bf16[128,4,7168]{2,0,1:T(8,128)(2,1)} %all-gather.4.cloned.1.call-done) | copy-start | bytes 22020100
  170.6 5.4 %copy-start.4 = (bf16[1,7168,128]{2,1,0:T(8,128)(2,1)S(1)}, bf16[1,7168,128]{2,1,0:T(8,128)(2,1)}, u32[]{:S(2)}) copy-start(bf16[1,7168,128]{2,1,0:T(8,128)(2,1)} %param.11) | copy-start | bytes 5505028
  170.6 5.4 %copy-start.7 = (bf16[1,7168,128]{2,1,0:T(8,128)(2,1)S(1)}, bf16[1,7168,128]{2,1,0:T(8,128)(2,1)}, u32[]{:S(2)}) copy-start(bf16[1,7168,128]{2,1,0:T(8,128)(2,1)} %param.12) | copy-start | bytes 5505028
  179.8 2.0 copy-start.3
  181.7 1.5 copy-start.8
  181.7 117.8 %reduce-scatter.3.cloned.1.call-start = ((), (), s32[]{:S(2)}) async-start(), calls=%async_computation.7 | async-start | bytes 1966080 | tf_op jit(solution)/shard_map/reduce_scatter | solution.py:272
  183.2 1.5 copy-start.5
  256.2 43.3 %all-to-all-start.3 = ((bf16[32,4,4096]{2,1,0:T(4,128)(2,1)}), bf16[32,4,4096]{2,1,0:T(4,128)(2,1)S(1)}, u32[]{:S(2)}, u32[]{:S(2)}) async-start(bf16[32,4,4096]{2,1,0:T(4,128)(2,1)} %reshape.73), calls=%async_computation.5 | async-start | bytes 2097152 | tf_op jit(solution)/shard_map/all_to_all | solution.py:264
  289.6 6.6 %copy-start.14 = (bf16[512,7168]{1,0:T(8,128)(2,1)S(1)}, bf16[512,7168]{1,0:T(8,128)(2,1)}, u32[]{:S(2)}) copy-start(bf16[512,7168]{1,0:T(8,128)(2,1)} %reshape.74) | copy-start | bytes 22020100
  296.2 10.8 %copy-start.1 = (bf16[1,128,7168]{2,1,0:T(8,128)(2,1)S(1)}, bf16[1,128,7168]{2,1,0:T(8,128)(2,1)}, u32[]{:S(2)}) copy-start(bf16[1,128,7168]{2,1,0:T(8,128)(2,1)} %param.13) | copy-start | bytes 5505028
  299.6 1.0 copy-start.13
Sparse Core Ops, SparseCore 0:
  17.6 47.1 all-gather.5
  67.0 74.6 all-gather.3
  181.9 63.9 reduce-scatter.4
  254.0 21.2 reduce-scatter.2

commit v2 on v0

v2 whole, which is shorter than its diff:
```python
import functools

import jax
import jax.numpy as jnp
from jax import lax
from jax.experimental import pallas as pl
from jax.experimental.pallas import tpu as pltpu
from jax.sharding import PartitionSpec as P

CAP = 4
BF = jnp.bfloat16
F32 = jnp.float32
TILE = 1024


def contract_rows(left, right):
    return lax.dot_general(left, right, (((0,), (0,)), ((), ())), preferred_element_type=F32)


def contract_cols(left, right):
    return lax.dot_general(left, right, (((1,), (1,)), ((), ())), preferred_element_type=F32)


def whole(shape):
    return pl.BlockSpec(shape, lambda *_: (0,) * len(shape))


def call(kernel, name, flops, nbytes, mib=56, **kwargs):
    return pl.pallas_call(
        kernel,
        name=name,
        compiler_params=pltpu.CompilerParams(vmem_limit_bytes=mib << 20),
        cost_estimate=pl.CostEstimate(flops=flops, bytes_accessed=nbytes, transcendentals=0),
        **kwargs,
    )


def dispatch_kernel(ids_ref, w_ref, t_ref, g_ref, table_ref, xg_ref, gw_ref, pick, wtab):
    tok, topk = ids_ref.shape
    buf = wtab.shape[1]
    experts = buf // CAP
    unit = 2 * CAP

    @pl.when(pl.program_id(0) == 0)
    def _():
        def tables(columns, expert, want):
            chosen = jnp.zeros((tok, columns), F32)
            weight = jnp.zeros((tok, columns), F32)
            for k in range(topk):
                hit = ids_ref[:, k : k + 1] == expert
                chosen = jnp.where(hit, 1.0, chosen)
                weight = jnp.where(hit, w_ref[:, k : k + 1].astype(F32), weight)
            slot = jnp.dot(earlier, chosen.astype(BF), preferred_element_type=F32)
            mine = (chosen > 0.5) & (slot == want)
            return jnp.where(mine, 1.0, 0.0), jnp.where(mine, weight, 0.0)

        row = lax.broadcasted_iota(jnp.int32, (tok, tok), 0)
        col = lax.broadcasted_iota(jnp.int32, (tok, tok), 1)
        earlier = jnp.where(col < row, 1.0, 0.0).astype(BF)

        column = lax.broadcasted_iota(jnp.int32, (tok, buf), 1)
        table, weighted = tables(buf, lax.div(column, CAP), lax.rem(column, CAP).astype(F32))
        table_ref[...] = table.astype(BF)
        wtab[...] = weighted.astype(BF)

        column = lax.broadcasted_iota(jnp.int32, (tok, experts * unit), 1)
        table, weighted = tables(
            experts * unit, lax.div(column, unit), lax.rem(column, CAP).astype(F32)
        )
        is_token = lax.rem(column, unit) < CAP
        pick[0] = jnp.where(is_token, table, 0.0).astype(BF)
        pick[1] = jnp.where(is_token, 0.0, weighted).astype(BF)

    rows = contract_rows(pick[0], t_ref[...]) + contract_rows(pick[1], g_ref[...])
    rows = rows.astype(BF).reshape(experts, unit, rows.shape[1])
    xg_ref[0] = rows
    xg_ref[1] = rows
    gw_ref[...] = contract_rows(wtab[...], g_ref[...]).astype(BF)


def dispatch(ids, weights, tokens, grad_out, experts):
    tok, width = tokens.shape
    buf = experts * CAP
    return call(
        dispatch_kernel,
        "dispatch",
        12 * tok * buf * width,
        2 * width * (2 * tok + 5 * buf),
        grid=(width // TILE,),
        in_specs=[
            whole(ids.shape),
            whole(weights.shape),
            pl.BlockSpec((tok, TILE), lambda j: (0, j)),
            pl.BlockSpec((tok, TILE), lambda j: (0, j)),
        ],
        out_specs=[
            whole((tok, buf)),
            pl.BlockSpec((2, experts, 2 * CAP, TILE), lambda j: (0, 0, 0, j)),
            pl.BlockSpec((buf, TILE), lambda j: (0, j)),
        ],
        out_shape=[
            jax.ShapeDtypeStruct((tok, buf), BF),
            jax.ShapeDtypeStruct((2, experts, 2 * CAP, width), BF),
            jax.ShapeDtypeStruct((buf, width), BF),
        ],
        scratch_shapes=[pltpu.VMEM((2, tok, 2 * buf), BF), pltpu.VMEM((tok, buf), BF)],
    )(ids, weights, tokens, grad_out)


def regroup_kernel(here_ref, low_ref, high_ref, out_ref):
    groups, buf, tile = low_ref.shape
    experts = buf // CAP
    blocks = []
    for in_ref in (low_ref, high_ref):
        for step in range(1, groups):
            block = in_ref[lax.rem(here_ref[0] + step, groups)]
            blocks.append(block.astype(F32).reshape(experts, CAP, tile))
    rows = jnp.concatenate(blocks, axis=1).astype(BF)
    out_ref[0] = rows
    out_ref[1] = rows


def regroup(here, rows):
    groups, buf, width = rows.shape
    experts = buf // CAP
    depth = 2 * (groups - 1) * CAP
    tile = 896
    steps = width // 2 // tile
    return call(
        regroup_kernel,
        "regroup",
        0,
        2 * (groups + 2 * (groups - 1)) * buf * width,
        grid_spec=pltpu.PrefetchScalarGridSpec(
            num_scalar_prefetch=1,
            grid=(steps,),
            in_specs=[
                pl.BlockSpec((groups, buf, tile), lambda j, _: (0, 0, j)),
                pl.BlockSpec((groups, buf, tile), lambda j, _: (0, 0, j + steps)),
            ],
            out_specs=pl.BlockSpec((2, experts, depth, tile), lambda j, _: (0, 0, 0, j)),
        ),
        out_shape=jax.ShapeDtypeStruct((2, experts, depth, width // 2), BF),
    )(here, rows, rows)


def take_tokens_kernel(in_ref, out_ref):
    locs, _, tile = in_ref.shape
    rows = in_ref[...].astype(F32)[:, :CAP, :]
    out_ref[...] = rows.reshape(locs * CAP, tile).astype(BF)


def take_tokens(xg):
    locs, unit, width = xg.shape
    return call(
        take_tokens_kernel,
        "take_tokens",
        0,
        4 * locs * unit * width,
        grid=(width // TILE,),
        in_specs=[pl.BlockSpec((locs, unit, TILE), lambda j: (0, 0, j))],
        out_specs=pl.BlockSpec((locs * CAP, TILE), lambda j: (0, j)),
        out_shape=jax.ShapeDtypeStruct((locs * CAP, width), BF),
    )(xg)


def pre_kernel(x_ref, wg_ref, wu_ref, xg_ref, wd_ref, pg_ref, pu_ref, own_ref):
    @pl.when(pl.program_id(0) == 0)
    def _():
        pg_ref[...] = jnp.zeros_like(pg_ref)
        pu_ref[...] = jnp.zeros_like(pu_ref)
        own_ref[...] = jnp.zeros_like(own_ref)

    pg_ref[...] += jnp.dot(x_ref[...], wg_ref[...], preferred_element_type=F32)
    pu_ref[...] += jnp.dot(x_ref[...], wu_ref[...], preferred_element_type=F32)
    own_ref[...] += contract_cols(xg_ref[...], wd_ref[...])


def pre(x_rows, w_gate, w_up, xg_rows, w_down):
    rows, width = x_rows.shape
    own, ff = xg_rows.shape[0], w_gate.shape[1]
    return call(
        pre_kernel,
        "pre",
        2 * width * ff * (2 * rows + own),
        2 * width * (rows + own + 3 * ff),
        grid=(width // TILE,),
        in_specs=[
            pl.BlockSpec((rows, TILE), lambda j: (0, j)),
            pl.BlockSpec((TILE, ff), lambda j: (j, 0)),
            pl.BlockSpec((TILE, ff), lambda j: (j, 0)),
            pl.BlockSpec((own, TILE), lambda j: (0, j)),
            pl.BlockSpec((ff, TILE), lambda j: (0, j)),
        ],
        out_specs=[whole((rows, ff)), whole((rows, ff)), whole((own, ff))],
        out_shape=[
            jax.ShapeDtypeStruct((rows, ff), F32),
            jax.ShapeDtypeStruct((rows, ff), F32),
            jax.ShapeDtypeStruct((own, ff), F32),
        ],
    )(x_rows, w_gate, w_up, xg_rows, w_down)


def delta_kernel(
    here_ref, g_ref, low_ref, high_ref, pg_ref, pu_ref, own_ref, gx_ref, ux_ref, gl_ref, ul_ref, uo_ref, ur_ref, rest
):
    groups, span, ff = pg_ref.shape
    locs = span // CAP
    depth = (groups - 1) * CAP

    @pl.when(pl.program_id(0) == 0)
    def _():
        rest[...] = jnp.zeros_like(rest)

    both = jnp.concatenate([low_ref[...], high_ref[...]], axis=0)
    rest[...] += contract_cols(g_ref[...], both)

    @pl.when(pl.program_id(0) == pl.num_programs(0) - 1)
    def _():
        halves = rest[...].reshape(locs, 2 * depth, 2 * ff)
        gate_blocks, up_blocks, outer_blocks = [], [], []
        for step in range(groups):
            group = lax.rem(here_ref[0] + step, groups)
            if step == 0:
                hidden = own_ref[...][:, CAP:, :]
            else:
                first = (step - 1) * CAP
                hidden = (
                    halves[:, first : first + CAP, :ff]
                    + halves[:, depth + first : depth + first + CAP, ff:]
                )
            hidden = hidden.reshape(span, ff)
            gate, up = pg_ref[group], pu_ref[group]
            sig = 1.0 / (1.0 + jnp.exp(-gate))
            swish = gate * sig
            gate_delta = hidden * up * sig * (1.0 + gate * (1.0 - sig))
            up_delta = hidden * swish
            gx_ref[group] = gate_delta.astype(BF)
            ux_ref[group] = up_delta.astype(BF)
            gate_blocks.append(gate_delta.reshape(locs, CAP, ff))
            up_blocks.append(up_delta.reshape(locs, CAP, ff))
            outer_blocks.append((swish * up).reshape(locs, CAP, ff))
        gl_ref[...] = jnp.concatenate(gate_blocks, axis=1).astype(BF)
        ul_ref[...] = jnp.concatenate(up_blocks, axis=1).astype(BF)
        zero = jnp.zeros((locs, CAP, ff), F32)
        uo_ref[...] = jnp.concatenate([zero, outer_blocks[0]], axis=1).astype(BF)
        outer = jnp.concatenate(outer_blocks[1:], axis=1)
        zero = jnp.zeros((locs, depth, ff), F32)
        low = jnp.concatenate([outer, zero], axis=1)
        high = jnp.concatenate([zero, outer], axis=1)
        outer = jnp.concatenate([low, high], axis=2).astype(BF)
        ur_ref[...] = outer.reshape(locs * 2 * depth, 2 * ff)


def deltas(here, g_rest, w_down, pre_gate, pre_up, own):
    groups, span, ff = pre_gate.shape
    rest, cols = g_rest.shape
    locs = span // CAP
    tile = 896
    steps = cols // tile
    small = lambda *shape: jax.ShapeDtypeStruct(shape, BF)
    outs = [
        small(groups, span, ff),
        small(groups, span, ff),
        small(locs, groups * CAP, ff),
        small(locs, groups * CAP, ff),
        small(locs, 2 * CAP, ff),
        small(rest, 2 * ff),
    ]
    return call(
        delta_kernel,
        "deltas",
        4 * rest * cols * ff,
        2 * cols * (rest + 2 * ff) + 14 * groups * span * ff,
        grid_spec=pltpu.PrefetchScalarGridSpec(
            num_scalar_prefetch=1,
            grid=(steps,),
            in_specs=[
                pl.BlockSpec((rest, tile), lambda j, _: (0, j)),
                pl.BlockSpec((ff, tile), lambda j, _: (0, j)),
                pl.BlockSpec((ff, tile), lambda j, _: (0, j + steps)),
                whole(pre_gate.shape),
                whole(pre_up.shape),
                whole(own.shape),
            ],
            out_specs=[whole(o.shape) for o in outs],
            scratch_shapes=[pltpu.VMEM((rest, 2 * ff), F32)],
        ),
        out_shape=outs,
    )(here, g_rest, w_down, w_down, pre_gate, pre_up, own)


def row_part_kernel(gd_ref, ud_ref, wg_ref, wu_ref, out_ref):
    total = contract_cols(gd_ref[...], wg_ref[...]) + contract_cols(ud_ref[...], wu_ref[...])
    out_ref[...] = total.astype(BF)


def row_part(gate_delta, up_delta, w_gate, w_up, first, count):
    rows, ff = gate_delta.shape
    skip = first // TILE
    return call(
        row_part_kernel,
        "row_part",
        4 * rows * ff * count,
        2 * count * (rows + 2 * ff),
        grid=(count // TILE,),
        in_specs=[
            whole((rows, ff)),
            whole((rows, ff)),
            pl.BlockSpec((TILE, ff), lambda j: (j + skip, 0)),
            pl.BlockSpec((TILE, ff), lambda j: (j + skip, 0)),
        ],
        out_specs=pl.BlockSpec((rows, TILE), lambda j: (0, j)),
        out_shape=jax.ShapeDtypeStruct((rows, count), BF),
    )(gate_delta, up_delta, w_gate, w_up)


def row_grads_kernel(x_ref, gd_ref, ud_ref, gate_ref, up_ref):
    gate_ref[...] = contract_rows(x_ref[...], gd_ref[...]).astype(BF)
    up_ref[...] = contract_rows(x_ref[...], ud_ref[...]).astype(BF)


def row_grads(x_rows, gate_delta, up_delta):
    rows, width = x_rows.shape
    ff = gate_delta.shape[1]
    return call(
        row_grads_kernel,
        "row_grads",
        4 * rows * width * ff,
        2 * width * (rows + 2 * ff),
        grid=(width // TILE,),
        in_specs=[
            pl.BlockSpec((rows, TILE), lambda j: (0, j)),
            whole((rows, ff)),
            whole((rows, ff)),
        ],
        out_specs=[pl.BlockSpec((TILE, ff), lambda j: (j, 0))] * 2,
        out_shape=[jax.ShapeDtypeStruct((width, ff), BF)] * 2,
    )(x_rows, gate_delta, up_delta)


def down_kernel(uo_ref, low_ref, high_ref, ur_ref, g_ref, out_ref):
    ff = uo_ref.shape[1]
    rest = contract_rows(ur_ref[...], g_ref[...])
    outer = uo_ref[...]
    out_ref[0] = (contract_rows(outer, low_ref[...]) + rest[:ff]).astype(BF)
    out_ref[1] = (contract_rows(outer, high_ref[...]) + rest[ff:]).astype(BF)


def down(outer_own, xg_rows, outer_rest, g_rest):
    own, ff = outer_own.shape
    rest, cols = g_rest.shape
    tile = 896
    steps = cols // tile
    halves = call(
        down_kernel,
        "down",
        4 * (own + rest) * cols * ff,
        2 * cols * (2 * own + rest + 2 * ff),
        grid=(steps,),
        in_specs=[
            whole((own, ff)),
            pl.BlockSpec((own, tile), lambda j: (0, j)),
            pl.BlockSpec((own, tile), lambda j: (0, j + steps)),
            whole((rest, 2 * ff)),
            pl.BlockSpec((rest, tile), lambda j: (0, j)),
        ],
        out_specs=pl.BlockSpec((2, ff, tile), lambda j: (0, 0, j)),
        out_shape=jax.ShapeDtypeStruct((2, ff, cols), BF),
    )(outer_own, xg_rows, xg_rows, outer_rest, g_rest)
    return jnp.concatenate([halves[0], halves[1]], axis=1)


def fold_kernel(here_ref, in_ref, out_ref):
    _, experts, depth, tile = in_ref.shape
    groups = depth // CAP
    total = in_ref[0].astype(F32) + in_ref[1].astype(F32)
    for step in range(groups):
        part = total[:, step * CAP : (step + 1) * CAP, :]
        group = lax.rem(here_ref[0] + step, groups)
        out_ref[group] = part.reshape(experts * CAP, tile).astype(BF)


def fold(here, home):
    _, experts, depth, width = home.shape
    groups = depth // CAP
    return call(
        fold_kernel,
        "fold",
        experts * depth * width,
        6 * experts * depth * width,
        mib=20,
        grid_spec=pltpu.PrefetchScalarGridSpec(
            num_scalar_prefetch=1,
            grid=(width // TILE,),
            in_specs=[pl.BlockSpec((2, experts, depth, TILE), lambda j, _: (0, 0, 0, j))],
            out_specs=pl.BlockSpec((groups, experts * CAP, TILE), lambda j, _: (0, 0, j)),
        ),
        out_shape=jax.ShapeDtypeStruct((groups, experts * CAP, width), BF),
    )(here, home)


def combine_kernel(split, table_ref, ring_ref, wide_ref, out_ref):
    table = table_ref[...]

    @pl.when(pl.program_id(0) < split)
    def _():
        out_ref[...] = jnp.dot(table, ring_ref[...], preferred_element_type=F32).astype(BF)

    @pl.when(pl.program_id(0) >= split)
    def _():
        count, _, tile = wide_ref.shape
        rows = wide_ref[...].astype(F32).reshape(count * CAP, tile).astype(BF)
        both = jnp.concatenate([table, table], axis=1)
        out_ref[...] = jnp.dot(both, rows, preferred_element_type=F32).astype(BF)


def combine(table, ring, wide):
    tok, buf = table.shape
    width = ring.shape[1] + wide.shape[2]
    split = ring.shape[1] // TILE
    return call(
        functools.partial(combine_kernel, split),
        "combine",
        2 * tok * buf * width,
        2 * width * (tok + 2 * buf),
        mib=20,
        grid=(width // TILE,),
        in_specs=[
            whole((tok, buf)),
            pl.BlockSpec((buf, TILE), lambda j: (0, jnp.minimum(j, split - 1))),
            pl.BlockSpec((wide.shape[0], CAP, TILE), lambda j: (0, 0, jnp.maximum(j - split, 0))),
        ],
        out_specs=pl.BlockSpec((tok, TILE), lambda j: (0, j)),
        out_shape=jax.ShapeDtypeStruct((tok, width), BF),
    )(table, ring, wide)


def over_loc(a):
    return lax.all_to_all(a, "loc", split_axis=0, concat_axis=0, tiled=True)


def body(tokens, grad_out, expert_ids, route_weight, gate_weight, up_weight, down_weight):
    groups = lax.axis_size("grp")
    locs = lax.axis_size("loc")
    here = lax.axis_index("grp").astype(jnp.int32)[None]
    experts = locs // 2
    width = tokens.shape[1]
    buf = experts * CAP
    span = locs * CAP
    ring_cols = 3072
    wide_cols = width - ring_cols

    w_gate, w_up, w_down = gate_weight[0], up_weight[0], down_weight[0]
    ff = w_gate.shape[1]

    table, xg_send, g_send = dispatch(expert_ids, route_weight, tokens, grad_out, experts)

    xg = over_loc(xg_send.reshape(locs, 2 * CAP, width))
    g_ring = lax.all_gather(g_send, "grp", axis=0, tiled=False)
    x_rows = lax.all_gather(take_tokens(xg), "grp", axis=0, tiled=True)
    g_rest = over_loc(regroup(here, g_ring).reshape(locs, 2 * (groups - 1) * CAP, width // 2))
    g_rest = g_rest.reshape(locs * 2 * (groups - 1) * CAP, width // 2)
    xg_rows = xg.reshape(locs * 2 * CAP, width)

    pre_gate, pre_up, own = pre(x_rows, w_gate, w_up, xg_rows, w_down)
    gate_x, up_x, gate_l, up_l, outer_own, outer_rest = deltas(
        here,
        g_rest,
        w_down,
        pre_gate.reshape(groups, span, ff),
        pre_up.reshape(groups, span, ff),
        own.reshape(locs, 2 * CAP, ff),
    )
    rows = groups * span
    gate_x, up_x = gate_x.reshape(rows, ff), up_x.reshape(rows, ff)

    part_ring = row_part(gate_l.reshape(rows, ff), up_l.reshape(rows, ff), w_gate, w_up, 0, ring_cols)
    part_ring, gate_x, up_x = lax.optimization_barrier((part_ring, gate_x, up_x))
    home_ring = over_loc(part_ring.reshape(locs, groups * CAP, ring_cols))
    part_wide = row_part(gate_x, up_x, w_gate, w_up, ring_cols, wide_cols)
    reduced = lax.psum_scatter(
        part_wide.reshape(groups, span, wide_cols), "grp", scatter_dimension=0, tiled=True
    )

    part_wide, gate_x, up_x, outer_own, outer_rest = lax.optimization_barrier(
        (part_wide, gate_x, up_x, outer_own, outer_rest)
    )
    gate_grad, up_grad = row_grads(x_rows, gate_x, up_x)
    down_grad = down(outer_own.reshape(locs * 2 * CAP, ff), xg_rows, outer_rest, g_rest)
    home_ring, gate_grad, up_grad, down_grad = lax.optimization_barrier(
        (home_ring, gate_grad, up_grad, down_grad)
    )

    folded = fold(here, home_ring.reshape(2, experts, groups * CAP, ring_cols))
    ring = lax.psum_scatter(folded, "grp", scatter_dimension=0, tiled=True)
    home_wide = over_loc(reduced.reshape(locs, CAP, wide_cols))
    tokens_grad = combine(table, ring.reshape(buf, ring_cols), home_wide)
    return (tokens_grad, gate_grad[None], up_grad[None], down_grad[None])


def solution(mesh):
    in_specs = (
        P(("grp", "loc"), None),
        P(("grp", "loc"), None),
        P(("grp", "loc"), None),
        P(("grp", "loc"), None),
        P("loc", None, "grp"),
        P("loc", None, "grp"),
        P("loc", "grp", None),
    )
    out_specs = (
        P(("grp", "loc"), None),
        P("loc", None, "grp"),
        P("loc", None, "grp"),
        P("loc", "grp", None),
    )
    return jax.shard_map(body, mesh=mesh, in_specs=in_specs, out_specs=out_specs, check_vma=False)
```

time: 424 us -> 267 us (0.63)
  waiting for transfers between devices: 237 us -> 101 us
  Pallas kernels: 0 us -> 68.2 us
  local copies, waits for them, and re-layouts: 70.9 us -> 7.31 us
  matrix products: 59.3 us -> 0 us
  blocking collectives: 0 us -> 54.9 us
  starting transfers between devices: 33 us -> 18.5 us
  other arithmetic: 7.89 us -> 1.41 us
    all_to_all x4 -> x3, waiting for transfers between devices: 165 us -> 21.4 us  [over_loc(): return lax.all_to_all(a, 'loc', split_axis=0, concat_axis=0, tiled=True)]
    pallas_call x0 -> x11, Pallas kernels: none -> 68.2 us  [the longest x2 10.9 us: row_part(): call(row_part_kernel, 'row_part', 4 * rows * ff * count, 2 * count * (row...]
    all_gather x0 -> x2, waiting for transfers between devices: none -> 61.9 us  [the longest x1 61.9 us: body(): x_rows = lax.all_gather(take_tokens(xg), 'grp', axis=0, tiled=True)]
    dot_general x12 -> x0, matrix products: 59.3 us -> none  [the longest x3 23.2 us: contract_cols(): lax.dot_general(left, right, (((1,), (1,)), ((), ())), preferred_element_...]
    all_to_all x0 -> x1, blocking collectives: none -> 54.9 us  [over_loc(): return lax.all_to_all(a, 'loc', split_axis=0, concat_axis=0, tiled=True)]
    reduce_scatter x1 -> x2, waiting for transfers between devices: 71.4 us -> 17.5 us  [the longest x1 17.5 us: body(): ring = lax.psum_scatter(folded, 'grp', scatter_dimension=0, tiled=True)]
    reshape x4 -> x1, local copies, waits for them, and re-layouts: 27.4 us -> 2.24 us  [body(): home_wide = over_loc(reduced.reshape(locs, CAP, wide_cols))]
    convert_element_type x3 -> x0, local copies, waits for them, and re-layouts: 21.1 us -> none  [the longest x2 21 us: body(): reduced = lax.psum_scatter(partial_value.astype(jnp.float32).reshape(grou...]
  transfers between devices with their start and end apart: 5 -> 7, of which waited for: 5 -> 3; matrix products, arithmetic and copies ran while one was open for 11% -> 1% of each run, Pallas kernels for 0% -> 15%
where the time goes in v2:
time: 267 us; the launch traced here: 265 us
  waiting for transfers between devices  101 us (38%)
  Pallas kernels  68.2 us (26%)
  blocking collectives  54.9 us (21%)
  starting transfers between devices  18.5 us (7%)
  between operations  13.8 us (5%)
  local copies, waits for them, and re-layouts  7.31 us (3%)
    all_gather x1, waiting for transfers between devices, body(): x_rows = lax.all_gather(take_tokens(xg), 'grp', axis=0, tiled=True)  61.9 us
    all_to_all x1, blocking collectives, over_loc(): return lax.all_to_all(a, 'loc', split_axis=0, concat_axis=0, tiled=True)  54.9 us
    all_to_all x3, waiting for transfers between devices, over_loc(): return lax.all_to_all(a, 'loc', split_axis=0, concat_axis=0, tiled=True)  21.4 us
    all_to_all x3, starting transfers between devices, over_loc(): return lax.all_to_all(a, 'loc', split_axis=0, concat_axis=0, tiled=True)  18.3 us
    reduce_scatter x1, waiting for transfers between devices, body(): ring = lax.psum_scatter(folded, 'grp', scatter_dimension=0, tiled=True)  17.5 us
    pallas_call x2, Pallas kernels, row_part(): call(row_part_kernel, 'row_part', 4 * rows * ff * count, 2 * count * (row...  10.9 us
    pallas_call x1, Pallas kernels, pre(): call(pre_kernel, 'pre', 2 * width * ff * (2 * rows + own), 2 * width * (r...  10.6 us
    pallas_call x1, Pallas kernels, row_grads(): call(row_grads_kernel, 'row_grads', 4 * rows * width * ff, 2 * width * (r...  9.65 us
  transfers between devices with their start and end apart: 7, of which 3 were waited for; matrix products, arithmetic and copies ran while one was open for 1% of the time, Pallas kernels for 15%

profile of v2, /device:TPU:1, one launch (start us, length us, event | category | flops | bytes accessed | tf_op | source)
XLA Modules:
  0.0 265.1 jit_solution(8051957875099423353)
XLA Ops:
  7.2 1.4 copy.12.w_ref
  8.6 1.4 copy.11.ids_ref
  10.0 7.7 %dispatch.1 = (bf16[128,64]{1,0:T(8,128)(2,1)}, bf16[2,16,8,7168]{3,2,1,0:T(8,128)(2,1)}, bf16[64,7168]{1,0:T(8,128)(2,1)}) custom-call(s32[128,8]{1,0:T(8,128)} %copy.11.ids_ref, bf16[128,8]{1,0:T(8,128)(2,1)} %copy.12.w_ref, bf16[128,7168]{1,0:T(8,128)(2,1)} %t_ref.1, bf16[128,7168]{1,0:T(8,128)(2,1)} %g_ref.1), custom_call_target="tpu_custom_call" | custom-call | flops 704643072 | bytes 8257536 | tf_op jit(solution)/shard_map/dispatch/pallas_call | solution.py:84
  17.8 54.9 %all_to_all.20.in_ref = bf16[32,8,7168]{2,1,0:T(8,128)(2,1)} all-to-all(bf16[32,8,7168]{2,1,0:T(8,128)(2,1)} %bitcast.47), channel_id=1, replica_groups=mesh['grp'=4,'loc'=32] {'loc'}, dimensions={0} | all-to-all | bytes 7340032 | tf_op jit(solution)/shard_map/all_to_all | solution.py:440
  72.7 5.6 %take_tokens.1 = bf16[128,7168]{1,0:T(8,128)(2,1)} custom-call(bf16[32,8,7168]{2,1,0:T(8,128)(2,1)} %all_to_all.20.in_ref), custom_call_target="tpu_custom_call" | custom-call | bytes 7340032 | tf_op jit(solution)/shard_map/take_tokens/pallas_call | solution.py:155
  78.4 5.2 %regroup.1 = bf16[2,16,24,3584]{3,2,1,0:T(8,128)(2,1)} custom-call(s32[1]{0:T(128)} %bitcast.here_ref, bf16[4,64,7168]{2,1,0:T(8,128)(2,1)} %bitcast.44, bf16[4,64,7168]{2,1,0:T(8,128)(2,1)} %bitcast.45), custom_call_target="tpu_custom_call" | custom-call | bytes 9175040 | tf_op jit(solution)/shard_map/regroup/pallas_call | solution.py:129
  83.6 4.7 %all-to-all-start = ((bf16[32,24,3584]{2,1,0:T(8,128)(2,1)}), bf16[32,24,3584]{2,1,0:T(8,128)(2,1)}, u32[]{:S(2)}, u32[]{:S(2)}) async-start(bf16[32,24,3584]{2,1,0:T(8,128)(2,1)} %bitcast.33), calls=%async_computation | async-start | bytes 11010048 | tf_op jit(solution)/shard_map/all_to_all | solution.py:440
  88.4 61.9 %all-gather.4.cloned.1.call-done.x_ref = bf16[512,7168]{1,0:T(8,128)(2,1)} async-done(((bf16[128,7168]{1,0:T(8,128)(2,1)}), bf16[512,7168]{1,0:T(8,128)(2,1)}) %all-gather.4.cloned.1.call-update) | async-done | bytes 7340048 | tf_op jit(solution)/shard_map/all_gather | solution.py:461
  150.3 10.6 %pre.1 = (f32[512,128]{1,0:T(8,128)}, f32[512,128]{1,0:T(8,128)}, f32[256,128]{1,0:T(8,128)}) custom-call(bf16[512,7168]{1,0:T(8,128)(2,1)} %all-gather.4.cloned.1.call-done.x_ref, bf16[7168,128]{1,0:T(8,128)(2,1)} %bitcast.38, bf16[7168,128]{1,0:T(8,128)(2,1)} %bitcast.41, bf16[256,7168]{1,0:T(8,128)(2,1)} %bitcast.30, bf16[128,7168]{1,0:T(8,128)(2,1)} %bitcast.35), custom_call_target="tpu_custom_call" | custom-call | flops 2348810240 | bytes 16515072 | tf_op jit(solution)/shard_map/pre/pallas_call | solution.py:182
  160.9 6.6 %deltas.1 = (bf16[4,128,128]{2,1,0:T(8,128)(2,1)}, bf16[4,128,128]{2,1,0:T(8,128)(2,1)}, bf16[32,16,128]{2,1,0:T(8,128)(2,1)}, bf16[32,16,128]{2,1,0:T(8,128)(2,...) custom-call(s32[1]{0:T(128)} %bitcast.here_ref, bf16[768,3584]{1,0:T(8,128)(2,1)} %bitcast.3.g_ref, ...), custom_call_target="tpu_custom_call" | custom-call | flops 1409286144 | bytes 8257536 | tf_op jit(solution)/shard_map/deltas/pallas_call | solution.py:270
  167.6 5.1 %row_part.2 = bf16[512,3072]{1,0:T(8,128)(2,1)} custom-call(bf16[512,128]{1,0:T(8,128)(2,1)} %bitcast.56, bf16[512,128]{1,0:T(8,128)(2,1)} %bitcast.57, bf16[7168,128]{1,0:T(8,128)(2,1)} %bitcast.39, bf16[7168,128]{1,0:T(8,128)(2,1)} %bitcast.42), custom_call_target="tpu_custom_call" | custom-call | flops 805306368 | bytes 4718592 | tf_op jit(solution)/shard_map/row_part/pallas_call | solution.py:301
  172.7 5.8 %row_part.3 = bf16[512,4096]{1,0:T(8,128)(2,1)} custom-call(bf16[512,128]{1,0:T(8,128)(2,1)} %bitcast.49, bf16[512,128]{1,0:T(8,128)(2,1)} %bitcast.51, bf16[7168,128]{1,0:T(8,128)(2,1)} %bitcast.40, bf16[7168,128]{1,0:T(8,128)(2,1)} %bitcast.43), custom_call_target="tpu_custom_call" | custom-call | flops 1073741824 | bytes 6291456 | tf_op jit(solution)/shard_map/row_part/pallas_call | solution.py:301
  178.4 7.7 %all-to-all-start.2 = ((bf16[32,16,3072]{2,1,0:T(8,128)(2,1)}), bf16[32,16,3072]{2,1,0:T(8,128)(2,1)S(1)}, u32[]{:S(2)}, u32[]{:S(2)}) async-start(bf16[32,16,3072]{2,1,0:T(8,128)(2,1)} %bitcast.46), calls=%async_computation.2 | async-start | bytes 6291456 | tf_op jit(solution)/shard_map/all_to_all | solution.py:440
  186.2 7.1 %down.1 = bf16[2,128,3584]{2,1,0:T(8,128)(2,1)} custom-call(bf16[256,128]{1,0:T(8,128)(2,1)} %bitcast.58, bf16[256,7168]{1,0:T(8,128)(2,1)} %bitcast.31, bf16[256,7168]{1,0:T(8,128)(2,1)} %bitcast.32, bf16[768,256]{1,0:T(8,128)(2,1)} %get-tuple-element.49.ur_ref, bf16[768,3584]{1,0:T(8,128)(2,1)} %bitcast.3.g_ref), custom_call_target="tpu_custom_call" | custom-call | flops 1879048192 | bytes 11010048 | tf_op jit(solution)/shard_map/down/pallas_call | solution.py:355
  193.3 9.6 %row_grads.1 = (bf16[7168,128]{1,0:T(8,128)(2,1)}, bf16[7168,128]{1,0:T(8,128)(2,1)}) custom-call(bf16[512,7168]{1,0:T(8,128)(2,1)} %all-gather.4.cloned.1.call-done.x_ref, bf16[512,128]{1,0:T(8,128)(2,1)} %bitcast.50, bf16[512,128]{1,0:T(8,128)(2,1)} %bitcast.52), custom_call_target="tpu_custom_call" | custom-call | flops 1879048192 | bytes 11010048 | tf_op jit(solution)/shard_map/row_grads/pallas_call | solution.py:326
  203.1 1.4 pad_maximum_fusion
  204.5 21.4 %all-to-all-done.2 = bf16[32,16,3072]{2,1,0:T(8,128)(2,1)S(1)} async-done(((bf16[32,16,3072]{2,1,0:T(8,128)(2,1)}), bf16[32,16,3072]{2,1,0:T(8,128)(2,1)S(1)}, u32[]{:S(2)}, u32[]{:S(2)}) %all-to-all-start.2) | async-done | bytes 3145760 | tf_op jit(solution)/shard_map/all_to_all | solution.py:440
  225.9 0.9 fold.1
  226.8 1.1 copy-done
  228.0 2.2 reshape.75
  230.3 5.9 %all-to-all-start.3 = ((bf16[32,4,4096]{2,1,0:T(4,128)(2,1)}), bf16[32,4,4096]{2,1,0:T(4,128)(2,1)S(1)}, u32[]{:S(2)}, u32[]{:S(2)}) async-start(bf16[32,4,4096]{2,1,0:T(4,128)(2,1)} %reshape.75), calls=%async_computation.5 | async-start | bytes 2097152 | tf_op jit(solution)/shard_map/all_to_all | solution.py:440
  236.2 17.5 %reduce-scatter.3.cloned.1.call-done = bf16[1,64,3072]{2,1,0:T(8,128)(2,1)} async-done(((bf16[4,64,3072]{2,1,0:T(8,128)(2,1)}), bf16[1,64,3072]{2,1,0:T(8,128)(2,1)}) %reduce-scatter.3.cloned.1.call-update) | async-done | bytes 393232 | tf_op jit(solution)/shard_map/reduce_scatter | solution.py:496
  253.7 1.0 copy-done.1
  254.7 3.8 %combine.1 = bf16[128,7168]{1,0:T(8,128)(2,1)} custom-call(bf16[128,64]{1,0:T(8,128)(2,1)S(1)} %copy-done.2, bf16[64,3072]{1,0:T(8,128)(2,1)S(1)} %bitcast.29, bf16[32,4,4096]{2,1,0:T(4,128)(2,1)S(1)} %all-to-all-done.3.wide_ref), custom_call_target="tpu_custom_call" | custom-call | flops 117440512 | bytes 3670016 | tf_op jit(solution)/shard_map/combine/pallas_call | solution.py:422
  (19 shorter events, 0.4 us)
Async XLA Ops:
  7.2 71.2 %all-gather.6.cloned.1.call-start = ((), (), s32[]{:S(2)}) async-start(), calls=%async_computation.9 | async-start | bytes 4587520 | tf_op jit(solution)/shard_map/all_gather | solution.py:460
  17.8 132.5 %all-gather.4.cloned.1.call-start = ((), (), s32[]{:S(2)}) async-start(), calls=%async_computation.6 | async-start | bytes 9175040 | tf_op jit(solution)/shard_map/all_gather | solution.py:461
  83.6 77.3 %all-to-all-start = ((bf16[32,24,3584]{2,1,0:T(8,128)(2,1)}), bf16[32,24,3584]{2,1,0:T(8,128)(2,1)}, u32[]{:S(2)}, u32[]{:S(2)}) async-start(bf16[32,24,3584]{2,1,0:T(8,128)(2,1)} %bitcast.33), calls=%async_computation | async-start | bytes 11010048 | tf_op jit(solution)/shard_map/all_to_all | solution.py:440
  88.3 139.7 %reduce-scatter.5.cloned.1.call-start = ((), (), s32[]{:S(2)}) async-start(), calls=%async_computation.8 | async-start | bytes 5242880 | tf_op jit(solution)/shard_map/reduce_scatter | solution.py:482
  178.4 47.5 %all-to-all-start.2 = ((bf16[32,16,3072]{2,1,0:T(8,128)(2,1)}), bf16[32,16,3072]{2,1,0:T(8,128)(2,1)S(1)}, u32[]{:S(2)}, u32[]{:S(2)}) async-start(bf16[32,16,3072]{2,1,0:T(8,128)(2,1)} %bitcast.46), calls=%async_computation.2 | async-start | bytes 6291456 | tf_op jit(solution)/shard_map/all_to_all | solution.py:440
  186.2 67.5 %reduce-scatter.3.cloned.1.call-start = ((), (), s32[]{:S(2)}) async-start(), calls=%async_computation.7 | async-start | bytes 1966080 | tf_op jit(solution)/shard_map/reduce_scatter | solution.py:496
  193.3 9.7 %copy-start.3 = (bf16[2,128,3584]{2,1,0:T(8,128)(2,1)S(1)}, bf16[2,128,3584]{2,1,0:T(8,128)(2,1)}, u32[]{:S(2)}) copy-start(bf16[2,128,3584]{2,1,0:T(8,128)(2,1)} %down.1) | copy-start | bytes 5505028
  226.8 1.1 copy-start
  228.0 25.7 %copy-start.2 = (bf16[128,64]{1,0:T(8,128)(2,1)S(1)}, bf16[128,64]{1,0:T(8,128)(2,1)}, u32[]{:S(2)}) copy-start(bf16[128,64]{1,0:T(8,128)(2,1)} %get-tuple-element.29.table_ref) | copy-start | bytes 49156
  230.3 23.4 %all-to-all-start.3 = ((bf16[32,4,4096]{2,1,0:T(4,128)(2,1)}), bf16[32,4,4096]{2,1,0:T(4,128)(2,1)S(1)}, u32[]{:S(2)}, u32[]{:S(2)}) async-start(bf16[32,4,4096]{2,1,0:T(4,128)(2,1)} %reshape.75), calls=%async_computation.5 | async-start | bytes 2097152 | tf_op jit(solution)/shard_map/all_to_all | solution.py:440
  253.7 1.0 copy-start.1
Sparse Core Ops, SparseCore 0:
  17.9 47.1 all-gather.5
  78.5 71.7 all-gather.3
  178.6 47.6 reduce-scatter.4
  229.3 24.3 reduce-scatter.2

commit v3 on v2

v3 whole, which is shorter than its diff:
```python
import functools

import jax
import jax.numpy as jnp
from jax import lax
from jax.experimental import pallas as pl
from jax.experimental.pallas import tpu as pltpu
from jax.sharding import PartitionSpec as P

CAP = 4
BF = jnp.bfloat16
F32 = jnp.float32
TILE = 512


def contract_rows(left, right):
    return lax.dot_general(left, right, (((0,), (0,)), ((), ())), preferred_element_type=F32)


def contract_cols(left, right):
    return lax.dot_general(left, right, (((1,), (1,)), ((), ())), preferred_element_type=F32)


def whole(shape):
    return pl.BlockSpec(shape, lambda *_: (0,) * len(shape))


def call(kernel, name, flops, nbytes, mib=56, **kwargs):
    return pl.pallas_call(
        kernel,
        name=name,
        compiler_params=pltpu.CompilerParams(vmem_limit_bytes=mib << 20),
        cost_estimate=pl.CostEstimate(flops=flops, bytes_accessed=nbytes, transcendentals=0),
        **kwargs,
    )


def dispatch_kernel(ids_ref, w_ref, tl_ref, th_ref, gl_ref, gh_ref, table_ref, xg_ref, ring_ref, pick):
    topk, tok = ids_ref.shape
    experts = xg_ref.shape[1]
    buf = table_ref.shape[0]
    unit = 2 * CAP
    step = pl.program_id(0)

    def tables(count, per_expert):
        slot_row = lax.broadcasted_iota(jnp.int32, (count, tok), 0)
        expert = lax.div(slot_row, per_expert)
        weights = w_ref[...].astype(F32)
        chosen = jnp.zeros((count, tok), F32)
        weight = jnp.zeros((count, tok), F32)
        for k in range(topk):
            hit = ids_ref[k : k + 1, :] == expert
            chosen = jnp.where(hit, 1.0, chosen)
            weight = jnp.where(hit, weights[k : k + 1, :], weight)
        before = lax.broadcasted_iota(jnp.int32, (tok, tok), 0)
        after = lax.broadcasted_iota(jnp.int32, (tok, tok), 1)
        earlier = jnp.where(before < after, 1.0, 0.0).astype(BF)
        slot = jnp.dot(chosen.astype(BF), earlier, preferred_element_type=F32)
        mine = (chosen > 0.5) & (slot == lax.rem(slot_row, CAP).astype(F32))
        return jnp.where(mine, 1.0, 0.0), jnp.where(mine, weight, 0.0), slot_row

    @pl.when(step == 0)
    def _():
        table, weighted, slot_row = tables(experts * unit, unit)
        low = lax.rem(slot_row, unit) < CAP
        pick[0] = jnp.where(low, table, 0.0).astype(BF)
        pick[1] = jnp.where(low, 0.0, table).astype(BF)
        pick[2] = jnp.where(low, weighted, 0.0).astype(BF)
        pick[3] = jnp.where(low, 0.0, weighted).astype(BF)

    def rows(first, low_ref, high_ref):
        total = jnp.dot(pick[first], low_ref[...], preferred_element_type=F32)
        total += jnp.dot(pick[first + 1], high_ref[...], preferred_element_type=F32)
        return total.astype(BF)

    def put(value):
        value = value.reshape(experts, unit, value.shape[1])
        xg_ref[0] = value
        xg_ref[1] = value

    last = pl.num_programs(0) - 1

    @pl.when(step < last)
    def _():
        put(rows(0, tl_ref, th_ref))

    @pl.when(step == last)
    def _():
        put(rows(2, gl_ref, gh_ref))
        table_ref[...] = tables(buf, CAP)[0].astype(BF)

    @pl.when(step < last - 1)
    def _():
        ring_ref[...] = rows(2, gl_ref, gh_ref)


def dispatch(ids, weights, tokens, grad_out, experts):
    tok, width = tokens.shape
    buf = experts * CAP
    unit = 2 * CAP
    half = width // 2
    steps = half // TILE + 1
    parts = steps - 2
    g_low = lambda j: (0, jnp.where(j < parts, j + 2, 0))
    g_high = lambda j: (0, jnp.where(j < parts, j + 2 + parts, 1))
    return call(
        dispatch_kernel,
        "dispatch",
        8 * tok * buf * 2 * width,
        2 * width * (2 * tok + 4 * buf),
        grid=(steps,),
        in_specs=[
            whole(ids.shape),
            whole(weights.shape),
            pl.BlockSpec((tok, TILE), lambda j: (0, jnp.minimum(j, steps - 2))),
            pl.BlockSpec((tok, TILE), lambda j: (0, steps - 1 + jnp.minimum(j, steps - 2))),
            pl.BlockSpec((tok, TILE), g_low),
            pl.BlockSpec((tok, TILE), g_high),
        ],
        out_specs=[
            whole((buf, tok)),
            pl.BlockSpec((2, experts, unit, TILE), lambda j: (0, 0, 0, j)),
            pl.BlockSpec((experts * unit, TILE), lambda j: (0, jnp.minimum(j, parts - 1))),
        ],
        out_shape=[
            jax.ShapeDtypeStruct((buf, tok), BF),
            jax.ShapeDtypeStruct((2, experts, unit, half + TILE), BF),
            jax.ShapeDtypeStruct((experts * unit, half - TILE), BF),
        ],
        scratch_shapes=[pltpu.VMEM((4, experts * unit, tok), BF)],
    )(ids, weights, tokens, tokens, grad_out, grad_out)


def regroup_kernel(own_ref, next_ref, far_top_ref, far_low_ref, prev_ref, out_ref):
    _, experts, depth, tile = out_ref.shape
    unit = 2 * CAP
    mid = experts // 2

    def rows(ref):
        return ref[...].reshape(ref.shape[0] // unit, unit, tile)

    for h in range(2):
        out_ref[h, :, :unit, :] = rows(own_ref)
        out_ref[h, :, unit : 2 * unit, :] = rows(next_ref)
        out_ref[h, :mid, 2 * unit : 3 * unit, :] = rows(far_top_ref)
        out_ref[h, mid:, 2 * unit : 3 * unit, :] = rows(far_low_ref)
        out_ref[h, :, 3 * unit :, :] = rows(prev_ref)


def regroup(blocks):
    count, cols = blocks[0].shape
    unit = 2 * CAP
    experts = count // unit
    return call(
        regroup_kernel,
        "regroup",
        0,
        24 * count * cols,
        grid=(cols // TILE,),
        in_specs=[pl.BlockSpec((b.shape[0], TILE), lambda j: (0, j)) for b in blocks],
        out_specs=pl.BlockSpec((2, experts, 4 * unit, TILE), lambda j: (0, 0, 0, j)),
        out_shape=jax.ShapeDtypeStruct((2, experts, 4 * unit, cols), BF),
    )(*blocks)


def pre_kernel(x_ref, gl_ref, gh_ref, ul_ref, uh_ref, dl_ref, dh_ref, slope_ref, swish_ref, part_ref, outer_ref, acc):
    step = pl.program_id(0)
    last = pl.num_programs(0) - 1

    @pl.when(step == 0)
    def _():
        acc[...] = jnp.zeros_like(acc)

    @pl.when(step < last)
    def _():
        weights = jnp.concatenate([gl_ref[...], gh_ref[...], ul_ref[...], uh_ref[...]], axis=1)
        acc[...] += jnp.dot(x_ref[...], weights, preferred_element_type=F32)

    @pl.when(step == last)
    def _():
        count, ff = swish_ref.shape
        locs = count // CAP
        weights = jnp.concatenate([dl_ref[...], dh_ref[...]], axis=0)

        def fold_halves(value):
            value = value.reshape(locs, 2 * CAP, 2 * ff)
            return (value[:, :CAP, :ff] + value[:, CAP:, ff:]).reshape(count, ff)

        gate = fold_halves(acc[:, : 2 * ff])
        up = fold_halves(acc[:, 2 * ff :])
        part_ref[...] = fold_halves(contract_cols(x_ref[...], weights))
        sig = 1.0 / (1.0 + jnp.exp(-gate))
        swish = gate * sig
        slope_ref[...] = up * sig * (1.0 + gate * (1.0 - sig))
        swish_ref[...] = swish
        outer_ref[...] = swish * up


def pre(block, w_gate, w_up, w_down):
    rows, cols = block.shape
    ff = w_gate.shape[1]
    steps = cols // TILE
    count = rows // 2
    low = pl.BlockSpec((TILE, ff), lambda j: (jnp.minimum(j, steps - 2), 0))
    high = pl.BlockSpec((TILE, ff), lambda j: (steps - 1 + jnp.minimum(j, steps - 2), 0))
    return call(
        pre_kernel,
        "pre",
        8 * rows * cols * ff,
        2 * cols * (rows + 4 * ff),
        mib=16,
        grid=(steps,),
        in_specs=[
            pl.BlockSpec((rows, TILE), lambda j: (0, j)),
            low,
            high,
            low,
            high,
            pl.BlockSpec((ff, TILE), lambda j: (0, 0)),
            pl.BlockSpec((ff, TILE), lambda j: (0, 1)),
        ],
        out_specs=[whole((count, ff))] * 4,
        out_shape=[jax.ShapeDtypeStruct((count, ff), F32)] * 4,
        scratch_shapes=[pltpu.VMEM((rows, 4 * ff), F32)],
    )(block, w_gate, w_gate, w_up, w_up, w_down, w_down)


def delta_kernel(here_ref, g_ref, low_ref, high_ref, *refs):
    slopes, swishes, parts = refs[:5], refs[5:10], refs[10:15]
    gx_ref, ux_ref, gl_ref, ul_ref, acc = refs[15:]
    groups, span, ff = gx_ref.shape
    locs = span // CAP
    unit = 2 * CAP

    @pl.when(pl.program_id(0) == 0)
    def _():
        acc[...] = jnp.zeros_like(acc)

    both = jnp.concatenate([low_ref[...], high_ref[...]], axis=0)
    acc[...] += contract_cols(g_ref[...], both)

    @pl.when(pl.program_id(0) == pl.num_programs(0) - 1)
    def _():
        def block(refs, step):
            own, after, top, bottom, before = refs
            if step == 2:
                return jnp.concatenate([top[...], bottom[...]], axis=0)
            return (own, after, None, before)[step][...]

        halves = acc[...].reshape(locs, groups * unit, 2 * ff)
        for step in range(groups):
            group = lax.rem(here_ref[0] + step, groups)
            first = step * unit
            hidden = (
                halves[:, first : first + CAP, :ff] + halves[:, first + CAP : first + unit, ff:]
            ).reshape(span, ff) + block(parts, step)
            gate = hidden * block(slopes, step)
            up = hidden * block(swishes, step)
            gx_ref[group] = gate.astype(BF)
            ux_ref[group] = up.astype(BF)
            gl_ref[:, step * CAP : (step + 1) * CAP, :] = gate.reshape(locs, CAP, ff).astype(BF)
            ul_ref[:, step * CAP : (step + 1) * CAP, :] = up.reshape(locs, CAP, ff).astype(BF)


def deltas(here, g_rows, w_down, slopes, swishes, parts):
    rows, cols = g_rows.shape
    ff = w_down.shape[0]
    groups = 4
    span = rows // 2 // groups
    locs = span // CAP
    steps = cols // TILE
    small = lambda *shape: jax.ShapeDtypeStruct(shape, BF)
    outs = [
        small(groups, span, ff),
        small(groups, span, ff),
        small(locs, groups * CAP, ff),
        small(locs, groups * CAP, ff),
    ]
    blocks = [*slopes, *swishes, *parts]
    return call(
        delta_kernel,
        "deltas",
        4 * rows * cols * ff,
        2 * cols * (rows + 2 * ff) + 16 * groups * span * ff,
        grid_spec=pltpu.PrefetchScalarGridSpec(
            num_scalar_prefetch=1,
            grid=(steps,),
            in_specs=[
                pl.BlockSpec((rows, TILE), lambda j, _: (0, j)),
                pl.BlockSpec((ff, TILE), lambda j, _: (0, j + 2)),
                pl.BlockSpec((ff, TILE), lambda j, _: (0, j + 2 + steps)),
                *[whole(b.shape) for b in blocks],
            ],
            out_specs=[whole(o.shape) for o in outs],
            scratch_shapes=[pltpu.VMEM((rows, 2 * ff), F32)],
        ),
        out_shape=outs,
    )(here, g_rows, w_down, w_down, *blocks)


def row_part_kernel(gd_ref, ud_ref, wg_ref, wu_ref, out_ref):
    total = contract_cols(gd_ref[...], wg_ref[...]) + contract_cols(ud_ref[...], wu_ref[...])
    out_ref[...] = total.astype(BF)


def row_part(gate_delta, up_delta, w_gate, w_up, first, count):
    rows, ff = gate_delta.shape
    skip = first // TILE
    return call(
        row_part_kernel,
        "row_part",
        4 * rows * ff * count,
        2 * count * (rows + 2 * ff),
        grid=(count // TILE,),
        in_specs=[
            whole((rows, ff)),
            whole((rows, ff)),
            pl.BlockSpec((TILE, ff), lambda j: (j + skip, 0)),
            pl.BlockSpec((TILE, ff), lambda j: (j + skip, 0)),
        ],
        out_specs=pl.BlockSpec((rows, TILE), lambda j: (0, j)),
        out_shape=jax.ShapeDtypeStruct((rows, count), BF),
    )(gate_delta, up_delta, w_gate, w_up)


def row_grads_kernel(here_ref, gx_ref, ux_ref, own_ref, next_ref, top_ref, bottom_ref, prev_ref, gate_ref, up_ref, wide):
    groups, span, ff = gx_ref.shape
    locs = span // CAP
    rows = 2 * span

    @pl.when(pl.program_id(0) == 0)
    def _():
        zero = jnp.zeros((locs, CAP, ff), F32)
        for step in range(groups):
            group = lax.rem(here_ref[0] + step, groups)
            gate = gx_ref[group].astype(F32).reshape(locs, CAP, ff)
            up = ux_ref[group].astype(F32).reshape(locs, CAP, ff)
            low = jnp.concatenate([gate, zero, up, zero], axis=2)
            high = jnp.concatenate([zero, gate, zero, up], axis=2)
            both = jnp.concatenate([low, high], axis=1)
            wide[step] = both.reshape(rows, 4 * ff).astype(BF)

    total = contract_rows(own_ref[...], wide[0]) + contract_rows(next_ref[...], wide[1])
    total += contract_rows(top_ref[...], wide[2, :span]) + contract_rows(bottom_ref[...], wide[2, span:])
    total += contract_rows(prev_ref[...], wide[3])
    total = total.astype(BF)
    gate_ref[0] = total[:, :ff]
    gate_ref[1] = total[:, ff : 2 * ff]
    up_ref[0] = total[:, 2 * ff : 3 * ff]
    up_ref[1] = total[:, 3 * ff :]


def row_grads(here, gate_x, up_x, blocks):
    groups, span, ff = gate_x.shape
    half = blocks[0].shape[1] - TILE
    out = jax.ShapeDtypeStruct((2, half, ff), BF)
    gate, up = call(
        row_grads_kernel,
        "row_grads",
        16 * groups * span * half * ff,
        4 * half * (groups * span + 2 * ff),
        grid_spec=pltpu.PrefetchScalarGridSpec(
            num_scalar_prefetch=1,
            grid=(half // TILE,),
            in_specs=[
                whole(gate_x.shape),
                whole(up_x.shape),
                *[pl.BlockSpec((b.shape[0], TILE), lambda j, _: (0, j)) for b in blocks],
            ],
            out_specs=[pl.BlockSpec((2, TILE, ff), lambda j, _: (0, j, 0))] * 2,
            scratch_shapes=[pltpu.VMEM((groups, 2 * span, 4 * ff), BF)],
        ),
        out_shape=[out, out],
    )(here, gate_x, up_x, *blocks)
    return gate.reshape(2 * half, ff), up.reshape(2 * half, ff)


def down_kernel(g_ref, *refs):
    outers, blocks, out_ref, wide = refs[:5], refs[5:10], refs[10], refs[11]
    span, ff = outers[0].shape
    locs = span // CAP
    unit = 2 * CAP
    step = pl.program_id(0)
    tile = g_ref.shape[1]

    def spread(outer):
        rows = outer.reshape(outer.shape[0] // CAP, CAP, ff)
        zero = jnp.zeros_like(rows)
        low = jnp.concatenate([rows, zero], axis=2)
        high = jnp.concatenate([zero, rows], axis=2)
        return jnp.concatenate([low, high], axis=1)

    def put(total, low, high):
        total = total.astype(BF)
        out_ref[:, pl.ds(pl.multiple_of(low, tile), tile)] = total[:ff]
        out_ref[:, pl.ds(pl.multiple_of(high, tile), tile)] = total[ff:]

    @pl.when(step == 0)
    def _():
        own, after, top, bottom, before = [r[...] for r in outers]
        ordered = [own, after, jnp.concatenate([top, bottom], axis=0), before]
        for k, outer in enumerate(ordered):
            wide[:, k * unit : (k + 1) * unit, :] = spread(outer).astype(BF)
        total = jnp.zeros((2 * ff, tile), F32)
        for outer, block in zip(outers, blocks):
            rows = 2 * outer.shape[0]
            total += contract_rows(spread(outer[...]).reshape(rows, 2 * ff).astype(BF), block[...])
        put(total, 0, tile)

    rows = wide[...].reshape(g_ref.shape[0], 2 * ff)
    first = (step + 2) * tile
    put(contract_rows(rows, g_ref[...]), first, first + pl.num_programs(0) * tile)


def down(g_rows, outers, blocks):
    rows, cols = g_rows.shape
    ff = outers[0].shape[1]
    steps = cols // TILE
    last = blocks[0].shape[1] // TILE - 1
    locs = outers[0].shape[0] // CAP
    width = 2 * (cols + TILE)
    return call(
        down_kernel,
        "down",
        4 * rows * (cols + TILE) * ff,
        2 * (cols + TILE) * (rows + 2 * ff),
        grid=(steps,),
        in_specs=[
            pl.BlockSpec((rows, TILE), lambda j: (0, j)),
            *[whole(o.shape) for o in outers],
            *[pl.BlockSpec((b.shape[0], TILE), lambda j: (0, last)) for b in blocks],
        ],
        out_specs=whole((ff, width)),
        out_shape=jax.ShapeDtypeStruct((ff, width), BF),
        scratch_shapes=[pltpu.VMEM((locs, rows // locs, 2 * ff), BF)],
    )(g_rows, *outers, *blocks)


def fold_kernel(here_ref, in_ref, out_ref):
    _, experts, depth, tile = in_ref.shape
    groups = depth // CAP
    total = in_ref[0].astype(F32) + in_ref[1].astype(F32)
    for step in range(groups):
        part = total[:, step * CAP : (step + 1) * CAP, :]
        group = lax.rem(here_ref[0] + step, groups)
        out_ref[group] = part.reshape(experts * CAP, tile).astype(BF)


def fold(here, home):
    _, experts, depth, width = home.shape
    groups = depth // CAP
    return call(
        fold_kernel,
        "fold",
        experts * depth * width,
        6 * experts * depth * width,
        mib=20,
        grid_spec=pltpu.PrefetchScalarGridSpec(
            num_scalar_prefetch=1,
            grid=(width // TILE,),
            in_specs=[pl.BlockSpec((2, experts, depth, TILE), lambda j, _: (0, 0, 0, j))],
            out_specs=pl.BlockSpec((groups, experts * CAP, TILE), lambda j, _: (0, 0, j)),
        ),
        out_shape=jax.ShapeDtypeStruct((groups, experts * CAP, width), BF),
    )(here, home)


def combine_kernel(split, table_ref, ring_ref, wide_ref, out_ref):
    table = table_ref[...]

    @pl.when(pl.program_id(0) < split)
    def _():
        out_ref[...] = contract_rows(table, ring_ref[...]).astype(BF)

    @pl.when(pl.program_id(0) >= split)
    def _():
        count, _, tile = wide_ref.shape
        rows = wide_ref[...].astype(F32).reshape(count * CAP, tile).astype(BF)
        both = jnp.concatenate([table, table], axis=0)
        out_ref[...] = contract_rows(both, rows).astype(BF)


def combine(table, ring, wide):
    buf, tok = table.shape
    width = ring.shape[1] + wide.shape[2]
    split = ring.shape[1] // TILE
    return call(
        functools.partial(combine_kernel, split),
        "combine",
        2 * tok * buf * width,
        2 * width * (tok + 2 * buf),
        mib=20,
        grid=(width // TILE,),
        in_specs=[
            whole((buf, tok)),
            pl.BlockSpec((buf, TILE), lambda j: (0, jnp.minimum(j, split - 1))),
            pl.BlockSpec((wide.shape[0], CAP, TILE), lambda j: (0, 0, jnp.maximum(j - split, 0))),
        ],
        out_specs=pl.BlockSpec((tok, TILE), lambda j: (0, j)),
        out_shape=jax.ShapeDtypeStruct((tok, width), BF),
    )(table, ring, wide)


def over_loc(a):
    return lax.all_to_all(a, "loc", split_axis=0, concat_axis=0, tiled=True)


def ring_gather(own):
    groups = lax.axis_size("grp")
    up = [(i, (i + 1) % groups) for i in range(groups)]
    down_ring = [(i, (i - 1) % groups) for i in range(groups)]
    mid = own.shape[0] // 2
    before = lax.ppermute(own, "grp", up)
    after = lax.ppermute(own, "grp", down_ring)
    top = lax.ppermute(before[:mid], "grp", up)
    bottom = lax.ppermute(after[mid:], "grp", down_ring)
    return [own, after, top, bottom, before]


def body(tokens, grad_out, expert_ids, route_weight, gate_weight, up_weight, down_weight):
    groups = lax.axis_size("grp")
    locs = lax.axis_size("loc")
    here = lax.axis_index("grp").astype(jnp.int32)[None]
    experts = locs // 2
    width = tokens.shape[1]
    buf = experts * CAP
    span = locs * CAP
    unit = 2 * CAP
    ring_cols = 3072
    wide_cols = width - ring_cols

    w_gate, w_up, w_down = gate_weight[0], up_weight[0], down_weight[0]
    ff = w_gate.shape[1]

    table, xg_send, g_send = dispatch(expert_ids.T, route_weight.T, tokens, grad_out, experts)

    xg = over_loc(xg_send.reshape(locs, unit, xg_send.shape[3]))
    g_out = regroup(ring_gather(g_send))
    g_rows = over_loc(g_out.reshape(locs, groups * unit, g_out.shape[3]))
    g_rows = g_rows.reshape(locs * groups * unit, g_out.shape[3])
    blocks = ring_gather(xg.reshape(locs * unit, xg.shape[2]))

    slopes, swishes, parts, outers = zip(*[pre(b, w_gate, w_up, w_down) for b in blocks])
    gate_x, up_x, gate_l, up_l = deltas(here, g_rows, w_down, slopes, swishes, parts)
    rows = groups * span

    part_ring = row_part(gate_l.reshape(rows, ff), up_l.reshape(rows, ff), w_gate, w_up, 0, ring_cols)
    part_ring, gate_x, up_x = lax.optimization_barrier((part_ring, gate_x, up_x))
    home_ring = over_loc(part_ring.reshape(locs, groups * CAP, ring_cols))
    part_wide = row_part(
        gate_x.reshape(rows, ff), up_x.reshape(rows, ff), w_gate, w_up, ring_cols, wide_cols
    )
    reduced = lax.psum_scatter(
        part_wide.reshape(groups, span, wide_cols), "grp", scatter_dimension=0, tiled=True
    )

    part_wide, gate_x, up_x, outers = lax.optimization_barrier((part_wide, gate_x, up_x, outers))
    gate_grad, up_grad = row_grads(here, gate_x, up_x, blocks)
    down_grad = down(g_rows, outers, blocks)
    home_ring, gate_grad, up_grad, down_grad = lax.optimization_barrier(
        (home_ring, gate_grad, up_grad, down_grad)
    )

    folded = fold(here, home_ring.reshape(2, experts, groups * CAP, ring_cols))
    ring = lax.psum_scatter(folded, "grp", scatter_dimension=0, tiled=True)
    home_wide = over_loc(reduced.reshape(locs, CAP, wide_cols))
    tokens_grad = combine(table, ring.reshape(buf, ring_cols), home_wide)
    return (tokens_grad, gate_grad[None], up_grad[None], down_grad[None])


def solution(mesh):
    in_specs = (
        P(("grp", "loc"), None),
        P(("grp", "loc"), None),
        P(("grp", "loc"), None),
        P(("grp", "loc"), None),
        P("loc", None, "grp"),
        P("loc", None, "grp"),
        P("loc", "grp", None),
    )
    out_specs = (
        P(("grp", "loc"), None),
        P("loc", None, "grp"),
        P("loc", None, "grp"),
        P("loc", "grp", None),
    )
    return jax.shard_map(body, mesh=mesh, in_specs=in_specs, out_specs=out_specs, check_vma=False)
```

time: 267 us -> 273 us (1.022)
  blocking collectives: 54.9 us -> 0 us
  starting transfers between devices: 18.5 us -> 43.3 us
  local copies, waits for them, and re-layouts: 7.31 us -> 21.6 us
  waiting for transfers between devices: 101 us -> 115 us
  Pallas kernels: 68.2 us -> 77.2 us
    ppermute x0 -> x8, waiting for transfers between devices: none -> 76.7 us  [the longest x2 63.2 us: ring_gather(): before = lax.ppermute(own, 'grp', up)]
    all_gather x2 -> x0, waiting for transfers between devices: 61.9 us -> none  [the longest x1 61.9 us: body(): x_rows = lax.all_gather(take_tokens(xg), 'grp', axis=0, tiled=True)]
    all_to_all x1 -> x0, blocking collectives: 54.9 us -> none  [over_loc(): return lax.all_to_all(a, 'loc', split_axis=0, concat_axis=0, tiled=True)]
    all_to_all x3 -> x4, starting transfers between devices: 18.3 us -> 32.1 us  [over_loc(): return lax.all_to_all(a, 'loc', split_axis=0, concat_axis=0, tiled=True)]
    unnamed x10 -> x80, local copies, waits for them, and re-layouts: 4.96 us -> 17 us
    ppermute x0 -> x8, starting transfers between devices: none -> 11.1 us  [the longest x2 5.38 us: ring_gather(): bottom = lax.ppermute(after[mid:], 'grp', down_ring)]
    pallas_call x2, Pallas kernels: 10.9 us -> 14.2 us  [row_part(): call(row_part_kernel, 'row_part', 4 * rows * ff * count, 2 * count * (row...]
    pallas_call x7 -> x10, Pallas kernels: 52.6 us -> 55.6 us  [the longest x5 15.9 us: pre(): call(pre_kernel, 'pre', 8 * rows * cols * ff, 2 * cols * (rows + 4 * ff),...]
  transfers between devices with their start and end apart: 7 -> 14, of which waited for: 3 -> 7; matrix products, arithmetic and copies ran while one was open for 1% -> 2% of each run, Pallas kernels for 15% -> 15%
where the time goes in v3:
time: 273 us; the launch traced here: 271 us
  waiting for transfers between devices  115 us (42%)
  Pallas kernels  77.2 us (28%)
  starting transfers between devices  43.3 us (16%)
  local copies, waits for them, and re-layouts  21.6 us (8%)
  between operations  14.4 us (5%)
    ppermute x2, waiting for transfers between devices, ring_gather(): before = lax.ppermute(own, 'grp', up)  63.2 us
    all_to_all x4, starting transfers between devices, over_loc(): return lax.all_to_all(a, 'loc', split_axis=0, concat_axis=0, tiled=True)  32.1 us
    all_to_all x4, waiting for transfers between devices, over_loc(): return lax.all_to_all(a, 'loc', split_axis=0, concat_axis=0, tiled=True)  21.5 us
    unnamed x80, local copies, waits for them, and re-layouts  17 us
    reduce_scatter x1, waiting for transfers between devices, body(): ring = lax.psum_scatter(folded, 'grp', scatter_dimension=0, tiled=True)  16.6 us
    pallas_call x5, Pallas kernels, pre(): call(pre_kernel, 'pre', 8 * rows * cols * ff, 2 * cols * (rows + 4 * ff),...  15.9 us
    pallas_call x2, Pallas kernels, row_part(): call(row_part_kernel, 'row_part', 4 * rows * ff * count, 2 * count * (row...  14.2 us
    ppermute x2, waiting for transfers between devices, ring_gather(): top = lax.ppermute(before[:mid], 'grp', up)  13.5 us
  transfers between devices with their start and end apart: 14, of which 7 were waited for; matrix products, arithmetic and copies ran while one was open for 2% of the time, Pallas kernels for 15%

profile of v3, /device:TPU:1, one launch (start us, length us, event | category | flops | bytes accessed | tf_op | source)
XLA Modules:
  0.0 271.4 jit_solution(18394082968762107289)
XLA Ops:
  7.2 7.7 %dispatch.1 = (bf16[64,128]{1,0:T(8,128)(2,1)}, bf16[2,16,8,4096]{3,2,1,0:T(8,128)(2,1)}, bf16[128,3072]{1,0:T(8,128)(2,1)}) custom-call(s32[8,128]{1,0:T(8,128)} %bitcast.75, bf16[8,128]{1,0:T(8,128)(2,1)} %bitcast.76, bf16[128,7168]{1,0:T(8,128)(2,1)} %th_ref.1, bf16[128,7168]{1,0:T(8,128)(2,1)} %th_ref.1, bf16[128,7168]{1,0:T(8,128)(2,1)} %gh_ref.1, ...), custom_call_target="tpu_custom_call" | custom-call | flops 939524096 | bytes 7340032 | tf_op jit(solution)/shard_map/dispatch/pallas_call | solution.py:106
  14.8 9.6 %all-to-all-start.1 = ((bf16[32,8,4096]{2,1,0:T(8,128)(2,1)}), bf16[32,8,4096]{2,1,0:T(8,128)(2,1)S(1)}, u32[]{:S(2)}, u32[]{:S(2)}) async-start(bf16[32,8,4096]{2,1,0:T(8,128)(2,1)} %bitcast.69), calls=%async_computation.1 | async-start | bytes 4194304 | tf_op jit(solution)/shard_map/all_to_all | solution.py:505
  27.3 17.5 %collective-permute-done.1.prev_ref = bf16[128,3072]{1,0:T(8,128)(2,1)S(1)} collective-permute-done((bf16[128,3072]{1,0:T(8,128)(2,1)S(1)}, bf16[128,3072]{1,0:T(8,128)(2,1)S(1)}, u32[]{:S(2)}, u32[]{:S(2)}) %collective-permute-start.1) | collective-permute-done | bytes 786464 | tf_op jit(solution)/shard_map/ppermute | solution.py:513
  44.9 2.7 collective-permute-start.3
  47.7 8.1 %collective-permute-done.2.far_top_ref = bf16[64,3072]{1,0:T(8,128)(2,1)S(1)} collective-permute-done((bf16[64,3072]{1,0:T(8,128)(2,1)S(1)}, bf16[64,3072]{1,0:T(8,128)(2,1)S(1)}, u32[]{:S(2)}, u32[]{:S(2)}) %collective-permute-start.2) | collective-permute-done | bytes 393248 | tf_op jit(solution)/shard_map/ppermute | solution.py:515
  57.3 6.1 %regroup.1 = bf16[2,16,32,3072]{3,2,1,0:T(8,128)(2,1)} custom-call(bf16[128,3072]{1,0:T(8,128)(2,1)} %get-tuple-element.48.own_ref, bf16[128,3072]{1,0:T(8,128)(2,1)} %copy-done.36, bf16[64,3072]{1,0:T(8,128)(2,1)} %copy-done.38, bf16[64,3072]{1,0:T(8,128)(2,1)} %copy-done.39, bf16[128,3072]{1,0:T(8,128)(2,1)} %copy-done.35), custom_call_target="tpu_custom_call" | custom-call | bytes 9437184 | tf_op jit(solution)/shard_map/regroup/pallas_call | solution.py:154
  64.7 8.8 %all-to-all-start = ((bf16[32,32,3072]{2,1,0:T(8,128)(2,1)}), bf16[32,32,3072]{2,1,0:T(8,128)(2,1)}, u32[]{:S(2)}, u32[]{:S(2)}) async-start(bf16[32,32,3072]{2,1,0:T(8,128)(2,1)} %bitcast.66), calls=%async_computation | async-start | bytes 12582912 | tf_op jit(solution)/shard_map/all_to_all | solution.py:505
  76.3 45.8 %collective-permute-done.5.x_ref.prev_ref.refs_9_ = bf16[256,4096]{1,0:T(8,128)(2,1)S(1)} collective-permute-done((bf16[256,4096]{1,0:T(8,128)(2,1)}, bf16[256,4096]{1,0:T(8,128)(2,1)S(1)}, u32[]{:S(2)}, u32[]{:S(2)}) %collective-permute-start.5) | collective-permute-done | bytes 2097184 | tf_op jit(solution)/shard_map/ppermute | solution.py:513
  124.4 2.7 collective-permute-start.7
  131.6 2.9 %pre.5 = (f32[128,128]{1,0:T(8,128)S(1)}, f32[128,128]{1,0:T(8,128)S(1)}, f32[128,128]{1,0:T(8,128)S(1)}, f32[128,128]{1,0:T(8,128)S(1)}) custom-call(bf16[256,4096]{1,0:T(8,128)(2,1)S(1)} %bitcast.63, bf16[7168,128]{1,0:T(8,128)(2,1)S(1)} %bitcast.37, bf16[7168,128]{1,0:T(8,128)(2,1)S(1)} %bitcast.38, bf16[7168,128]{1,0:T(8,128)(2,1)S(1)} %bitcast.49, ...), custom_call_target="tpu_custom_call" | custom-call | flops 1073741824 | bytes 6291456 | tf_op jit(solution)/shard_map/pre/pallas_call | solution.py:206
  134.6 2.9 %pre.9 = (f32[128,128]{1,0:T(8,128)S(1)}, f32[128,128]{1,0:T(8,128)S(1)}, f32[128,128]{1,0:T(8,128)S(1)}, f32[128,128]{1,0:T(8,128)S(1)}) custom-call(bf16[256,4096]{1,0:T(8,128)(2,1)S(1)} %copy-done.8, bf16[7168,128]{1,0:T(8,128)(2,1)S(1)} %bitcast.39, bf16[7168,128]{1,0:T(8,128)(2,1)S(1)} %bitcast.40, bf16[7168,128]{1,0:T(8,128)(2,1)S(1)} %bitcast.51, ...), custom_call_target="tpu_custom_call" | custom-call | flops 1073741824 | bytes 6291456 | tf_op jit(solution)/shard_map/pre/pallas_call | solution.py:206
  140.1 2.9 %pre.6 = (f32[128,128]{1,0:T(8,128)S(1)}, f32[128,128]{1,0:T(8,128)S(1)}, f32[128,128]{1,0:T(8,128)S(1)}, f32[128,128]{1,0:T(8,128)S(1)}) custom-call(bf16[256,4096]{1,0:T(8,128)(2,1)S(1)} %copy-done.10, bf16[7168,128]{1,0:T(8,128)(2,1)S(1)} %bitcast.41, bf16[7168,128]{1,0:T(8,128)(2,1)S(1)} %bitcast.42, bf16[7168,128]{1,0:T(8,128)(2,1)S(1)} %bitcast.53, ...), custom_call_target="tpu_custom_call" | custom-call | flops 1073741824 | bytes 6291456 | tf_op jit(solution)/shard_map/pre/pallas_call | solution.py:206
  143.0 5.4 %collective-permute-done.6.x_ref.top_ref.refs_7_ = bf16[128,4096]{1,0:T(8,128)(2,1)S(1)} collective-permute-done((bf16[128,4096]{1,0:T(8,128)(2,1)}, bf16[128,4096]{1,0:T(8,128)(2,1)S(1)}, u32[]{:S(2)}, u32[]{:S(2)}) %collective-permute-start.6) | collective-permute-done | bytes 1048608 | tf_op jit(solution)/shard_map/ppermute | solution.py:515
  153.2 5.0 %pre.8 = (f32[64,128]{1,0:T(8,128)S(1)}, f32[64,128]{1,0:T(8,128)S(1)}, f32[64,128]{1,0:T(8,128)S(1)}, f32[64,128]{1,0:T(8,128)S(1)}) custom-call(bf16[128,4096]{1,0:T(8,128)(2,1)} %collective-permute-done.7.x_ref.bottom_ref.refs_8_, bf16[7168,128]{1,0:T(8,128)(2,1)S(1)} %bitcast.45, bf16[7168,128]{1,0:T(8,128)(2,1)S(1)} %bitcast.46, ...), custom_call_target="tpu_custom_call" | custom-call | flops 536870912 | bytes 5242880 | tf_op jit(solution)/shard_map/pre/pallas_call | solution.py:206
  160.6 7.4 %deltas.1 = (bf16[4,128,128]{2,1,0:T(8,128)(2,1)}, bf16[4,128,128]{2,1,0:T(8,128)(2,1)}, bf16[32,16,128]{2,1,0:T(8,128)(2,1)}, bf16[32,16,128]{2,1,0:T(8,128)(2,1)}) custom-call(s32[1]{0:T(128)} %bitcast.2.here_ref, bf16[1024,3072]{1,0:T(8,128)(2,1)} %bitcast.4.g_ref, bf16[128,7168]{1,0:T(8,128)(2,1)} %bitcast.23, bf16[128,7168]{1,0:T(8,128)(2,1)} %bitcast.24, ...), custom_call_target="tpu_custom_call" | custom-call | flops 1610612736 | bytes 8912896 | tf_op jit(solution)/shard_map/deltas/pallas_call | solution.py:280
  168.0 6.3 %row_part.2 = bf16[512,3072]{1,0:T(8,128)(2,1)} custom-call(bf16[512,128]{1,0:T(8,128)(2,1)} %bitcast.73, bf16[512,128]{1,0:T(8,128)(2,1)} %bitcast.74, bf16[7168,128]{1,0:T(8,128)(2,1)} %bitcast.35, bf16[7168,128]{1,0:T(8,128)(2,1)} %bitcast.47), custom_call_target="tpu_custom_call" | custom-call | flops 805306368 | bytes 4718592 | tf_op jit(solution)/shard_map/row_part/pallas_call | solution.py:309
  174.3 7.9 %row_part.3 = bf16[512,4096]{1,0:T(8,128)(2,1)} custom-call(bf16[512,128]{1,0:T(8,128)(2,1)} %bitcast.71, bf16[512,128]{1,0:T(8,128)(2,1)} %bitcast.72, bf16[7168,128]{1,0:T(8,128)(2,1)} %bitcast.36, bf16[7168,128]{1,0:T(8,128)(2,1)} %bitcast.48), custom_call_target="tpu_custom_call" | custom-call | flops 1073741824 | bytes 6291456 | tf_op jit(solution)/shard_map/row_part/pallas_call | solution.py:309
  182.2 8.8 %all-to-all-start.2 = ((bf16[32,16,3072]{2,1,0:T(8,128)(2,1)}), bf16[32,16,3072]{2,1,0:T(8,128)(2,1)S(1)}, u32[]{:S(2)}, u32[]{:S(2)}) async-start(bf16[32,16,3072]{2,1,0:T(8,128)(2,1)} %bitcast.68), calls=%async_computation.2 | async-start | bytes 6291456 | tf_op jit(solution)/shard_map/all_to_all | solution.py:505
  191.1 8.4 %down.1 = bf16[128,7168]{1,0:T(8,128)(2,1)} custom-call(bf16[1024,3072]{1,0:T(8,128)(2,1)} %bitcast.4.g_ref, f32[128,128]{1,0:T(8,128)} %copy-done.14, f32[128,128]{1,0:T(8,128)} %copy-done.16, f32[64,128]{1,0:T(8,128)} %copy-done.26, f32[64,128]{1,0:T(8,128)} %copy-done.27, f32[128,128]{1,0:T(8,128)} %copy-done.15, bf16[256,4096]{1,0:T(8,128)(2,1)} %bitcast.61, ...), custom_call_target="tpu_custom_call" | custom-call | flops 1879048192 | bytes 9175040 | tf_op jit(solution)/shard_map/down/pallas_call | solution.py:422
  199.5 10.1 %row_grads.1 = (bf16[2,3584,128]{2,1,0:T(8,128)(2,1)}, bf16[2,3584,128]{2,1,0:T(8,128)(2,1)}) custom-call(s32[1]{0:T(128)} %bitcast.2.here_ref, bf16[4,128,128]{2,1,0:T(8,128)(2,1)} %get-tuple-element.77.gx_ref, bf16[4,128,128]{2,1,0:T(8,128)(2,1)} %get-tuple-element.78.ux_ref, bf16[256,4096]{1,0:T(8,128)(2,1)} %bitcast.62, bf16[256,4096]{1,0:T(8,128)(2,1)} %copy-done.9, ...), custom_call_target="tpu_custom_call" | custom-call | flops 3758096384 | bytes 11010048 | tf_op jit(solution)/shard_map/row_grads/pallas_call | solution.py:357
  209.7 21.1 %all-to-all-done.2 = bf16[32,16,3072]{2,1,0:T(8,128)(2,1)S(1)} async-done(((bf16[32,16,3072]{2,1,0:T(8,128)(2,1)}), bf16[32,16,3072]{2,1,0:T(8,128)(2,1)S(1)}, u32[]{:S(2)}, u32[]{:S(2)}) %all-to-all-start.2) | async-done | bytes 3145760 | tf_op jit(solution)/shard_map/all_to_all | solution.py:505
  235.2 5.0 %all-to-all-start.3 = ((bf16[32,4,4096]{2,1,0:T(4,128)(2,1)}), bf16[32,4,4096]{2,1,0:T(4,128)(2,1)S(1)}, u32[]{:S(2)}, u32[]{:S(2)}) async-start(bf16[32,4,4096]{2,1,0:T(4,128)(2,1)} %reshape.67), calls=%async_computation.5 | async-start | bytes 2097152 | tf_op jit(solution)/shard_map/all_to_all | solution.py:505
  240.2 16.6 %reduce-scatter.3.cloned.1.call-done = bf16[1,64,3072]{2,1,0:T(8,128)(2,1)} async-done(((bf16[4,64,3072]{2,1,0:T(8,128)(2,1)}), bf16[1,64,3072]{2,1,0:T(8,128)(2,1)}) %reduce-scatter.3.cloned.1.call-update) | async-done | bytes 393232 | tf_op jit(solution)/shard_map/reduce_scatter | solution.py:565
  258.1 6.4 %combine.1 = bf16[128,7168]{1,0:T(8,128)(2,1)} custom-call(bf16[64,128]{1,0:T(8,128)(2,1)S(1)} %copy-done.34, bf16[64,3072]{1,0:T(8,128)(2,1)S(1)} %bitcast.65, bf16[32,4,4096]{2,1,0:T(4,128)(2,1)S(1)} %all-to-all-done.3.wide_ref), custom_call_target="tpu_custom_call" | custom-call | flops 117440512 | bytes 3670016 | tf_op jit(solution)/shard_map/combine/pallas_call | solution.py:487
  (105 shorter events, 31.0 us)
Async XLA Ops:
  14.8 9.6 %copy-start.37 = (bf16[128,3072]{1,0:T(8,128)(2,1)S(1)}, bf16[128,3072]{1,0:T(8,128)(2,1)}, u32[]{:S(2)}) copy-start(bf16[128,3072]{1,0:T(8,128)(2,1)} %get-tuple-element.48.own_ref) | copy-start | bytes 2359300
  14.8 48.5 %all-to-all-start.1 = ((bf16[32,8,4096]{2,1,0:T(8,128)(2,1)}), bf16[32,8,4096]{2,1,0:T(8,128)(2,1)S(1)}, u32[]{:S(2)}, u32[]{:S(2)}) async-start(bf16[32,8,4096]{2,1,0:T(8,128)(2,1)} %bitcast.69), calls=%async_computation.1 | async-start | bytes 4194304 | tf_op jit(solution)/shard_map/all_to_all | solution.py:505
  24.4 20.4 %collective-permute-start.1 = (bf16[128,3072]{1,0:T(8,128)(2,1)S(1)}, bf16[128,3072]{1,0:T(8,128)(2,1)S(1)}, u32[]{:S(2)}, u32[]{:S(2)}) collective-permute-start(bf16[128,3072]{1,0:T(8,128)(2,1)S(1)} %copy-done.37), channel_id=1, source_target_pairs={{0,32},{32,64},{64,96},{96,0},{1,33},{33,65},{65,97},{97,1},{2,34}... | collective-permute-start | bytes 2359304 | tf_op jit(solution)/shard_map/ppermute | solution.py:513
  25.8 19.1 %collective-permute-start = (bf16[128,3072]{1,0:T(8,128)(2,1)S(1)}, bf16[128,3072]{1,0:T(8,128)(2,1)S(1)}, u32[]{:S(2)}, u32[]{:S(2)}) collective-permute-start(bf16[128,3072]{1,0:T(8,128)(2,1)S(1)} %copy-done.37), channel_id=1, source_target_pairs={{0,96},{32,0},{64,32},{96,64},{1,97},{33,1},{65,33},{97,65},{2,98}... | collective-permute-start | bytes 2359304 | tf_op jit(solution)/shard_map/ppermute | solution.py:514
  44.8 11.0 %copy-start.35 = (bf16[128,3072]{1,0:T(8,128)(2,1)}, bf16[128,3072]{1,0:T(8,128)(2,1)S(1)}, u32[]{:S(2)}) copy-start(bf16[128,3072]{1,0:T(8,128)(2,1)S(1)} %collective-permute-done.1.prev_ref) | copy-start | bytes 2359300
  44.8 10.9 %collective-permute-start.2 = (bf16[64,3072]{1,0:T(8,128)(2,1)S(1)}, bf16[64,3072]{1,0:T(8,128)(2,1)S(1)}, u32[]{:S(2)}, u32[]{:S(2)}) collective-permute-start(bf16[64,3072]{1,0:T(8,128)(2,1)S(1)} %slice.16), channel_id=1, source_target_pairs={{0,32},{32,64},{64,96},{96,0},{1,33},{33,65},{65,97},{97,1},{2,34}... | collective-permute-start | bytes 1179656 | tf_op jit(solution)/shard_map/ppermute | solution.py:515
  44.9 10.9 %copy-start.36 = (bf16[128,3072]{1,0:T(8,128)(2,1)}, bf16[128,3072]{1,0:T(8,128)(2,1)S(1)}, u32[]{:S(2)}) copy-start(bf16[128,3072]{1,0:T(8,128)(2,1)S(1)} %collective-permute-done.next_ref) | copy-start | bytes 2359300
  44.9 10.8 %collective-permute-start.3 = (bf16[64,3072]{1,0:T(8,128)(2,1)S(1)}, bf16[64,3072]{1,0:T(8,128)(2,1)S(1)}, u32[]{:S(2)}, u32[]{:S(2)}) collective-permute-start(bf16[64,3072]{1,0:T(8,128)(2,1)S(1)} %slice.17), channel_id=1, source_target_pairs={{0,96},{32,0},{64,32},{96,64},{1,97},{33,1},{65,33},{97,65},{2,98}... | collective-permute-start | bytes 1179656 | tf_op jit(solution)/shard_map/ppermute | solution.py:516
  64.7 95.9 %all-to-all-start = ((bf16[32,32,3072]{2,1,0:T(8,128)(2,1)}), bf16[32,32,3072]{2,1,0:T(8,128)(2,1)}, u32[]{:S(2)}, u32[]{:S(2)}) async-start(bf16[32,32,3072]{2,1,0:T(8,128)(2,1)} %bitcast.66), calls=%async_computation | async-start | bytes 12582912 | tf_op jit(solution)/shard_map/all_to_all | solution.py:505
  73.5 159.4 %reduce-scatter.5.cloned.1.call-start = ((), (), s32[]{:S(2)}) async-start(), calls=%async_computation.7 | async-start | bytes 5242880 | tf_op jit(solution)/shard_map/reduce_scatter | solution.py:553
  73.5 53.5 %copy-start = (bf16[1,128,7168]{2,1,0:T(8,128)(2,1)S(1)}, bf16[1,128,7168]{2,1,0:T(8,128)(2,1)}, u32[]{:S(2)}) copy-start(bf16[1,128,7168]{2,1,0:T(8,128)(2,1)} %param.13) | copy-start | bytes 5505028
  73.6 48.5 %collective-permute-start.5 = (bf16[256,4096]{1,0:T(8,128)(2,1)}, bf16[256,4096]{1,0:T(8,128)(2,1)S(1)}, u32[]{:S(2)}, u32[]{:S(2)}) collective-permute-start(bf16[256,4096]{1,0:T(8,128)(2,1)} %bitcast.59), channel_id=1, source_target_pairs={{0,32},{32,64},{64,96},{96,0},{1,33},{33,65},{65,97},{97,1},{2,34}... | collective-permute-start | bytes 6291464 | tf_op jit(solution)/shard_map/ppermute | solution.py:513
  73.6 49.6 %collective-permute-start.4 = (bf16[256,4096]{1,0:T(8,128)(2,1)}, bf16[256,4096]{1,0:T(8,128)(2,1)S(1)}, u32[]{:S(2)}, u32[]{:S(2)}) collective-permute-start(bf16[256,4096]{1,0:T(8,128)(2,1)} %bitcast.60), channel_id=1, source_target_pairs={{0,96},{32,0},{64,32},{96,64},{1,97},{33,1},{65,33},{97,65},{2,98}... | collective-permute-start | bytes 6291464 | tf_op jit(solution)/shard_map/ppermute | solution.py:514
  123.2 25.2 %collective-permute-start.6 = (bf16[128,4096]{1,0:T(8,128)(2,1)}, bf16[128,4096]{1,0:T(8,128)(2,1)S(1)}, u32[]{:S(2)}, u32[]{:S(2)}) collective-permute-start(bf16[128,4096]{1,0:T(8,128)(2,1)} %slice.18), channel_id=1, source_target_pairs={{0,32},{32,64},{64,96},{96,0},{1,33},{33,65},{65,97},{97,1},{2,34}... | collective-permute-start | bytes 3145736 | tf_op jit(solution)/shard_map/ppermute | solution.py:515
  124.4 28.8 %collective-permute-start.7 = (bf16[128,4096]{1,0:T(8,128)(2,1)}, bf16[128,4096]{1,0:T(8,128)(2,1)}, u32[]{:S(2)}, u32[]{:S(2)}) collective-permute-start(bf16[128,4096]{1,0:T(8,128)(2,1)} %slice.19), channel_id=1, source_target_pairs={{0,96},{32,0},{64,32},{96,64},{1,97},{33,1},{65,33},{97,65},{2,98}... | collective-permute-start | bytes 3145736 | tf_op jit(solution)/shard_map/ppermute | solution.py:516
  134.6 5.5 %copy-start.10 = (bf16[256,4096]{1,0:T(8,128)(2,1)S(1)}, bf16[256,4096]{1,0:T(8,128)(2,1)}, u32[]{:S(2)}) copy-start(bf16[256,4096]{1,0:T(8,128)(2,1)} %copy-done.9) | copy-start | bytes 6291460
  142.9 7.7 %copy-start.16 = (f32[128,128]{1,0:T(8,128)}, f32[128,128]{1,0:T(8,128)S(1)}, u32[]{:S(2)}) copy-start(f32[128,128]{1,0:T(8,128)S(1)} %get-tuple-element.82.refs_1_) | copy-start | bytes 196612
  143.0 7.7 %copy-start.23 = (f32[128,128]{1,0:T(8,128)}, f32[128,128]{1,0:T(8,128)S(1)}, u32[]{:S(2)}) copy-start(f32[128,128]{1,0:T(8,128)S(1)} %get-tuple-element.51.refs_1_) | copy-start | bytes 196612
  143.0 7.7 %copy-start.24 = (f32[128,128]{1,0:T(8,128)}, f32[128,128]{1,0:T(8,128)S(1)}, u32[]{:S(2)}) copy-start(f32[128,128]{1,0:T(8,128)S(1)} %get-tuple-element.56.refs_6_) | copy-start | bytes 196612
  143.0 7.7 %copy-start.25 = (f32[128,128]{1,0:T(8,128)}, f32[128,128]{1,0:T(8,128)S(1)}, u32[]{:S(2)}) copy-start(f32[128,128]{1,0:T(8,128)S(1)} %get-tuple-element.61.refs_11_) | copy-start | bytes 196612
  182.2 48.5 %all-to-all-start.2 = ((bf16[32,16,3072]{2,1,0:T(8,128)(2,1)}), bf16[32,16,3072]{2,1,0:T(8,128)(2,1)S(1)}, u32[]{:S(2)}, u32[]{:S(2)}) async-start(bf16[32,16,3072]{2,1,0:T(8,128)(2,1)} %bitcast.68), calls=%async_computation.2 | async-start | bytes 6291456 | tf_op jit(solution)/shard_map/all_to_all | solution.py:505
  191.0 65.8 %reduce-scatter.3.cloned.1.call-start = ((), (), s32[]{:S(2)}) async-start(), calls=%async_computation.6 | async-start | bytes 1966080 | tf_op jit(solution)/shard_map/reduce_scatter | solution.py:565
  232.9 24.2 %copy-start.34 = (bf16[64,128]{1,0:T(8,128)(2,1)S(1)}, bf16[64,128]{1,0:T(8,128)(2,1)}, u32[]{:S(2)}) copy-start(bf16[64,128]{1,0:T(8,128)(2,1)} %get-tuple-element.47.table_ref) | copy-start | bytes 49156
  235.2 21.9 %all-to-all-start.3 = ((bf16[32,4,4096]{2,1,0:T(4,128)(2,1)}), bf16[32,4,4096]{2,1,0:T(4,128)(2,1)S(1)}, u32[]{:S(2)}, u32[]{:S(2)}) async-start(bf16[32,4,4096]{2,1,0:T(4,128)(2,1)} %reshape.67), calls=%async_computation.5 | async-start | bytes 2097152 | tf_op jit(solution)/shard_map/all_to_all | solution.py:505
  (30 other events, 46.0 us)
Sparse Core Ops, SparseCore 0:
  182.4 46.7 reduce-scatter.4
  233.0 23.7 reduce-scatter.2

commit v4 on v0

v4 whole, which is shorter than its diff:
```python
import functools

import jax
import jax.numpy as jnp
from jax import lax
from jax.experimental import pallas as pl
from jax.experimental.pallas import tpu as pltpu
from jax.sharding import PartitionSpec as P

CAP = 4
BF = jnp.bfloat16
F32 = jnp.float32
TILE = 512
ANY = pl.BlockSpec(memory_space=pl.ANY)
VMEM = pl.BlockSpec(memory_space=pltpu.VMEM)


def contract_rows(left, right):
    return lax.dot_general(left, right, (((0,), (0,)), ((), ())), preferred_element_type=F32)


def contract_cols(left, right):
    return lax.dot_general(left, right, (((1,), (1,)), ((), ())), preferred_element_type=F32)


def whole(shape):
    return pl.BlockSpec(shape, lambda *_: (0,) * len(shape))


def call(kernel, name, flops, nbytes, mib=56, **kwargs):
    return pl.pallas_call(
        kernel,
        name=name,
        compiler_params=pltpu.CompilerParams(vmem_limit_bytes=mib << 20),
        cost_estimate=pl.CostEstimate(flops=flops, bytes_accessed=nbytes, transcendentals=0),
        **kwargs,
    )


def dispatch_gradient_kernel(ids_ref, w_ref, g_ref, table_ref, pick_ref, share_ref, ring_ref, held, sem):
    load = pltpu.make_async_copy(g_ref, held, sem.at[0])
    load.start()
    topk, tok = ids_ref.shape
    buf = table_ref.shape[0]
    unit = 2 * CAP
    share = share_ref.shape[1]
    cols = ring_ref.shape[1]

    def tables(count, per_expert):
        slot_row = lax.broadcasted_iota(jnp.int32, (count, tok), 0)
        expert = lax.div(slot_row, per_expert)
        weights = w_ref[...].astype(F32)
        chosen = jnp.zeros((count, tok), F32)
        weight = jnp.zeros((count, tok), F32)
        for k in range(topk):
            hit = ids_ref[k : k + 1, :] == expert
            chosen = jnp.where(hit, 1.0, chosen)
            weight = jnp.where(hit, weights[k : k + 1, :], weight)
        before = lax.broadcasted_iota(jnp.int32, (tok, tok), 0)
        after = lax.broadcasted_iota(jnp.int32, (tok, tok), 1)
        earlier = jnp.where(before < after, 1.0, 0.0).astype(BF)
        slot = jnp.dot(chosen.astype(BF), earlier, preferred_element_type=F32)
        mine = (chosen > 0.5) & (slot == lax.rem(slot_row, CAP).astype(F32))
        return jnp.where(mine, 1.0, 0.0), jnp.where(mine, weight, 0.0), slot_row

    table_ref[...] = tables(buf, CAP)[0].astype(BF)
    table, weighted, slot_row = tables(2 * buf, unit)
    low = lax.rem(slot_row, unit) < CAP
    pick_ref[0] = jnp.where(low, table, 0.0).astype(BF)
    pick_ref[1] = jnp.where(low, 0.0, table).astype(BF)
    both = jnp.concatenate(
        [jnp.where(low, weighted, 0.0).astype(BF), jnp.where(low, 0.0, weighted).astype(BF)], axis=1
    )
    load.wait()

    def rows(first, second, count):
        parts = jnp.concatenate(
            [held[:, first : first + count], held[:, second : second + count]], axis=0
        )
        return jnp.dot(both, parts, preferred_element_type=F32).astype(BF)

    share_ref[...] = rows(0, share, share)
    for first in range(0, cols, TILE):
        start = 2 * share + first
        ring_ref[:, first : first + TILE] = rows(start, start + cols, TILE)


def dispatch_gradient(ids, weights, grad_out, experts, share):
    tok, width = grad_out.shape
    buf = experts * CAP
    small = lambda *shape: jax.ShapeDtypeStruct(shape, BF)
    return call(
        dispatch_gradient_kernel,
        "dispatch_gradient",
        4 * tok * buf * width,
        2 * width * (tok + buf),
        in_specs=[VMEM, VMEM, ANY],
        out_specs=[VMEM] * 4,
        out_shape=[
            small(buf, tok),
            small(2, 2 * buf, tok),
            small(2 * buf, share),
            small(2 * buf, width // 2 - share),
        ],
        scratch_shapes=[pltpu.VMEM((tok, width), BF), pltpu.SemaphoreType.DMA((1,))],
    )(ids, weights, grad_out)


def dispatch_token_kernel(pick_ref, share_ref, t_ref, out_ref, held, staged, sem):
    load = pltpu.make_async_copy(t_ref, held, sem.at[0])
    load.start()
    _, experts, unit, cols = out_ref.shape
    share = share_ref.shape[1]
    half = cols - share
    both = jnp.concatenate([pick_ref[0], pick_ref[1]], axis=1)
    staged[:, :, half:] = share_ref[...].reshape(experts, unit, share)
    load.wait()
    for first in range(0, half, TILE):
        parts = jnp.concatenate(
            [held[:, first : first + TILE], held[:, half + first : half + first + TILE]], axis=0
        )
        rows = jnp.dot(both, parts, preferred_element_type=F32).astype(BF)
        staged[:, :, first : first + TILE] = rows.reshape(experts, unit, TILE)
    stores = [pltpu.make_async_copy(staged, out_ref.at[h], sem.at[1 + h]) for h in range(2)]
    for store in stores:
        store.start()
    for store in stores:
        store.wait()


def dispatch_token(pick, share, tokens, experts):
    tok, width = tokens.shape
    unit = 2 * CAP
    cols = width // 2 + share.shape[1]
    return call(
        dispatch_token_kernel,
        "dispatch_token",
        4 * tok * experts * CAP * width,
        2 * width * (tok + 2 * experts * CAP),
        in_specs=[VMEM, VMEM, ANY],
        out_specs=ANY,
        out_shape=jax.ShapeDtypeStruct((2, experts, unit, cols), BF),
        scratch_shapes=[
            pltpu.VMEM((tok, width), BF),
            pltpu.VMEM((experts, unit, cols), BF),
            pltpu.SemaphoreType.DMA((3,)),
        ],
    )(pick, share, tokens)


def regroup_kernel(own_ref, next_ref, top_ref, bottom_ref, prev_ref, out_ref, sem):
    unit = own_ref.shape[1]
    mid = top_ref.shape[0]
    copies = []
    for h in range(2):
        places = [
            (own_ref, out_ref.at[h, :, :unit, :]),
            (next_ref, out_ref.at[h, :, unit : 2 * unit, :]),
            (top_ref, out_ref.at[h, :mid, 2 * unit : 3 * unit, :]),
            (bottom_ref, out_ref.at[h, mid:, 2 * unit : 3 * unit, :]),
            (prev_ref, out_ref.at[h, :, 3 * unit :, :]),
        ]
        for source, target in places:
            copies.append(pltpu.make_async_copy(source, target, sem.at[len(copies)]))
    for copy in copies:
        copy.start()
    for copy in copies:
        copy.wait()


def regroup(blocks):
    count, cols = blocks[0].shape
    unit = 2 * CAP
    experts = count // unit
    return call(
        regroup_kernel,
        "regroup",
        0,
        24 * count * cols,
        in_specs=[ANY] * 5,
        out_specs=ANY,
        out_shape=jax.ShapeDtypeStruct((2, experts, 4 * unit, cols), BF),
        scratch_shapes=[pltpu.SemaphoreType.DMA((10,))],
    )(*[b.reshape(b.shape[0] // unit, unit, cols) for b in blocks])


def pre_kernel(x_ref, wg_ref, wu_ref, wd_ref, slope_ref, swish_ref, part_ref, outer_ref, x, w, d, acc, sem):
    rows, cols = x.shape
    ff = w.shape[2] // 4
    count = rows // 2
    share = d.shape[1]
    half = cols - share
    steps = half // TILE
    weights = []
    for k, ref in enumerate((wg_ref, wu_ref)):
        for h in range(2):
            lane = (2 * k + h) * ff
            for t in range(steps):
                source = ref.at[h * half + t * TILE : h * half + (t + 1) * TILE, :]
                weights.append((t, source, w.at[t, :, lane : lane + ff]))
    copies = [[] for _ in range(steps + 1)]
    index = 0
    for t in range(steps):
        window = slice(t * TILE, (t + 1) * TILE)
        copies[t].append(pltpu.make_async_copy(x_ref.at[:, window], x.at[:, window], sem.at[index]))
        index += 1
        for step, source, target in weights:
            if step == t:
                copies[t].append(pltpu.make_async_copy(source, target, sem.at[index]))
                index += 1
    copies[steps].append(pltpu.make_async_copy(x_ref.at[:, half:], x.at[:, half:], sem.at[index]))
    for h in range(2):
        source = wd_ref.at[:, h * share : (h + 1) * share]
        target = d.at[h * ff : (h + 1) * ff, :]
        copies[steps].append(pltpu.make_async_copy(source, target, sem.at[index + 1 + h]))
    for group in copies:
        for copy in group:
            copy.start()
    for t in range(steps):
        for copy in copies[t]:
            copy.wait()
        value = jnp.dot(x[:, t * TILE : (t + 1) * TILE], w[t], preferred_element_type=F32)
        if t == 0:
            acc[...] = value
        else:
            acc[...] += value
    for copy in copies[steps]:
        copy.wait()

    def fold_halves(value):
        value = value.reshape(rows // (2 * CAP), 2 * CAP, 2 * ff)
        return (value[:, :CAP, :ff] + value[:, CAP:, ff:]).reshape(part_ref.shape)

    part_ref[...] = fold_halves(contract_cols(x[:, half:], d[...]))
    gate = fold_halves(acc[:, : 2 * ff])
    up = fold_halves(acc[:, 2 * ff :])
    sig = 1.0 / (1.0 + jnp.exp(-gate))
    swish = gate * sig
    slope_ref[...] = up * sig * (1.0 + gate * (1.0 - sig))
    swish_ref[...] = swish
    outer_ref[...] = swish * up


def pre(block, w_gate, w_up, w_down, groups, share):
    rows, cols = block.shape
    ff = w_gate.shape[1]
    steps = (cols - share) // TILE
    span = rows // 2 // groups
    return call(
        pre_kernel,
        "pre",
        8 * rows * cols * ff,
        2 * cols * (rows + 4 * ff),
        in_specs=[ANY] * 4,
        out_specs=[VMEM] * 4,
        out_shape=[jax.ShapeDtypeStruct((groups, span, ff), F32)] * 4,
        scratch_shapes=[
            pltpu.VMEM((rows, cols), BF),
            pltpu.VMEM((steps, TILE, 4 * ff), BF),
            pltpu.VMEM((2 * ff, share), BF),
            pltpu.VMEM((rows, 4 * ff), F32),
            pltpu.SemaphoreType.DMA((5 * steps + 3,)),
        ],
    )(block, w_gate, w_up, w_down)


def back_kernel(
    here_ref, g_ref, wd_ref, wg_ref, wu_ref, slope_ref, swish_ref, part_ref,
    gx_ref, ux_ref, ring_ref, wide_ref, g, d, w, near, far, staged, sem,
):
    groups, span, ff = gx_ref.shape
    locs = span // CAP
    unit = 2 * CAP
    rows, cols = g.shape
    first_col = wd_ref.shape[1] - 2 * cols
    chunk = 2 * TILE
    tile = cols // 4
    loads = []
    for t in range(4):
        window = slice(t * tile, (t + 1) * tile)
        group = [pltpu.make_async_copy(g_ref.at[:, window], g.at[:, window], sem.at[3 * t])]
        for h in range(2):
            start = first_col + h * cols + t * tile
            source = wd_ref.at[:, start : start + tile]
            target = d.at[h * ff : (h + 1) * ff, window]
            group.append(pltpu.make_async_copy(source, target, sem.at[3 * t + 1 + h]))
        loads.append(group)
    loads.append(
        [
            pltpu.make_async_copy(ref, w.at[:, k * ff : (k + 1) * ff], sem.at[12 + k])
            for k, ref in enumerate((wg_ref, wu_ref))
        ]
    )
    for group in loads:
        for load in group:
            load.start()
    total = None
    for t in range(4):
        for load in loads[t]:
            load.wait()
        window = slice(t * tile, (t + 1) * tile)
        value = contract_cols(g[:, window], d[:, window])
        total = value if total is None else total + value
    halves = total.reshape(locs, groups * unit, 2 * ff)
    for step in range(groups):
        group = lax.rem(here_ref[0] + step, groups)
        first = step * unit
        hidden = (
            halves[:, first : first + CAP, :ff] + halves[:, first + CAP : first + unit, ff:]
        ).reshape(span, ff) + part_ref[group]
        gate = hidden * slope_ref[group]
        up = hidden * swish_ref[group]
        gx_ref[group] = gate.astype(BF)
        ux_ref[group] = up.astype(BF)
        both = jnp.concatenate([gate, up], axis=1)
        far[group] = both.astype(BF)
        near[:, step * CAP : (step + 1) * CAP, :] = both.reshape(locs, CAP, 2 * ff).astype(BF)
    for load in loads[4]:
        load.wait()
    ring_cols = ring_ref.shape[1]
    stores = []
    for c in range(w.shape[0] // chunk):
        first = c * chunk
        window = slice(first, first + chunk)
        left = near[...] if first < ring_cols else far[...]
        value = contract_cols(left.reshape(groups * span, 2 * ff), w[window, :])
        staged[:, window] = value.astype(BF)
        if first < ring_cols:
            target = ring_ref.at[:, window]
        else:
            target = wide_ref.at[:, first - ring_cols : first - ring_cols + chunk]
        stores.append(pltpu.make_async_copy(staged.at[:, window], target, sem.at[14 + c]))
        stores[-1].start()
    for store in stores:
        store.wait()


def back(here, g_rows, w_down, w_gate, w_up, slope, swish, part, ring_cols):
    rows, cols = g_rows.shape
    groups, span, ff = slope.shape
    width = w_gate.shape[0]
    small = lambda *shape: jax.ShapeDtypeStruct(shape, BF)
    return call(
        back_kernel,
        "back",
        4 * rows * cols * ff + 4 * groups * span * ff * width,
        2 * (rows * cols + 3 * width * ff + groups * span * width),
        in_specs=[pl.BlockSpec(memory_space=pltpu.SMEM), ANY, ANY, ANY, ANY, VMEM, VMEM, VMEM],
        out_specs=[VMEM, VMEM, ANY, ANY],
        out_shape=[
            small(groups, span, ff),
            small(groups, span, ff),
            small(groups * span, ring_cols),
            small(groups * span, width - ring_cols),
        ],
        scratch_shapes=[
            pltpu.VMEM((rows, cols), BF),
            pltpu.VMEM((2 * ff, cols), BF),
            pltpu.VMEM((width, 2 * ff), BF),
            pltpu.VMEM((span // CAP, groups * CAP, 2 * ff), BF),
            pltpu.VMEM((groups, span, 2 * ff), BF),
            pltpu.VMEM((groups * span, width), BF),
            pltpu.SemaphoreType.DMA((14 + width // (2 * TILE),)),
        ],
    )(here, g_rows, w_down, w_gate, w_up, slope, swish, part)


def row_grads_kernel(gx_ref, ux_ref, x_ref, gate_ref, up_ref, wide):
    groups, span, ff = gx_ref.shape
    locs = span // CAP

    @pl.when(pl.program_id(0) == 0)
    def _():
        zero = jnp.zeros((locs, CAP, ff), F32)
        for group in range(groups):
            gate = gx_ref[group].astype(F32).reshape(locs, CAP, ff)
            up = ux_ref[group].astype(F32).reshape(locs, CAP, ff)
            low = jnp.concatenate([gate, zero, up, zero], axis=2)
            high = jnp.concatenate([zero, gate, zero, up], axis=2)
            both = jnp.concatenate([low, high], axis=1).reshape(2 * span, 4 * ff)
            wide[2 * span * group : 2 * span * (group + 1), :] = both.astype(BF)

    total = contract_rows(x_ref[...], wide[...]).astype(BF)
    gate_ref[0] = total[:, :ff]
    gate_ref[1] = total[:, ff : 2 * ff]
    up_ref[0] = total[:, 2 * ff : 3 * ff]
    up_ref[1] = total[:, 3 * ff :]


def row_grads(gate_x, up_x, x_rows, share):
    groups, span, ff = gate_x.shape
    rows, cols = x_rows.shape
    half = cols - share
    out = jax.ShapeDtypeStruct((2, half, ff), BF)
    gate, up = call(
        row_grads_kernel,
        "row_grads",
        8 * rows * half * ff,
        2 * half * (rows + 4 * ff),
        grid=(half // TILE,),
        in_specs=[
            whole(gate_x.shape),
            whole(up_x.shape),
            pl.BlockSpec((rows, TILE), lambda j: (0, j)),
        ],
        out_specs=[pl.BlockSpec((2, TILE, ff), lambda j: (0, j, 0))] * 2,
        out_shape=[out, out],
        scratch_shapes=[pltpu.VMEM((rows, 4 * ff), BF)],
    )(gate_x, up_x, x_rows)
    return gate.reshape(2 * half, ff), up.reshape(2 * half, ff)


def down_kernel(here_ref, outer_ref, x_ref, g_ref, out_ref, wide):
    groups, span, ff = outer_ref.shape
    locs = span // CAP
    unit = 2 * CAP
    step = pl.program_id(0)
    tile = g_ref.shape[1]
    share = x_ref.shape[1]

    def spread(outer):
        rows = outer.reshape(locs, CAP, ff)
        zero = jnp.zeros_like(rows)
        low = jnp.concatenate([rows, zero], axis=2)
        high = jnp.concatenate([zero, rows], axis=2)
        return jnp.concatenate([low, high], axis=1)

    @pl.when(step == 0)
    def _():
        rows = []
        for k in range(groups):
            other = outer_ref[lax.rem(here_ref[0] + k, groups)]
            wide[:, k * unit : (k + 1) * unit, :] = spread(other).astype(BF)
            rows.append(spread(outer_ref[k]).reshape(2 * span, 2 * ff).astype(BF))
        total = contract_rows(jnp.concatenate(rows, axis=0), x_ref[...]).astype(BF)
        out_ref[:, :share] = total[:ff]
        out_ref[:, share : 2 * share] = total[ff:]

    rows = wide[...].reshape(g_ref.shape[0], 2 * ff)
    total = contract_rows(rows, g_ref[...]).astype(BF)
    low = 2 * share + step * tile
    high = low + pl.num_programs(0) * tile
    out_ref[:, pl.ds(pl.multiple_of(low, 128), tile)] = total[:ff]
    out_ref[:, pl.ds(pl.multiple_of(high, 128), tile)] = total[ff:]


def down(here, outer, x_rows, g_rows, share):
    rows, cols = g_rows.shape
    groups, span, ff = outer.shape
    width = 2 * (cols + share)
    last = x_rows.shape[1] // share - 1
    return call(
        down_kernel,
        "down",
        4 * rows * (cols + share) * ff,
        2 * (cols + share) * (rows + 2 * ff),
        grid_spec=pltpu.PrefetchScalarGridSpec(
            num_scalar_prefetch=1,
            grid=(cols // TILE,),
            in_specs=[
                whole(outer.shape),
                pl.BlockSpec((rows, share), lambda j, _: (0, last)),
                pl.BlockSpec((rows, TILE), lambda j, _: (0, j)),
            ],
            out_specs=whole((ff, width)),
            scratch_shapes=[pltpu.VMEM((span // CAP, 2 * groups * CAP, 2 * ff), BF)],
        ),
        out_shape=jax.ShapeDtypeStruct((ff, width), BF),
    )(here, outer, x_rows, g_rows)


def fold_kernel(here_ref, in_ref, out_ref):
    _, experts, depth, tile = in_ref.shape
    groups = depth // CAP
    total = in_ref[0].astype(F32) + in_ref[1].astype(F32)
    for step in range(groups):
        part = total[:, step * CAP : (step + 1) * CAP, :]
        group = lax.rem(here_ref[0] + step, groups)
        out_ref[group] = part.reshape(experts * CAP, tile).astype(BF)


def fold(here, home):
    _, experts, depth, width = home.shape
    groups = depth // CAP
    return call(
        fold_kernel,
        "fold",
        experts * depth * width,
        6 * experts * depth * width,
        mib=20,
        grid_spec=pltpu.PrefetchScalarGridSpec(
            num_scalar_prefetch=1,
            grid=(width // (2 * TILE),),
            in_specs=[pl.BlockSpec((2, experts, depth, 2 * TILE), lambda j, _: (0, 0, 0, j))],
            out_specs=pl.BlockSpec((groups, experts * CAP, 2 * TILE), lambda j, _: (0, 0, j)),
        ),
        out_shape=jax.ShapeDtypeStruct((groups, experts * CAP, width), BF),
    )(here, home)


def combine_kernel(split, table_ref, ring_ref, wide_ref, out_ref):
    table = table_ref[...]

    @pl.when(pl.program_id(0) < split)
    def _():
        out_ref[...] = contract_rows(table, ring_ref[...]).astype(BF)

    @pl.when(pl.program_id(0) >= split)
    def _():
        count, _, tile = wide_ref.shape
        rows = wide_ref[...].astype(F32).reshape(count * CAP, tile).astype(BF)
        both = jnp.concatenate([table, table], axis=0)
        out_ref[...] = contract_rows(both, rows).astype(BF)


def combine(table, ring, wide):
    buf, tok = table.shape
    width = ring.shape[1] + wide.shape[2]
    tile = 2 * TILE
    split = ring.shape[1] // tile
    return call(
        functools.partial(combine_kernel, split),
        "combine",
        2 * tok * buf * width,
        2 * width * (tok + 2 * buf),
        mib=20,
        grid=(width // tile,),
        in_specs=[
            whole((buf, tok)),
            pl.BlockSpec((buf, tile), lambda j: (0, jnp.minimum(j, split - 1))),
            pl.BlockSpec((wide.shape[0], CAP, tile), lambda j: (0, 0, jnp.maximum(j - split, 0))),
        ],
        out_specs=pl.BlockSpec((tok, tile), lambda j: (0, j)),
        out_shape=jax.ShapeDtypeStruct((tok, width), BF),
    )(table, ring, wide)


def over_loc(a):
    return lax.all_to_all(a, "loc", split_axis=0, concat_axis=0, tiled=True)


def ring_gather(own):
    groups = lax.axis_size("grp")
    up = [(i, (i + 1) % groups) for i in range(groups)]
    down_ring = [(i, (i - 1) % groups) for i in range(groups)]
    mid = own.shape[0] // 2
    before = lax.ppermute(own, "grp", up)
    after = lax.ppermute(own, "grp", down_ring)
    top = lax.ppermute(before[:mid], "grp", up)
    bottom = lax.ppermute(after[mid:], "grp", down_ring)
    return [own, after, top, bottom, before]


def body(tokens, grad_out, expert_ids, route_weight, gate_weight, up_weight, down_weight):
    groups = lax.axis_size("grp")
    locs = lax.axis_size("loc")
    here = lax.axis_index("grp").astype(jnp.int32)[None]
    experts = locs // 2
    width = tokens.shape[1]
    buf = experts * CAP
    span = locs * CAP
    unit = 2 * CAP
    ring_cols = 3072
    wide_cols = width - ring_cols

    share = TILE

    w_gate, w_up, w_down = gate_weight[0], up_weight[0], down_weight[0]

    table, pick, g_share, g_send = dispatch_gradient(
        expert_ids.T, route_weight.T, grad_out, experts, share
    )
    g_blocks = ring_gather(g_send)
    xg_send = dispatch_token(pick, g_share, tokens, experts)
    xg = over_loc(xg_send.reshape(locs, unit, xg_send.shape[3]))
    xg, *g_blocks = lax.optimization_barrier((xg, *g_blocks))
    g_out = regroup(g_blocks)
    g_rows = over_loc(g_out.reshape(locs, groups * unit, g_out.shape[3]))
    g_rows = g_rows.reshape(locs * groups * unit, g_out.shape[3])
    x_rows = lax.all_gather(xg.reshape(locs * unit, xg.shape[2]), "grp", axis=0, tiled=True)

    slope, swish, part, outer = pre(x_rows, w_gate, w_up, w_down, groups, share)
    gate_x, up_x, part_ring, part_wide = back(
        here, g_rows, w_down, w_gate, w_up, slope, swish, part, ring_cols
    )

    home_ring = over_loc(part_ring.reshape(locs, groups * CAP, ring_cols))
    reduced = lax.psum_scatter(
        part_wide.reshape(groups, span, wide_cols), "grp", scatter_dimension=0, tiled=True
    )
    gate_grad, up_grad = row_grads(gate_x, up_x, x_rows, share)
    outer, gate_x = lax.optimization_barrier((outer, gate_x))
    down_grad = down(here, outer, x_rows, g_rows, share)
    home_ring, gate_grad, up_grad, down_grad = lax.optimization_barrier(
        (home_ring, gate_grad, up_grad, down_grad)
    )

    folded = fold(here, home_ring.reshape(2, experts, groups * CAP, ring_cols))
    ring = lax.psum_scatter(folded, "grp", scatter_dimension=0, tiled=True)
    home_wide = over_loc(reduced.reshape(locs, CAP, wide_cols))
    tokens_grad = combine(table, ring.reshape(buf, ring_cols), home_wide)
    return (tokens_grad, gate_grad[None], up_grad[None], down_grad[None])


def solution(mesh):
    in_specs = (
        P(("grp", "loc"), None),
        P(("grp", "loc"), None),
        P(("grp", "loc"), None),
        P(("grp", "loc"), None),
        P("loc", None, "grp"),
        P("loc", None, "grp"),
        P("loc", "grp", None),
    )
    out_specs = (
        P(("grp", "loc"), None),
        P("loc", None, "grp"),
        P("loc", None, "grp"),
        P("loc", "grp", None),
    )
    return jax.shard_map(body, mesh=mesh, in_specs=in_specs, out_specs=out_specs, check_vma=False)
```

time: 424 us -> 444 us (1.047)
  Pallas kernels: 0 us -> 243 us
  waiting for transfers between devices: 237 us -> 135 us
  local copies, waits for them, and re-layouts: 70.9 us -> 5.85 us
  matrix products: 59.3 us -> 0 us
  starting transfers between devices: 33 us -> 45.3 us
  other arithmetic: 7.89 us -> 0 us
    pallas_call x0 -> x9, Pallas kernels: none -> 243 us  [the longest x1 192 us: regroup(): call(regroup_kernel, 'regroup', 0, 24 * count * cols, in_specs=[ANY] * 5,...]
    all_to_all x4, waiting for transfers between devices: 165 us -> 91.6 us  [over_loc(): return lax.all_to_all(a, 'loc', split_axis=0, concat_axis=0, tiled=True)]
    dot_general x12 -> x0, matrix products: 59.3 us -> none  [the longest x3 23.2 us: contract_cols(): lax.dot_general(left, right, (((1,), (1,)), ((), ())), preferred_element_...]
    reduce_scatter x1 -> x2, waiting for transfers between devices: 71.4 us -> 17.7 us  [the longest x1 17.7 us: body(): ring = lax.psum_scatter(folded, 'grp', scatter_dimension=0, tiled=True)]
    ppermute x0 -> x4, waiting for transfers between devices: none -> 25.7 us  [the longest x1 17.7 us: ring_gather(): before = lax.ppermute(own, 'grp', up)]
    reshape x4 -> x1, local copies, waits for them, and re-layouts: 27.4 us -> 2.26 us  [body(): home_wide = over_loc(reduced.reshape(locs, CAP, wide_cols))]
    convert_element_type x3 -> x0, local copies, waits for them, and re-layouts: 21.1 us -> none  [the longest x2 21 us: body(): reduced = lax.psum_scatter(partial_value.astype(jnp.float32).reshape(grou...]
    another operation x9 -> x0, local copies, waits for them, and re-layouts: 14.8 us -> none  [the longest x2 7.27 us: body(): jnp.tile(x_unit, (copies, 1, 1, 1))]
  transfers between devices with their start and end apart: 5 -> 11, of which waited for: 5 -> 5; matrix products, arithmetic and copies ran while one was open for 11% -> 1% of each run, Pallas kernels for 0% -> 49%
where the time goes in v4:
time: 444 us; the launch traced here: 443 us
  Pallas kernels  243 us (55%)
  waiting for transfers between devices  135 us (30%)
  starting transfers between devices  45.3 us (10%)
  between operations  13.9 us (3%)
  local copies, waits for them, and re-layouts  5.85 us (1%)
    pallas_call x1, Pallas kernels, regroup(): call(regroup_kernel, 'regroup', 0, 24 * count * cols, in_specs=[ANY] * 5,...  192 us
    all_to_all x4, waiting for transfers between devices, over_loc(): return lax.all_to_all(a, 'loc', split_axis=0, concat_axis=0, tiled=True)  91.6 us
    all_to_all x4, starting transfers between devices, over_loc(): return lax.all_to_all(a, 'loc', split_axis=0, concat_axis=0, tiled=True)  39.3 us
    reduce_scatter x1, waiting for transfers between devices, body(): ring = lax.psum_scatter(folded, 'grp', scatter_dimension=0, tiled=True)  17.7 us
    ppermute x1, waiting for transfers between devices, ring_gather(): before = lax.ppermute(own, 'grp', up)  17.7 us
    pallas_call x1, Pallas kernels, back(): call(back_kernel, 'back', 4 * rows * cols * ff + 4 * groups * span * ff *...  12.5 us
    pallas_call x1, Pallas kernels, row_grads(): call(row_grads_kernel, 'row_grads', 8 * rows * half * ff, 2 * half * (row...  9.54 us
  transfers between devices with their start and end apart: 11, of which 5 were waited for; matrix products, arithmetic and copies ran while one was open for 1% of the time, Pallas kernels for 49%

profile of v4, /device:TPU:1, one launch (start us, length us, event | category | flops | bytes accessed | tf_op | source)
XLA Modules:
  0.0 442.8 jit_solution(12627327233581367005)
XLA Ops:
  7.2 3.5 dispatch_gradient.1
  10.7 4.2 dispatch_token.1
  14.9 9.4 %all-to-all-start = ((bf16[32,8,4096]{2,1,0:T(8,128)(2,1)}), bf16[32,8,4096]{2,1,0:T(8,128)(2,1)S(1)}, u32[]{:S(2)}, u32[]{:S(2)}) async-start(bf16[32,8,4096]{2,1,0:T(8,128)(2,1)} %bitcast.28), calls=%async_computation | async-start | bytes 4194304 | tf_op jit(solution)/shard_map/all_to_all | solution.py:539
  24.4 1.4 collective-permute-start.1
  25.8 1.5 collective-permute-start
  27.3 17.7 %collective-permute-done.1 = bf16[128,3072]{1,0:T(8,128)(2,1)S(1)} collective-permute-done((bf16[128,3072]{1,0:T(8,128)(2,1)}, bf16[128,3072]{1,0:T(8,128)(2,1)S(1)}, u32[]{:S(2)}, u32[]{:S(2)}) %collective-permute-start.1) | collective-permute-done | bytes 786464 | tf_op jit(solution)/shard_map/ppermute | solution.py:547
  45.1 2.7 collective-permute-start.3
  47.8 8.1 %collective-permute-done.2 = bf16[64,3072]{1,0:T(8,128)(2,1)S(1)} collective-permute-done((bf16[64,3072]{1,0:T(8,128)(2,1)S(1)}, bf16[64,3072]{1,0:T(8,128)(2,1)S(1)}, u32[]{:S(2)}, u32[]{:S(2)}) %collective-permute-start.2) | collective-permute-done | bytes 393248 | tf_op jit(solution)/shard_map/ppermute | solution.py:549
  55.9 1.4 copy-done.3
  57.3 191.8 %regroup.1 = bf16[2,16,32,3072]{3,2,1,0:T(8,128)(2,1)} custom-call(bf16[16,8,3072]{2,1,0:T(8,128)(2,1)} %bitcast.34, bf16[16,8,3072]{2,1,0:T(8,128)(2,1)} %bitcast.33, bf16[8,8,3072]{2,1,0:T(8,128)(2,1)} %bitcast.35, bf16[8,8,3072]{2,1,0:T(8,128)(2,1)} %bitcast.7.bottom_ref, bf16[16,8,3072]{2,1,0:T(8,128)(2,1)} %bitcast.32), custom_call_target="tpu_custom_call" | custom-call | bytes 9437184 | tf_op jit(solution)/shard_map/regroup/pallas_call | solution.py:175
  249.1 8.8 %all-to-all-start.1 = ((bf16[32,32,3072]{2,1,0:T(8,128)(2,1)}), bf16[32,32,3072]{2,1,0:T(8,128)(2,1)}, u32[]{:S(2)}, u32[]{:S(2)}) async-start(bf16[32,32,3072]{2,1,0:T(8,128)(2,1)} %bitcast.26), calls=%async_computation.1 | async-start | bytes 12582912 | tf_op jit(solution)/shard_map/all_to_all | solution.py:539
  258.2 8.1 %pre.1 = (f32[4,128,128]{2,1,0:T(8,128)}, f32[4,128,128]{2,1,0:T(8,128)}, f32[4,128,128]{2,1,0:T(8,128)}, f32[4,128,128]{2,1,0:T(8,128)}) custom-call(bf16[1024,4096]{1,0:T(8,128)(2,1)} %all-gather.2.cloned.1.call-done.x_ref, bf16[7168,128]{1,0:T(8,128)(2,1)} %bitcast.40, bf16[7168,128]{1,0:T(8,128)(2,1)} %bitcast.42, bf16[128,7168]{1,0:T(8,128)(2,1)} %bitcast.38), custom_call_target="tpu_custom_call" | custom-call | flops 4294967296 | bytes 12582912 | tf_op jit(solution)/shard_map/pre/pallas_call | solution.py:249
  266.4 69.5 %all-to-all-done.1 = bf16[32,32,3072]{2,1,0:T(8,128)(2,1)} async-done(((bf16[32,32,3072]{2,1,0:T(8,128)(2,1)}), bf16[32,32,3072]{2,1,0:T(8,128)(2,1)}, u32[]{:S(2)}, u32[]{:S(2)}) %all-to-all-start.1) | async-done | bytes 6291488 | tf_op jit(solution)/shard_map/all_to_all | solution.py:539
  335.9 12.5 %back.1 = (bf16[4,128,128]{2,1,0:T(8,128)(2,1)}, bf16[4,128,128]{2,1,0:T(8,128)(2,1)}, bf16[512,3072]{1,0:T(8,128)(2,1)}, bf16[512,4096]{1,0:T(8,128)(2,1)}) custom-call(s32[1]{0:T(128)} %bitcast.2.here_ref, bf16[1024,3072]{1,0:T(8,128)(2,1)} %bitcast.10.g_ref, bf16[128,7168]{1,0:T(8,128)(2,1)} %bitcast.39, bf16[7168,128]{1,0:T(8,128)(2,1)} %bitcast.41, ...), custom_call_target="tpu_custom_call" | custom-call | flops 3489660928 | bytes 19136512 | tf_op jit(solution)/shard_map/back/pallas_call | solution.py:343
  348.5 14.5 %all-to-all-start.2 = ((bf16[32,16,3072]{2,1,0:T(8,128)(2,1)}), bf16[32,16,3072]{2,1,0:T(8,128)(2,1)S(1)}, u32[]{:S(2)}, u32[]{:S(2)}) async-start(bf16[32,16,3072]{2,1,0:T(8,128)(2,1)} %bitcast.30), calls=%async_computation.2 | async-start | bytes 6291456 | tf_op jit(solution)/shard_map/all_to_all | solution.py:539
  363.1 8.1 %down.1 = bf16[128,7168]{1,0:T(8,128)(2,1)} custom-call(s32[1]{0:T(128)} %bitcast.2.here_ref, f32[4,128,128]{2,1,0:T(8,128)} %get-tuple-element.48.outer_ref, bf16[1024,4096]{1,0:T(8,128)(2,1)} %all-gather.2.cloned.1.call-done.x_ref, bf16[1024,3072]{1,0:T(8,128)(2,1)} %bitcast.10.g_ref), custom_call_target="tpu_custom_call" | custom-call | flops 1879048192 | bytes 9175040 | tf_op jit(solution)/shard_map/down/pallas_call | solution.py:452
  371.2 9.5 %row_grads.1 = (bf16[2,3584,128]{2,1,0:T(8,128)(2,1)}, bf16[2,3584,128]{2,1,0:T(8,128)(2,1)}) custom-call(bf16[4,128,128]{2,1,0:T(8,128)(2,1)} %get-tuple-element.43.gx_ref, bf16[4,128,128]{2,1,0:T(8,128)(2,1)} %get-tuple-element.44.ux_ref, bf16[1024,4096]{1,0:T(8,128)(2,1)} %all-gather.2.cloned.1.call-done.x_ref), custom_call_target="tpu_custom_call" | custom-call | flops 3758096384 | bytes 11010048 | tf_op jit(solution)/shard_map/row_grads/pallas_call | solution.py:395
  380.8 22.0 %all-to-all-done.2 = bf16[32,16,3072]{2,1,0:T(8,128)(2,1)S(1)} async-done(((bf16[32,16,3072]{2,1,0:T(8,128)(2,1)}), bf16[32,16,3072]{2,1,0:T(8,128)(2,1)S(1)}, u32[]{:S(2)}, u32[]{:S(2)}) %all-to-all-start.2) | async-done | bytes 3145760 | tf_op jit(solution)/shard_map/all_to_all | solution.py:539
  403.7 1.1 copy-done
  404.9 2.3 reshape.71
  407.2 6.5 %all-to-all-start.3 = ((bf16[32,4,4096]{2,1,0:T(4,128)(2,1)}), bf16[32,4,4096]{2,1,0:T(4,128)(2,1)S(1)}, u32[]{:S(2)}, u32[]{:S(2)}) async-start(bf16[32,4,4096]{2,1,0:T(4,128)(2,1)} %reshape.71), calls=%async_computation.5 | async-start | bytes 2097152 | tf_op jit(solution)/shard_map/all_to_all | solution.py:539
  413.7 17.7 %reduce-scatter.3.cloned.1.call-done = bf16[1,64,3072]{2,1,0:T(8,128)(2,1)} async-done(((bf16[4,64,3072]{2,1,0:T(8,128)(2,1)}), bf16[1,64,3072]{2,1,0:T(8,128)(2,1)}) %reduce-scatter.3.cloned.1.call-update) | async-done | bytes 393232 | tf_op jit(solution)/shard_map/reduce_scatter | solution.py:599
  431.4 1.0 copy-done.1
  432.4 3.9 combine.1
  (27 shorter events, 1.4 us)
Async XLA Ops:
  14.9 41.0 %all-to-all-start = ((bf16[32,8,4096]{2,1,0:T(8,128)(2,1)}), bf16[32,8,4096]{2,1,0:T(8,128)(2,1)S(1)}, u32[]{:S(2)}, u32[]{:S(2)}) async-start(bf16[32,8,4096]{2,1,0:T(8,128)(2,1)} %bitcast.28), calls=%async_computation | async-start | bytes 4194304 | tf_op jit(solution)/shard_map/all_to_all | solution.py:539
  24.3 233.9 %all-gather.2.cloned.1.call-start = ((), (), s32[]{:S(2)}) async-start(), calls=%async_computation.6 | async-start | bytes 10485760 | tf_op jit(solution)/shard_map/all_gather | solution.py:580
  24.4 20.5 %collective-permute-start.1 = (bf16[128,3072]{1,0:T(8,128)(2,1)}, bf16[128,3072]{1,0:T(8,128)(2,1)S(1)}, u32[]{:S(2)}, u32[]{:S(2)}) collective-permute-start(bf16[128,3072]{1,0:T(8,128)(2,1)} %get-tuple-element.33), channel_id=1, source_target_pairs={{0,32},{32,64},{64,96},{96,0},{1,33},{33,65},{65,97},{97,1},{2,34}... | collective-permute-start | bytes 2359304 | tf_op jit(solution)/shard_map/ppermute | solution.py:547
  25.8 19.3 %collective-permute-start = (bf16[128,3072]{1,0:T(8,128)(2,1)}, bf16[128,3072]{1,0:T(8,128)(2,1)S(1)}, u32[]{:S(2)}, u32[]{:S(2)}) collective-permute-start(bf16[128,3072]{1,0:T(8,128)(2,1)} %get-tuple-element.33), channel_id=1, source_target_pairs={{0,96},{32,0},{64,32},{96,64},{1,97},{33,1},{65,33},{97,65},{2,98}... | collective-permute-start | bytes 2359304 | tf_op jit(solution)/shard_map/ppermute | solution.py:548
  44.9 12.4 %copy-start.4 = (bf16[128,3072]{1,0:T(8,128)(2,1)}, bf16[128,3072]{1,0:T(8,128)(2,1)S(1)}, u32[]{:S(2)}) copy-start(bf16[128,3072]{1,0:T(8,128)(2,1)S(1)} %collective-permute-done.1) | copy-start | bytes 2359300
  45.0 10.9 %collective-permute-start.2 = (bf16[64,3072]{1,0:T(8,128)(2,1)S(1)}, bf16[64,3072]{1,0:T(8,128)(2,1)S(1)}, u32[]{:S(2)}, u32[]{:S(2)}) collective-permute-start(bf16[64,3072]{1,0:T(8,128)(2,1)S(1)} %slice.8), channel_id=1, source_target_pairs={{0,32},{32,64},{64,96},{96,0},{1,33},{33,65},{65,97},{97,1},{2,34}... | collective-permute-start | bytes 1179656 | tf_op jit(solution)/shard_map/ppermute | solution.py:549
  45.1 10.8 %copy-start.5 = (bf16[128,3072]{1,0:T(8,128)(2,1)}, bf16[128,3072]{1,0:T(8,128)(2,1)S(1)}, u32[]{:S(2)}) copy-start(bf16[128,3072]{1,0:T(8,128)(2,1)S(1)} %collective-permute-done) | copy-start | bytes 2359300
  45.1 10.8 %collective-permute-start.3 = (bf16[64,3072]{1,0:T(8,128)(2,1)S(1)}, bf16[64,3072]{1,0:T(8,128)(2,1)}, u32[]{:S(2)}, u32[]{:S(2)}) collective-permute-start(bf16[64,3072]{1,0:T(8,128)(2,1)S(1)} %slice.9), channel_id=1, source_target_pairs={{0,96},{32,0},{64,32},{96,64},{1,97},{33,1},{65,33},{97,65},{2,98}... | collective-permute-start | bytes 1179656 | tf_op jit(solution)/shard_map/ppermute | solution.py:550
  55.9 1.4 copy-start.6
  55.9 1.4 copy-start.3
  249.1 86.8 %all-to-all-start.1 = ((bf16[32,32,3072]{2,1,0:T(8,128)(2,1)}), bf16[32,32,3072]{2,1,0:T(8,128)(2,1)}, u32[]{:S(2)}, u32[]{:S(2)}) async-start(bf16[32,32,3072]{2,1,0:T(8,128)(2,1)} %bitcast.26), calls=%async_computation.1 | async-start | bytes 12582912 | tf_op jit(solution)/shard_map/all_to_all | solution.py:539
  258.0 146.9 %reduce-scatter.5.cloned.1.call-start = ((), (), s32[]{:S(2)}) async-start(), calls=%async_computation.8 | async-start | bytes 5242880 | tf_op jit(solution)/shard_map/reduce_scatter | solution.py:588
  348.5 54.3 %all-to-all-start.2 = ((bf16[32,16,3072]{2,1,0:T(8,128)(2,1)}), bf16[32,16,3072]{2,1,0:T(8,128)(2,1)S(1)}, u32[]{:S(2)}, u32[]{:S(2)}) async-start(bf16[32,16,3072]{2,1,0:T(8,128)(2,1)} %bitcast.30), calls=%async_computation.2 | async-start | bytes 6291456 | tf_op jit(solution)/shard_map/all_to_all | solution.py:539
  363.1 68.3 %reduce-scatter.3.cloned.1.call-start = ((), (), s32[]{:S(2)}) async-start(), calls=%async_computation.7 | async-start | bytes 1966080 | tf_op jit(solution)/shard_map/reduce_scatter | solution.py:599
  403.7 1.1 copy-start
  404.9 26.5 %copy-start.2 = (bf16[64,128]{1,0:T(8,128)(2,1)S(1)}, bf16[64,128]{1,0:T(8,128)(2,1)}, u32[]{:S(2)}) copy-start(bf16[64,128]{1,0:T(8,128)(2,1)} %get-tuple-element.29.table_ref) | copy-start | bytes 49156
  407.2 24.2 %all-to-all-start.3 = ((bf16[32,4,4096]{2,1,0:T(4,128)(2,1)}), bf16[32,4,4096]{2,1,0:T(4,128)(2,1)S(1)}, u32[]{:S(2)}, u32[]{:S(2)}) async-start(bf16[32,4,4096]{2,1,0:T(4,128)(2,1)} %reshape.71), calls=%async_computation.5 | async-start | bytes 2097152 | tf_op jit(solution)/shard_map/all_to_all | solution.py:539
  431.4 1.0 copy-start.1
Sparse Core Ops, SparseCore 0:
  57.4 85.5 all-gather.1
  348.6 55.1 reduce-scatter.4
  406.9 24.4 reduce-scatter.2

commit v5 on v4

--- a/solution.py
+++ b/solution.py
@@ -148,40 +148,45 @@
     )(pick, share, tokens)
 
 
-def regroup_kernel(own_ref, next_ref, top_ref, bottom_ref, prev_ref, out_ref, sem):
-    unit = own_ref.shape[1]
-    mid = top_ref.shape[0]
-    copies = []
-    for h in range(2):
-        places = [
-            (own_ref, out_ref.at[h, :, :unit, :]),
-            (next_ref, out_ref.at[h, :, unit : 2 * unit, :]),
-            (top_ref, out_ref.at[h, :mid, 2 * unit : 3 * unit, :]),
-            (bottom_ref, out_ref.at[h, mid:, 2 * unit : 3 * unit, :]),
-            (prev_ref, out_ref.at[h, :, 3 * unit :, :]),
-        ]
-        for source, target in places:
-            copies.append(pltpu.make_async_copy(source, target, sem.at[len(copies)]))
-    for copy in copies:
-        copy.start()
-    for copy in copies:
-        copy.wait()
-
-
-def regroup(blocks):
-    count, cols = blocks[0].shape
-    unit = 2 * CAP
-    experts = count // unit
+def regroup_kernel(in_ref, out_ref, held, sem):
+    groups, experts, unit, _ = in_ref.shape
+    parts = 4
+    size = experts // parts
+    loads, stores = [], []
+    for p in range(parts):
+        window = slice(p * size, (p + 1) * size)
+        for y in range(groups):
+            source = in_ref.at[y, window, :, :]
+            target = held.at[window, y * unit : (y + 1) * unit, :]
+            loads.append(pltpu.make_async_copy(source, target, sem.at[p * groups + y]))
+            loads[-1].start()
+    for p in range(parts):
+        window = slice(p * size, (p + 1) * size)
+        for y in range(groups):
+            loads[p * groups + y].wait()
+        for h in range(2):
+            index = parts * groups + 2 * p + h
+            stores.append(pltpu.make_async_copy(held.at[window], out_ref.at[h, window], sem.at[index]))
+            stores[-1].start()
+    for store in stores:
+        store.wait()
+
+
+def regroup(rows):
+    groups, experts, unit, cols = rows.shape
     return call(
         regroup_kernel,
         "regroup",
         0,
-        24 * count * cols,
-        in_specs=[ANY] * 5,
+        6 * groups * experts * unit * cols,
+        in_specs=[ANY],
         out_specs=ANY,
-        out_shape=jax.ShapeDtypeStruct((2, experts, 4 * unit, cols), BF),
-        scratch_shapes=[pltpu.SemaphoreType.DMA((10,))],
-    )(*[b.reshape(b.shape[0] // unit, unit, cols) for b in blocks])
+        out_shape=jax.ShapeDtypeStruct((2, experts, groups * unit, cols), BF),
+        scratch_shapes=[
+            pltpu.VMEM((experts, groups * unit, cols), BF),
+            pltpu.SemaphoreType.DMA((4 * groups + 8,)),
+        ],
+    )(rows)
 
 
 def pre_kernel(x_ref, wg_ref, wu_ref, wd_ref, slope_ref, swish_ref, part_ref, outer_ref, x, w, d, acc, sem):
@@ -264,15 +269,17 @@
     )(block, w_gate, w_up, w_down)
 
 
-def back_kernel(
-    here_ref, g_ref, wd_ref, wg_ref, wu_ref, slope_ref, swish_ref, part_ref,
-    gx_ref, ux_ref, ring_ref, wide_ref, g, d, w, near, far, staged, sem,
+def hidden_kernel(
+    g_ref, wd_ref, wg_ref, wu_ref, slope_ref, swish_ref, part_ref,
+    gx_ref, ux_ref, near_ref, wide_ref, g, d, w, far, staged, sem,
 ):
     groups, span, ff = gx_ref.shape
     locs = span // CAP
     unit = 2 * CAP
-    rows, cols = g.shape
+    cols = g.shape[1]
+    wide_cols = wide_ref.shape[1]
     first_col = wd_ref.shape[1] - 2 * cols
+    first_row = wg_ref.shape[0] - wide_cols
     chunk = 2 * TILE
     tile = cols // 4
     loads = []
@@ -285,12 +292,11 @@
             target = d.at[h * ff : (h + 1) * ff, window]
             group.append(pltpu.make_async_copy(source, target, sem.at[3 * t + 1 + h]))
         loads.append(group)
-    loads.append(
-        [
-            pltpu.make_async_copy(ref, w.at[:, k * ff : (k + 1) * ff], sem.at[12 + k])
-            for k, ref in enumerate((wg_ref, wu_ref))
-        ]
-    )
+    group = []
+    for k, ref in enumerate((wg_ref, wu_ref)):
+        source = ref.at[first_row : first_row + wide_cols, :]
+        group.append(pltpu.make_async_copy(source, w.at[:, k * ff : (k + 1) * ff], sem.at[12 + k]))
+    loads.append(group)
     for group in loads:
         for load in group:
             load.start()
@@ -302,9 +308,8 @@
         value = contract_cols(g[:, window], d[:, window])
         total = value if total is None else total + value
     halves = total.reshape(locs, groups * unit, 2 * ff)
-    for step in range(groups):
-        group = lax.rem(here_ref[0] + step, groups)
-        first = step * unit
+    for group in range(groups):
+        first = group * unit
         hidden = (
             halves[:, first : first + CAP, :ff] + halves[:, first + CAP : first + unit, ff:]
         ).reshape(span, ff) + part_ref[group]
@@ -314,55 +319,88 @@
         ux_ref[group] = up.astype(BF)
         both = jnp.concatenate([gate, up], axis=1)
         far[group] = both.astype(BF)
-        near[:, step * CAP : (step + 1) * CAP, :] = both.reshape(locs, CAP, 2 * ff).astype(BF)
+        near_ref[:, group * CAP : (group + 1) * CAP, :] = both.reshape(locs, CAP, 2 * ff).astype(BF)
     for load in loads[4]:
         load.wait()
-    ring_cols = ring_ref.shape[1]
+    left = far[...].reshape(groups * span, 2 * ff)
     stores = []
-    for c in range(w.shape[0] // chunk):
-        first = c * chunk
-        window = slice(first, first + chunk)
-        left = near[...] if first < ring_cols else far[...]
-        value = contract_cols(left.reshape(groups * span, 2 * ff), w[window, :])
-        staged[:, window] = value.astype(BF)
-        if first < ring_cols:
-            target = ring_ref.at[:, window]
-        else:
-            target = wide_ref.at[:, first - ring_cols : first - ring_cols + chunk]
+    for c in range(wide_cols // chunk):
+        window = slice(c * chunk, (c + 1) * chunk)
+        staged[:, window] = contract_cols(left, w[window, :]).astype(BF)
+        target = wide_ref.at[:, window]
         stores.append(pltpu.make_async_copy(staged.at[:, window], target, sem.at[14 + c]))
         stores[-1].start()
     for store in stores:
         store.wait()
 
 
-def back(here, g_rows, w_down, w_gate, w_up, slope, swish, part, ring_cols):
+def hidden(g_rows, w_down, w_gate, w_up, slope, swish, part, wide_cols):
     rows, cols = g_rows.shape
     groups, span, ff = slope.shape
-    width = w_gate.shape[0]
     small = lambda *shape: jax.ShapeDtypeStruct(shape, BF)
     return call(
-        back_kernel,
-        "back",
-        4 * rows * cols * ff + 4 * groups * span * ff * width,
-        2 * (rows * cols + 3 * width * ff + groups * span * width),
-        in_specs=[pl.BlockSpec(memory_space=pltpu.SMEM), ANY, ANY, ANY, ANY, VMEM, VMEM, VMEM],
-        out_specs=[VMEM, VMEM, ANY, ANY],
+        hidden_kernel,
+        "hidden",
+        4 * rows * cols * ff + 4 * groups * span * ff * wide_cols,
+        2 * (rows * cols + 3 * wide_cols * ff + groups * span * wide_cols),
+        in_specs=[ANY, ANY, ANY, ANY, VMEM, VMEM, VMEM],
+        out_specs=[VMEM, VMEM, VMEM, ANY],
         out_shape=[
             small(groups, span, ff),
             small(groups, span, ff),
-            small(groups * span, ring_cols),
-            small(groups * span, width - ring_cols),
+            small(span // CAP, groups * CAP, 2 * ff),
+            small(groups * span, wide_cols),
         ],
         scratch_shapes=[
             pltpu.VMEM((rows, cols), BF),
             pltpu.VMEM((2 * ff, cols), BF),
-            pltpu.VMEM((width, 2 * ff), BF),
-            pltpu.VMEM((span // CAP, groups * CAP, 2 * ff), BF),
+            pltpu.VMEM((wide_cols, 2 * ff), BF),
             pltpu.VMEM((groups, span, 2 * ff), BF),
-            pltpu.VMEM((groups * span, width), BF),
-            pltpu.SemaphoreType.DMA((14 + width // (2 * TILE),)),
-        ],
-    )(here, g_rows, w_down, w_gate, w_up, slope, swish, part)
+            pltpu.VMEM((groups * span, wide_cols), BF),
+            pltpu.SemaphoreType.DMA((14 + wide_cols // (2 * TILE),)),
+        ],
+    )(g_rows, w_down, w_gate, w_up, slope, swish, part)
+
+
+def ring_part_kernel(near_ref, wg_ref, wu_ref, out_ref, w, staged, sem):
+    rows, ring_cols = out_ref.shape
+    ff = wg_ref.shape[1]
+    loads = []
+    for k, ref in enumerate((wg_ref, wu_ref)):
+        target = w.at[:, k * ff : (k + 1) * ff]
+        loads.append(pltpu.make_async_copy(ref.at[:ring_cols, :], target, sem.at[k]))
+        loads[-1].start()
+    for load in loads:
+        load.wait()
+    left = near_ref[...].reshape(rows, 2 * ff)
+    stores = []
+    for c in range(ring_cols // TILE):
+        window = slice(c * TILE, (c + 1) * TILE)
+        staged[:, window] = contract_cols(left, w[window, :]).astype(BF)
+        target = out_ref.at[:, window]
+        stores.append(pltpu.make_async_copy(staged.at[:, window], target, sem.at[2 + c]))
+        stores[-1].start()
+    for store in stores:
+        store.wait()
+
+
+def ring_part(near, w_gate, w_up, ring_cols):
+    locs, depth, double = near.shape
+    rows = locs * depth
+    return call(
+        ring_part_kernel,
+        "ring_part",
+        2 * rows * double * ring_cols,
+        2 * ring_cols * (rows + double),
+        in_specs=[VMEM, ANY, ANY],
+        out_specs=ANY,
+        out_shape=jax.ShapeDtypeStruct((rows, ring_cols), BF),
+        scratch_shapes=[
+            pltpu.VMEM((ring_cols, double), BF),
+            pltpu.VMEM((rows, ring_cols), BF),
+            pltpu.SemaphoreType.DMA((2 + ring_cols // TILE,)),
+        ],
+    )(near, w_gate, w_up)
 
 
 def row_grads_kernel(gx_ref, ux_ref, x_ref, gate_ref, up_ref, wide):
@@ -410,7 +448,7 @@
     return gate.reshape(2 * half, ff), up.reshape(2 * half, ff)
 
 
-def down_kernel(here_ref, outer_ref, x_ref, g_ref, out_ref, wide):
+def down_kernel(outer_ref, x_ref, g_ref, out_ref, wide):
     groups, span, ff = outer_ref.shape
     locs = span // CAP
     unit = 2 * CAP
@@ -429,9 +467,9 @@
     def _():
         rows = []
         for k in range(groups):
-            other = outer_ref[lax.rem(here_ref[0] + k, groups)]
-            wide[:, k * unit : (k + 1) * unit, :] = spread(other).astype(BF)
-            rows.append(spread(outer_ref[k]).reshape(2 * span, 2 * ff).astype(BF))
+            block = spread(outer_ref[k]).astype(BF)
+            wide[:, k * unit : (k + 1) * unit, :] = block
+            rows.append(block.reshape(2 * span, 2 * ff))
         total = contract_rows(jnp.concatenate(rows, axis=0), x_ref[...]).astype(BF)
         out_ref[:, :share] = total[:ff]
         out_ref[:, share : 2 * share] = total[ff:]
@@ -444,7 +482,7 @@
     out_ref[:, pl.ds(pl.multiple_of(high, 128), tile)] = total[ff:]
 
 
-def down(here, outer, x_rows, g_rows, share):
+def down(outer, x_rows, g_rows, share):
     rows, cols = g_rows.shape
     groups, span, ff = outer.shape
     width = 2 * (cols + share)
@@ -454,48 +492,42 @@
         "down",
         4 * rows * (cols + share) * ff,
         2 * (cols + share) * (rows + 2 * ff),
-        grid_spec=pltpu.PrefetchScalarGridSpec(
-            num_scalar_prefetch=1,
-            grid=(cols // TILE,),
-            in_specs=[
-                whole(outer.shape),
-                pl.BlockSpec((rows, share), lambda j, _: (0, last)),
-                pl.BlockSpec((rows, TILE), lambda j, _: (0, j)),
-            ],
-            out_specs=whole((ff, width)),
-            scratch_shapes=[pltpu.VMEM((span // CAP, 2 * groups * CAP, 2 * ff), BF)],
-        ),
+        grid=(cols // TILE,),
+        in_specs=[
+            whole(outer.shape),
+            pl.BlockSpec((rows, share), lambda j: (0, last)),
+            pl.BlockSpec((rows, TILE), lambda j: (0, j)),
+        ],
+        out_specs=whole((ff, width)),
         out_shape=jax.ShapeDtypeStruct((ff, width), BF),
-    )(here, outer, x_rows, g_rows)
-
-
-def fold_kernel(here_ref, in_ref, out_ref):
+        scratch_shapes=[pltpu.VMEM((span // CAP, 2 * groups * CAP, 2 * ff), BF)],
+    )(outer, x_rows, g_rows)
+
+
+def fold_kernel(in_ref, out_ref):
     _, experts, depth, tile = in_ref.shape
     groups = depth // CAP
     total = in_ref[0].astype(F32) + in_ref[1].astype(F32)
     for step in range(groups):
         part = total[:, step * CAP : (step + 1) * CAP, :]
-        group = lax.rem(here_ref[0] + step, groups)
-        out_ref[group] = part.reshape(experts * CAP, tile).astype(BF)
-
-
-def fold(here, home):
+        out_ref[step] = part.reshape(experts * CAP, tile).astype(BF)
+
+
+def fold(home):
     _, experts, depth, width = home.shape
     groups = depth // CAP
+    tile = 2 * TILE
     return call(
         fold_kernel,
         "fold",
         experts * depth * width,
         6 * experts * depth * width,
         mib=20,
-        grid_spec=pltpu.PrefetchScalarGridSpec(
-            num_scalar_prefetch=1,
-            grid=(width // (2 * TILE),),
-            in_specs=[pl.BlockSpec((2, experts, depth, 2 * TILE), lambda j, _: (0, 0, 0, j))],
-            out_specs=pl.BlockSpec((groups, experts * CAP, 2 * TILE), lambda j, _: (0, 0, j)),
-        ),
+        grid=(width // tile,),
+        in_specs=[pl.BlockSpec((2, experts, depth, tile), lambda j: (0, 0, 0, j))],
+        out_specs=pl.BlockSpec((groups, experts * CAP, tile), lambda j: (0, 0, j)),
         out_shape=jax.ShapeDtypeStruct((groups, experts * CAP, width), BF),
-    )(here, home)
+    )(home)
 
 
 def combine_kernel(split, table_ref, ring_ref, wide_ref, out_ref):
@@ -539,22 +571,9 @@
     return lax.all_to_all(a, "loc", split_axis=0, concat_axis=0, tiled=True)
 
 
-def ring_gather(own):
-    groups = lax.axis_size("grp")
-    up = [(i, (i + 1) % groups) for i in range(groups)]
-    down_ring = [(i, (i - 1) % groups) for i in range(groups)]
-    mid = own.shape[0] // 2
-    before = lax.ppermute(own, "grp", up)
-    after = lax.ppermute(own, "grp", down_ring)
-    top = lax.ppermute(before[:mid], "grp", up)
-    bottom = lax.ppermute(after[mid:], "grp", down_ring)
-    return [own, after, top, bottom, before]
-
-
 def body(tokens, grad_out, expert_ids, route_weight, gate_weight, up_weight, down_weight):
     groups = lax.axis_size("grp")
     locs = lax.axis_size("loc")
-    here = lax.axis_index("grp").astype(jnp.int32)[None]
     experts = locs // 2
     width = tokens.shape[1]
     buf = experts * CAP
@@ -570,32 +589,31 @@
     table, pick, g_share, g_send = dispatch_gradient(
         expert_ids.T, route_weight.T, grad_out, experts, share
     )
-    g_blocks = ring_gather(g_send)
+    g_ring = lax.all_gather(g_send, "grp", axis=0, tiled=True)
     xg_send = dispatch_token(pick, g_share, tokens, experts)
     xg = over_loc(xg_send.reshape(locs, unit, xg_send.shape[3]))
-    xg, *g_blocks = lax.optimization_barrier((xg, *g_blocks))
-    g_out = regroup(g_blocks)
+    x_rows = lax.all_gather(xg.reshape(locs * unit, xg.shape[2]), "grp", axis=0, tiled=True)
+    g_out = regroup(g_ring.reshape(groups, experts, unit, g_ring.shape[1]))
     g_rows = over_loc(g_out.reshape(locs, groups * unit, g_out.shape[3]))
     g_rows = g_rows.reshape(locs * groups * unit, g_out.shape[3])
-    x_rows = lax.all_gather(xg.reshape(locs * unit, xg.shape[2]), "grp", axis=0, tiled=True)
 
     slope, swish, part, outer = pre(x_rows, w_gate, w_up, w_down, groups, share)
-    gate_x, up_x, part_ring, part_wide = back(
-        here, g_rows, w_down, w_gate, w_up, slope, swish, part, ring_cols
-    )
+    gate_x, up_x, near, part_wide = hidden(g_rows, w_down, w_gate, w_up, slope, swish, part, wide_cols)
+    part_wide, near = lax.optimization_barrier((part_wide, near))
+    part_ring = ring_part(near, w_gate, w_up, ring_cols)
 
     home_ring = over_loc(part_ring.reshape(locs, groups * CAP, ring_cols))
     reduced = lax.psum_scatter(
         part_wide.reshape(groups, span, wide_cols), "grp", scatter_dimension=0, tiled=True
     )
+    part_ring, gate_x, up_x, outer = lax.optimization_barrier((part_ring, gate_x, up_x, outer))
     gate_grad, up_grad = row_grads(gate_x, up_x, x_rows, share)
-    outer, gate_x = lax.optimization_barrier((outer, gate_x))
-    down_grad = down(here, outer, x_rows, g_rows, share)
+    down_grad = down(outer, x_rows, g_rows, share)
     home_ring, gate_grad, up_grad, down_grad = lax.optimization_barrier(
         (home_ring, gate_grad, up_grad, down_grad)
     )
 
-    folded = fold(here, home_ring.reshape(2, experts, groups * CAP, ring_cols))
+    folded = fold(home_ring.reshape(2, experts, groups * CAP, ring_cols))
     ring = lax.psum_scatter(folded, "grp", scatter_dimension=0, tiled=True)
     home_wide = over_loc(reduced.reshape(locs, CAP, wide_cols))
     tokens_grad = combine(table, ring.reshape(buf, ring_cols), home_wide)

time: 444 us -> 251 us (0.57)
  Pallas kernels: 243 us -> 57.2 us
  blocking collectives: 0 us -> 37.7 us
  waiting for transfers between devices: 135 us -> 113 us
  starting transfers between devices: 45.3 us -> 24.2 us
    pallas_call x2 -> x3, Pallas kernels: 204 us -> 19.1 us  [the longest x1 10.6 us: hidden(): call(hidden_kernel, 'hidden', 4 * rows * cols * ff + 4 * groups * span *...]
    all_gather x1, waiting for transfers between devices: 0.02 us -> 73.2 us  [body(): lax.all_gather(xg.reshape(locs * unit, xg.shape[2]), 'grp', axis=0, tiled...]
    all_to_all x4 -> x3, waiting for transfers between devices: 91.6 us -> 23.9 us  [over_loc(): return lax.all_to_all(a, 'loc', split_axis=0, concat_axis=0, tiled=True)]
    all_to_all x0 -> x1, blocking collectives: none -> 37.7 us  [over_loc(): return lax.all_to_all(a, 'loc', split_axis=0, concat_axis=0, tiled=True)]
    ppermute x4 -> x0, waiting for transfers between devices: 25.7 us -> none  [the longest x1 17.7 us: ring_gather(): before = lax.ppermute(own, 'grp', up)]
    all_to_all x4 -> x3, starting transfers between devices: 39.3 us -> 23.8 us  [over_loc(): return lax.all_to_all(a, 'loc', split_axis=0, concat_axis=0, tiled=True)]
    ppermute x4 -> x0, starting transfers between devices: 5.68 us -> none  [the longest x1 2.71 us: ring_gather(): bottom = lax.ppermute(after[mid:], 'grp', down_ring)]
  transfers between devices with their start and end apart: 11 -> 7, of which waited for: 5 -> 5; matrix products, arithmetic and copies ran while one was open for 1% -> 1% of each run, Pallas kernels for 49% -> 16%
where the time goes in v5:
time: 251 us; the launch traced here: 250 us
  waiting for transfers between devices  113 us (45%)
  Pallas kernels  57.2 us (23%)
  blocking collectives  37.7 us (15%)
  starting transfers between devices  24.2 us (10%)
  between operations  13.9 us (6%)
  local copies, waits for them, and re-layouts  4.38 us (2%)
    all_gather x1, waiting for transfers between devices, body(): lax.all_gather(xg.reshape(locs * unit, xg.shape[2]), 'grp', axis=0, tiled...  73.2 us
    all_to_all x1, blocking collectives, over_loc(): return lax.all_to_all(a, 'loc', split_axis=0, concat_axis=0, tiled=True)  37.7 us
    all_to_all x3, waiting for transfers between devices, over_loc(): return lax.all_to_all(a, 'loc', split_axis=0, concat_axis=0, tiled=True)  23.9 us
    all_to_all x3, starting transfers between devices, over_loc(): return lax.all_to_all(a, 'loc', split_axis=0, concat_axis=0, tiled=True)  23.8 us
    reduce_scatter x1, waiting for transfers between devices, body(): ring = lax.psum_scatter(folded, 'grp', scatter_dimension=0, tiled=True)  15.1 us
    pallas_call x1, Pallas kernels, hidden(): call(hidden_kernel, 'hidden', 4 * rows * cols * ff + 4 * groups * span *...  10.6 us
    pallas_call x1, Pallas kernels, row_grads(): call(row_grads_kernel, 'row_grads', 8 * rows * half * ff, 2 * half * (row...  9.55 us
    pallas_call x1, Pallas kernels, pre(): call(pre_kernel, 'pre', 8 * rows * cols * ff, 2 * cols * (rows + 4 * ff),...  8.15 us
  transfers between devices with their start and end apart: 7, of which 5 were waited for; matrix products, arithmetic and copies ran while one was open for 1% of the time, Pallas kernels for 16%

profile of v5, /device:TPU:1, one launch (start us, length us, event | category | flops | bytes accessed | tf_op | source)
XLA Modules:
  0.0 250.5 jit_solution(9944303111135503240)
XLA Ops:
  7.2 3.5 %dispatch_gradient.1 = (bf16[64,128]{1,0:T(8,128)(2,1)}, bf16[2,128,128]{2,1,0:T(8,128)(2,1)}, bf16[128,512]{1,0:T(8,128)(2,1)}, bf16[128,3072]{1,0:T(8,128)(2,1)}) custom-call(s32[8,128]{1,0:T(8,128)} %bitcast.36, bf16[8,128]{1,0:T(8,128)(2,1)} %bitcast.37, bf16[128,7168]{1,0:T(8,128)(2,1)} %g_ref.1), custom_call_target="tpu_custom_call" | custom-call | flops 234881024 | bytes 2752512 | tf_op jit(solution)/shard_map/dispatch_gradient/pallas_call | solution.py:92
  10.7 0.0 all-gather.5.cloned.1.call-start
  10.8 4.2 %dispatch_token.1 = bf16[2,16,8,4096]{3,2,1,0:T(8,128)(2,1)} custom-call(bf16[2,128,128]{2,1,0:T(8,128)(2,1)} %get-tuple-element.29.pick_ref, bf16[128,512]{1,0:T(8,128)(2,1)} %get-tuple-element.30.share_ref, bf16[128,7168]{1,0:T(8,128)(2,1)} %t_ref.1), custom_call_target="tpu_custom_call" | custom-call | flops 234881024 | bytes 3670016 | tf_op jit(solution)/shard_map/dispatch_token/pallas_call | solution.py:135
  15.0 37.7 %all_to_all.20 = bf16[32,8,4096]{2,1,0:T(8,128)(2,1)} all-to-all(bf16[32,8,4096]{2,1,0:T(8,128)(2,1)} %bitcast.24), channel_id=1, replica_groups=mesh['grp'=4,'loc'=32] {'loc'}, dimensions={0} | all-to-all | bytes 4194304 | tf_op jit(solution)/shard_map/all_to_all | solution.py:571
  52.7 0.9 all-gather.3.cloned.1.call-done
  53.7 4.0 %regroup.1 = bf16[2,16,32,3072]{3,2,1,0:T(8,128)(2,1)} custom-call(bf16[4,16,8,3072]{3,2,1,0:T(8,128)(2,1)} %bitcast.32), custom_call_target="tpu_custom_call" | custom-call | bytes 9437184 | tf_op jit(solution)/shard_map/regroup/pallas_call | solution.py:177
  57.7 7.7 %all-to-all-start = ((bf16[32,32,3072]{2,1,0:T(8,128)(2,1)}), bf16[32,32,3072]{2,1,0:T(8,128)(2,1)}, u32[]{:S(2)}, u32[]{:S(2)}) async-start(bf16[32,32,3072]{2,1,0:T(8,128)(2,1)} %bitcast.21), calls=%async_computation | async-start | bytes 12582912 | tf_op jit(solution)/shard_map/all_to_all | solution.py:571
  65.5 73.2 %all-gather.5.cloned.1.call-done.x_ref = bf16[1024,4096]{1,0:T(8,128)(2,1)} async-done(((bf16[256,4096]{1,0:T(8,128)(2,1)}), bf16[1024,4096]{1,0:T(8,128)(2,1)}) %all-gather.5.cloned.1.call-update) | async-done | bytes 8388624 | tf_op jit(solution)/shard_map/all_gather | solution.py:595
  138.7 8.2 %pre.1 = (f32[4,128,128]{2,1,0:T(8,128)}, f32[4,128,128]{2,1,0:T(8,128)}, f32[4,128,128]{2,1,0:T(8,128)}, f32[4,128,128]{2,1,0:T(8,128)}) custom-call(bf16[1024,4096]{1,0:T(8,128)(2,1)} %all-gather.5.cloned.1.call-done.x_ref, bf16[7168,128]{1,0:T(8,128)(2,1)} %bitcast.25, bf16[7168,128]{1,0:T(8,128)(2,1)} %bitcast.28, bf16[128,7168]{1,0:T(8,128)(2,1)} %bitcast.33), custom_call_target="tpu_custom_call" | custom-call | flops 4294967296 | bytes 12582912 | tf_op jit(solution)/shard_map/pre/pallas_call | solution.py:254
  146.8 10.6 %hidden.1 = (bf16[4,128,128]{2,1,0:T(8,128)(2,1)}, bf16[4,128,128]{2,1,0:T(8,128)(2,1)}, bf16[32,16,256]{2,1,0:T(8,128)(2,1)}, bf16[512,4096]{1,0:T(8,128)(2,1)}) custom-call(bf16[1024,3072]{1,0:T(8,128)(2,1)} %bitcast.4.g_ref, bf16[128,7168]{1,0:T(8,128)(2,1)} %bitcast.34, bf16[7168,128]{1,0:T(8,128)(2,1)} %bitcast.26, bf16[7168,128]{1,0:T(8,128)(2,1)} %bitcast.29, ...), custom_call_target="tpu_custom_call" | custom-call | flops 2684354560 | bytes 13631488 | tf_op jit(solution)/shard_map/hidden/pallas_call | solution.py:341
  157.5 4.5 %ring_part.1 = bf16[512,3072]{1,0:T(8,128)(2,1)} custom-call(bf16[32,16,256]{2,1,0:T(8,128)(2,1)} %get-tuple-element.36.near_ref, bf16[7168,128]{1,0:T(8,128)(2,1)} %bitcast.27, bf16[7168,128]{1,0:T(8,128)(2,1)} %bitcast.30), custom_call_target="tpu_custom_call" | custom-call | flops 805306368 | bytes 4718592 | tf_op jit(solution)/shard_map/ring_part/pallas_call | solution.py:390
  161.9 11.1 %all-to-all-start.2 = ((bf16[32,16,3072]{2,1,0:T(8,128)(2,1)}), bf16[32,16,3072]{2,1,0:T(8,128)(2,1)S(1)}, u32[]{:S(2)}, u32[]{:S(2)}) async-start(bf16[32,16,3072]{2,1,0:T(8,128)(2,1)} %bitcast.22), calls=%async_computation.2 | async-start | bytes 6291456 | tf_op jit(solution)/shard_map/all_to_all | solution.py:571
  173.1 0.2 reduce-scatter.3.cloned.1.call-start
  173.3 7.9 %down.1 = bf16[128,7168]{1,0:T(8,128)(2,1)} custom-call(f32[4,128,128]{2,1,0:T(8,128)} %get-tuple-element.44.outer_ref, bf16[1024,4096]{1,0:T(8,128)(2,1)} %all-gather.5.cloned.1.call-done.x_ref, bf16[1024,3072]{1,0:T(8,128)(2,1)} %bitcast.4.g_ref), custom_call_target="tpu_custom_call" | custom-call | flops 1879048192 | bytes 9175040 | tf_op jit(solution)/shard_map/down/pallas_call | solution.py:490
  181.2 9.5 %row_grads.1 = (bf16[2,3584,128]{2,1,0:T(8,128)(2,1)}, bf16[2,3584,128]{2,1,0:T(8,128)(2,1)}) custom-call(bf16[4,128,128]{2,1,0:T(8,128)(2,1)} %get-tuple-element.40.gx_ref, bf16[4,128,128]{2,1,0:T(8,128)(2,1)} %get-tuple-element.41.ux_ref, bf16[1024,4096]{1,0:T(8,128)(2,1)} %all-gather.5.cloned.1.call-done.x_ref), custom_call_target="tpu_custom_call" | custom-call | flops 3758096384 | bytes 11010048 | tf_op jit(solution)/shard_map/row_grads/pallas_call | solution.py:433
  190.7 22.1 %all-to-all-done.2 = bf16[32,16,3072]{2,1,0:T(8,128)(2,1)S(1)} async-done(((bf16[32,16,3072]{2,1,0:T(8,128)(2,1)}), bf16[32,16,3072]{2,1,0:T(8,128)(2,1)S(1)}, u32[]{:S(2)}, u32[]{:S(2)}) %all-to-all-start.2) | async-done | bytes 3145760 | tf_op jit(solution)/shard_map/all_to_all | solution.py:571
  212.8 0.9 fold.1
  213.7 1.1 copy-done
  214.9 2.2 reshape.55
  217.1 5.0 %all-to-all-start.3 = ((bf16[32,4,4096]{2,1,0:T(4,128)(2,1)}), bf16[32,4,4096]{2,1,0:T(4,128)(2,1)S(1)}, u32[]{:S(2)}, u32[]{:S(2)}) async-start(bf16[32,4,4096]{2,1,0:T(4,128)(2,1)} %reshape.55), calls=%async_computation.5 | async-start | bytes 2097152 | tf_op jit(solution)/shard_map/all_to_all | solution.py:571
  222.1 15.1 %reduce-scatter.3.cloned.1.call-done = bf16[1,64,3072]{2,1,0:T(8,128)(2,1)} async-done(((bf16[4,64,3072]{2,1,0:T(8,128)(2,1)}), bf16[1,64,3072]{2,1,0:T(8,128)(2,1)}) %reduce-scatter.3.cloned.1.call-update) | async-done | bytes 393232 | tf_op jit(solution)/shard_map/reduce_scatter | solution.py:617
  237.2 1.8 all-to-all-done.3.wide_ref
  239.1 1.0 copy-done.1
  240.0 3.9 %combine.1 = bf16[128,7168]{1,0:T(8,128)(2,1)} custom-call(bf16[64,128]{1,0:T(8,128)(2,1)S(1)} %copy-done.2, bf16[64,3072]{1,0:T(8,128)(2,1)S(1)} %bitcast.20, bf16[32,4,4096]{2,1,0:T(4,128)(2,1)S(1)} %all-to-all-done.3.wide_ref), custom_call_target="tpu_custom_call" | custom-call | flops 117440512 | bytes 3670016 | tf_op jit(solution)/shard_map/combine/pallas_call | solution.py:553
  (12 shorter events, 0.2 us)
Async XLA Ops:
  7.2 46.5 %all-gather.3.cloned.1.call-start = ((), (), s32[]{:S(2)}) async-start(), calls=%async_computation.6 | async-start | bytes 3932160 | tf_op jit(solution)/shard_map/all_gather | solution.py:592
  10.7 127.9 %all-gather.5.cloned.1.call-start = ((), (), s32[]{:S(2)}) async-start(), calls=%async_computation.7 | async-start | bytes 10485760 | tf_op jit(solution)/shard_map/all_gather | solution.py:595
  57.7 89.1 %all-to-all-start = ((bf16[32,32,3072]{2,1,0:T(8,128)(2,1)}), bf16[32,32,3072]{2,1,0:T(8,128)(2,1)}, u32[]{:S(2)}, u32[]{:S(2)}) async-start(bf16[32,32,3072]{2,1,0:T(8,128)(2,1)} %bitcast.21), calls=%async_computation | async-start | bytes 12582912 | tf_op jit(solution)/shard_map/all_to_all | solution.py:571
  65.4 149.5 %reduce-scatter.5.cloned.1.call-start = ((), (), s32[]{:S(2)}) async-start(), calls=%async_computation.9 | async-start | bytes 5242880 | tf_op jit(solution)/shard_map/reduce_scatter | solution.py:606
  161.9 50.9 %all-to-all-start.2 = ((bf16[32,16,3072]{2,1,0:T(8,128)(2,1)}), bf16[32,16,3072]{2,1,0:T(8,128)(2,1)S(1)}, u32[]{:S(2)}, u32[]{:S(2)}) async-start(bf16[32,16,3072]{2,1,0:T(8,128)(2,1)} %bitcast.22), calls=%async_computation.2 | async-start | bytes 6291456 | tf_op jit(solution)/shard_map/all_to_all | solution.py:571
  173.1 64.2 %reduce-scatter.3.cloned.1.call-start = ((), (), s32[]{:S(2)}) async-start(), calls=%async_computation.8 | async-start | bytes 1966080 | tf_op jit(solution)/shard_map/reduce_scatter | solution.py:617
  213.7 1.1 copy-start
  214.9 24.2 %copy-start.2 = (bf16[64,128]{1,0:T(8,128)(2,1)S(1)}, bf16[64,128]{1,0:T(8,128)(2,1)}, u32[]{:S(2)}) copy-start(bf16[64,128]{1,0:T(8,128)(2,1)} %get-tuple-element.27.table_ref) | copy-start | bytes 49156
  217.1 21.9 %all-to-all-start.3 = ((bf16[32,4,4096]{2,1,0:T(4,128)(2,1)}), bf16[32,4,4096]{2,1,0:T(4,128)(2,1)S(1)}, u32[]{:S(2)}, u32[]{:S(2)}) async-start(bf16[32,4,4096]{2,1,0:T(4,128)(2,1)} %reshape.55), calls=%async_computation.5 | async-start | bytes 2097152 | tf_op jit(solution)/shard_map/all_to_all | solution.py:571
  239.1 1.0 copy-start.1
Sparse Core Ops, SparseCore 0:
  10.9 42.7 all-gather.2
  55.3 83.2 all-gather.4
  157.6 50.4 reduce-scatter.4
  215.0 22.1 reduce-scatter.2

commit v6 on v5

v6 whole, which is shorter than its diff:
```python
import functools

import jax
import jax.numpy as jnp
from jax import lax
from jax.experimental import pallas as pl
from jax.experimental.pallas import tpu as pltpu
from jax.sharding import PartitionSpec as P

CAP = 4
BF = jnp.bfloat16
F32 = jnp.float32
TILE = 512
ANY = pl.BlockSpec(memory_space=pl.ANY)
VMEM = pl.BlockSpec(memory_space=pltpu.VMEM)


def contract_rows(left, right):
    return lax.dot_general(left, right, (((0,), (0,)), ((), ())), preferred_element_type=F32)


def contract_cols(left, right):
    return lax.dot_general(left, right, (((1,), (1,)), ((), ())), preferred_element_type=F32)


def whole(shape):
    return pl.BlockSpec(shape, lambda *_: (0,) * len(shape))


def call(kernel, name, flops, nbytes, mib=56, **kwargs):
    return pl.pallas_call(
        kernel,
        name=name,
        compiler_params=pltpu.CompilerParams(vmem_limit_bytes=mib << 20),
        cost_estimate=pl.CostEstimate(flops=flops, bytes_accessed=nbytes, transcendentals=0),
        **kwargs,
    )


def dispatch_gradient_kernel(ids_ref, w_ref, g_ref, table_ref, pick_ref, share_ref, ring_ref, held, sem):
    load = pltpu.make_async_copy(g_ref, held, sem.at[0])
    load.start()
    topk, tok = ids_ref.shape
    buf = table_ref.shape[0]
    unit = 2 * CAP
    share = share_ref.shape[1]
    cols = ring_ref.shape[1]

    def tables(count, per_expert):
        slot_row = lax.broadcasted_iota(jnp.int32, (count, tok), 0)
        expert = lax.div(slot_row, per_expert)
        weights = w_ref[...].astype(F32)
        chosen = jnp.zeros((count, tok), F32)
        weight = jnp.zeros((count, tok), F32)
        for k in range(topk):
            hit = ids_ref[k : k + 1, :] == expert
            chosen = jnp.where(hit, 1.0, chosen)
            weight = jnp.where(hit, weights[k : k + 1, :], weight)
        before = lax.broadcasted_iota(jnp.int32, (tok, tok), 0)
        after = lax.broadcasted_iota(jnp.int32, (tok, tok), 1)
        earlier = jnp.where(before < after, 1.0, 0.0).astype(BF)
        slot = jnp.dot(chosen.astype(BF), earlier, preferred_element_type=F32)
        mine = (chosen > 0.5) & (slot == lax.rem(slot_row, CAP).astype(F32))
        return jnp.where(mine, 1.0, 0.0), jnp.where(mine, weight, 0.0), slot_row

    table_ref[...] = tables(buf, CAP)[0].astype(BF)
    table, weighted, slot_row = tables(2 * buf, unit)
    low = lax.rem(slot_row, unit) < CAP
    pick_ref[0] = jnp.where(low, table, 0.0).astype(BF)
    pick_ref[1] = jnp.where(low, 0.0, table).astype(BF)
    both = jnp.concatenate(
        [jnp.where(low, weighted, 0.0).astype(BF), jnp.where(low, 0.0, weighted).astype(BF)], axis=1
    )
    load.wait()

    def rows(first, second, count):
        parts = jnp.concatenate(
            [held[:, first : first + count], held[:, second : second + count]], axis=0
        )
        return jnp.dot(both, parts, preferred_element_type=F32).astype(BF)

    share_ref[...] = rows(0, share, share)
    part = TILE // 2
    for first in range(0, cols, part):
        start = 2 * share + first
        ring_ref[:, first : first + part] = rows(start, start + cols, part)


def dispatch_gradient(ids, weights, grad_out, experts, share):
    tok, width = grad_out.shape
    buf = experts * CAP
    small = lambda *shape: jax.ShapeDtypeStruct(shape, BF)
    return call(
        dispatch_gradient_kernel,
        "dispatch_gradient",
        4 * tok * buf * width,
        2 * width * (tok + buf),
        in_specs=[VMEM, VMEM, ANY],
        out_specs=[VMEM] * 4,
        out_shape=[
            small(buf, tok),
            small(2, 2 * buf, tok),
            small(2 * buf, share),
            small(2 * buf, width // 2 - share),
        ],
        scratch_shapes=[pltpu.VMEM((tok, width), BF), pltpu.SemaphoreType.DMA((1,))],
    )(ids, weights, grad_out)


def dispatch_token_kernel(pick_ref, share_ref, t_ref, out_ref, held, staged, sem):
    load = pltpu.make_async_copy(t_ref, held, sem.at[0])
    load.start()
    _, experts, unit, cols = out_ref.shape
    share = share_ref.shape[1]
    half = cols - share
    both = jnp.concatenate([pick_ref[0], pick_ref[1]], axis=1)
    staged[:, :, half:] = share_ref[...].reshape(experts, unit, share)
    load.wait()
    for first in range(0, half, TILE):
        parts = jnp.concatenate(
            [held[:, first : first + TILE], held[:, half + first : half + first + TILE]], axis=0
        )
        rows = jnp.dot(both, parts, preferred_element_type=F32).astype(BF)
        staged[:, :, first : first + TILE] = rows.reshape(experts, unit, TILE)
    stores = [pltpu.make_async_copy(staged, out_ref.at[h], sem.at[1 + h]) for h in range(2)]
    for store in stores:
        store.start()
    for store in stores:
        store.wait()


def dispatch_token(pick, share, tokens, experts):
    tok, width = tokens.shape
    unit = 2 * CAP
    cols = width // 2 + share.shape[1]
    return call(
        dispatch_token_kernel,
        "dispatch_token",
        4 * tok * experts * CAP * width,
        2 * width * (tok + 2 * experts * CAP),
        in_specs=[VMEM, VMEM, ANY],
        out_specs=ANY,
        out_shape=jax.ShapeDtypeStruct((2, experts, unit, cols), BF),
        scratch_shapes=[
            pltpu.VMEM((tok, width), BF),
            pltpu.VMEM((experts, unit, cols), BF),
            pltpu.SemaphoreType.DMA((3,)),
        ],
    )(pick, share, tokens)


def regroup_kernel(own_ref, next_ref, top_ref, bottom_ref, prev_ref, out_ref, held, sem):
    experts, unit, _ = own_ref.shape
    parts = 4
    size = experts // parts
    loads, stores = [], []
    for p in range(parts):
        window = slice(p * size, (p + 1) * size)
        if p < parts // 2:
            far = top_ref.at[window]
        else:
            far = bottom_ref.at[p * size - experts // 2 : (p + 1) * size - experts // 2]
        sources = [own_ref.at[window], next_ref.at[window], far, prev_ref.at[window]]
        for k, source in enumerate(sources):
            target = held.at[window, k * unit : (k + 1) * unit, :]
            loads.append(pltpu.make_async_copy(source, target, sem.at[p * 4 + k]))
            loads[-1].start()
    for p in range(parts):
        window = slice(p * size, (p + 1) * size)
        for k in range(4):
            loads[p * 4 + k].wait()
        for h in range(2):
            index = parts * 4 + 2 * p + h
            stores.append(pltpu.make_async_copy(held.at[window], out_ref.at[h, window], sem.at[index]))
            stores[-1].start()
    for store in stores:
        store.wait()


def regroup(blocks):
    count, cols = blocks[0].shape
    unit = 2 * CAP
    experts = count // unit
    return call(
        regroup_kernel,
        "regroup",
        0,
        24 * count * cols,
        in_specs=[ANY] * 5,
        out_specs=ANY,
        out_shape=jax.ShapeDtypeStruct((2, experts, 4 * unit, cols), BF),
        scratch_shapes=[
            pltpu.VMEM((experts, 4 * unit, cols), BF),
            pltpu.SemaphoreType.DMA((24,)),
        ],
    )(*[b.reshape(b.shape[0] // unit, unit, cols) for b in blocks])


def pre_kernel(count, *refs):
    x_refs = refs[:count]
    wg_ref, wu_ref, wd_ref, slope_ref, swish_ref, part_ref, outer_ref, x, w, d, acc, sem = refs[count:]
    rows, cols = x.shape
    ff = w.shape[2] // 4
    share = d.shape[1]
    half = cols - share
    steps = half // TILE
    copies = [[] for _ in range(steps + 1)]
    index = 0

    def add(step, source, target):
        nonlocal index
        copies[step].append(pltpu.make_async_copy(source, target, sem.at[index]))
        index += 1

    for t in range(steps + 1):
        window = slice(t * TILE, (t + 1) * TILE) if t < steps else slice(half, cols)
        at = 0
        for ref in x_refs:
            add(t, ref.at[:, window], x.at[at : at + ref.shape[0], window])
            at += ref.shape[0]
        if t < steps:
            for k, ref in enumerate((wg_ref, wu_ref)):
                for h in range(2):
                    lane = (2 * k + h) * ff
                    source = ref.at[h * half + t * TILE : h * half + (t + 1) * TILE, :]
                    add(t, source, w.at[t, :, lane : lane + ff])
        else:
            for h in range(2):
                source = wd_ref.at[:, h * share : (h + 1) * share]
                add(t, source, d.at[h * ff : (h + 1) * ff, :])
    for group in copies:
        for copy in group:
            copy.start()
    for t in range(steps):
        for copy in copies[t]:
            copy.wait()
        value = jnp.dot(x[:, t * TILE : (t + 1) * TILE], w[t], preferred_element_type=F32)
        if t == 0:
            acc[...] = value
        else:
            acc[...] += value
    for copy in copies[steps]:
        copy.wait()

    def fold_halves(value):
        value = value.reshape(rows // (2 * CAP), 2 * CAP, 2 * ff)
        return (value[:, :CAP, :ff] + value[:, CAP:, ff:]).reshape(rows // 2, ff)

    part_ref[...] = fold_halves(contract_cols(x[:, half:], d[...]))
    gate = fold_halves(acc[:, : 2 * ff])
    up = fold_halves(acc[:, 2 * ff :])
    sig = 1.0 / (1.0 + jnp.exp(-gate))
    swish = gate * sig
    slope_ref[...] = up * sig * (1.0 + gate * (1.0 - sig))
    swish_ref[...] = swish
    outer_ref[...] = swish * up


def pre(blocks, w_gate, w_up, w_down, share):
    cols = blocks[0].shape[1]
    rows = sum(b.shape[0] for b in blocks)
    ff = w_gate.shape[1]
    steps = (cols - share) // TILE
    copies = (len(blocks) + 4) * steps + len(blocks) + 2
    return call(
        functools.partial(pre_kernel, len(blocks)),
        "pre",
        8 * rows * cols * ff,
        2 * cols * (rows + 4 * ff),
        in_specs=[ANY] * (len(blocks) + 3),
        out_specs=[VMEM] * 4,
        out_shape=[jax.ShapeDtypeStruct((rows // 2, ff), F32)] * 4,
        scratch_shapes=[
            pltpu.VMEM((rows, cols), BF),
            pltpu.VMEM((steps, TILE, 4 * ff), BF),
            pltpu.VMEM((2 * ff, share), BF),
            pltpu.VMEM((rows, 4 * ff), F32),
            pltpu.SemaphoreType.DMA((copies,)),
        ],
    )(*blocks, w_gate, w_up, w_down)


def load_weights(wg_ref, wu_ref, w, first, sem, index):
    count = w.shape[0]
    ff = wg_ref.shape[1]
    copies = []
    for k, ref in enumerate((wg_ref, wu_ref)):
        source = ref.at[first : first + count, :]
        target = w.at[:, k * ff : (k + 1) * ff]
        copies.append(pltpu.make_async_copy(source, target, sem.at[index + k]))
    return copies


def start_all(copies):
    for copy in copies:
        copy.start()


def wait_all(copies):
    for copy in copies:
        copy.wait()


def hidden_kernel(
    g_ref, wd_ref, wg_ref, wu_ref, *refs
):
    own, side, far = refs[0:3], refs[3:6], refs[6:9]
    gu_ref, near_ref, top_ref, bottom_ref, g, d, w, small, staged, sem = refs[9:]
    groups, span, double = gu_ref.shape
    ff = double // 2
    locs = span // CAP
    unit = 2 * CAP
    cols = g.shape[1]
    wide_cols = top_ref.shape[1]
    first_col = wd_ref.shape[1] - 2 * cols
    steps = 2
    tile = cols // steps
    loads = []
    for t in range(steps):
        window = slice(t * tile, (t + 1) * tile)
        loads.append(pltpu.make_async_copy(g_ref.at[:, window], g.at[:, window], sem.at[3 * t]))
        for h in range(2):
            start = first_col + h * cols + t * tile
            source = wd_ref.at[:, start : start + tile]
            target = d.at[h * ff : (h + 1) * ff, window]
            loads.append(pltpu.make_async_copy(source, target, sem.at[3 * t + 1 + h]))
    more = []
    index = 3 * steps
    for k in range(3):
        places = [(own[k], 0), (side[k].at[:span], 1), (far[k], 2), (side[k].at[span:], 3)]
        for source, group in places:
            more.append(pltpu.make_async_copy(source, small.at[k, group], sem.at[index]))
            index += 1
    weights = load_weights(wg_ref, wu_ref, w, wg_ref.shape[0] - wide_cols, sem, index)
    start_all(loads)
    start_all(more)
    start_all(weights)
    total = None
    for t in range(steps):
        wait_all(loads[3 * t : 3 * t + 3])
        window = slice(t * tile, (t + 1) * tile)
        value = contract_cols(g[:, window], d[:, window])
        total = value if total is None else total + value
    wait_all(more)
    halves = total.reshape(locs, groups * unit, double)
    for group in range(groups):
        first = group * unit
        hidden = (
            halves[:, first : first + CAP, :ff] + halves[:, first + CAP : first + unit, ff:]
        ).reshape(span, ff) + small[2, group]
        gate = hidden * small[0, group]
        up = hidden * small[1, group]
        both = jnp.concatenate([gate, up], axis=1)
        gu_ref[group] = both.astype(BF)
        near_ref[:, group * CAP : (group + 1) * CAP, :] = both.reshape(locs, CAP, double).astype(BF)
    wait_all(weights)
    staged[...] = contract_cols(gu_ref[2], w[...]).astype(BF)
    stores = [
        pltpu.make_async_copy(staged.at[: span // 2], top_ref, sem.at[index + 2]),
        pltpu.make_async_copy(staged.at[span // 2 :], bottom_ref, sem.at[index + 3]),
    ]
    start_all(stores)
    wait_all(stores)


def hidden(g_rows, w_down, w_gate, w_up, own, side, far, wide_cols):
    rows, cols = g_rows.shape
    span, ff = own[0].shape
    groups = rows // 2 // span
    small = lambda *shape: jax.ShapeDtypeStruct(shape, BF)
    return call(
        hidden_kernel,
        "hidden",
        4 * rows * cols * ff + 4 * span * ff * wide_cols,
        2 * (rows * cols + 2 * wide_cols * ff + span * wide_cols),
        in_specs=[ANY] * 13,
        out_specs=[VMEM, VMEM, ANY, ANY],
        out_shape=[
            small(groups, span, 2 * ff),
            small(span // CAP, groups * CAP, 2 * ff),
            small(span // 2, wide_cols),
            small(span // 2, wide_cols),
        ],
        scratch_shapes=[
            pltpu.VMEM((rows, cols), BF),
            pltpu.VMEM((2 * ff, cols), BF),
            pltpu.VMEM((wide_cols, 2 * ff), BF),
            pltpu.VMEM((3, groups, span, ff), F32),
            pltpu.VMEM((span, wide_cols), BF),
            pltpu.SemaphoreType.DMA((6 + 12 + 4,)),
        ],
    )(g_rows, w_down, w_gate, w_up, *own, *side, *far)


def ring_part_kernel(near_ref, wg_ref, wu_ref, out_ref, w, staged, sem):
    rows, ring_cols = out_ref.shape
    loads = load_weights(wg_ref, wu_ref, w, 0, sem, 0)
    start_all(loads)
    wait_all(loads)
    left = near_ref[...].reshape(rows, w.shape[1])
    stores = []
    for c in range(ring_cols // TILE):
        window = slice(c * TILE, (c + 1) * TILE)
        staged[:, window] = contract_cols(left, w[window, :]).astype(BF)
        target = out_ref.at[:, window]
        stores.append(pltpu.make_async_copy(staged.at[:, window], target, sem.at[2 + c]))
        stores[-1].start()
    wait_all(stores)


def ring_part(near, w_gate, w_up, ring_cols):
    locs, depth, double = near.shape
    rows = locs * depth
    return call(
        ring_part_kernel,
        "ring_part",
        2 * rows * double * ring_cols,
        2 * ring_cols * (rows + double),
        in_specs=[VMEM, ANY, ANY],
        out_specs=ANY,
        out_shape=jax.ShapeDtypeStruct((rows, ring_cols), BF),
        scratch_shapes=[
            pltpu.VMEM((ring_cols, double), BF),
            pltpu.VMEM((rows, ring_cols), BF),
            pltpu.SemaphoreType.DMA((2 + ring_cols // TILE,)),
        ],
    )(near, w_gate, w_up)


def side_kernel(gu_ref, wg_ref, wu_ref, top_ref, bottom_ref, next_ref, prev_ref, own_ref, w, held, staged, sem):
    _, span, double = gu_ref.shape
    wide_cols = next_ref.shape[1]
    weights = load_weights(wg_ref, wu_ref, w, wg_ref.shape[0] - wide_cols, sem, 0)
    came = [
        pltpu.make_async_copy(top_ref, held.at[0], sem.at[2]),
        pltpu.make_async_copy(bottom_ref, held.at[1], sem.at[3]),
    ]
    start_all(weights)
    start_all(came)
    wait_all(weights)
    wait_all(came)
    left = jnp.concatenate([gu_ref[1], gu_ref[3], gu_ref[0]], axis=0)
    mid = span // 2
    stores = []
    for c in range(wide_cols // TILE):
        window = slice(c * TILE, (c + 1) * TILE)
        value = contract_cols(left, w[window, :])
        top = held[0, :, window].astype(F32)
        bottom = held[1, :, window].astype(F32)
        staged[0, :mid, window] = (value[:mid] + top).astype(BF)
        staged[0, mid:, window] = value[mid:span].astype(BF)
        staged[1, :mid, window] = value[span : span + mid].astype(BF)
        staged[1, mid:, window] = (value[span + mid : 2 * span] + bottom).astype(BF)
        staged[2, :, window] = value[2 * span :].astype(BF)
        for k, ref in enumerate((next_ref, prev_ref, own_ref)):
            copy = pltpu.make_async_copy(
                staged.at[k, :, window], ref.at[:, window], sem.at[4 + 3 * c + k]
            )
            copy.start()
            stores.append(copy)
    wait_all(stores)


def side_part(gu, w_gate, w_up, top, bottom):
    _, span, double = gu.shape
    wide_cols = top.shape[1]
    return call(
        side_kernel,
        "side_part",
        6 * span * double * wide_cols,
        2 * wide_cols * (4 * span + double),
        in_specs=[VMEM, ANY, ANY, ANY, ANY],
        out_specs=[ANY] * 3,
        out_shape=[jax.ShapeDtypeStruct((span, wide_cols), BF)] * 3,
        scratch_shapes=[
            pltpu.VMEM((wide_cols, double), BF),
            pltpu.VMEM((2, span // 2, wide_cols), BF),
            pltpu.VMEM((3, span, wide_cols), BF),
            pltpu.SemaphoreType.DMA((4 + 3 * (wide_cols // TILE),)),
        ],
    )(gu, w_gate, w_up, top, bottom)


def sum_kernel(a_ref, b_ref, c_ref, out_ref, held, staged, sem):
    locs, _, cols = out_ref.shape
    steps = cols // TILE
    loads, stores = [], []
    for t in range(steps):
        window = slice(t * TILE, (t + 1) * TILE)
        for k, ref in enumerate((a_ref, b_ref, c_ref)):
            loads.append(
                pltpu.make_async_copy(ref.at[:, window], held.at[k, :, window], sem.at[4 * t + k])
            )
    start_all(loads)
    for t in range(steps):
        wait_all(loads[3 * t : 3 * t + 3])
        window = slice(t * TILE, (t + 1) * TILE)
        total = sum(held[k, :, window].astype(F32) for k in range(3))
        staged[:, :, window] = total.reshape(locs, CAP, TILE).astype(BF)
        source = staged.at[:, :, window]
        stores.append(pltpu.make_async_copy(source, out_ref.at[:, :, window], sem.at[4 * t + 3]))
        stores[-1].start()
    wait_all(stores)


def sum_blocks(a, b, c):
    rows, cols = a.shape
    return call(
        sum_kernel,
        "sum_blocks",
        2 * rows * cols,
        8 * rows * cols,
        in_specs=[ANY] * 3,
        out_specs=ANY,
        out_shape=jax.ShapeDtypeStruct((rows // CAP, CAP, cols), BF),
        scratch_shapes=[
            pltpu.VMEM((3, rows, cols), BF),
            pltpu.VMEM((rows // CAP, CAP, cols), BF),
            pltpu.SemaphoreType.DMA((4 * (cols // TILE),)),
        ],
    )(a, b, c)


def row_grads_kernel(gu_ref, own_ref, next_ref, top_ref, bottom_ref, prev_ref, gate_ref, up_ref, wide):
    groups, span, double = gu_ref.shape
    ff = double // 2
    locs = span // CAP

    @pl.when(pl.program_id(0) == 0)
    def _():
        zero = jnp.zeros((locs, CAP, ff), F32)
        for group in range(groups):
            both = gu_ref[group].astype(F32).reshape(locs, CAP, double)
            gate, up = both[:, :, :ff], both[:, :, ff:]
            low = jnp.concatenate([gate, zero, up, zero], axis=2)
            high = jnp.concatenate([zero, gate, zero, up], axis=2)
            both = jnp.concatenate([low, high], axis=1).reshape(2 * span, 4 * ff)
            wide[2 * span * group : 2 * span * (group + 1), :] = both.astype(BF)

    x = jnp.concatenate(
        [own_ref[...], next_ref[...], top_ref[...], bottom_ref[...], prev_ref[...]], axis=0
    )
    total = contract_rows(x, wide[...]).astype(BF)
    gate_ref[0] = total[:, :ff]
    gate_ref[1] = total[:, ff : 2 * ff]
    up_ref[0] = total[:, 2 * ff : 3 * ff]
    up_ref[1] = total[:, 3 * ff :]


def row_grads(gu, blocks, share):
    groups, span, double = gu.shape
    ff = double // 2
    rows = 2 * groups * span
    half = blocks[0].shape[1] - share
    out = jax.ShapeDtypeStruct((2, half, ff), BF)
    gate, up = call(
        row_grads_kernel,
        "row_grads",
        8 * rows * half * ff,
        2 * half * (rows + 4 * ff),
        grid=(half // TILE,),
        in_specs=[
            whole(gu.shape),
            *[pl.BlockSpec((b.shape[0], TILE), lambda j: (0, j)) for b in blocks],
        ],
        out_specs=[pl.BlockSpec((2, TILE, ff), lambda j: (0, j, 0))] * 2,
        out_shape=[out, out],
        scratch_shapes=[pltpu.VMEM((rows, 4 * ff), BF)],
    )(gu, *blocks)
    return gate.reshape(2 * half, ff), up.reshape(2 * half, ff)


def down_kernel(g_ref, *refs):
    outers, blocks = refs[:3], refs[3:8]
    out_ref, wide, held, sem = refs[8:]
    own, side, far = outers
    span, ff = own.shape
    locs = span // CAP
    unit = 2 * CAP
    step = pl.program_id(0)
    tile = g_ref.shape[1]
    share = held.shape[1]

    def spread(outer):
        rows = outer.reshape(locs, CAP, ff)
        zero = jnp.zeros_like(rows)
        low = jnp.concatenate([rows, zero], axis=2)
        high = jnp.concatenate([zero, rows], axis=2)
        return jnp.concatenate([low, high], axis=1)

    @pl.when(step == 0)
    def _():
        copies = []
        at = 0
        for k, ref in enumerate(blocks):
            source = ref.at[:, ref.shape[1] - share :]
            copies.append(
                pltpu.make_async_copy(source, held.at[at : at + ref.shape[0], :], sem.at[k])
            )
            at += ref.shape[0]
        start_all(copies)
        rows = []
        for k, outer in enumerate((own[...], side[:span], far[...], side[span:])):
            block = spread(outer).astype(BF)
            wide[:, k * unit : (k + 1) * unit, :] = block
            rows.append(block.reshape(2 * span, 2 * ff))
        wait_all(copies)
        total = contract_rows(jnp.concatenate(rows, axis=0), held[...]).astype(BF)
        out_ref[:, :share] = total[:ff]
        out_ref[:, share : 2 * share] = total[ff:]

    rows = wide[...].reshape(g_ref.shape[0], 2 * ff)
    total = contract_rows(rows, g_ref[...]).astype(BF)
    low = 2 * share + step * tile
    high = low + pl.num_programs(0) * tile
    out_ref[:, pl.ds(pl.multiple_of(low, 128), tile)] = total[:ff]
    out_ref[:, pl.ds(pl.multiple_of(high, 128), tile)] = total[ff:]


def down(outers, blocks, g_rows, share):
    rows, cols = g_rows.shape
    span, ff = outers[0].shape
    width = 2 * (cols + share)
    tile = TILE if cols % TILE == 0 else TILE // 2
    return call(
        down_kernel,
        "down",
        4 * rows * (cols + share) * ff,
        2 * (cols + share) * (rows + 2 * ff),
        grid=(cols // tile,),
        in_specs=[
            pl.BlockSpec((rows, tile), lambda j: (0, j)),
            *[whole(o.shape) for o in outers],
            *[ANY] * 5,
        ],
        out_specs=whole((ff, width)),
        out_shape=jax.ShapeDtypeStruct((ff, width), BF),
        scratch_shapes=[
            pltpu.VMEM((span // CAP, rows * CAP // span, 2 * ff), BF),
            pltpu.VMEM((rows, share), BF),
            pltpu.SemaphoreType.DMA((5,)),
        ],
    )(g_rows, *outers, *blocks)


def fold_kernel(in_ref, top_ref, bottom_ref, rest_ref):
    _, experts, depth, tile = in_ref.shape
    total = in_ref[0].astype(F32) + in_ref[1].astype(F32)
    at = 0
    for step in range(depth // CAP):
        part = total[:, step * CAP : (step + 1) * CAP, :].reshape(experts * CAP, tile).astype(BF)
        if step == 2:
            top_ref[...] = part[: experts * CAP // 2]
            bottom_ref[...] = part[experts * CAP // 2 :]
        else:
            rest_ref[at] = part
            at += 1


def fold(home):
    _, experts, depth, width = home.shape
    buf = experts * CAP
    tile = TILE
    return call(
        fold_kernel,
        "fold",
        experts * depth * width,
        6 * experts * depth * width,
        mib=20,
        grid=(width // tile,),
        in_specs=[pl.BlockSpec((2, experts, depth, tile), lambda j: (0, 0, 0, j))],
        out_specs=[
            pl.BlockSpec((buf // 2, tile), lambda j: (0, j)),
            pl.BlockSpec((buf // 2, tile), lambda j: (0, j)),
            pl.BlockSpec((3, buf, tile), lambda j: (0, 0, j)),
        ],
        out_shape=[
            jax.ShapeDtypeStruct((buf // 2, width), BF),
            jax.ShapeDtypeStruct((buf // 2, width), BF),
            jax.ShapeDtypeStruct((3, buf, width), BF),
        ],
    )(home)


def add_kernel(rest_ref, top_ref, bottom_ref, next_ref, prev_ref):
    mid = top_ref.shape[0]
    next_ref[:mid] = (rest_ref[1, :mid].astype(F32) + top_ref[...].astype(F32)).astype(BF)
    next_ref[mid:] = rest_ref[1, mid:]
    prev_ref[:mid] = rest_ref[2, :mid]
    prev_ref[mid:] = (rest_ref[2, mid:].astype(F32) + bottom_ref[...].astype(F32)).astype(BF)


def add_far(rest, top, bottom):
    _, buf, cols = rest.shape
    return call(
        add_kernel,
        "add_far",
        buf * cols,
        10 * buf * cols,
        mib=20,
        in_specs=[VMEM] * 3,
        out_specs=[VMEM] * 2,
        out_shape=[jax.ShapeDtypeStruct((buf, cols), BF)] * 2,
    )(rest, top, bottom)


def combine_kernel(split, table_ref, own_ref, left_ref, right_ref, wide_ref, out_ref):
    table = table_ref[...]

    @pl.when(pl.program_id(0) < split)
    def _():
        rows = jnp.concatenate([own_ref[...], left_ref[...], right_ref[...]], axis=0)
        thrice = jnp.concatenate([table] * 3, axis=0)
        out_ref[...] = contract_rows(thrice, rows).astype(BF)

    @pl.when(pl.program_id(0) >= split)
    def _():
        count, _, tile = wide_ref.shape
        rows = wide_ref[...].astype(F32).reshape(count * CAP, tile).astype(BF)
        both = jnp.concatenate([table, table], axis=0)
        out_ref[...] = contract_rows(both, rows).astype(BF)


def combine(table, rest, left, right, wide):
    buf, tok = table.shape
    width = left.shape[1] + wide.shape[2]
    tile = TILE
    split = left.shape[1] // tile
    block = pl.BlockSpec((buf, tile), lambda j: (0, jnp.minimum(j, split - 1)))
    return call(
        functools.partial(combine_kernel, split),
        "combine",
        2 * tok * buf * width,
        2 * width * (tok + 2 * buf),
        mib=20,
        grid=(width // tile,),
        in_specs=[
            whole((buf, tok)),
            pl.BlockSpec((None, buf, tile), lambda j: (0, 0, jnp.minimum(j, split - 1))),
            block,
            block,
            pl.BlockSpec((wide.shape[0], CAP, tile), lambda j: (0, 0, jnp.maximum(j - split, 0))),
        ],
        out_specs=pl.BlockSpec((tok, tile), lambda j: (0, j)),
        out_shape=jax.ShapeDtypeStruct((tok, width), BF),
    )(table, rest, left, right, wide)


def over_loc(a):
    return lax.all_to_all(a, "loc", split_axis=0, concat_axis=0, tiled=True)


def shift(a, step):
    groups = lax.axis_size("grp")
    return lax.ppermute(a, "grp", [(i, (i + step) % groups) for i in range(groups)])


def ring_gather(own):
    mid = own.shape[0] // 2
    before, after = shift(own, 1), shift(own, -1)
    return [own, after, shift(before[:mid], 1), shift(after[mid:], -1), before]


def body(tokens, grad_out, expert_ids, route_weight, gate_weight, up_weight, down_weight):
    groups = lax.axis_size("grp")
    locs = lax.axis_size("loc")
    experts = locs // 2
    width = tokens.shape[1]
    buf = experts * CAP
    unit = 2 * CAP
    share = 768
    ring_cols = 2560
    wide_cols = width - ring_cols

    w_gate, w_up, w_down = gate_weight[0], up_weight[0], down_weight[0]

    table, pick, g_share, g_send = dispatch_gradient(
        expert_ids.T, route_weight.T, grad_out, experts, share
    )
    g_blocks = ring_gather(g_send)
    xg_send = dispatch_token(pick, g_share, tokens, experts)
    xg = over_loc(xg_send.reshape(locs, unit, xg_send.shape[3]))
    xg, *g_blocks = lax.optimization_barrier((xg, *g_blocks))
    blocks = ring_gather(xg.reshape(locs * unit, xg.shape[2]))
    g_out = regroup(g_blocks)
    g_rows = over_loc(g_out.reshape(locs, groups * unit, g_out.shape[3]))
    g_rows = g_rows.reshape(locs * groups * unit, g_out.shape[3])

    own, after, top, bottom, before = blocks
    *pre_own, outer_own = pre([own], w_gate, w_up, w_down, share)
    *pre_side, outer_side = pre([after, before], w_gate, w_up, w_down, share)
    *pre_far, outer_far = pre([top, bottom], w_gate, w_up, w_down, share)
    gu, near, far_top, far_bottom = hidden(
        g_rows, w_down, w_gate, w_up, pre_own, pre_side, pre_far, wide_cols
    )

    came_top, came_bottom = shift(far_top, 1), shift(far_bottom, -1)
    part_ring = ring_part(near, w_gate, w_up, ring_cols)
    part_ring, gu = lax.optimization_barrier((part_ring, gu))
    home_ring = over_loc(part_ring.reshape(locs, groups * CAP, ring_cols))
    part_next, part_prev, part_own = side_part(gu, w_gate, w_up, came_top, came_bottom)
    from_before, from_after = shift(part_next, 1), shift(part_prev, -1)

    outers = (outer_own, outer_side, outer_far)
    part_own, gu, outers = lax.optimization_barrier((part_own, gu, outers))
    gate_grad, up_grad = row_grads(gu, blocks, share)
    down_grad = down(outers, blocks, g_rows, share)
    part_own, gate_grad, up_grad, down_grad = lax.optimization_barrier(
        (part_own, gate_grad, up_grad, down_grad)
    )
    home_wide = over_loc(sum_blocks(part_own, from_before, from_after))

    fold_top, fold_bottom, rest = fold(home_ring.reshape(2, experts, groups * CAP, ring_cols))
    fold_next, fold_prev = add_far(rest, shift(fold_top, 1), shift(fold_bottom, -1))
    tokens_grad = combine(table, rest, shift(fold_next, 1), shift(fold_prev, -1), home_wide)
    return (tokens_grad, gate_grad[None], up_grad[None], down_grad[None])


def solution(mesh):
    in_specs = (
        P(("grp", "loc"), None),
        P(("grp", "loc"), None),
        P(("grp", "loc"), None),
        P(("grp", "loc"), None),
        P("loc", None, "grp"),
        P("loc", None, "grp"),
        P("loc", "grp", None),
    )
    out_specs = (
        P(("grp", "loc"), None),
        P("loc", None, "grp"),
        P("loc", None, "grp"),
        P("loc", "grp", None),
    )
    return jax.shard_map(body, mesh=mesh, in_specs=in_specs, out_specs=out_specs, check_vma=False)
```

time: 251 us -> 264 us (1.052)
  blocking collectives: 37.7 us -> 0 us
  starting transfers between devices: 24.2 us -> 57.7 us
  Pallas kernels: 57.2 us -> 79.1 us
  between operations: 13.9 us -> 0.93 us
  local copies, waits for them, and re-layouts: 4.38 us -> 10.1 us
    ppermute x0 -> x16, waiting for transfers between devices: none -> 107 us  [shift(): lax.ppermute(a, 'grp', [(i, (i + step) % groups) for i in range(groups)])]
    all_gather x2 -> x0, waiting for transfers between devices: 74.1 us -> none  [the longest x1 73.2 us: body(): lax.all_gather(xg.reshape(locs * unit, xg.shape[2]), 'grp', axis=0, tiled...]
    all_to_all x1 -> x0, blocking collectives: 37.7 us -> none  [over_loc(): return lax.all_to_all(a, 'loc', split_axis=0, concat_axis=0, tiled=True)]
    ppermute x0 -> x16, starting transfers between devices: none -> 21.9 us  [shift(): lax.ppermute(a, 'grp', [(i, (i + step) % groups) for i in range(groups)])]
    all_to_all x3 -> x4, waiting for transfers between devices: 23.9 us -> 7.33 us  [over_loc(): return lax.all_to_all(a, 'loc', split_axis=0, concat_axis=0, tiled=True)]
    reduce_scatter x2 -> x0, waiting for transfers between devices: 15.1 us -> none  [the longest x1 15.1 us: body(): ring = lax.psum_scatter(folded, 'grp', scatter_dimension=0, tiled=True)]
    pallas_call x3 -> x8, Pallas kernels: 22.7 us -> 36.1 us  [the longest x3 14.4 us: pre(): call(functools.partial(pre_kernel, len(blocks)), 'pre', 8 * rows * cols *...]
    all_to_all x3 -> x4, starting transfers between devices: 23.8 us -> 35.7 us  [over_loc(): return lax.all_to_all(a, 'loc', split_axis=0, concat_axis=0, tiled=True)]
  transfers between devices with their start and end apart: 7 -> 20, of which waited for: 5 -> 9; matrix products, arithmetic and copies ran while one was open for 1% -> 0% of each run, Pallas kernels for 16% -> 17%
where the time goes in v6:
time: 264 us; the launch traced here: 262 us
  waiting for transfers between devices  114 us (43%)
  Pallas kernels  79.1 us (30%)
  starting transfers between devices  57.7 us (22%)
  local copies, waits for them, and re-layouts  10.1 us (4%)
    ppermute x16, waiting for transfers between devices, shift(): lax.ppermute(a, 'grp', [(i, (i + step) % groups) for i in range(groups)])  107 us
    all_to_all x4, starting transfers between devices, over_loc(): return lax.all_to_all(a, 'loc', split_axis=0, concat_axis=0, tiled=True)  35.7 us
    ppermute x16, starting transfers between devices, shift(): lax.ppermute(a, 'grp', [(i, (i + step) % groups) for i in range(groups)])  21.9 us
    pallas_call x3, Pallas kernels, pre(): call(functools.partial(pre_kernel, len(blocks)), 'pre', 8 * rows * cols *...  14.4 us
    pallas_call x1, Pallas kernels, down(): call(down_kernel, 'down', 4 * rows * (cols + share) * ff, 2 * (cols + sha...  11.8 us
    pallas_call x1, Pallas kernels, row_grads(): call(row_grads_kernel, 'row_grads', 8 * rows * half * ff, 2 * half * (row...  9.47 us
    pallas_call x1, Pallas kernels, hidden(): call(hidden_kernel, 'hidden', 4 * rows * cols * ff + 4 * span * ff * wide...  9.04 us
    pallas_call x1, Pallas kernels, combine(): call(functools.partial(combine_kernel, split), 'combine', 2 * tok * buf *...  8.92 us
  transfers between devices with their start and end apart: 20, of which 9 were waited for; matrix products, arithmetic and copies ran while one was open for 0% of the time, Pallas kernels for 17%

profile of v6, /device:TPU:1, one launch (start us, length us, event | category | flops | bytes accessed | tf_op | source)
XLA Modules:
  0.0 262.2 jit_solution(16676484276752344394)
XLA Ops:
  0.6 3.5 %dispatch_gradient.1 = (bf16[64,128]{1,0:T(8,128)(2,1)}, bf16[2,128,128]{2,1,0:T(8,128)(2,1)}, bf16[128,768]{1,0:T(8,128)(2,1)}, bf16[128,2816]{1,0:T(8,128)(2,1)}) custom-call(s32[8,128]{1,0:T(8,128)} %bitcast.51, bf16[8,128]{1,0:T(8,128)(2,1)} %bitcast.52, bf16[128,7168]{1,0:T(8,128)(2,1)} %g_ref.1), custom_call_target="tpu_custom_call" | custom-call | flops 234881024 | bytes 2752512 | tf_op jit(solution)/shard_map/dispatch_gradient/pallas_call | solution.py:93
  4.1 4.3 %dispatch_token.1 = bf16[2,16,8,4352]{3,2,1,0:T(8,128)(2,1)} custom-call(bf16[2,128,128]{2,1,0:T(8,128)(2,1)} %get-tuple-element.52.pick_ref, bf16[128,768]{1,0:T(8,128)(2,1)} %get-tuple-element.53.share_ref, bf16[128,7168]{1,0:T(8,128)(2,1)} %t_ref.1), custom_call_target="tpu_custom_call" | custom-call | flops 234881024 | bytes 3670016 | tf_op jit(solution)/shard_map/dispatch_token/pallas_call | solution.py:136
  8.4 9.4 %all-to-all-start = ((bf16[32,8,4352]{2,1,0:T(8,128)(2,1)}), bf16[32,8,4352]{2,1,0:T(8,128)(2,1)S(1)}, u32[]{:S(2)}, u32[]{:S(2)}) async-start(bf16[32,8,4352]{2,1,0:T(8,128)(2,1)} %bitcast.45), calls=%async_computation | async-start | bytes 4456448 | tf_op jit(solution)/shard_map/all_to_all | solution.py:750
  20.8 16.2 %collective-permute-done.1 = bf16[128,2816]{1,0:T(8,128)(2,1)S(1)} collective-permute-done((bf16[128,2816]{1,0:T(8,128)(2,1)}, bf16[128,2816]{1,0:T(8,128)(2,1)S(1)}, u32[]{:S(2)}, u32[]{:S(2)}) %collective-permute-start.1) | collective-permute-done | bytes 720928 | tf_op jit(solution)/shard_map/ppermute | solution.py:755
  39.9 7.4 %collective-permute-done.2 = bf16[64,2816]{1,0:T(8,128)(2,1)S(1)} collective-permute-done((bf16[64,2816]{1,0:T(8,128)(2,1)S(1)}, bf16[64,2816]{1,0:T(8,128)(2,1)S(1)}, u32[]{:S(2)}, u32[]{:S(2)}) %collective-permute-start.2) | collective-permute-done | bytes 360480 | tf_op jit(solution)/shard_map/ppermute | solution.py:755
  48.0 4.2 %regroup.1 = bf16[2,16,32,2816]{3,2,1,0:T(8,128)(2,1)} custom-call(bf16[16,8,2816]{2,1,0:T(8,128)(2,1)} %bitcast.49, bf16[16,8,2816]{2,1,0:T(8,128)(2,1)} %bitcast.48, bf16[8,8,2816]{2,1,0:T(8,128)(2,1)} %bitcast.50, bf16[8,8,2816]{2,1,0:T(8,128)(2,1)} %bitcast.6.bottom_ref, bf16[16,8,2816]{2,1,0:T(8,128)(2,1)} %bitcast.47), custom_call_target="tpu_custom_call" | custom-call | bytes 8650752 | tf_op jit(solution)/shard_map/regroup/pallas_call | solution.py:184
  52.2 8.6 %all-to-all-start.1 = ((bf16[32,32,2816]{2,1,0:T(8,128)(2,1)}), bf16[32,32,2816]{2,1,0:T(8,128)(2,1)}, u32[]{:S(2)}, u32[]{:S(2)}) async-start(bf16[32,32,2816]{2,1,0:T(8,128)(2,1)} %bitcast.38), calls=%async_computation.1 | async-start | bytes 11534336 | tf_op jit(solution)/shard_map/all_to_all | solution.py:750
  63.8 48.4 %collective-permute-done.5.refs_1_.prev_ref.refs_7_ = bf16[256,4352]{1,0:T(8,128)(2,1)S(1)} collective-permute-done((bf16[256,4352]{1,0:T(8,128)(2,1)S(1)}, bf16[256,4352]{1,0:T(8,128)(2,1)S(1)}, u32[]{:S(2)}, u32[]{:S(2)}) %collective-permute-start.5) | collective-permute-done | bytes 2228256 | tf_op jit(solution)/shard_map/ppermute | solution.py:755
  116.4 4.3 %pre.3 = (f32[128,128]{1,0:T(8,128)}, f32[128,128]{1,0:T(8,128)}, f32[128,128]{1,0:T(8,128)}, f32[128,128]{1,0:T(8,128)}) custom-call(bf16[256,4352]{1,0:T(8,128)(2,1)} %bitcast.41, bf16[7168,128]{1,0:T(8,128)(2,1)} %bitcast.22, bf16[7168,128]{1,0:T(8,128)(2,1)} %bitcast.28, bf16[128,7168]{1,0:T(8,128)(2,1)} %bitcast.34), custom_call_target="tpu_custom_call" | custom-call | flops 1140850688 | bytes 6684672 | tf_op jit(solution)/shard_map/pre/pallas_call | solution.py:265
  120.8 5.6 %pre.4 = (f32[256,128]{1,0:T(8,128)}, f32[256,128]{1,0:T(8,128)}, f32[256,128]{1,0:T(8,128)}, f32[256,128]{1,0:T(8,128)}) custom-call(bf16[256,4352]{1,0:T(8,128)(2,1)} %copy-done.5, bf16[256,4352]{1,0:T(8,128)(2,1)} %copy-done.4, bf16[7168,128]{1,0:T(8,128)(2,1)} %bitcast.23, bf16[7168,128]{1,0:T(8,128)(2,1)} %bitcast.29, bf16[128,7168]{1,0:T(8,128)(2,1)} %bitcast.35), custom_call_target="tpu_custom_call" | custom-call | flops 2281701376 | bytes 8912896 | tf_op jit(solution)/shard_map/pre/pallas_call | solution.py:265
  126.4 13.6 %collective-permute-done.6.refs_0_.top_ref.refs_5_ = bf16[128,4352]{1,0:T(8,128)(2,1)S(1)} collective-permute-done((bf16[128,4352]{1,0:T(8,128)(2,1)}, bf16[128,4352]{1,0:T(8,128)(2,1)S(1)}, u32[]{:S(2)}, u32[]{:S(2)}) %collective-permute-start.6) | collective-permute-done | bytes 1114144 | tf_op jit(solution)/shard_map/ppermute | solution.py:755
  142.1 4.4 %pre.5 = (f32[128,128]{1,0:T(8,128)}, f32[128,128]{1,0:T(8,128)}, f32[128,128]{1,0:T(8,128)}, f32[128,128]{1,0:T(8,128)}) custom-call(bf16[128,4352]{1,0:T(8,128)(2,1)} %copy-done.6, bf16[128,4352]{1,0:T(8,128)(2,1)} %copy-done.7, bf16[7168,128]{1,0:T(8,128)(2,1)} %bitcast.24, bf16[7168,128]{1,0:T(8,128)(2,1)} %bitcast.30, bf16[128,7168]{1,0:T(8,128)(2,1)} %bitcast.36), custom_call_target="tpu_custom_call" | custom-call | flops 1140850688 | bytes 6684672 | tf_op jit(solution)/shard_map/pre/pallas_call | solution.py:265
  146.5 9.0 %hidden.1 = (bf16[4,128,256]{2,1,0:T(8,128)(2,1)}, bf16[32,16,256]{2,1,0:T(8,128)(2,1)}, bf16[64,4608]{1,0:T(8,128)(2,1)}, bf16[64,4608]{1,0:T(8,128)(2,1)}) custom-call(bf16[1024,2816]{1,0:T(8,128)(2,1)} %bitcast.9.g_ref, bf16[128,7168]{1,0:T(8,128)(2,1)} %bitcast.37, bf16[7168,128]{1,0:T(8,128)(2,1)} %bitcast.25, bf16[7168,128]{1,0:T(8,128)(2,1)} %bitcast.31, ...), custom_call_target="tpu_custom_call" | custom-call | flops 1778384896 | bytes 9306112 | tf_op jit(solution)/shard_map/hidden/pallas_call | solution.py:371
  155.6 4.2 %ring_part.1 = bf16[512,2560]{1,0:T(8,128)(2,1)} custom-call(bf16[32,16,256]{2,1,0:T(8,128)(2,1)} %get-tuple-element.70.near_ref, bf16[7168,128]{1,0:T(8,128)(2,1)} %bitcast.26, bf16[7168,128]{1,0:T(8,128)(2,1)} %bitcast.32), custom_call_target="tpu_custom_call" | custom-call | flops 671088640 | bytes 3932160 | tf_op jit(solution)/shard_map/ring_part/pallas_call | solution.py:414
  159.8 8.8 %all-to-all-start.2 = ((bf16[32,16,2560]{2,1,0:T(8,128)(2,1)}), bf16[32,16,2560]{2,1,0:T(8,128)(2,1)S(1)}, u32[]{:S(2)}, u32[]{:S(2)}) async-start(bf16[32,16,2560]{2,1,0:T(8,128)(2,1)} %bitcast.44), calls=%async_computation.2 | async-start | bytes 5242880 | tf_op jit(solution)/shard_map/all_to_all | solution.py:750
  171.3 13.4 %collective-permute-done.12.top_ref = bf16[64,4608]{1,0:T(8,128)(2,1)S(1)} collective-permute-done((bf16[64,4608]{1,0:T(8,128)(2,1)}, bf16[64,4608]{1,0:T(8,128)(2,1)S(1)}, u32[]{:S(2)}, u32[]{:S(2)}) %collective-permute-start.12) | collective-permute-done | bytes 589856 | tf_op jit(solution)/shard_map/ppermute | solution.py:755
  186.4 5.2 %side_part.1 = (bf16[128,4608]{1,0:T(8,128)(2,1)}, bf16[128,4608]{1,0:T(8,128)(2,1)}, bf16[128,4608]{1,0:T(8,128)(2,1)}) custom-call(bf16[4,128,256]{2,1,0:T(8,128)(2,1)} %get-tuple-element.86.gu_ref, bf16[7168,128]{1,0:T(8,128)(2,1)} %bitcast.27, bf16[7168,128]{1,0:T(8,128)(2,1)} %bitcast.33, bf16[64,4608]{1,0:T(8,128)(2,1)} %copy-done.12, ...), custom_call_target="tpu_custom_call" | custom-call | flops 905969664 | bytes 7077888 | tf_op jit(solution)/shard_map/side_part/pallas_call | solution.py:467
  194.4 11.8 %down.1 = bf16[128,7168]{1,0:T(8,128)(2,1)} custom-call(bf16[1024,2816]{1,0:T(8,128)(2,1)} %bitcast.9.g_ref, f32[128,128]{1,0:T(8,128)} %get-tuple-element.89.refs_0_, f32[256,128]{1,0:T(8,128)} %get-tuple-element.90.refs_1_, f32[128,128]{1,0:T(8,128)} %get-tuple-element.91.refs_2_, bf16[256,4352]{1,0:T(8,128)(2,1)} %bitcast.42, ...), custom_call_target="tpu_custom_call" | custom-call | flops 1879048192 | bytes 9175040 | tf_op jit(solution)/shard_map/down/pallas_call | solution.py:625
  206.2 9.5 %row_grads.1 = (bf16[2,3584,128]{2,1,0:T(8,128)(2,1)}, bf16[2,3584,128]{2,1,0:T(8,128)(2,1)}) custom-call(bf16[4,128,256]{2,1,0:T(8,128)(2,1)} %get-tuple-element.86.gu_ref, bf16[256,4352]{1,0:T(8,128)(2,1)} %bitcast.43, bf16[256,4352]{1,0:T(8,128)(2,1)} %copy-done.5, bf16[128,4352]{1,0:T(8,128)(2,1)} %copy-done.6, bf16[128,4352]{1,0:T(8,128)(2,1)} %copy-done.7, ...), custom_call_target="tpu_custom_call" | custom-call | flops 3758096384 | bytes 11010048 | tf_op jit(solution)/shard_map/row_grads/pallas_call | solution.py:556
  215.7 3.8 %collective-permute-done.14.b_ref = bf16[128,4608]{1,0:T(8,128)(2,1)S(1)} collective-permute-done((bf16[128,4608]{1,0:T(8,128)(2,1)}, bf16[128,4608]{1,0:T(8,128)(2,1)S(1)}, u32[]{:S(2)}, u32[]{:S(2)}) %collective-permute-start.14) | collective-permute-done | bytes 1179680 | tf_op jit(solution)/shard_map/ppermute | solution.py:755
  224.8 8.9 %all-to-all-start.3 = ((bf16[32,4,4608]{2,1,0:T(4,128)(2,1)}), bf16[32,4,4608]{2,1,0:T(4,128)(2,1)}, u32[]{:S(2)}, u32[]{:S(2)}) async-start(bf16[32,4,4608]{2,1,0:T(4,128)(2,1)} %sum_blocks.1), calls=%async_computation.3 | async-start | bytes 2359296 | tf_op jit(solution)/shard_map/all_to_all | solution.py:750
  237.2 4.1 %collective-permute-done.8.top_ref = bf16[32,2560]{1,0:T(8,128)(2,1)S(1)} collective-permute-done((bf16[32,2560]{1,0:T(8,128)(2,1)S(1)}, bf16[32,2560]{1,0:T(8,128)(2,1)S(1)}, u32[]{:S(2)}, u32[]{:S(2)}) %collective-permute-start.8) | collective-permute-done | bytes 163872 | tf_op jit(solution)/shard_map/ppermute | solution.py:755
  245.1 7.0 %all-to-all-done.3.wide_ref = bf16[32,4,4608]{2,1,0:T(4,128)(2,1)} async-done(((bf16[32,4,4608]{2,1,0:T(4,128)(2,1)}), bf16[32,4,4608]{2,1,0:T(4,128)(2,1)}, u32[]{:S(2)}, u32[]{:S(2)}) %all-to-all-start.3) | async-done | bytes 1179680 | tf_op jit(solution)/shard_map/all_to_all | solution.py:750
  253.3 8.9 %combine.1 = bf16[128,7168]{1,0:T(8,128)(2,1)} custom-call(bf16[64,128]{1,0:T(8,128)(2,1)S(1)} %copy-done.2, bf16[3,64,2560]{2,1,0:T(8,128)(2,1)S(1)} %copy-done.1, bf16[64,2560]{1,0:T(8,128)(2,1)S(1)} %collective-permute-done.10.left_ref, bf16[64,2560]{1,0:T(8,128)(2,1)S(1)} %collective-permute-done.11.right_ref, bf16[32,4,4608]{2,1,0:T(4,128)(2,1)} %all-to-all-done.3.wide_ref), custom_call_target="tpu_custom_call" | custom-call | flops 117440512 | bytes 3670016 | tf_op jit(solution)/shard_map/combine/pallas_call | solution.py:730
  (67 shorter events, 36.4 us)
Async XLA Ops:
  8.4 39.2 %all-to-all-start = ((bf16[32,8,4352]{2,1,0:T(8,128)(2,1)}), bf16[32,8,4352]{2,1,0:T(8,128)(2,1)S(1)}, u32[]{:S(2)}, u32[]{:S(2)}) async-start(bf16[32,8,4352]{2,1,0:T(8,128)(2,1)} %bitcast.45), calls=%async_computation | async-start | bytes 4456448 | tf_op jit(solution)/shard_map/all_to_all | solution.py:750
  17.9 19.1 %collective-permute-start.1 = (bf16[128,2816]{1,0:T(8,128)(2,1)}, bf16[128,2816]{1,0:T(8,128)(2,1)S(1)}, u32[]{:S(2)}, u32[]{:S(2)}) collective-permute-start(bf16[128,2816]{1,0:T(8,128)(2,1)} %get-tuple-element.55), channel_id=1, source_target_pairs={{0,32},{32,64},{64,96},{96,0},{1,33},{33,65},{65,97},{97,1},{2,34}... | collective-permute-start | bytes 2162696 | tf_op jit(solution)/shard_map/ppermute | solution.py:755
  19.2 17.9 %collective-permute-start = (bf16[128,2816]{1,0:T(8,128)(2,1)}, bf16[128,2816]{1,0:T(8,128)(2,1)S(1)}, u32[]{:S(2)}, u32[]{:S(2)}) collective-permute-start(bf16[128,2816]{1,0:T(8,128)(2,1)} %get-tuple-element.55), channel_id=1, source_target_pairs={{0,96},{32,0},{64,32},{96,64},{1,97},{33,1},{65,33},{97,65},{2,98}... | collective-permute-start | bytes 2162696 | tf_op jit(solution)/shard_map/ppermute | solution.py:755
  37.0 10.6 %copy-start.8 = (bf16[128,2816]{1,0:T(8,128)(2,1)}, bf16[128,2816]{1,0:T(8,128)(2,1)S(1)}, u32[]{:S(2)}) copy-start(bf16[128,2816]{1,0:T(8,128)(2,1)S(1)} %collective-permute-done.1) | copy-start | bytes 2162692
  37.0 10.2 %collective-permute-start.2 = (bf16[64,2816]{1,0:T(8,128)(2,1)S(1)}, bf16[64,2816]{1,0:T(8,128)(2,1)S(1)}, u32[]{:S(2)}, u32[]{:S(2)}) collective-permute-start(bf16[64,2816]{1,0:T(8,128)(2,1)S(1)} %slice.16), channel_id=1, source_target_pairs={{0,32},{32,64},{64,96},{96,0},{1,33},{33,65},{65,97},{97,1},{2,34}... | collective-permute-start | bytes 1081352 | tf_op jit(solution)/shard_map/ppermute | solution.py:755
  37.1 10.1 %copy-start.9 = (bf16[128,2816]{1,0:T(8,128)(2,1)}, bf16[128,2816]{1,0:T(8,128)(2,1)S(1)}, u32[]{:S(2)}) copy-start(bf16[128,2816]{1,0:T(8,128)(2,1)S(1)} %collective-permute-done) | copy-start | bytes 2162692
  37.2 10.1 %collective-permute-start.3 = (bf16[64,2816]{1,0:T(8,128)(2,1)S(1)}, bf16[64,2816]{1,0:T(8,128)(2,1)}, u32[]{:S(2)}, u32[]{:S(2)}) collective-permute-start(bf16[64,2816]{1,0:T(8,128)(2,1)S(1)} %slice.17), channel_id=1, source_target_pairs={{0,96},{32,0},{64,32},{96,64},{1,97},{33,1},{65,33},{97,65},{2,98}... | collective-permute-start | bytes 1081352 | tf_op jit(solution)/shard_map/ppermute | solution.py:755
  47.6 13.5 %copy-start.3 = (bf16[32,8,4352]{2,1,0:T(8,128)(2,1)}, bf16[32,8,4352]{2,1,0:T(8,128)(2,1)S(1)}, u32[]{:S(2)}) copy-start(bf16[32,8,4352]{2,1,0:T(8,128)(2,1)S(1)} %all-to-all-done) | copy-start | bytes 6684676
  52.2 94.3 %all-to-all-start.1 = ((bf16[32,32,2816]{2,1,0:T(8,128)(2,1)}), bf16[32,32,2816]{2,1,0:T(8,128)(2,1)}, u32[]{:S(2)}, u32[]{:S(2)}) async-start(bf16[32,32,2816]{2,1,0:T(8,128)(2,1)} %bitcast.38), calls=%async_computation.1 | async-start | bytes 11534336 | tf_op jit(solution)/shard_map/all_to_all | solution.py:750
  60.9 51.4 %collective-permute-start.5 = (bf16[256,4352]{1,0:T(8,128)(2,1)S(1)}, bf16[256,4352]{1,0:T(8,128)(2,1)S(1)}, u32[]{:S(2)}, u32[]{:S(2)}) collective-permute-start(bf16[256,4352]{1,0:T(8,128)(2,1)S(1)} %bitcast.39), channel_id=1, source_target_pairs={{0,32},{32,64},{64,96},{96,0},{1,33},{33,65},{65,97},{97,1},{2,34}... | collective-permute-start | bytes 6684680 | tf_op jit(solution)/shard_map/ppermute | solution.py:755
  61.1 52.3 %collective-permute-start.4 = (bf16[256,4352]{1,0:T(8,128)(2,1)S(1)}, bf16[256,4352]{1,0:T(8,128)(2,1)S(1)}, u32[]{:S(2)}, u32[]{:S(2)}) collective-permute-start(bf16[256,4352]{1,0:T(8,128)(2,1)S(1)} %bitcast.40), channel_id=1, source_target_pairs={{0,96},{32,0},{64,32},{96,64},{1,97},{33,1},{65,33},{97,65},{2,98}... | collective-permute-start | bytes 6684680 | tf_op jit(solution)/shard_map/ppermute | solution.py:755
  113.4 26.6 %collective-permute-start.6 = (bf16[128,4352]{1,0:T(8,128)(2,1)}, bf16[128,4352]{1,0:T(8,128)(2,1)S(1)}, u32[]{:S(2)}, u32[]{:S(2)}) collective-permute-start(bf16[128,4352]{1,0:T(8,128)(2,1)} %slice.18), channel_id=1, source_target_pairs={{0,32},{32,64},{64,96},{96,0},{1,33},{33,65},{65,97},{97,1},{2,34}... | collective-permute-start | bytes 3342344 | tf_op jit(solution)/shard_map/ppermute | solution.py:755
  114.0 26.0 %collective-permute-start.7 = (bf16[128,4352]{1,0:T(8,128)(2,1)S(1)}, bf16[128,4352]{1,0:T(8,128)(2,1)S(1)}, u32[]{:S(2)}, u32[]{:S(2)}) collective-permute-start(bf16[128,4352]{1,0:T(8,128)(2,1)S(1)} %slice.19), channel_id=1, source_target_pairs={{0,96},{32,0},{64,32},{96,64},{1,97},{33,1},{65,33},{97,65},{2,98}... | collective-permute-start | bytes 3342344 | tf_op jit(solution)/shard_map/ppermute | solution.py:755
  159.8 65.0 %all-to-all-start.2 = ((bf16[32,16,2560]{2,1,0:T(8,128)(2,1)}), bf16[32,16,2560]{2,1,0:T(8,128)(2,1)S(1)}, u32[]{:S(2)}, u32[]{:S(2)}) async-start(bf16[32,16,2560]{2,1,0:T(8,128)(2,1)} %bitcast.44), calls=%async_computation.2 | async-start | bytes 5242880 | tf_op jit(solution)/shard_map/all_to_all | solution.py:750
  168.6 16.2 %collective-permute-start.12 = (bf16[64,4608]{1,0:T(8,128)(2,1)}, bf16[64,4608]{1,0:T(8,128)(2,1)S(1)}, u32[]{:S(2)}, u32[]{:S(2)}) collective-permute-start(bf16[64,4608]{1,0:T(8,128)(2,1)} %get-tuple-element.79), channel_id=1, source_target_pairs={{0,32},{32,64},{64,96},{96,0},{1,33},{33,65},{65,97},{97,1},{2,34}... | collective-permute-start | bytes 1769480 | tf_op jit(solution)/shard_map/ppermute | solution.py:755
  168.7 16.1 %collective-permute-start.13 = (bf16[64,4608]{1,0:T(8,128)(2,1)S(1)}, bf16[64,4608]{1,0:T(8,128)(2,1)S(1)}, u32[]{:S(2)}, u32[]{:S(2)}) collective-permute-start(bf16[64,4608]{1,0:T(8,128)(2,1)S(1)} %copy-done.15), channel_id=1, source_target_pairs={{0,96},{32,0},{64,32},{96,64},{1,97},{33,1},{65,33},{97,65},{2,98}... | collective-permute-start | bytes 1769480 | tf_op jit(solution)/shard_map/ppermute | solution.py:755
  191.6 27.9 %collective-permute-start.14 = (bf16[128,4608]{1,0:T(8,128)(2,1)}, bf16[128,4608]{1,0:T(8,128)(2,1)S(1)}, u32[]{:S(2)}, u32[]{:S(2)}) collective-permute-start(bf16[128,4608]{1,0:T(8,128)(2,1)} %get-tuple-element.93), channel_id=1, source_target_pairs={{0,32},{32,64},{64,96},{96,0},{1,33},{33,65},{65,97},{97,1},{2,34}... | collective-permute-start | bytes 3538952 | tf_op jit(solution)/shard_map/ppermute | solution.py:755
  191.7 27.8 %collective-permute-start.15 = (bf16[128,4608]{1,0:T(8,128)(2,1)}, bf16[128,4608]{1,0:T(8,128)(2,1)S(1)}, u32[]{:S(2)}, u32[]{:S(2)}) collective-permute-start(bf16[128,4608]{1,0:T(8,128)(2,1)} %get-tuple-element.94), channel_id=1, source_target_pairs={{0,96},{32,0},{64,32},{96,64},{1,97},{33,1},{65,33},{97,65},{2,98}... | collective-permute-start | bytes 3538952 | tf_op jit(solution)/shard_map/ppermute | solution.py:755
  224.8 27.3 %all-to-all-start.3 = ((bf16[32,4,4608]{2,1,0:T(4,128)(2,1)}), bf16[32,4,4608]{2,1,0:T(4,128)(2,1)}, u32[]{:S(2)}, u32[]{:S(2)}) async-start(bf16[32,4,4608]{2,1,0:T(4,128)(2,1)} %sum_blocks.1), calls=%async_computation.3 | async-start | bytes 2359296 | tf_op jit(solution)/shard_map/all_to_all | solution.py:750
  233.7 18.4 %copy-start.2 = (bf16[64,128]{1,0:T(8,128)(2,1)S(1)}, bf16[64,128]{1,0:T(8,128)(2,1)}, u32[]{:S(2)}) copy-start(bf16[64,128]{1,0:T(8,128)(2,1)} %get-tuple-element.51.table_ref) | copy-start | bytes 49156
  234.5 6.9 %collective-permute-start.8 = (bf16[32,2560]{1,0:T(8,128)(2,1)S(1)}, bf16[32,2560]{1,0:T(8,128)(2,1)S(1)}, u32[]{:S(2)}, u32[]{:S(2)}) collective-permute-start(bf16[32,2560]{1,0:T(8,128)(2,1)S(1)} %get-tuple-element.74), channel_id=1, source_target_pairs={{0,32},{32,64},{64,96},{96,0},{1,33},{33,65},{65,97},{97,1},{2,34}... | collective-permute-start | bytes 491528 | tf_op jit(solution)/shard_map/ppermute | solution.py:755
  234.6 6.8 %collective-permute-start.9 = (bf16[32,2560]{1,0:T(8,128)(2,1)S(1)}, bf16[32,2560]{1,0:T(8,128)(2,1)S(1)}, u32[]{:S(2)}, u32[]{:S(2)}) collective-permute-start(bf16[32,2560]{1,0:T(8,128)(2,1)S(1)} %get-tuple-element.75), channel_id=1, source_target_pairs={{0,96},{32,0},{64,32},{96,64},{1,97},{33,1},{65,33},{97,65},{2,98}... | collective-permute-start | bytes 491528 | tf_op jit(solution)/shard_map/ppermute | solution.py:755
  242.4 9.7 %collective-permute-start.10 = (bf16[64,2560]{1,0:T(8,128)(2,1)S(1)}, bf16[64,2560]{1,0:T(8,128)(2,1)S(1)}, u32[]{:S(2)}, u32[]{:S(2)}) collective-permute-start(bf16[64,2560]{1,0:T(8,128)(2,1)S(1)} %get-tuple-element.76), channel_id=1, source_target_pairs={{0,32},{32,64},{64,96},{96,0},{1,33},{33,65},{65,97},{97,1},{2,34}... | collective-permute-start | bytes 983048 | tf_op jit(solution)/shard_map/ppermute | solution.py:755
  242.4 9.7 %collective-permute-start.11 = (bf16[64,2560]{1,0:T(8,128)(2,1)S(1)}, bf16[64,2560]{1,0:T(8,128)(2,1)S(1)}, u32[]{:S(2)}, u32[]{:S(2)}) collective-permute-start(bf16[64,2560]{1,0:T(8,128)(2,1)S(1)} %get-tuple-element.77), channel_id=1, source_target_pairs={{0,96},{32,0},{64,32},{96,64},{1,97},{33,1},{65,33},{97,65},{2,98}... | collective-permute-start | bytes 983048 | tf_op jit(solution)/shard_map/ppermute | solution.py:755
  (12 other events, 26.6 us)

commit v7 on v6

--- a/solution.py
+++ b/solution.py
@@ -469,6 +469,7 @@
         "side_part",
         6 * span * double * wide_cols,
         2 * wide_cols * (4 * span + double),
+        mib=24,
         in_specs=[VMEM, ANY, ANY, ANY, ANY],
         out_specs=[ANY] * 3,
         out_shape=[jax.ShapeDtypeStruct((span, wide_cols), BF)] * 3,
@@ -510,6 +511,7 @@
         "sum_blocks",
         2 * rows * cols,
         8 * rows * cols,
+        mib=24,
         in_specs=[ANY] * 3,
         out_specs=ANY,
         out_shape=jax.ShapeDtypeStruct((rows // CAP, CAP, cols), BF),
@@ -704,45 +706,61 @@
     )(rest, top, bottom)
 
 
-def combine_kernel(split, table_ref, own_ref, left_ref, right_ref, wide_ref, out_ref):
+def combine_kernel(table_ref, rest_ref, left_ref, right_ref, wide_ref, out_ref, ring, wide, staged, sem):
+    buf = table_ref.shape[0]
+    ring_cols = ring.shape[1]
+    locs, _, wide_cols = wide.shape
+    loads, stores = [], []
+
+    def add(source, target):
+        loads.append(pltpu.make_async_copy(source, target, sem.at[len(loads)]))
+
+    for k, ref in enumerate((rest_ref.at[0], left_ref, right_ref)):
+        add(ref, ring.at[k * buf : (k + 1) * buf, :])
+    for first in range(0, wide_cols, TILE):
+        window = slice(first, first + TILE)
+        add(wide_ref.at[:, :, window], wide.at[:, :, window])
+    start_all(loads)
     table = table_ref[...]
-
-    @pl.when(pl.program_id(0) < split)
-    def _():
-        rows = jnp.concatenate([own_ref[...], left_ref[...], right_ref[...]], axis=0)
-        thrice = jnp.concatenate([table] * 3, axis=0)
-        out_ref[...] = contract_rows(thrice, rows).astype(BF)
-
-    @pl.when(pl.program_id(0) >= split)
-    def _():
-        count, _, tile = wide_ref.shape
-        rows = wide_ref[...].astype(F32).reshape(count * CAP, tile).astype(BF)
-        both = jnp.concatenate([table, table], axis=0)
-        out_ref[...] = contract_rows(both, rows).astype(BF)
+    twice = jnp.concatenate([table] * 2, axis=0)
+    thrice = jnp.concatenate([table] * 3, axis=0)
+    wait_all(loads[:3])
+    for t in range((ring_cols + wide_cols) // TILE):
+        window = slice(t * TILE, (t + 1) * TILE)
+        first = t * TILE - ring_cols
+        if first < 0:
+            total = contract_rows(thrice, ring[:, window])
+        else:
+            loads[3 + first // TILE].wait()
+            rows = wide[:, :, first : first + TILE].astype(F32).reshape(locs * CAP, TILE).astype(BF)
+            total = contract_rows(twice, rows)
+        staged[:, window] = total.astype(BF)
+        target = out_ref.at[:, window]
+        index = len(loads) + len(stores)
+        stores.append(pltpu.make_async_copy(staged.at[:, window], target, sem.at[index]))
+        stores[-1].start()
+    wait_all(stores)
 
 
 def combine(table, rest, left, right, wide):
     buf, tok = table.shape
-    width = left.shape[1] + wide.shape[2]
-    tile = TILE
-    split = left.shape[1] // tile
-    block = pl.BlockSpec((buf, tile), lambda j: (0, jnp.minimum(j, split - 1)))
-    return call(
-        functools.partial(combine_kernel, split),
+    ring_cols, wide_cols = left.shape[1], wide.shape[2]
+    width = ring_cols + wide_cols
+    return call(
+        combine_kernel,
         "combine",
         2 * tok * buf * width,
         2 * width * (tok + 2 * buf),
-        mib=20,
-        grid=(width // tile,),
-        in_specs=[
-            whole((buf, tok)),
-            pl.BlockSpec((None, buf, tile), lambda j: (0, 0, jnp.minimum(j, split - 1))),
-            block,
-            block,
-            pl.BlockSpec((wide.shape[0], CAP, tile), lambda j: (0, 0, jnp.maximum(j - split, 0))),
-        ],
-        out_specs=pl.BlockSpec((tok, tile), lambda j: (0, j)),
+        mib=24,
+        in_specs=[VMEM, ANY, ANY, ANY, ANY],
+        out_specs=ANY,
         out_shape=jax.ShapeDtypeStruct((tok, width), BF),
+        scratch_shapes=[
+            pltpu.VMEM((3 * buf, ring_cols), BF),
+            pltpu.VMEM((wide.shape[0], CAP, wide_cols), BF),
+            pltpu.VMEM((tok, width), BF),
+            pltpu.SemaphoreType.DMA((3 + wide_cols // TILE + width // TILE,)),
+        ],
     )(table, rest, left, right, wide)
 
 
@@ -768,8 +786,8 @@
     width = tokens.shape[1]
     buf = experts * CAP
     unit = 2 * CAP
-    share = 768
-    ring_cols = 2560
+    share = 512
+    ring_cols = 3584
     wide_cols = width - ring_cols
 
     w_gate, w_up, w_down = gate_weight[0], up_weight[0], down_weight[0]

time: 264 us -> 254 us (0.962)
  Pallas kernels: 79.1 us -> 72.1 us
  local copies, waits for them, and re-layouts: 10.1 us -> 5.88 us
    pallas_call x2, Pallas kernels: 12.1 us -> 5.23 us  [the longest x1 3.46 us: combine(): call(combine_kernel, 'combine', 2 * tok * buf * width, 2 * width * (tok +...]
    unnamed x32 -> x28, local copies, waits for them, and re-layouts: 8.79 us -> 4.61 us
    all_to_all x4, waiting for transfers between devices: 7.33 us -> 3.41 us  [over_loc(): return lax.all_to_all(a, 'loc', split_axis=0, concat_axis=0, tiled=True)]
    ppermute x16, waiting for transfers between devices: 107 us -> 111 us  [shift(): lax.ppermute(a, 'grp', [(i, (i + step) % groups) for i in range(groups)])]
    pallas_call x1, Pallas kernels: 0.78 us -> 4.67 us  [fold(): call(fold_kernel, 'fold', experts * depth * width, 6 * experts * depth *...]
    pallas_call x1, Pallas kernels: 11.8 us -> 8.77 us  [down(): call(down_kernel, 'down', 4 * rows * (cols + share) * ff, 2 * (cols + sha...]
  transfers between devices with their start and end apart: 20 -> 20, of which waited for: 9 -> 9; matrix products, arithmetic and copies ran while one was open for 0% -> 1% of each run, Pallas kernels for 17% -> 17%
where the time goes in v7:
time: 254 us; the launch traced here: 253 us
  waiting for transfers between devices  114 us (45%)
  Pallas kernels  72.1 us (28%)
  starting transfers between devices  59.1 us (23%)
  local copies, waits for them, and re-layouts  5.88 us (2%)
    ppermute x16, waiting for transfers between devices, shift(): lax.ppermute(a, 'grp', [(i, (i + step) % groups) for i in range(groups)])  111 us
    all_to_all x4, starting transfers between devices, over_loc(): return lax.all_to_all(a, 'loc', split_axis=0, concat_axis=0, tiled=True)  36.4 us
    ppermute x16, starting transfers between devices, shift(): lax.ppermute(a, 'grp', [(i, (i + step) % groups) for i in range(groups)])  22.7 us
    pallas_call x3, Pallas kernels, pre(): call(functools.partial(pre_kernel, len(blocks)), 'pre', 8 * rows * cols *...  14 us
    pallas_call x1, Pallas kernels, row_grads(): call(row_grads_kernel, 'row_grads', 8 * rows * half * ff, 2 * half * (row...  9.62 us
    pallas_call x1, Pallas kernels, down(): call(down_kernel, 'down', 4 * rows * (cols + share) * ff, 2 * (cols + sha...  8.77 us
    pallas_call x1, Pallas kernels, hidden(): call(hidden_kernel, 'hidden', 4 * rows * cols * ff + 4 * span * ff * wide...  8.72 us
  transfers between devices with their start and end apart: 20, of which 9 were waited for; matrix products, arithmetic and copies ran while one was open for 1% of the time, Pallas kernels for 17%

profile of v7, /device:TPU:1, one launch (start us, length us, event | category | flops | bytes accessed | tf_op | source)
XLA Modules:
  0.0 252.6 jit_solution(8279304137288127387)
XLA Ops:
  0.6 3.5 %dispatch_gradient.1 = (bf16[64,128]{1,0:T(8,128)(2,1)}, bf16[2,128,128]{2,1,0:T(8,128)(2,1)}, bf16[128,512]{1,0:T(8,128)(2,1)}, bf16[128,3072]{1,0:T(8,128)(2,1)}) custom-call(s32[8,128]{1,0:T(8,128)} %bitcast.50, bf16[8,128]{1,0:T(8,128)(2,1)} %bitcast.51, bf16[128,7168]{1,0:T(8,128)(2,1)} %g_ref.1), custom_call_target="tpu_custom_call" | custom-call | flops 234881024 | bytes 2752512 | tf_op jit(solution)/shard_map/dispatch_gradient/pallas_call | solution.py:93
  4.1 4.2 %dispatch_token.1 = bf16[2,16,8,4096]{3,2,1,0:T(8,128)(2,1)} custom-call(bf16[2,128,128]{2,1,0:T(8,128)(2,1)} %get-tuple-element.52.pick_ref, bf16[128,512]{1,0:T(8,128)(2,1)} %get-tuple-element.53.share_ref, bf16[128,7168]{1,0:T(8,128)(2,1)} %t_ref.1), custom_call_target="tpu_custom_call" | custom-call | flops 234881024 | bytes 3670016 | tf_op jit(solution)/shard_map/dispatch_token/pallas_call | solution.py:136
  8.4 9.4 %all-to-all-start = ((bf16[32,8,4096]{2,1,0:T(8,128)(2,1)}), bf16[32,8,4096]{2,1,0:T(8,128)(2,1)S(1)}, u32[]{:S(2)}, u32[]{:S(2)}) async-start(bf16[32,8,4096]{2,1,0:T(8,128)(2,1)} %bitcast.44), calls=%async_computation | async-start | bytes 4194304 | tf_op jit(solution)/shard_map/all_to_all | solution.py:768
  20.7 17.7 %collective-permute-done.1 = bf16[128,3072]{1,0:T(8,128)(2,1)S(1)} collective-permute-done((bf16[128,3072]{1,0:T(8,128)(2,1)}, bf16[128,3072]{1,0:T(8,128)(2,1)S(1)}, u32[]{:S(2)}, u32[]{:S(2)}) %collective-permute-start.1) | collective-permute-done | bytes 786464 | tf_op jit(solution)/shard_map/ppermute | solution.py:773
  41.3 8.1 %collective-permute-done.2 = bf16[64,3072]{1,0:T(8,128)(2,1)S(1)} collective-permute-done((bf16[64,3072]{1,0:T(8,128)(2,1)S(1)}, bf16[64,3072]{1,0:T(8,128)(2,1)S(1)}, u32[]{:S(2)}, u32[]{:S(2)}) %collective-permute-start.2) | collective-permute-done | bytes 393248 | tf_op jit(solution)/shard_map/ppermute | solution.py:773
  50.1 4.1 %regroup.1 = bf16[2,16,32,3072]{3,2,1,0:T(8,128)(2,1)} custom-call(bf16[16,8,3072]{2,1,0:T(8,128)(2,1)} %bitcast.48, bf16[16,8,3072]{2,1,0:T(8,128)(2,1)} %bitcast.47, bf16[8,8,3072]{2,1,0:T(8,128)(2,1)} %bitcast.49, bf16[8,8,3072]{2,1,0:T(8,128)(2,1)} %bitcast.6.bottom_ref, bf16[16,8,3072]{2,1,0:T(8,128)(2,1)} %bitcast.46), custom_call_target="tpu_custom_call" | custom-call | bytes 9437184 | tf_op jit(solution)/shard_map/regroup/pallas_call | solution.py:184
  54.2 8.8 %all-to-all-start.1 = ((bf16[32,32,3072]{2,1,0:T(8,128)(2,1)}), bf16[32,32,3072]{2,1,0:T(8,128)(2,1)}, u32[]{:S(2)}, u32[]{:S(2)}) async-start(bf16[32,32,3072]{2,1,0:T(8,128)(2,1)} %bitcast.37), calls=%async_computation.1 | async-start | bytes 12582912 | tf_op jit(solution)/shard_map/all_to_all | solution.py:768
  66.0 45.6 %collective-permute-done.5.refs_1_.prev_ref.refs_7_ = bf16[256,4096]{1,0:T(8,128)(2,1)S(1)} collective-permute-done((bf16[256,4096]{1,0:T(8,128)(2,1)S(1)}, bf16[256,4096]{1,0:T(8,128)(2,1)S(1)}, u32[]{:S(2)}, u32[]{:S(2)}) %collective-permute-start.5) | collective-permute-done | bytes 2097184 | tf_op jit(solution)/shard_map/ppermute | solution.py:773
  115.8 4.2 %pre.3 = (f32[128,128]{1,0:T(8,128)}, f32[128,128]{1,0:T(8,128)}, f32[128,128]{1,0:T(8,128)}, f32[128,128]{1,0:T(8,128)}) custom-call(bf16[256,4096]{1,0:T(8,128)(2,1)} %bitcast.40, bf16[7168,128]{1,0:T(8,128)(2,1)} %bitcast.21, bf16[7168,128]{1,0:T(8,128)(2,1)} %bitcast.27, bf16[128,7168]{1,0:T(8,128)(2,1)} %bitcast.33), custom_call_target="tpu_custom_call" | custom-call | flops 1073741824 | bytes 6291456 | tf_op jit(solution)/shard_map/pre/pallas_call | solution.py:265
  120.1 5.5 %pre.4 = (f32[256,128]{1,0:T(8,128)}, f32[256,128]{1,0:T(8,128)}, f32[256,128]{1,0:T(8,128)}, f32[256,128]{1,0:T(8,128)}) custom-call(bf16[256,4096]{1,0:T(8,128)(2,1)} %copy-done.6, bf16[256,4096]{1,0:T(8,128)(2,1)} %copy-done.5, bf16[7168,128]{1,0:T(8,128)(2,1)} %bitcast.22, bf16[7168,128]{1,0:T(8,128)(2,1)} %bitcast.28, bf16[128,7168]{1,0:T(8,128)(2,1)} %bitcast.34), custom_call_target="tpu_custom_call" | custom-call | flops 2147483648 | bytes 8388608 | tf_op jit(solution)/shard_map/pre/pallas_call | solution.py:265
  125.6 12.6 %collective-permute-done.6.refs_0_.top_ref.refs_5_ = bf16[128,4096]{1,0:T(8,128)(2,1)S(1)} collective-permute-done((bf16[128,4096]{1,0:T(8,128)(2,1)}, bf16[128,4096]{1,0:T(8,128)(2,1)S(1)}, u32[]{:S(2)}, u32[]{:S(2)}) %collective-permute-start.6) | collective-permute-done | bytes 1048608 | tf_op jit(solution)/shard_map/ppermute | solution.py:773
  140.1 4.4 %pre.5 = (f32[128,128]{1,0:T(8,128)}, f32[128,128]{1,0:T(8,128)}, f32[128,128]{1,0:T(8,128)}, f32[128,128]{1,0:T(8,128)}) custom-call(bf16[128,4096]{1,0:T(8,128)(2,1)} %copy-done.7, bf16[128,4096]{1,0:T(8,128)(2,1)} %copy-done.8, bf16[7168,128]{1,0:T(8,128)(2,1)} %bitcast.23, bf16[7168,128]{1,0:T(8,128)(2,1)} %bitcast.29, bf16[128,7168]{1,0:T(8,128)(2,1)} %bitcast.35), custom_call_target="tpu_custom_call" | custom-call | flops 1073741824 | bytes 6291456 | tf_op jit(solution)/shard_map/pre/pallas_call | solution.py:265
  144.5 8.7 %hidden.1 = (bf16[4,128,256]{2,1,0:T(8,128)(2,1)}, bf16[32,16,256]{2,1,0:T(8,128)(2,1)}, bf16[64,3584]{1,0:T(8,128)(2,1)}, bf16[64,3584]{1,0:T(8,128)(2,1)}) custom-call(bf16[1024,3072]{1,0:T(8,128)(2,1)} %bitcast.9.g_ref, bf16[128,7168]{1,0:T(8,128)(2,1)} %bitcast.36, bf16[7168,128]{1,0:T(8,128)(2,1)} %bitcast.24, bf16[7168,128]{1,0:T(8,128)(2,1)} %bitcast.30, ...), custom_call_target="tpu_custom_call" | custom-call | flops 1845493760 | bytes 9043968 | tf_op jit(solution)/shard_map/hidden/pallas_call | solution.py:371
  153.2 4.7 %ring_part.1 = bf16[512,3584]{1,0:T(8,128)(2,1)} custom-call(bf16[32,16,256]{2,1,0:T(8,128)(2,1)} %get-tuple-element.70.near_ref, bf16[7168,128]{1,0:T(8,128)(2,1)} %bitcast.25, bf16[7168,128]{1,0:T(8,128)(2,1)} %bitcast.31), custom_call_target="tpu_custom_call" | custom-call | flops 939524096 | bytes 5505024 | tf_op jit(solution)/shard_map/ring_part/pallas_call | solution.py:414
  158.0 11.4 %all-to-all-start.2 = ((bf16[32,16,3584]{2,1,0:T(8,128)(2,1)}), bf16[32,16,3584]{2,1,0:T(8,128)(2,1)}, u32[]{:S(2)}, u32[]{:S(2)}) async-start(bf16[32,16,3584]{2,1,0:T(8,128)(2,1)} %bitcast.43), calls=%async_computation.2 | async-start | bytes 7340032 | tf_op jit(solution)/shard_map/all_to_all | solution.py:768
  172.4 10.5 %collective-permute-done.12.top_ref = bf16[64,3584]{1,0:T(8,128)(2,1)S(1)} collective-permute-done((bf16[64,3584]{1,0:T(8,128)(2,1)S(1)}, bf16[64,3584]{1,0:T(8,128)(2,1)S(1)}, u32[]{:S(2)}, u32[]{:S(2)}) %collective-permute-start.12) | collective-permute-done | bytes 458784 | tf_op jit(solution)/shard_map/ppermute | solution.py:773
  184.4 3.4 %side_part.1 = (bf16[128,3584]{1,0:T(8,128)(2,1)S(1)}, bf16[128,3584]{1,0:T(8,128)(2,1)S(1)}, bf16[128,3584]{1,0:T(8,128)(2,1)S(1)}) custom-call(bf16[4,128,256]{2,1,0:T(8,128)(2,1)S(1)} %copy-done.2, bf16[7168,128]{1,0:T(8,128)(2,1)S(1)} %bitcast.26, bf16[7168,128]{1,0:T(8,128)(2,1)S(1)} %bitcast.32, bf16[64,3584]{1,0:T(8,128)(2,1)S(1)} %collective-permute-done.12.top_ref, ...), custom_call_target="tpu_custom_call" | custom-call | flops 704643072 | bytes 5505024 | tf_op jit(solution)/shard_map/side_part/pallas_call | solution.py:467
  190.7 8.8 %down.1 = bf16[128,7168]{1,0:T(8,128)(2,1)} custom-call(bf16[1024,3072]{1,0:T(8,128)(2,1)} %bitcast.9.g_ref, f32[128,128]{1,0:T(8,128)} %get-tuple-element.89.refs_0_, f32[256,128]{1,0:T(8,128)} %get-tuple-element.90.refs_1_, f32[128,128]{1,0:T(8,128)} %get-tuple-element.91.refs_2_, bf16[256,4096]{1,0:T(8,128)(2,1)} %bitcast.41, ...), custom_call_target="tpu_custom_call" | custom-call | flops 1879048192 | bytes 9175040 | tf_op jit(solution)/shard_map/down/pallas_call | solution.py:627
  199.5 9.6 %row_grads.1 = (bf16[2,3584,128]{2,1,0:T(8,128)(2,1)}, bf16[2,3584,128]{2,1,0:T(8,128)(2,1)}) custom-call(bf16[4,128,256]{2,1,0:T(8,128)(2,1)} %get-tuple-element.86.gu_ref, bf16[256,4096]{1,0:T(8,128)(2,1)} %bitcast.42, bf16[256,4096]{1,0:T(8,128)(2,1)} %copy-done.6, bf16[128,4096]{1,0:T(8,128)(2,1)} %copy-done.7, bf16[128,4096]{1,0:T(8,128)(2,1)} %copy-done.8, ...), custom_call_target="tpu_custom_call" | custom-call | flops 3758096384 | bytes 11010048 | tf_op jit(solution)/shard_map/row_grads/pallas_call | solution.py:558
  215.4 6.7 %all-to-all-start.3 = ((bf16[32,4,3584]{2,1,0:T(4,128)(2,1)}), bf16[32,4,3584]{2,1,0:T(4,128)(2,1)S(1)}, u32[]{:S(2)}, u32[]{:S(2)}) async-start(bf16[32,4,3584]{2,1,0:T(4,128)(2,1)} %sum_blocks.1), calls=%async_computation.3 | async-start | bytes 1835008 | tf_op jit(solution)/shard_map/all_to_all | solution.py:768
  222.1 4.7 %fold.1 = (bf16[32,3584]{1,0:T(8,128)(2,1)S(1)}, bf16[32,3584]{1,0:T(8,128)(2,1)S(1)}, bf16[3,64,3584]{2,1,0:T(8,128)(2,1)S(1)}) custom-call(bf16[2,16,16,3584]{3,2,1,0:T(8,128)(2,1)} %bitcast.15.in_ref), custom_call_target="tpu_custom_call" | custom-call | flops 917504 | bytes 5505024 | tf_op jit(solution)/shard_map/fold/pallas_call | solution.py:666
  229.8 5.6 %collective-permute-done.8.top_ref = bf16[32,3584]{1,0:T(8,128)(2,1)S(1)} collective-permute-done((bf16[32,3584]{1,0:T(8,128)(2,1)S(1)}, bf16[32,3584]{1,0:T(8,128)(2,1)S(1)}, u32[]{:S(2)}, u32[]{:S(2)}) %collective-permute-start.8) | collective-permute-done | bytes 229408 | tf_op jit(solution)/shard_map/ppermute | solution.py:773
  239.1 9.9 %collective-permute-done.10.left_ref = bf16[64,3584]{1,0:T(8,128)(2,1)S(1)} collective-permute-done((bf16[64,3584]{1,0:T(8,128)(2,1)}, bf16[64,3584]{1,0:T(8,128)(2,1)S(1)}, u32[]{:S(2)}, u32[]{:S(2)}) %collective-permute-start.10) | collective-permute-done | bytes 458784 | tf_op jit(solution)/shard_map/ppermute | solution.py:773
  249.0 3.5 %combine.1 = bf16[128,7168]{1,0:T(8,128)(2,1)} custom-call(bf16[64,128]{1,0:T(8,128)(2,1)S(1)} %copy-done.3, bf16[3,64,3584]{2,1,0:T(8,128)(2,1)S(1)} %get-tuple-element.73.rest_ref, bf16[64,3584]{1,0:T(8,128)(2,1)S(1)} %collective-permute-done.10.left_ref, bf16[64,3584]{1,0:T(8,128)(2,1)S(1)} %collective-permute-done.11.right_ref, ...), custom_call_target="tpu_custom_call" | custom-call | flops 117440512 | bytes 3670016 | tf_op jit(solution)/shard_map/combine/pallas_call | solution.py:749
  (63 shorter events, 35.8 us)
Async XLA Ops:
  8.4 41.0 %all-to-all-start = ((bf16[32,8,4096]{2,1,0:T(8,128)(2,1)}), bf16[32,8,4096]{2,1,0:T(8,128)(2,1)S(1)}, u32[]{:S(2)}, u32[]{:S(2)}) async-start(bf16[32,8,4096]{2,1,0:T(8,128)(2,1)} %bitcast.44), calls=%async_computation | async-start | bytes 4194304 | tf_op jit(solution)/shard_map/all_to_all | solution.py:768
  17.8 20.5 %collective-permute-start.1 = (bf16[128,3072]{1,0:T(8,128)(2,1)}, bf16[128,3072]{1,0:T(8,128)(2,1)S(1)}, u32[]{:S(2)}, u32[]{:S(2)}) collective-permute-start(bf16[128,3072]{1,0:T(8,128)(2,1)} %get-tuple-element.55), channel_id=1, source_target_pairs={{0,32},{32,64},{64,96},{96,0},{1,33},{33,65},{65,97},{97,1},{2,34}... | collective-permute-start | bytes 2359304 | tf_op jit(solution)/shard_map/ppermute | solution.py:773
  19.2 19.3 %collective-permute-start = (bf16[128,3072]{1,0:T(8,128)(2,1)}, bf16[128,3072]{1,0:T(8,128)(2,1)S(1)}, u32[]{:S(2)}, u32[]{:S(2)}) collective-permute-start(bf16[128,3072]{1,0:T(8,128)(2,1)} %get-tuple-element.55), channel_id=1, source_target_pairs={{0,96},{32,0},{64,32},{96,64},{1,97},{33,1},{65,33},{97,65},{2,98}... | collective-permute-start | bytes 2359304 | tf_op jit(solution)/shard_map/ppermute | solution.py:773
  38.4 10.9 %collective-permute-start.2 = (bf16[64,3072]{1,0:T(8,128)(2,1)S(1)}, bf16[64,3072]{1,0:T(8,128)(2,1)S(1)}, u32[]{:S(2)}, u32[]{:S(2)}) collective-permute-start(bf16[64,3072]{1,0:T(8,128)(2,1)S(1)} %slice.16), channel_id=1, source_target_pairs={{0,32},{32,64},{64,96},{96,0},{1,33},{33,65},{65,97},{97,1},{2,34}... | collective-permute-start | bytes 1179656 | tf_op jit(solution)/shard_map/ppermute | solution.py:773
  38.5 10.8 %collective-permute-start.3 = (bf16[64,3072]{1,0:T(8,128)(2,1)S(1)}, bf16[64,3072]{1,0:T(8,128)(2,1)}, u32[]{:S(2)}, u32[]{:S(2)}) collective-permute-start(bf16[64,3072]{1,0:T(8,128)(2,1)S(1)} %slice.17), channel_id=1, source_target_pairs={{0,96},{32,0},{64,32},{96,64},{1,97},{33,1},{65,33},{97,65},{2,98}... | collective-permute-start | bytes 1179656 | tf_op jit(solution)/shard_map/ppermute | solution.py:773
  49.3 13.9 %copy-start.4 = (bf16[32,8,4096]{2,1,0:T(8,128)(2,1)}, bf16[32,8,4096]{2,1,0:T(8,128)(2,1)S(1)}, u32[]{:S(2)}) copy-start(bf16[32,8,4096]{2,1,0:T(8,128)(2,1)S(1)} %all-to-all-done) | copy-start | bytes 6291460
  54.2 90.2 %all-to-all-start.1 = ((bf16[32,32,3072]{2,1,0:T(8,128)(2,1)}), bf16[32,32,3072]{2,1,0:T(8,128)(2,1)}, u32[]{:S(2)}, u32[]{:S(2)}) async-start(bf16[32,32,3072]{2,1,0:T(8,128)(2,1)} %bitcast.37), calls=%async_computation.1 | async-start | bytes 12582912 | tf_op jit(solution)/shard_map/all_to_all | solution.py:768
  63.1 48.6 %collective-permute-start.5 = (bf16[256,4096]{1,0:T(8,128)(2,1)S(1)}, bf16[256,4096]{1,0:T(8,128)(2,1)S(1)}, u32[]{:S(2)}, u32[]{:S(2)}) collective-permute-start(bf16[256,4096]{1,0:T(8,128)(2,1)S(1)} %bitcast.38), channel_id=1, source_target_pairs={{0,32},{32,64},{64,96},{96,0},{1,33},{33,65},{65,97},{97,1},{2,34}... | collective-permute-start | bytes 6291464 | tf_op jit(solution)/shard_map/ppermute | solution.py:773
  63.3 49.5 %collective-permute-start.4 = (bf16[256,4096]{1,0:T(8,128)(2,1)S(1)}, bf16[256,4096]{1,0:T(8,128)(2,1)S(1)}, u32[]{:S(2)}, u32[]{:S(2)}) collective-permute-start(bf16[256,4096]{1,0:T(8,128)(2,1)S(1)} %bitcast.39), channel_id=1, source_target_pairs={{0,96},{32,0},{64,32},{96,64},{1,97},{33,1},{65,33},{97,65},{2,98}... | collective-permute-start | bytes 6291464 | tf_op jit(solution)/shard_map/ppermute | solution.py:773
  112.8 25.3 %collective-permute-start.6 = (bf16[128,4096]{1,0:T(8,128)(2,1)}, bf16[128,4096]{1,0:T(8,128)(2,1)S(1)}, u32[]{:S(2)}, u32[]{:S(2)}) collective-permute-start(bf16[128,4096]{1,0:T(8,128)(2,1)} %slice.18), channel_id=1, source_target_pairs={{0,32},{32,64},{64,96},{96,0},{1,33},{33,65},{65,97},{97,1},{2,34}... | collective-permute-start | bytes 3145736 | tf_op jit(solution)/shard_map/ppermute | solution.py:773
  113.3 24.8 %collective-permute-start.7 = (bf16[128,4096]{1,0:T(8,128)(2,1)S(1)}, bf16[128,4096]{1,0:T(8,128)(2,1)S(1)}, u32[]{:S(2)}, u32[]{:S(2)}) collective-permute-start(bf16[128,4096]{1,0:T(8,128)(2,1)S(1)} %slice.19), channel_id=1, source_target_pairs={{0,96},{32,0},{64,32},{96,64},{1,97},{33,1},{65,33},{97,65},{2,98}... | collective-permute-start | bytes 3145736 | tf_op jit(solution)/shard_map/ppermute | solution.py:773
  158.0 24.9 %copy-start = (bf16[1,7168,128]{2,1,0:T(8,128)(2,1)S(1)}, bf16[1,7168,128]{2,1,0:T(8,128)(2,1)}, u32[]{:S(2)}) copy-start(bf16[1,7168,128]{2,1,0:T(8,128)(2,1)} %param.11) | copy-start | bytes 5505028
  158.0 24.9 %copy-start.2 = (bf16[4,128,256]{2,1,0:T(8,128)(2,1)S(1)}, bf16[4,128,256]{2,1,0:T(8,128)(2,1)}, u32[]{:S(2)}) copy-start(bf16[4,128,256]{2,1,0:T(8,128)(2,1)} %get-tuple-element.86.gu_ref) | copy-start | bytes 786436
  158.0 57.4 %all-to-all-start.2 = ((bf16[32,16,3584]{2,1,0:T(8,128)(2,1)}), bf16[32,16,3584]{2,1,0:T(8,128)(2,1)}, u32[]{:S(2)}, u32[]{:S(2)}) async-start(bf16[32,16,3584]{2,1,0:T(8,128)(2,1)} %bitcast.43), calls=%async_computation.2 | async-start | bytes 7340032 | tf_op jit(solution)/shard_map/all_to_all | solution.py:768
  169.4 13.5 %collective-permute-start.12 = (bf16[64,3584]{1,0:T(8,128)(2,1)S(1)}, bf16[64,3584]{1,0:T(8,128)(2,1)S(1)}, u32[]{:S(2)}, u32[]{:S(2)}) collective-permute-start(bf16[64,3584]{1,0:T(8,128)(2,1)S(1)} %copy-done.13), channel_id=1, source_target_pairs={{0,32},{32,64},{64,96},{96,0},{1,33},{33,65},{65,97},{97,1},{2,34}... | collective-permute-start | bytes 1376264 | tf_op jit(solution)/shard_map/ppermute | solution.py:773
  169.6 13.3 %collective-permute-start.13 = (bf16[64,3584]{1,0:T(8,128)(2,1)S(1)}, bf16[64,3584]{1,0:T(8,128)(2,1)S(1)}, u32[]{:S(2)}, u32[]{:S(2)}) collective-permute-start(bf16[64,3584]{1,0:T(8,128)(2,1)S(1)} %copy-done.12), channel_id=1, source_target_pairs={{0,96},{32,0},{64,32},{96,64},{1,97},{33,1},{65,33},{97,65},{2,98}... | collective-permute-start | bytes 1376264 | tf_op jit(solution)/shard_map/ppermute | solution.py:773
  187.8 22.4 %collective-permute-start.14 = (bf16[128,3584]{1,0:T(8,128)(2,1)S(1)}, bf16[128,3584]{1,0:T(8,128)(2,1)S(1)}, u32[]{:S(2)}, u32[]{:S(2)}) collective-permute-start(bf16[128,3584]{1,0:T(8,128)(2,1)S(1)} %get-tuple-element.93), channel_id=1, source_target_pairs={{0,32},{32,64},{64,96},{96,0},{1,33},{33,65},{65,97},{97,1},{2,34}... | collective-permute-start | bytes 2752520 | tf_op jit(solution)/shard_map/ppermute | solution.py:773
  188.6 21.6 %collective-permute-start.15 = (bf16[128,3584]{1,0:T(8,128)(2,1)S(1)}, bf16[128,3584]{1,0:T(8,128)(2,1)S(1)}, u32[]{:S(2)}, u32[]{:S(2)}) collective-permute-start(bf16[128,3584]{1,0:T(8,128)(2,1)S(1)} %get-tuple-element.94), channel_id=1, source_target_pairs={{0,96},{32,0},{64,32},{96,64},{1,97},{33,1},{65,33},{97,65},{2,98}... | collective-permute-start | bytes 2752520 | tf_op jit(solution)/shard_map/ppermute | solution.py:773
  215.4 23.7 %all-to-all-start.3 = ((bf16[32,4,3584]{2,1,0:T(4,128)(2,1)}), bf16[32,4,3584]{2,1,0:T(4,128)(2,1)S(1)}, u32[]{:S(2)}, u32[]{:S(2)}) async-start(bf16[32,4,3584]{2,1,0:T(4,128)(2,1)} %sum_blocks.1), calls=%async_computation.3 | async-start | bytes 1835008 | tf_op jit(solution)/shard_map/all_to_all | solution.py:768
  226.8 22.1 %copy-start.3 = (bf16[64,128]{1,0:T(8,128)(2,1)S(1)}, bf16[64,128]{1,0:T(8,128)(2,1)}, u32[]{:S(2)}) copy-start(bf16[64,128]{1,0:T(8,128)(2,1)} %get-tuple-element.51.table_ref) | copy-start | bytes 49156
  226.8 8.6 %collective-permute-start.8 = (bf16[32,3584]{1,0:T(8,128)(2,1)S(1)}, bf16[32,3584]{1,0:T(8,128)(2,1)S(1)}, u32[]{:S(2)}, u32[]{:S(2)}) collective-permute-start(bf16[32,3584]{1,0:T(8,128)(2,1)S(1)} %get-tuple-element.74), channel_id=1, source_target_pairs={{0,32},{32,64},{64,96},{96,0},{1,33},{33,65},{65,97},{97,1},{2,34}... | collective-permute-start | bytes 688136 | tf_op jit(solution)/shard_map/ppermute | solution.py:773
  227.1 8.3 %collective-permute-start.9 = (bf16[32,3584]{1,0:T(8,128)(2,1)S(1)}, bf16[32,3584]{1,0:T(8,128)(2,1)S(1)}, u32[]{:S(2)}, u32[]{:S(2)}) collective-permute-start(bf16[32,3584]{1,0:T(8,128)(2,1)S(1)} %get-tuple-element.75), channel_id=1, source_target_pairs={{0,96},{32,0},{64,32},{96,64},{1,97},{33,1},{65,33},{97,65},{2,98}... | collective-permute-start | bytes 688136 | tf_op jit(solution)/shard_map/ppermute | solution.py:773
  236.4 12.6 %collective-permute-start.10 = (bf16[64,3584]{1,0:T(8,128)(2,1)}, bf16[64,3584]{1,0:T(8,128)(2,1)S(1)}, u32[]{:S(2)}, u32[]{:S(2)}) collective-permute-start(bf16[64,3584]{1,0:T(8,128)(2,1)} %get-tuple-element.76), channel_id=1, source_target_pairs={{0,32},{32,64},{64,96},{96,0},{1,33},{33,65},{65,97},{97,1},{2,34}... | collective-permute-start | bytes 1376264 | tf_op jit(solution)/shard_map/ppermute | solution.py:773
  237.1 11.9 %collective-permute-start.11 = (bf16[64,3584]{1,0:T(8,128)(2,1)}, bf16[64,3584]{1,0:T(8,128)(2,1)S(1)}, u32[]{:S(2)}, u32[]{:S(2)}) collective-permute-start(bf16[64,3584]{1,0:T(8,128)(2,1)} %get-tuple-element.77), channel_id=1, source_target_pairs={{0,96},{32,0},{64,32},{96,64},{1,97},{33,1},{65,33},{97,65},{2,98}... | collective-permute-start | bytes 1376264 | tf_op jit(solution)/shard_map/ppermute | solution.py:773
  (10 other events, 58.1 us)

commit v8 on v7

--- a/solution.py
+++ b/solution.py
@@ -265,8 +265,8 @@
     return call(
         functools.partial(pre_kernel, len(blocks)),
         "pre",
-        8 * rows * cols * ff,
-        2 * cols * (rows + 4 * ff),
+        200 * (8 * rows * cols * ff),
+        200 * (2 * cols * (rows + 4 * ff)),
         in_specs=[ANY] * (len(blocks) + 3),
         out_specs=[VMEM] * 4,
         out_shape=[jax.ShapeDtypeStruct((rows // 2, ff), F32)] * 4,
@@ -467,8 +467,8 @@
     return call(
         side_kernel,
         "side_part",
-        6 * span * double * wide_cols,
-        2 * wide_cols * (4 * span + double),
+        40 * (6 * span * double * wide_cols),
+        40 * (2 * wide_cols * (4 * span + double)),
         mib=24,
         in_specs=[VMEM, ANY, ANY, ANY, ANY],
         out_specs=[ANY] * 3,
@@ -786,8 +786,8 @@
     width = tokens.shape[1]
     buf = experts * CAP
     unit = 2 * CAP
-    share = 512
-    ring_cols = 3584
+    share = 768
+    ring_cols = 3072
     wide_cols = width - ring_cols
 
     w_gate, w_up, w_down = gate_weight[0], up_weight[0], down_weight[0]

time: 254 us -> 235 us (0.925)
  waiting for transfers between devices: 114 us -> 90.8 us
  local copies, waits for them, and re-layouts: 5.88 us -> 11 us
    ppermute x16, waiting for transfers between devices: 111 us -> 80.4 us  [shift(): lax.ppermute(a, 'grp', [(i, (i + step) % groups) for i in range(groups)])]
    all_to_all x4, waiting for transfers between devices: 3.41 us -> 10.4 us  [over_loc(): return lax.all_to_all(a, 'loc', split_axis=0, concat_axis=0, tiled=True)]
    pallas_call x1, Pallas kernels: 4.67 us -> 0.92 us  [fold(): call(fold_kernel, 'fold', experts * depth * width, 6 * experts * depth *...]
    slice x4, local copies, waits for them, and re-layouts: 1.27 us -> 4.67 us  [ring_gather(): return [own, after, shift(before[:mid], 1), shift(after[mid:], -1), before]]
    pallas_call x1, Pallas kernels: 8.77 us -> 11.8 us  [down(): call(down_kernel, 'down', 4 * rows * (cols + share) * ff, 2 * (cols + sha...]
    unnamed x28 -> x24, local copies, waits for them, and re-layouts: 4.61 us -> 6.28 us
  transfers between devices with their start and end apart: 20 -> 20, of which waited for: 9 -> 12; matrix products, arithmetic and copies ran while one was open for 1% -> 2% of each run, Pallas kernels for 17% -> 22%
where the time goes in v8:
time: 235 us; the launch traced here: 233 us
  waiting for transfers between devices  90.8 us (39%)
  Pallas kernels  72.4 us (31%)
  starting transfers between devices  58.2 us (25%)
  local copies, waits for them, and re-layouts  11 us (5%)
    ppermute x16, waiting for transfers between devices, shift(): lax.ppermute(a, 'grp', [(i, (i + step) % groups) for i in range(groups)])  80.4 us
    all_to_all x4, starting transfers between devices, over_loc(): return lax.all_to_all(a, 'loc', split_axis=0, concat_axis=0, tiled=True)  36 us
    ppermute x16, starting transfers between devices, shift(): lax.ppermute(a, 'grp', [(i, (i + step) % groups) for i in range(groups)])  22.2 us
    pallas_call x3, Pallas kernels, pre(): call(functools.partial(pre_kernel, len(blocks)), 'pre', 200 * (8 * rows *...  14.4 us
    pallas_call x1, Pallas kernels, down(): call(down_kernel, 'down', 4 * rows * (cols + share) * ff, 2 * (cols + sha...  11.8 us
    all_to_all x4, waiting for transfers between devices, over_loc(): return lax.all_to_all(a, 'loc', split_axis=0, concat_axis=0, tiled=True)  10.4 us
    pallas_call x1, Pallas kernels, row_grads(): call(row_grads_kernel, 'row_grads', 8 * rows * half * ff, 2 * half * (row...  9.47 us
    pallas_call x1, Pallas kernels, hidden(): call(hidden_kernel, 'hidden', 4 * rows * cols * ff + 4 * span * ff * wide...  8.77 us
  transfers between devices with their start and end apart: 20, of which 12 were waited for; matrix products, arithmetic and copies ran while one was open for 2% of the time, Pallas kernels for 22%

profile of v8, /device:TPU:1, one launch (start us, length us, event | category | flops | bytes accessed | tf_op | source)
XLA Modules:
  0.0 233.4 jit_solution(8765418433420374416)
XLA Ops:
  0.6 3.5 %dispatch_gradient.1 = (bf16[64,128]{1,0:T(8,128)(2,1)}, bf16[2,128,128]{2,1,0:T(8,128)(2,1)}, bf16[128,768]{1,0:T(8,128)(2,1)}, bf16[128,2816]{1,0:T(8,128)(2,1)}) custom-call(s32[8,128]{1,0:T(8,128)} %bitcast.47, bf16[8,128]{1,0:T(8,128)(2,1)} %bitcast.48, bf16[128,7168]{1,0:T(8,128)(2,1)} %g_ref.1), custom_call_target="tpu_custom_call" | custom-call | flops 234881024 | bytes 2752512 | tf_op jit(solution)/shard_map/dispatch_gradient/pallas_call | solution.py:93
  4.1 4.3 %dispatch_token.1 = bf16[2,16,8,4352]{3,2,1,0:T(8,128)(2,1)} custom-call(bf16[2,128,128]{2,1,0:T(8,128)(2,1)} %get-tuple-element.52.pick_ref, bf16[128,768]{1,0:T(8,128)(2,1)} %get-tuple-element.53.share_ref, bf16[128,7168]{1,0:T(8,128)(2,1)} %t_ref.1), custom_call_target="tpu_custom_call" | custom-call | flops 234881024 | bytes 3670016 | tf_op jit(solution)/shard_map/dispatch_token/pallas_call | solution.py:136
  8.4 9.6 %all-to-all-start = ((bf16[32,8,4352]{2,1,0:T(8,128)(2,1)}), bf16[32,8,4352]{2,1,0:T(8,128)(2,1)}, u32[]{:S(2)}, u32[]{:S(2)}) async-start(bf16[32,8,4352]{2,1,0:T(8,128)(2,1)} %bitcast.36), calls=%async_computation | async-start | bytes 4456448 | tf_op jit(solution)/shard_map/all_to_all | solution.py:768
  21.0 16.1 %collective-permute-done.1 = bf16[128,2816]{1,0:T(8,128)(2,1)S(1)} collective-permute-done((bf16[128,2816]{1,0:T(8,128)(2,1)S(1)}, bf16[128,2816]{1,0:T(8,128)(2,1)S(1)}, u32[]{:S(2)}, u32[]{:S(2)}) %collective-permute-start.1) | collective-permute-done | bytes 720928 | tf_op jit(solution)/shard_map/ppermute | solution.py:773
  37.2 2.7 %collective-permute-start.3 = (bf16[64,2816]{1,0:T(8,128)(2,1)S(1)}, bf16[64,2816]{1,0:T(8,128)(2,1)S(1)}, u32[]{:S(2)}, u32[]{:S(2)}) collective-permute-start(bf16[64,2816]{1,0:T(8,128)(2,1)S(1)} %slice.17), channel_id=1, source_target_pairs={{0,96},{32,0},{64,32},{96,64},{1,97},{33,1},{65,33},{97,65},{2,98}... | collective-permute-start | bytes 1081352 | tf_op jit(solution)/shard_map/ppermute | solution.py:773
  39.9 7.4 %collective-permute-done.2 = bf16[64,2816]{1,0:T(8,128)(2,1)S(1)} collective-permute-done((bf16[64,2816]{1,0:T(8,128)(2,1)S(1)}, bf16[64,2816]{1,0:T(8,128)(2,1)S(1)}, u32[]{:S(2)}, u32[]{:S(2)}) %collective-permute-start.2) | collective-permute-done | bytes 360480 | tf_op jit(solution)/shard_map/ppermute | solution.py:773
  50.6 3.9 %regroup.1 = bf16[2,16,32,2816]{3,2,1,0:T(8,128)(2,1)} custom-call(bf16[16,8,2816]{2,1,0:T(8,128)(2,1)} %bitcast.44, bf16[16,8,2816]{2,1,0:T(8,128)(2,1)} %bitcast.43, bf16[8,8,2816]{2,1,0:T(8,128)(2,1)} %bitcast.45, bf16[8,8,2816]{2,1,0:T(8,128)(2,1)} %bitcast.46, bf16[16,8,2816]{2,1,0:T(8,128)(2,1)} %bitcast.42), custom_call_target="tpu_custom_call" | custom-call | bytes 8650752 | tf_op jit(solution)/shard_map/regroup/pallas_call | solution.py:184
  54.5 8.9 %all-to-all-start.1 = ((bf16[32,32,2816]{2,1,0:T(8,128)(2,1)}), bf16[32,32,2816]{2,1,0:T(8,128)(2,1)}, u32[]{:S(2)}, u32[]{:S(2)}) async-start(bf16[32,32,2816]{2,1,0:T(8,128)(2,1)} %bitcast.34), calls=%async_computation.1 | async-start | bytes 11534336 | tf_op jit(solution)/shard_map/all_to_all | solution.py:768
  63.4 4.3 %pre.3 = (f32[128,128]{1,0:T(8,128)}, f32[128,128]{1,0:T(8,128)}, f32[128,128]{1,0:T(8,128)}, f32[128,128]{1,0:T(8,128)}) custom-call(bf16[256,4352]{1,0:T(8,128)(2,1)} %bitcast.13.refs_0_.own_ref.refs_3_, bf16[7168,128]{1,0:T(8,128)(2,1)} %bitcast.22, bf16[7168,128]{1,0:T(8,128)(2,1)} %bitcast.28, bf16[128,7168]{1,0:T(8,128)(2,1)} %bitcast.37), custom_call_target="tpu_custom_call" | custom-call | flops 228170137600 | bytes 1336934400 | tf_op jit(solution)/shard_map/pre/pallas_call | solution.py:265
  67.7 30.3 %collective-permute-done.5.refs_1_.prev_ref.refs_7_ = bf16[256,4352]{1,0:T(8,128)(2,1)} collective-permute-done((bf16[256,4352]{1,0:T(8,128)(2,1)}, bf16[256,4352]{1,0:T(8,128)(2,1)}, u32[]{:S(2)}, u32[]{:S(2)}) %collective-permute-start.5) | collective-permute-done | bytes 2228256 | tf_op jit(solution)/shard_map/ppermute | solution.py:773
  105.3 5.6 %pre.4 = (f32[256,128]{1,0:T(8,128)}, f32[256,128]{1,0:T(8,128)}, f32[256,128]{1,0:T(8,128)}, f32[256,128]{1,0:T(8,128)}) custom-call(bf16[256,4352]{1,0:T(8,128)(2,1)} %collective-permute-done.4.refs_0_.next_ref.refs_4_, bf16[256,4352]{1,0:T(8,128)(2,1)} %collective-permute-done.5.refs_1_.prev_ref.refs_7_, bf16[7168,128]{1,0:T(8,128)(2,1)} %bitcast.23, ...), custom_call_target="tpu_custom_call" | custom-call | flops 456340275200 | bytes 1782579200 | tf_op jit(solution)/shard_map/pre/pallas_call | solution.py:265
  110.9 14.7 %collective-permute-done.6.refs_0_.top_ref.refs_5_ = bf16[128,4352]{1,0:T(8,128)(2,1)} collective-permute-done((bf16[128,4352]{1,0:T(8,128)(2,1)}, bf16[128,4352]{1,0:T(8,128)(2,1)}, u32[]{:S(2)}, u32[]{:S(2)}) %collective-permute-start.6) | collective-permute-done | bytes 1114144 | tf_op jit(solution)/shard_map/ppermute | solution.py:773
  127.4 4.4 %pre.5 = (f32[128,128]{1,0:T(8,128)}, f32[128,128]{1,0:T(8,128)}, f32[128,128]{1,0:T(8,128)}, f32[128,128]{1,0:T(8,128)}) custom-call(bf16[128,4352]{1,0:T(8,128)(2,1)} %collective-permute-done.6.refs_0_.top_ref.refs_5_, bf16[128,4352]{1,0:T(8,128)(2,1)} %collective-permute-done.7.refs_1_.bottom_ref.refs_6_, bf16[7168,128]{1,0:T(8,128)(2,1)} %bitcast.24, ...), custom_call_target="tpu_custom_call" | custom-call | flops 228170137600 | bytes 1336934400 | tf_op jit(solution)/shard_map/pre/pallas_call | solution.py:265
  134.4 8.8 %hidden.1 = (bf16[4,128,256]{2,1,0:T(8,128)(2,1)}, bf16[32,16,256]{2,1,0:T(8,128)(2,1)}, bf16[64,4096]{1,0:T(8,128)(2,1)}, bf16[64,4096]{1,0:T(8,128)(2,1)}) custom-call(bf16[1024,2816]{1,0:T(8,128)(2,1)} %bitcast.9.g_ref, bf16[128,7168]{1,0:T(8,128)(2,1)} %bitcast.40, bf16[7168,128]{1,0:T(8,128)(2,1)} %bitcast.25, bf16[7168,128]{1,0:T(8,128)(2,1)} %bitcast.31, ...), custom_call_target="tpu_custom_call" | custom-call | flops 1744830464 | bytes 8912896 | tf_op jit(solution)/shard_map/hidden/pallas_call | solution.py:371
  146.1 4.4 %ring_part.1 = bf16[512,3072]{1,0:T(8,128)(2,1)} custom-call(bf16[32,16,256]{2,1,0:T(8,128)(2,1)} %get-tuple-element.70.near_ref, bf16[7168,128]{1,0:T(8,128)(2,1)} %bitcast.26, bf16[7168,128]{1,0:T(8,128)(2,1)} %bitcast.32), custom_call_target="tpu_custom_call" | custom-call | flops 805306368 | bytes 4718592 | tf_op jit(solution)/shard_map/ring_part/pallas_call | solution.py:414
  150.5 12.0 %all-to-all-start.2 = ((bf16[32,16,3072]{2,1,0:T(8,128)(2,1)}), bf16[32,16,3072]{2,1,0:T(8,128)(2,1)S(1)}, u32[]{:S(2)}, u32[]{:S(2)}) async-start(bf16[32,16,3072]{2,1,0:T(8,128)(2,1)} %bitcast.35), calls=%async_computation.2 | async-start | bytes 6291456 | tf_op jit(solution)/shard_map/all_to_all | solution.py:768
  165.6 5.2 %side_part.1 = (bf16[128,4096]{1,0:T(8,128)(2,1)}, bf16[128,4096]{1,0:T(8,128)(2,1)S(1)}, bf16[128,4096]{1,0:T(8,128)(2,1)S(1)}) custom-call(bf16[4,128,256]{2,1,0:T(8,128)(2,1)S(1)} %copy-done.6, bf16[7168,128]{1,0:T(8,128)(2,1)S(1)} %bitcast.27, bf16[7168,128]{1,0:T(8,128)(2,1)S(1)} %bitcast.33, bf16[64,4096]{1,0:T(8,128)(2,1)} %collective-permute-done.12.top_ref, ...), custom_call_target="tpu_custom_call" | custom-call | flops 32212254720 | bytes 251658240 | tf_op jit(solution)/shard_map/side_part/pallas_call | solution.py:467
  173.5 11.8 %down.1 = bf16[128,7168]{1,0:T(8,128)(2,1)} custom-call(bf16[1024,2816]{1,0:T(8,128)(2,1)} %bitcast.9.g_ref, f32[128,128]{1,0:T(8,128)} %get-tuple-element.89.refs_0_, f32[256,128]{1,0:T(8,128)} %get-tuple-element.90.refs_1_, f32[128,128]{1,0:T(8,128)} %get-tuple-element.91.refs_2_, bf16[256,4352]{1,0:T(8,128)(2,1)} %bitcast.13.refs_0_.own_ref.refs_3_, ...), custom_call_target="tpu_custom_call" | custom-call | flops 1879048192 | bytes 9175040 | tf_op jit(solution)/shard_map/down/pallas_call | solution.py:627
  185.4 9.5 %row_grads.1 = (bf16[2,3584,128]{2,1,0:T(8,128)(2,1)}, bf16[2,3584,128]{2,1,0:T(8,128)(2,1)}) custom-call(bf16[4,128,256]{2,1,0:T(8,128)(2,1)} %get-tuple-element.86.gu_ref, bf16[256,4352]{1,0:T(8,128)(2,1)} %bitcast.13.refs_0_.own_ref.refs_3_, bf16[256,4352]{1,0:T(8,128)(2,1)} %collective-permute-done.4.refs_0_.next_ref.refs_4_, ...), custom_call_target="tpu_custom_call" | custom-call | flops 3758096384 | bytes 11010048 | tf_op jit(solution)/shard_map/row_grads/pallas_call | solution.py:558
  202.3 5.4 %all-to-all-start.3 = ((bf16[32,4,4096]{2,1,0:T(4,128)(2,1)}), bf16[32,4,4096]{2,1,0:T(4,128)(2,1)}, u32[]{:S(2)}, u32[]{:S(2)}) async-start(bf16[32,4,4096]{2,1,0:T(4,128)(2,1)} %copy-done.4), calls=%async_computation.3 | async-start | bytes 2097152 | tf_op jit(solution)/shard_map/all_to_all | solution.py:768
  211.4 4.8 %collective-permute-done.8.top_ref = bf16[32,3072]{1,0:T(8,128)(2,1)S(1)} collective-permute-done((bf16[32,3072]{1,0:T(8,128)(2,1)S(1)}, bf16[32,3072]{1,0:T(8,128)(2,1)S(1)}, u32[]{:S(2)}, u32[]{:S(2)}) %collective-permute-start.8) | collective-permute-done | bytes 196640 | tf_op jit(solution)/shard_map/ppermute | solution.py:773
  220.1 4.7 %all-to-all-done.3.wide_ref = bf16[32,4,4096]{2,1,0:T(4,128)(2,1)} async-done(((bf16[32,4,4096]{2,1,0:T(4,128)(2,1)}), bf16[32,4,4096]{2,1,0:T(4,128)(2,1)}, u32[]{:S(2)}, u32[]{:S(2)}) %all-to-all-start.3) | async-done | bytes 1048608 | tf_op jit(solution)/shard_map/all_to_all | solution.py:768
  224.7 3.5 %collective-permute-done.10.left_ref = bf16[64,3072]{1,0:T(8,128)(2,1)S(1)} collective-permute-done((bf16[64,3072]{1,0:T(8,128)(2,1)S(1)}, bf16[64,3072]{1,0:T(8,128)(2,1)S(1)}, u32[]{:S(2)}, u32[]{:S(2)}) %collective-permute-start.10) | collective-permute-done | bytes 393248 | tf_op jit(solution)/shard_map/ppermute | solution.py:773
  229.5 3.8 %combine.1 = bf16[128,7168]{1,0:T(8,128)(2,1)} custom-call(bf16[64,128]{1,0:T(8,128)(2,1)S(1)} %copy-done.5, bf16[3,64,3072]{2,1,0:T(8,128)(2,1)S(1)} %copy-done.3, bf16[64,3072]{1,0:T(8,128)(2,1)S(1)} %collective-permute-done.10.left_ref, bf16[64,3072]{1,0:T(8,128)(2,1)S(1)} %collective-permute-done.11.right_ref, bf16[32,4,4096]{2,1,0:T(4,128)(2,1)} %all-to-all-done.3.wide_ref), custom_call_target="tpu_custom_call" | custom-call | flops 117440512 | bytes 3670016 | tf_op jit(solution)/shard_map/combine/pallas_call | solution.py:749
  (59 shorter events, 42.8 us)
Async XLA Ops:
  8.4 39.4 %all-to-all-start = ((bf16[32,8,4352]{2,1,0:T(8,128)(2,1)}), bf16[32,8,4352]{2,1,0:T(8,128)(2,1)}, u32[]{:S(2)}, u32[]{:S(2)}) async-start(bf16[32,8,4352]{2,1,0:T(8,128)(2,1)} %bitcast.36), calls=%async_computation | async-start | bytes 4456448 | tf_op jit(solution)/shard_map/all_to_all | solution.py:768
  18.1 19.0 %collective-permute-start.1 = (bf16[128,2816]{1,0:T(8,128)(2,1)S(1)}, bf16[128,2816]{1,0:T(8,128)(2,1)S(1)}, u32[]{:S(2)}, u32[]{:S(2)}) collective-permute-start(bf16[128,2816]{1,0:T(8,128)(2,1)S(1)} %copy-done.9), channel_id=1, source_target_pairs={{0,32},{32,64},{64,96},{96,0},{1,33},{33,65},{65,97},{97,1},{2,34}... | collective-permute-start | bytes 2162696 | tf_op jit(solution)/shard_map/ppermute | solution.py:773
  19.4 17.7 %collective-permute-start = (bf16[128,2816]{1,0:T(8,128)(2,1)S(1)}, bf16[128,2816]{1,0:T(8,128)(2,1)S(1)}, u32[]{:S(2)}, u32[]{:S(2)}) collective-permute-start(bf16[128,2816]{1,0:T(8,128)(2,1)S(1)} %copy-done.9), channel_id=1, source_target_pairs={{0,96},{32,0},{64,32},{96,64},{1,97},{33,1},{65,33},{97,65},{2,98}... | collective-permute-start | bytes 2162696 | tf_op jit(solution)/shard_map/ppermute | solution.py:773
  37.0 13.5 %copy-start.7 = (bf16[128,2816]{1,0:T(8,128)(2,1)}, bf16[128,2816]{1,0:T(8,128)(2,1)S(1)}, u32[]{:S(2)}) copy-start(bf16[128,2816]{1,0:T(8,128)(2,1)S(1)} %collective-permute-done.1) | copy-start | bytes 2162692
  37.0 10.3 %collective-permute-start.2 = (bf16[64,2816]{1,0:T(8,128)(2,1)S(1)}, bf16[64,2816]{1,0:T(8,128)(2,1)S(1)}, u32[]{:S(2)}, u32[]{:S(2)}) collective-permute-start(bf16[64,2816]{1,0:T(8,128)(2,1)S(1)} %slice.16), channel_id=1, source_target_pairs={{0,32},{32,64},{64,96},{96,0},{1,33},{33,65},{65,97},{97,1},{2,34}... | collective-permute-start | bytes 1081352 | tf_op jit(solution)/shard_map/ppermute | solution.py:773
  37.1 13.4 %copy-start.8 = (bf16[128,2816]{1,0:T(8,128)(2,1)}, bf16[128,2816]{1,0:T(8,128)(2,1)S(1)}, u32[]{:S(2)}) copy-start(bf16[128,2816]{1,0:T(8,128)(2,1)S(1)} %collective-permute-done) | copy-start | bytes 2162692
  37.2 10.1 %collective-permute-start.3 = (bf16[64,2816]{1,0:T(8,128)(2,1)S(1)}, bf16[64,2816]{1,0:T(8,128)(2,1)S(1)}, u32[]{:S(2)}, u32[]{:S(2)}) collective-permute-start(bf16[64,2816]{1,0:T(8,128)(2,1)S(1)} %slice.17), channel_id=1, source_target_pairs={{0,96},{32,0},{64,32},{96,64},{1,97},{33,1},{65,33},{97,65},{2,98}... | collective-permute-start | bytes 1081352 | tf_op jit(solution)/shard_map/ppermute | solution.py:773
  47.8 50.2 %collective-permute-start.5 = (bf16[256,4352]{1,0:T(8,128)(2,1)}, bf16[256,4352]{1,0:T(8,128)(2,1)}, u32[]{:S(2)}, u32[]{:S(2)}) collective-permute-start(bf16[256,4352]{1,0:T(8,128)(2,1)} %bitcast.13.refs_0_.own_ref.refs_3_), channel_id=1, source_target_pairs={{0,32},{32,64},{64,96},{96,0},{1,33},{33,65},{65,97},{97,1},{2,34}... | collective-permute-start | bytes 6684680 | tf_op jit(solution)/shard_map/ppermute | solution.py:773
  49.1 51.7 %collective-permute-start.4 = (bf16[256,4352]{1,0:T(8,128)(2,1)}, bf16[256,4352]{1,0:T(8,128)(2,1)}, u32[]{:S(2)}, u32[]{:S(2)}) collective-permute-start(bf16[256,4352]{1,0:T(8,128)(2,1)} %bitcast.13.refs_0_.own_ref.refs_3_), channel_id=1, source_target_pairs={{0,96},{32,0},{64,32},{96,64},{1,97},{33,1},{65,33},{97,65},{2,98}... | collective-permute-start | bytes 6684680 | tf_op jit(solution)/shard_map/ppermute | solution.py:773
  54.5 79.9 %all-to-all-start.1 = ((bf16[32,32,2816]{2,1,0:T(8,128)(2,1)}), bf16[32,32,2816]{2,1,0:T(8,128)(2,1)}, u32[]{:S(2)}, u32[]{:S(2)}) async-start(bf16[32,32,2816]{2,1,0:T(8,128)(2,1)} %bitcast.34), calls=%async_computation.1 | async-start | bytes 11534336 | tf_op jit(solution)/shard_map/all_to_all | solution.py:768
  100.3 25.3 %collective-permute-start.6 = (bf16[128,4352]{1,0:T(8,128)(2,1)}, bf16[128,4352]{1,0:T(8,128)(2,1)}, u32[]{:S(2)}, u32[]{:S(2)}) collective-permute-start(bf16[128,4352]{1,0:T(8,128)(2,1)} %slice.18), channel_id=1, source_target_pairs={{0,32},{32,64},{64,96},{96,0},{1,33},{33,65},{65,97},{97,1},{2,34}... | collective-permute-start | bytes 3342344 | tf_op jit(solution)/shard_map/ppermute | solution.py:773
  103.1 24.3 %collective-permute-start.7 = (bf16[128,4352]{1,0:T(8,128)(2,1)}, bf16[128,4352]{1,0:T(8,128)(2,1)}, u32[]{:S(2)}, u32[]{:S(2)}) collective-permute-start(bf16[128,4352]{1,0:T(8,128)(2,1)} %slice.19), channel_id=1, source_target_pairs={{0,96},{32,0},{64,32},{96,64},{1,97},{33,1},{65,33},{97,65},{2,98}... | collective-permute-start | bytes 3342344 | tf_op jit(solution)/shard_map/ppermute | solution.py:773
  143.2 19.4 %collective-permute-start.12 = (bf16[64,4096]{1,0:T(8,128)(2,1)}, bf16[64,4096]{1,0:T(8,128)(2,1)}, u32[]{:S(2)}, u32[]{:S(2)}) collective-permute-start(bf16[64,4096]{1,0:T(8,128)(2,1)} %get-tuple-element.79), channel_id=1, source_target_pairs={{0,32},{32,64},{64,96},{96,0},{1,33},{33,65},{65,97},{97,1},{2,34}... | collective-permute-start | bytes 1572872 | tf_op jit(solution)/shard_map/ppermute | solution.py:773
  143.4 19.1 %collective-permute-start.13 = (bf16[64,4096]{1,0:T(8,128)(2,1)}, bf16[64,4096]{1,0:T(8,128)(2,1)}, u32[]{:S(2)}, u32[]{:S(2)}) collective-permute-start(bf16[64,4096]{1,0:T(8,128)(2,1)} %get-tuple-element.80), channel_id=1, source_target_pairs={{0,96},{32,0},{64,32},{96,64},{1,97},{33,1},{65,33},{97,65},{2,98}... | collective-permute-start | bytes 1572872 | tf_op jit(solution)/shard_map/ppermute | solution.py:773
  150.5 12.0 %copy-start.6 = (bf16[4,128,256]{2,1,0:T(8,128)(2,1)S(1)}, bf16[4,128,256]{2,1,0:T(8,128)(2,1)}, u32[]{:S(2)}) copy-start(bf16[4,128,256]{2,1,0:T(8,128)(2,1)} %get-tuple-element.86.gu_ref) | copy-start | bytes 786436
  150.5 51.8 %all-to-all-start.2 = ((bf16[32,16,3072]{2,1,0:T(8,128)(2,1)}), bf16[32,16,3072]{2,1,0:T(8,128)(2,1)S(1)}, u32[]{:S(2)}, u32[]{:S(2)}) async-start(bf16[32,16,3072]{2,1,0:T(8,128)(2,1)} %bitcast.35), calls=%async_computation.2 | async-start | bytes 6291456 | tf_op jit(solution)/shard_map/all_to_all | solution.py:768
  170.8 26.0 %collective-permute-start.14 = (bf16[128,4096]{1,0:T(8,128)(2,1)}, bf16[128,4096]{1,0:T(8,128)(2,1)S(1)}, u32[]{:S(2)}, u32[]{:S(2)}) collective-permute-start(bf16[128,4096]{1,0:T(8,128)(2,1)} %get-tuple-element.93), channel_id=1, source_target_pairs={{0,32},{32,64},{64,96},{96,0},{1,33},{33,65},{65,97},{97,1},{2,34}... | collective-permute-start | bytes 3145736 | tf_op jit(solution)/shard_map/ppermute | solution.py:773
  170.9 25.9 %collective-permute-start.15 = (bf16[128,4096]{1,0:T(8,128)(2,1)S(1)}, bf16[128,4096]{1,0:T(8,128)(2,1)S(1)}, u32[]{:S(2)}, u32[]{:S(2)}) collective-permute-start(bf16[128,4096]{1,0:T(8,128)(2,1)S(1)} %get-tuple-element.94), channel_id=1, source_target_pairs={{0,96},{32,0},{64,32},{96,64},{1,97},{33,1},{65,33},{97,65},{2,98}... | collective-permute-start | bytes 3145736 | tf_op jit(solution)/shard_map/ppermute | solution.py:773
  202.3 22.4 %all-to-all-start.3 = ((bf16[32,4,4096]{2,1,0:T(4,128)(2,1)}), bf16[32,4,4096]{2,1,0:T(4,128)(2,1)}, u32[]{:S(2)}, u32[]{:S(2)}) async-start(bf16[32,4,4096]{2,1,0:T(4,128)(2,1)} %copy-done.4), calls=%async_computation.3 | async-start | bytes 2097152 | tf_op jit(solution)/shard_map/all_to_all | solution.py:768
  207.8 20.4 %copy-start.5 = (bf16[64,128]{1,0:T(8,128)(2,1)S(1)}, bf16[64,128]{1,0:T(8,128)(2,1)}, u32[]{:S(2)}) copy-start(bf16[64,128]{1,0:T(8,128)(2,1)} %get-tuple-element.51.table_ref) | copy-start | bytes 49156
  208.7 7.6 %collective-permute-start.8 = (bf16[32,3072]{1,0:T(8,128)(2,1)S(1)}, bf16[32,3072]{1,0:T(8,128)(2,1)S(1)}, u32[]{:S(2)}, u32[]{:S(2)}) collective-permute-start(bf16[32,3072]{1,0:T(8,128)(2,1)S(1)} %get-tuple-element.74), channel_id=1, source_target_pairs={{0,32},{32,64},{64,96},{96,0},{1,33},{33,65},{65,97},{97,1},{2,34}... | collective-permute-start | bytes 589832 | tf_op jit(solution)/shard_map/ppermute | solution.py:773
  208.8 7.5 %collective-permute-start.9 = (bf16[32,3072]{1,0:T(8,128)(2,1)S(1)}, bf16[32,3072]{1,0:T(8,128)(2,1)S(1)}, u32[]{:S(2)}, u32[]{:S(2)}) collective-permute-start(bf16[32,3072]{1,0:T(8,128)(2,1)S(1)} %get-tuple-element.75), channel_id=1, source_target_pairs={{0,96},{32,0},{64,32},{96,64},{1,97},{33,1},{65,33},{97,65},{2,98}... | collective-permute-start | bytes 589832 | tf_op jit(solution)/shard_map/ppermute | solution.py:773
  217.4 10.8 %collective-permute-start.10 = (bf16[64,3072]{1,0:T(8,128)(2,1)S(1)}, bf16[64,3072]{1,0:T(8,128)(2,1)S(1)}, u32[]{:S(2)}, u32[]{:S(2)}) collective-permute-start(bf16[64,3072]{1,0:T(8,128)(2,1)S(1)} %get-tuple-element.76), channel_id=1, source_target_pairs={{0,32},{32,64},{64,96},{96,0},{1,33},{33,65},{65,97},{97,1},{2,34}... | collective-permute-start | bytes 1179656 | tf_op jit(solution)/shard_map/ppermute | solution.py:773
  218.0 10.1 %collective-permute-start.11 = (bf16[64,3072]{1,0:T(8,128)(2,1)S(1)}, bf16[64,3072]{1,0:T(8,128)(2,1)S(1)}, u32[]{:S(2)}, u32[]{:S(2)}) collective-permute-start(bf16[64,3072]{1,0:T(8,128)(2,1)S(1)} %get-tuple-element.77), channel_id=1, source_target_pairs={{0,96},{32,0},{64,32},{96,64},{1,97},{33,1},{65,33},{97,65},{2,98}... | collective-permute-start | bytes 1179656 | tf_op jit(solution)/shard_map/ppermute | solution.py:773
  (8 other events, 22.4 us)

commit v9 on v8

--- a/solution.py
+++ b/solution.py
@@ -13,6 +13,7 @@
 TILE = 512
 ANY = pl.BlockSpec(memory_space=pl.ANY)
 VMEM = pl.BlockSpec(memory_space=pltpu.VMEM)
+HBM = pl.BlockSpec(memory_space=pltpu.HBM)
 
 
 def contract_rows(left, right):
@@ -267,7 +268,7 @@
         "pre",
         200 * (8 * rows * cols * ff),
         200 * (2 * cols * (rows + 4 * ff)),
-        in_specs=[ANY] * (len(blocks) + 3),
+        in_specs=[ANY] * len(blocks) + [HBM] * 3,
         out_specs=[VMEM] * 4,
         out_shape=[jax.ShapeDtypeStruct((rows // 2, ff), F32)] * 4,
         scratch_shapes=[
@@ -313,15 +314,15 @@
     cols = g.shape[1]
     wide_cols = top_ref.shape[1]
     first_col = wd_ref.shape[1] - 2 * cols
-    steps = 2
-    tile = cols // steps
+    tile = 3 * TILE // 2
+    windows = [slice(at, min(at + tile, cols)) for at in range(0, cols, tile)]
+    steps = len(windows)
     loads = []
-    for t in range(steps):
-        window = slice(t * tile, (t + 1) * tile)
+    for t, window in enumerate(windows):
         loads.append(pltpu.make_async_copy(g_ref.at[:, window], g.at[:, window], sem.at[3 * t]))
         for h in range(2):
-            start = first_col + h * cols + t * tile
-            source = wd_ref.at[:, start : start + tile]
+            start = first_col + h * cols + window.start
+            source = wd_ref.at[:, start : start + window.stop - window.start]
             target = d.at[h * ff : (h + 1) * ff, window]
             loads.append(pltpu.make_async_copy(source, target, sem.at[3 * t + 1 + h]))
     more = []
@@ -336,9 +337,8 @@
     start_all(more)
     start_all(weights)
     total = None
-    for t in range(steps):
+    for t, window in enumerate(windows):
         wait_all(loads[3 * t : 3 * t + 3])
-        window = slice(t * tile, (t + 1) * tile)
         value = contract_cols(g[:, window], d[:, window])
         total = value if total is None else total + value
     wait_all(more)
@@ -373,7 +373,7 @@
         "hidden",
         4 * rows * cols * ff + 4 * span * ff * wide_cols,
         2 * (rows * cols + 2 * wide_cols * ff + span * wide_cols),
-        in_specs=[ANY] * 13,
+        in_specs=[ANY] + [HBM] * 3 + [ANY] * 9,
         out_specs=[VMEM, VMEM, ANY, ANY],
         out_shape=[
             small(groups, span, 2 * ff),
@@ -387,7 +387,7 @@
             pltpu.VMEM((wide_cols, 2 * ff), BF),
             pltpu.VMEM((3, groups, span, ff), F32),
             pltpu.VMEM((span, wide_cols), BF),
-            pltpu.SemaphoreType.DMA((6 + 12 + 4,)),
+            pltpu.SemaphoreType.DMA((3 * pl.cdiv(cols, 3 * TILE // 2) + 12 + 4,)),
         ],
     )(g_rows, w_down, w_gate, w_up, *own, *side, *far)
 
@@ -416,7 +416,7 @@
         "ring_part",
         2 * rows * double * ring_cols,
         2 * ring_cols * (rows + double),
-        in_specs=[VMEM, ANY, ANY],
+        in_specs=[VMEM, HBM, HBM],
         out_specs=ANY,
         out_shape=jax.ShapeDtypeStruct((rows, ring_cols), BF),
         scratch_shapes=[
@@ -469,8 +469,7 @@
         "side_part",
         40 * (6 * span * double * wide_cols),
         40 * (2 * wide_cols * (4 * span + double)),
-        mib=24,
-        in_specs=[VMEM, ANY, ANY, ANY, ANY],
+        in_specs=[VMEM, HBM, HBM, ANY, ANY],
         out_specs=[ANY] * 3,
         out_shape=[jax.ShapeDtypeStruct((span, wide_cols), BF)] * 3,
         scratch_shapes=[
@@ -511,8 +510,7 @@
         "sum_blocks",
         2 * rows * cols,
         8 * rows * cols,
-        mib=24,
-        in_specs=[ANY] * 3,
+        in_specs=[HBM, ANY, ANY],
         out_specs=ANY,
         out_shape=jax.ShapeDtypeStruct((rows // CAP, CAP, cols), BF),
         scratch_shapes=[
@@ -645,18 +643,18 @@
     )(g_rows, *outers, *blocks)
 
 
-def fold_kernel(in_ref, top_ref, bottom_ref, rest_ref):
+def fold_kernel(in_ref, own_ref, top_ref, bottom_ref, side_ref):
     _, experts, depth, tile = in_ref.shape
     total = in_ref[0].astype(F32) + in_ref[1].astype(F32)
-    at = 0
     for step in range(depth // CAP):
         part = total[:, step * CAP : (step + 1) * CAP, :].reshape(experts * CAP, tile).astype(BF)
         if step == 2:
             top_ref[...] = part[: experts * CAP // 2]
             bottom_ref[...] = part[experts * CAP // 2 :]
+        elif step == 0:
+            own_ref[...] = part
         else:
-            rest_ref[at] = part
-            at += 1
+            side_ref[step // 2] = part
 
 
 def fold(home):
@@ -672,28 +670,30 @@
         grid=(width // tile,),
         in_specs=[pl.BlockSpec((2, experts, depth, tile), lambda j: (0, 0, 0, j))],
         out_specs=[
+            pl.BlockSpec((buf, tile), lambda j: (0, j)),
             pl.BlockSpec((buf // 2, tile), lambda j: (0, j)),
             pl.BlockSpec((buf // 2, tile), lambda j: (0, j)),
-            pl.BlockSpec((3, buf, tile), lambda j: (0, 0, j)),
+            pl.BlockSpec((2, buf, tile), lambda j: (0, 0, j)),
         ],
         out_shape=[
+            jax.ShapeDtypeStruct((buf, width), BF),
             jax.ShapeDtypeStruct((buf // 2, width), BF),
             jax.ShapeDtypeStruct((buf // 2, width), BF),
-            jax.ShapeDtypeStruct((3, buf, width), BF),
+            jax.ShapeDtypeStruct((2, buf, width), BF),
         ],
     )(home)
 
 
-def add_kernel(rest_ref, top_ref, bottom_ref, next_ref, prev_ref):
+def add_kernel(side_ref, top_ref, bottom_ref, next_ref, prev_ref):
     mid = top_ref.shape[0]
-    next_ref[:mid] = (rest_ref[1, :mid].astype(F32) + top_ref[...].astype(F32)).astype(BF)
-    next_ref[mid:] = rest_ref[1, mid:]
-    prev_ref[:mid] = rest_ref[2, :mid]
-    prev_ref[mid:] = (rest_ref[2, mid:].astype(F32) + bottom_ref[...].astype(F32)).astype(BF)
-
-
-def add_far(rest, top, bottom):
-    _, buf, cols = rest.shape
+    next_ref[:mid] = (side_ref[0, :mid].astype(F32) + top_ref[...].astype(F32)).astype(BF)
+    next_ref[mid:] = side_ref[0, mid:]
+    prev_ref[:mid] = side_ref[1, :mid]
+    prev_ref[mid:] = (side_ref[1, mid:].astype(F32) + bottom_ref[...].astype(F32)).astype(BF)
+
+
+def add_far(side, top, bottom):
+    _, buf, cols = side.shape
     return call(
         add_kernel,
         "add_far",
@@ -703,10 +703,10 @@
         in_specs=[VMEM] * 3,
         out_specs=[VMEM] * 2,
         out_shape=[jax.ShapeDtypeStruct((buf, cols), BF)] * 2,
-    )(rest, top, bottom)
-
-
-def combine_kernel(table_ref, rest_ref, left_ref, right_ref, wide_ref, out_ref, ring, wide, staged, sem):
+    )(side, top, bottom)
+
+
+def combine_kernel(table_ref, own_ref, left_ref, right_ref, wide_ref, out_ref, ring, wide, staged, sem):
     buf = table_ref.shape[0]
     ring_cols = ring.shape[1]
     locs, _, wide_cols = wide.shape
@@ -715,7 +715,7 @@
     def add(source, target):
         loads.append(pltpu.make_async_copy(source, target, sem.at[len(loads)]))
 
-    for k, ref in enumerate((rest_ref.at[0], left_ref, right_ref)):
+    for k, ref in enumerate((own_ref, left_ref, right_ref)):
         add(ref, ring.at[k * buf : (k + 1) * buf, :])
     for first in range(0, wide_cols, TILE):
         window = slice(first, first + TILE)
@@ -742,7 +742,7 @@
     wait_all(stores)
 
 
-def combine(table, rest, left, right, wide):
+def combine(table, own, left, right, wide):
     buf, tok = table.shape
     ring_cols, wide_cols = left.shape[1], wide.shape[2]
     width = ring_cols + wide_cols
@@ -752,7 +752,7 @@
         2 * tok * buf * width,
         2 * width * (tok + 2 * buf),
         mib=24,
-        in_specs=[VMEM, ANY, ANY, ANY, ANY],
+        in_specs=[VMEM, HBM, ANY, ANY, ANY],
         out_specs=ANY,
         out_shape=jax.ShapeDtypeStruct((tok, width), BF),
         scratch_shapes=[
@@ -761,7 +761,7 @@
             pltpu.VMEM((tok, width), BF),
             pltpu.SemaphoreType.DMA((3 + wide_cols // TILE + width // TILE,)),
         ],
-    )(table, rest, left, right, wide)
+    )(table, own, left, right, wide)
 
 
 def over_loc(a):
@@ -787,7 +787,7 @@
     buf = experts * CAP
     unit = 2 * CAP
     share = 768
-    ring_cols = 3072
+    ring_cols = 2560
     wide_cols = width - ring_cols
 
     w_gate, w_up, w_down = gate_weight[0], up_weight[0], down_weight[0]
@@ -826,11 +826,13 @@
     part_own, gate_grad, up_grad, down_grad = lax.optimization_barrier(
         (part_own, gate_grad, up_grad, down_grad)
     )
+    fold_own, fold_top, fold_bottom, fold_side = fold(
+        home_ring.reshape(2, experts, groups * CAP, ring_cols)
+    )
+    part_own, fold_top, fold_bottom = lax.optimization_barrier((part_own, fold_top, fold_bottom))
     home_wide = over_loc(sum_blocks(part_own, from_before, from_after))
-
-    fold_top, fold_bottom, rest = fold(home_ring.reshape(2, experts, groups * CAP, ring_cols))
-    fold_next, fold_prev = add_far(rest, shift(fold_top, 1), shift(fold_bottom, -1))
-    tokens_grad = combine(table, rest, shift(fold_next, 1), shift(fold_prev, -1), home_wide)
+    fold_next, fold_prev = add_far(fold_side, shift(fold_top, 1), shift(fold_bottom, -1))
+    tokens_grad = combine(table, fold_own, shift(fold_next, 1), shift(fold_prev, -1), home_wide)
     return (tokens_grad, gate_grad[None], up_grad[None], down_grad[None])
 
 

time: 235 us -> 231 us (0.983)
  local copies, waits for them, and re-layouts: 11 us -> 6.88 us
    unnamed x24 -> x22, local copies, waits for them, and re-layouts: 6.28 us -> 2.21 us
  transfers between devices with their start and end apart: 20 -> 20, of which waited for: 12 -> 11; matrix products, arithmetic and copies ran while one was open for 2% -> 2% of each run, Pallas kernels for 22% -> 22%
where the time goes in v9:
time: 231 us; the launch traced here: 230 us
  waiting for transfers between devices  89.7 us (39%)
  Pallas kernels  72.5 us (31%)
  starting transfers between devices  60 us (26%)
  local copies, waits for them, and re-layouts  6.88 us (3%)
    ppermute x16, waiting for transfers between devices, shift(): lax.ppermute(a, 'grp', [(i, (i + step) % groups) for i in range(groups)])  80.9 us
    all_to_all x4, starting transfers between devices, over_loc(): return lax.all_to_all(a, 'loc', split_axis=0, concat_axis=0, tiled=True)  37.7 us
    ppermute x16, starting transfers between devices, shift(): lax.ppermute(a, 'grp', [(i, (i + step) % groups) for i in range(groups)])  22.3 us
    pallas_call x3, Pallas kernels, pre(): call(functools.partial(pre_kernel, len(blocks)), 'pre', 200 * (8 * rows *...  14.3 us
    pallas_call x1, Pallas kernels, down(): call(down_kernel, 'down', 4 * rows * (cols + share) * ff, 2 * (cols + sha...  11.8 us
    pallas_call x1, Pallas kernels, row_grads(): call(row_grads_kernel, 'row_grads', 8 * rows * half * ff, 2 * half * (row...  9.47 us
    all_to_all x4, waiting for transfers between devices, over_loc(): return lax.all_to_all(a, 'loc', split_axis=0, concat_axis=0, tiled=True)  8.79 us
    pallas_call x1, Pallas kernels, hidden(): call(hidden_kernel, 'hidden', 4 * rows * cols * ff + 4 * span * ff * wide...  8.44 us
  transfers between devices with their start and end apart: 20, of which 11 were waited for; matrix products, arithmetic and copies ran while one was open for 2% of the time, Pallas kernels for 22%

profile of v9, /device:TPU:1, one launch (start us, length us, event | category | flops | bytes accessed | tf_op | source)
XLA Modules:
  0.0 230.2 jit_solution(3349313800561594058)
XLA Ops:
  0.6 3.5 %dispatch_gradient.1 = (bf16[64,128]{1,0:T(8,128)(2,1)}, bf16[2,128,128]{2,1,0:T(8,128)(2,1)}, bf16[128,768]{1,0:T(8,128)(2,1)}, bf16[128,2816]{1,0:T(8,128)(2,1)}) custom-call(s32[8,128]{1,0:T(8,128)} %bitcast.47, bf16[8,128]{1,0:T(8,128)(2,1)} %bitcast.48, bf16[128,7168]{1,0:T(8,128)(2,1)} %g_ref.1), custom_call_target="tpu_custom_call" | custom-call | flops 234881024 | bytes 2752512 | tf_op jit(solution)/shard_map/dispatch_gradient/pallas_call | solution.py:94
  4.1 4.3 %dispatch_token.1 = bf16[2,16,8,4352]{3,2,1,0:T(8,128)(2,1)} custom-call(bf16[2,128,128]{2,1,0:T(8,128)(2,1)} %get-tuple-element.56.pick_ref, bf16[128,768]{1,0:T(8,128)(2,1)} %get-tuple-element.57.share_ref, bf16[128,7168]{1,0:T(8,128)(2,1)} %t_ref.1), custom_call_target="tpu_custom_call" | custom-call | flops 234881024 | bytes 3670016 | tf_op jit(solution)/shard_map/dispatch_token/pallas_call | solution.py:137
  8.4 9.6 %all-to-all-start = ((bf16[32,8,4352]{2,1,0:T(8,128)(2,1)}), bf16[32,8,4352]{2,1,0:T(8,128)(2,1)}, u32[]{:S(2)}, u32[]{:S(2)}) async-start(bf16[32,8,4352]{2,1,0:T(8,128)(2,1)} %bitcast.24), calls=%async_computation | async-start | bytes 4456448 | tf_op jit(solution)/shard_map/all_to_all | solution.py:768
  21.0 16.1 %collective-permute-done.1 = bf16[128,2816]{1,0:T(8,128)(2,1)S(1)} collective-permute-done((bf16[128,2816]{1,0:T(8,128)(2,1)S(1)}, bf16[128,2816]{1,0:T(8,128)(2,1)S(1)}, u32[]{:S(2)}, u32[]{:S(2)}) %collective-permute-start.1) | collective-permute-done | bytes 720928 | tf_op jit(solution)/shard_map/ppermute | solution.py:773
  39.9 7.4 %collective-permute-done.2 = bf16[64,2816]{1,0:T(8,128)(2,1)S(1)} collective-permute-done((bf16[64,2816]{1,0:T(8,128)(2,1)S(1)}, bf16[64,2816]{1,0:T(8,128)(2,1)S(1)}, u32[]{:S(2)}, u32[]{:S(2)}) %collective-permute-start.2) | collective-permute-done | bytes 360480 | tf_op jit(solution)/shard_map/ppermute | solution.py:773
  50.6 3.9 %regroup.1 = bf16[2,16,32,2816]{3,2,1,0:T(8,128)(2,1)} custom-call(bf16[16,8,2816]{2,1,0:T(8,128)(2,1)} %bitcast.44, bf16[16,8,2816]{2,1,0:T(8,128)(2,1)} %bitcast.43, bf16[8,8,2816]{2,1,0:T(8,128)(2,1)} %bitcast.45, bf16[8,8,2816]{2,1,0:T(8,128)(2,1)} %bitcast.46, bf16[16,8,2816]{2,1,0:T(8,128)(2,1)} %bitcast.42), custom_call_target="tpu_custom_call" | custom-call | bytes 8650752 | tf_op jit(solution)/shard_map/regroup/pallas_call | solution.py:185
  54.5 8.9 %all-to-all-start.1 = ((bf16[32,32,2816]{2,1,0:T(8,128)(2,1)}), bf16[32,32,2816]{2,1,0:T(8,128)(2,1)}, u32[]{:S(2)}, u32[]{:S(2)}) async-start(bf16[32,32,2816]{2,1,0:T(8,128)(2,1)} %bitcast.22), calls=%async_computation.1 | async-start | bytes 11534336 | tf_op jit(solution)/shard_map/all_to_all | solution.py:768
  63.5 4.3 %pre.3 = (f32[128,128]{1,0:T(8,128)}, f32[128,128]{1,0:T(8,128)}, f32[128,128]{1,0:T(8,128)}, f32[128,128]{1,0:T(8,128)}) custom-call(bf16[256,4352]{1,0:T(8,128)(2,1)} %bitcast.13.refs_0_.own_ref.refs_3_, bf16[7168,128]{1,0:T(8,128)(2,1)} %bitcast.25, bf16[7168,128]{1,0:T(8,128)(2,1)} %bitcast.31, bf16[128,7168]{1,0:T(8,128)(2,1)} %bitcast.37), custom_call_target="tpu_custom_call" | custom-call | flops 228170137600 | bytes 1336934400 | tf_op jit(solution)/shard_map/pre/pallas_call | solution.py:266
  67.8 30.3 %collective-permute-done.5.refs_1_.prev_ref.refs_7_ = bf16[256,4352]{1,0:T(8,128)(2,1)} collective-permute-done((bf16[256,4352]{1,0:T(8,128)(2,1)}, bf16[256,4352]{1,0:T(8,128)(2,1)}, u32[]{:S(2)}, u32[]{:S(2)}) %collective-permute-start.5) | collective-permute-done | bytes 2228256 | tf_op jit(solution)/shard_map/ppermute | solution.py:773
  105.3 5.6 %pre.4 = (f32[256,128]{1,0:T(8,128)}, f32[256,128]{1,0:T(8,128)}, f32[256,128]{1,0:T(8,128)}, f32[256,128]{1,0:T(8,128)}) custom-call(bf16[256,4352]{1,0:T(8,128)(2,1)} %collective-permute-done.4.refs_0_.next_ref.refs_4_, bf16[256,4352]{1,0:T(8,128)(2,1)} %collective-permute-done.5.refs_1_.prev_ref.refs_7_, bf16[7168,128]{1,0:T(8,128)(2,1)} %bitcast.26, ...), custom_call_target="tpu_custom_call" | custom-call | flops 456340275200 | bytes 1782579200 | tf_op jit(solution)/shard_map/pre/pallas_call | solution.py:266
  110.9 14.7 %collective-permute-done.6.refs_0_.top_ref.refs_5_ = bf16[128,4352]{1,0:T(8,128)(2,1)} collective-permute-done((bf16[128,4352]{1,0:T(8,128)(2,1)}, bf16[128,4352]{1,0:T(8,128)(2,1)}, u32[]{:S(2)}, u32[]{:S(2)}) %collective-permute-start.6) | collective-permute-done | bytes 1114144 | tf_op jit(solution)/shard_map/ppermute | solution.py:773
  127.4 4.4 %pre.5 = (f32[128,128]{1,0:T(8,128)}, f32[128,128]{1,0:T(8,128)}, f32[128,128]{1,0:T(8,128)}, f32[128,128]{1,0:T(8,128)}) custom-call(bf16[128,4352]{1,0:T(8,128)(2,1)} %collective-permute-done.6.refs_0_.top_ref.refs_5_, bf16[128,4352]{1,0:T(8,128)(2,1)} %collective-permute-done.7.refs_1_.bottom_ref.refs_6_, bf16[7168,128]{1,0:T(8,128)(2,1)} %bitcast.27, ...), custom_call_target="tpu_custom_call" | custom-call | flops 228170137600 | bytes 1336934400 | tf_op jit(solution)/shard_map/pre/pallas_call | solution.py:266
  134.4 8.4 %hidden.1 = (bf16[4,128,256]{2,1,0:T(8,128)(2,1)}, bf16[32,16,256]{2,1,0:T(8,128)(2,1)}, bf16[64,4608]{1,0:T(8,128)(2,1)}, bf16[64,4608]{1,0:T(8,128)(2,1)}) custom-call(bf16[1024,2816]{1,0:T(8,128)(2,1)} %bitcast.9.g_ref, bf16[128,7168]{1,0:T(8,128)(2,1)} %bitcast.40, bf16[7168,128]{1,0:T(8,128)(2,1)} %bitcast.28, bf16[7168,128]{1,0:T(8,128)(2,1)} %bitcast.34, ...), custom_call_target="tpu_custom_call" | custom-call | flops 1778384896 | bytes 9306112 | tf_op jit(solution)/shard_map/hidden/pallas_call | solution.py:371
  145.8 4.1 %ring_part.1 = bf16[512,2560]{1,0:T(8,128)(2,1)} custom-call(bf16[32,16,256]{2,1,0:T(8,128)(2,1)} %get-tuple-element.74.near_ref, bf16[7168,128]{1,0:T(8,128)(2,1)} %bitcast.29, bf16[7168,128]{1,0:T(8,128)(2,1)} %bitcast.35), custom_call_target="tpu_custom_call" | custom-call | flops 671088640 | bytes 3932160 | tf_op jit(solution)/shard_map/ring_part/pallas_call | solution.py:414
  150.0 11.9 %all-to-all-start.2 = ((bf16[32,16,2560]{2,1,0:T(8,128)(2,1)}), bf16[32,16,2560]{2,1,0:T(8,128)(2,1)S(1)}, u32[]{:S(2)}, u32[]{:S(2)}) async-start(bf16[32,16,2560]{2,1,0:T(8,128)(2,1)} %bitcast.23), calls=%async_computation.2 | async-start | bytes 5242880 | tf_op jit(solution)/shard_map/all_to_all | solution.py:768
  162.7 5.3 %side_part.1 = (bf16[128,4608]{1,0:T(8,128)(2,1)}, bf16[128,4608]{1,0:T(8,128)(2,1)}, bf16[128,4608]{1,0:T(8,128)(2,1)}) custom-call(bf16[4,128,256]{2,1,0:T(8,128)(2,1)} %get-tuple-element.87.gu_ref, bf16[7168,128]{1,0:T(8,128)(2,1)} %bitcast.30, bf16[7168,128]{1,0:T(8,128)(2,1)} %bitcast.36, bf16[64,4608]{1,0:T(8,128)(2,1)} %copy-done.10, ...), custom_call_target="tpu_custom_call" | custom-call | flops 36238786560 | bytes 283115520 | tf_op jit(solution)/shard_map/side_part/pallas_call | solution.py:467
  170.7 11.8 %down.1 = bf16[128,7168]{1,0:T(8,128)(2,1)} custom-call(bf16[1024,2816]{1,0:T(8,128)(2,1)} %bitcast.9.g_ref, f32[128,128]{1,0:T(8,128)} %get-tuple-element.90.refs_0_, f32[256,128]{1,0:T(8,128)} %get-tuple-element.91.refs_1_, f32[128,128]{1,0:T(8,128)} %get-tuple-element.92.refs_2_, bf16[256,4352]{1,0:T(8,128)(2,1)} %bitcast.13.refs_0_.own_ref.refs_3_, ...), custom_call_target="tpu_custom_call" | custom-call | flops 1879048192 | bytes 9175040 | tf_op jit(solution)/shard_map/down/pallas_call | solution.py:625
  182.5 9.5 %row_grads.1 = (bf16[2,3584,128]{2,1,0:T(8,128)(2,1)}, bf16[2,3584,128]{2,1,0:T(8,128)(2,1)}) custom-call(bf16[4,128,256]{2,1,0:T(8,128)(2,1)} %get-tuple-element.87.gu_ref, bf16[256,4352]{1,0:T(8,128)(2,1)} %bitcast.13.refs_0_.own_ref.refs_3_, bf16[256,4352]{1,0:T(8,128)(2,1)} %collective-permute-done.4.refs_0_.next_ref.refs_4_, ...), custom_call_target="tpu_custom_call" | custom-call | flops 3758096384 | bytes 11010048 | tf_op jit(solution)/shard_map/row_grads/pallas_call | solution.py:556
  192.0 3.7 %all-to-all-done.2 = bf16[32,16,2560]{2,1,0:T(8,128)(2,1)S(1)} async-done(((bf16[32,16,2560]{2,1,0:T(8,128)(2,1)}), bf16[32,16,2560]{2,1,0:T(8,128)(2,1)S(1)}, u32[]{:S(2)}, u32[]{:S(2)}) %all-to-all-start.2) | async-done | bytes 2621472 | tf_op jit(solution)/shard_map/all_to_all | solution.py:768
  197.9 3.2 %sum_blocks.1 = bf16[32,4,4608]{2,1,0:T(4,128)(2,1)} custom-call(bf16[128,4608]{1,0:T(8,128)(2,1)} %get-tuple-element.100.a_ref, bf16[128,4608]{1,0:T(8,128)(2,1)} %collective-permute-done.14.b_ref, bf16[128,4608]{1,0:T(8,128)(2,1)} %collective-permute-done.15.c_ref), custom_call_target="tpu_custom_call" | custom-call | flops 1179648 | bytes 4718592 | tf_op jit(solution)/shard_map/sum_blocks/pallas_call | solution.py:508
  201.1 7.3 %all-to-all-start.3 = ((bf16[32,4,4608]{2,1,0:T(4,128)(2,1)}), bf16[32,4,4608]{2,1,0:T(4,128)(2,1)S(1)}, u32[]{:S(2)}, u32[]{:S(2)}) async-start(bf16[32,4,4608]{2,1,0:T(4,128)(2,1)} %sum_blocks.1), calls=%async_computation.3 | async-start | bytes 2359296 | tf_op jit(solution)/shard_map/all_to_all | solution.py:768
  211.2 4.0 %collective-permute-done.10.top_ref = bf16[32,2560]{1,0:T(8,128)(2,1)S(1)} collective-permute-done((bf16[32,2560]{1,0:T(8,128)(2,1)S(1)}, bf16[32,2560]{1,0:T(8,128)(2,1)S(1)}, u32[]{:S(2)}, u32[]{:S(2)}) %collective-permute-start.10) | collective-permute-done | bytes 163872 | tf_op jit(solution)/shard_map/ppermute | solution.py:773
  218.1 6.7 %collective-permute-done.12.left_ref = bf16[64,2560]{1,0:T(8,128)(2,1)S(1)} collective-permute-done((bf16[64,2560]{1,0:T(8,128)(2,1)S(1)}, bf16[64,2560]{1,0:T(8,128)(2,1)S(1)}, u32[]{:S(2)}, u32[]{:S(2)}) %collective-permute-start.12) | collective-permute-done | bytes 327712 | tf_op jit(solution)/shard_map/ppermute | solution.py:773
  226.7 3.3 %combine.1 = bf16[128,7168]{1,0:T(8,128)(2,1)} custom-call(bf16[64,128]{1,0:T(8,128)(2,1)S(1)} %copy-done.2, bf16[64,2560]{1,0:T(8,128)(2,1)S(1)} %copy-done.1, bf16[64,2560]{1,0:T(8,128)(2,1)S(1)} %collective-permute-done.12.left_ref, bf16[64,2560]{1,0:T(8,128)(2,1)S(1)} %collective-permute-done.13.right_ref, bf16[32,4,4608]{2,1,0:T(4,128)(2,1)S(1)} %all-to-all-done.3.wide_ref), custom_call_target="tpu_custom_call" | custom-call | flops 117440512 | bytes 3670016 | tf_op jit(solution)/shard_map/combine/pallas_call | solution.py:749
  (57 shorter events, 36.9 us)
Async XLA Ops:
  8.4 39.4 %all-to-all-start = ((bf16[32,8,4352]{2,1,0:T(8,128)(2,1)}), bf16[32,8,4352]{2,1,0:T(8,128)(2,1)}, u32[]{:S(2)}, u32[]{:S(2)}) async-start(bf16[32,8,4352]{2,1,0:T(8,128)(2,1)} %bitcast.24), calls=%async_computation | async-start | bytes 4456448 | tf_op jit(solution)/shard_map/all_to_all | solution.py:768
  18.1 19.0 %collective-permute-start.1 = (bf16[128,2816]{1,0:T(8,128)(2,1)S(1)}, bf16[128,2816]{1,0:T(8,128)(2,1)S(1)}, u32[]{:S(2)}, u32[]{:S(2)}) collective-permute-start(bf16[128,2816]{1,0:T(8,128)(2,1)S(1)} %copy-done.7), channel_id=1, source_target_pairs={{0,32},{32,64},{64,96},{96,0},{1,33},{33,65},{65,97},{97,1},{2,34}... | collective-permute-start | bytes 2162696 | tf_op jit(solution)/shard_map/ppermute | solution.py:773
  19.5 17.7 %collective-permute-start = (bf16[128,2816]{1,0:T(8,128)(2,1)S(1)}, bf16[128,2816]{1,0:T(8,128)(2,1)S(1)}, u32[]{:S(2)}, u32[]{:S(2)}) collective-permute-start(bf16[128,2816]{1,0:T(8,128)(2,1)S(1)} %copy-done.7), channel_id=1, source_target_pairs={{0,96},{32,0},{64,32},{96,64},{1,97},{33,1},{65,33},{97,65},{2,98}... | collective-permute-start | bytes 2162696 | tf_op jit(solution)/shard_map/ppermute | solution.py:773
  37.1 13.5 %copy-start.5 = (bf16[128,2816]{1,0:T(8,128)(2,1)}, bf16[128,2816]{1,0:T(8,128)(2,1)S(1)}, u32[]{:S(2)}) copy-start(bf16[128,2816]{1,0:T(8,128)(2,1)S(1)} %collective-permute-done.1) | copy-start | bytes 2162692
  37.1 10.3 %collective-permute-start.2 = (bf16[64,2816]{1,0:T(8,128)(2,1)S(1)}, bf16[64,2816]{1,0:T(8,128)(2,1)S(1)}, u32[]{:S(2)}, u32[]{:S(2)}) collective-permute-start(bf16[64,2816]{1,0:T(8,128)(2,1)S(1)} %slice.16), channel_id=1, source_target_pairs={{0,32},{32,64},{64,96},{96,0},{1,33},{33,65},{65,97},{97,1},{2,34}... | collective-permute-start | bytes 1081352 | tf_op jit(solution)/shard_map/ppermute | solution.py:773
  37.2 13.4 %copy-start.6 = (bf16[128,2816]{1,0:T(8,128)(2,1)}, bf16[128,2816]{1,0:T(8,128)(2,1)S(1)}, u32[]{:S(2)}) copy-start(bf16[128,2816]{1,0:T(8,128)(2,1)S(1)} %collective-permute-done) | copy-start | bytes 2162692
  37.2 10.1 %collective-permute-start.3 = (bf16[64,2816]{1,0:T(8,128)(2,1)S(1)}, bf16[64,2816]{1,0:T(8,128)(2,1)S(1)}, u32[]{:S(2)}, u32[]{:S(2)}) collective-permute-start(bf16[64,2816]{1,0:T(8,128)(2,1)S(1)} %slice.17), channel_id=1, source_target_pairs={{0,96},{32,0},{64,32},{96,64},{1,97},{33,1},{65,33},{97,65},{2,98}... | collective-permute-start | bytes 1081352 | tf_op jit(solution)/shard_map/ppermute | solution.py:773
  47.8 50.2 %collective-permute-start.5 = (bf16[256,4352]{1,0:T(8,128)(2,1)}, bf16[256,4352]{1,0:T(8,128)(2,1)}, u32[]{:S(2)}, u32[]{:S(2)}) collective-permute-start(bf16[256,4352]{1,0:T(8,128)(2,1)} %bitcast.13.refs_0_.own_ref.refs_3_), channel_id=1, source_target_pairs={{0,32},{32,64},{64,96},{96,0},{1,33},{33,65},{65,97},{97,1},{2,34}... | collective-permute-start | bytes 6684680 | tf_op jit(solution)/shard_map/ppermute | solution.py:773
  49.1 51.7 %collective-permute-start.4 = (bf16[256,4352]{1,0:T(8,128)(2,1)}, bf16[256,4352]{1,0:T(8,128)(2,1)}, u32[]{:S(2)}, u32[]{:S(2)}) collective-permute-start(bf16[256,4352]{1,0:T(8,128)(2,1)} %bitcast.13.refs_0_.own_ref.refs_3_), channel_id=1, source_target_pairs={{0,96},{32,0},{64,32},{96,64},{1,97},{33,1},{65,33},{97,65},{2,98}... | collective-permute-start | bytes 6684680 | tf_op jit(solution)/shard_map/ppermute | solution.py:773
  54.5 79.9 %all-to-all-start.1 = ((bf16[32,32,2816]{2,1,0:T(8,128)(2,1)}), bf16[32,32,2816]{2,1,0:T(8,128)(2,1)}, u32[]{:S(2)}, u32[]{:S(2)}) async-start(bf16[32,32,2816]{2,1,0:T(8,128)(2,1)} %bitcast.22), calls=%async_computation.1 | async-start | bytes 11534336 | tf_op jit(solution)/shard_map/all_to_all | solution.py:768
  100.3 25.3 %collective-permute-start.6 = (bf16[128,4352]{1,0:T(8,128)(2,1)}, bf16[128,4352]{1,0:T(8,128)(2,1)}, u32[]{:S(2)}, u32[]{:S(2)}) collective-permute-start(bf16[128,4352]{1,0:T(8,128)(2,1)} %slice.18), channel_id=1, source_target_pairs={{0,32},{32,64},{64,96},{96,0},{1,33},{33,65},{65,97},{97,1},{2,34}... | collective-permute-start | bytes 3342344 | tf_op jit(solution)/shard_map/ppermute | solution.py:773
  103.1 24.3 %collective-permute-start.7 = (bf16[128,4352]{1,0:T(8,128)(2,1)}, bf16[128,4352]{1,0:T(8,128)(2,1)}, u32[]{:S(2)}, u32[]{:S(2)}) collective-permute-start(bf16[128,4352]{1,0:T(8,128)(2,1)} %slice.19), channel_id=1, source_target_pairs={{0,96},{32,0},{64,32},{96,64},{1,97},{33,1},{65,33},{97,65},{2,98}... | collective-permute-start | bytes 3342344 | tf_op jit(solution)/shard_map/ppermute | solution.py:773
  142.9 18.9 %collective-permute-start.8 = (bf16[64,4608]{1,0:T(8,128)(2,1)}, bf16[64,4608]{1,0:T(8,128)(2,1)S(1)}, u32[]{:S(2)}, u32[]{:S(2)}) collective-permute-start(bf16[64,4608]{1,0:T(8,128)(2,1)} %get-tuple-element.80), channel_id=1, source_target_pairs={{0,32},{32,64},{64,96},{96,0},{1,33},{33,65},{65,97},{97,1},{2,34}... | collective-permute-start | bytes 1769480 | tf_op jit(solution)/shard_map/ppermute | solution.py:773
  143.1 18.7 %collective-permute-start.9 = (bf16[64,4608]{1,0:T(8,128)(2,1)}, bf16[64,4608]{1,0:T(8,128)(2,1)}, u32[]{:S(2)}, u32[]{:S(2)}) collective-permute-start(bf16[64,4608]{1,0:T(8,128)(2,1)} %get-tuple-element.81), channel_id=1, source_target_pairs={{0,96},{32,0},{64,32},{96,64},{1,97},{33,1},{65,33},{97,65},{2,98}... | collective-permute-start | bytes 1769480 | tf_op jit(solution)/shard_map/ppermute | solution.py:773
  150.0 45.8 %all-to-all-start.2 = ((bf16[32,16,2560]{2,1,0:T(8,128)(2,1)}), bf16[32,16,2560]{2,1,0:T(8,128)(2,1)S(1)}, u32[]{:S(2)}, u32[]{:S(2)}) async-start(bf16[32,16,2560]{2,1,0:T(8,128)(2,1)} %bitcast.23), calls=%async_computation.2 | async-start | bytes 5242880 | tf_op jit(solution)/shard_map/all_to_all | solution.py:768
  167.9 30.0 %collective-permute-start.14 = (bf16[128,4608]{1,0:T(8,128)(2,1)}, bf16[128,4608]{1,0:T(8,128)(2,1)}, u32[]{:S(2)}, u32[]{:S(2)}) collective-permute-start(bf16[128,4608]{1,0:T(8,128)(2,1)} %get-tuple-element.101), channel_id=1, source_target_pairs={{0,32},{32,64},{64,96},{96,0},{1,33},{33,65},{65,97},{97,1},{2,34}... | collective-permute-start | bytes 3538952 | tf_op jit(solution)/shard_map/ppermute | solution.py:773
  168.0 29.9 %collective-permute-start.15 = (bf16[128,4608]{1,0:T(8,128)(2,1)}, bf16[128,4608]{1,0:T(8,128)(2,1)}, u32[]{:S(2)}, u32[]{:S(2)}) collective-permute-start(bf16[128,4608]{1,0:T(8,128)(2,1)} %get-tuple-element.102), channel_id=1, source_target_pairs={{0,96},{32,0},{64,32},{96,64},{1,97},{33,1},{65,33},{97,65},{2,98}... | collective-permute-start | bytes 3538952 | tf_op jit(solution)/shard_map/ppermute | solution.py:773
  201.1 25.7 %copy-start.1 = (bf16[64,2560]{1,0:T(8,128)(2,1)S(1)}, bf16[64,2560]{1,0:T(8,128)(2,1)}, u32[]{:S(2)}) copy-start(bf16[64,2560]{1,0:T(8,128)(2,1)} %copy-done) | copy-start | bytes 983044
  201.1 25.7 %copy-start.2 = (bf16[64,128]{1,0:T(8,128)(2,1)S(1)}, bf16[64,128]{1,0:T(8,128)(2,1)}, u32[]{:S(2)}) copy-start(bf16[64,128]{1,0:T(8,128)(2,1)} %get-tuple-element.55.table_ref) | copy-start | bytes 49156
  201.1 25.6 %all-to-all-start.3 = ((bf16[32,4,4608]{2,1,0:T(4,128)(2,1)}), bf16[32,4,4608]{2,1,0:T(4,128)(2,1)S(1)}, u32[]{:S(2)}, u32[]{:S(2)}) async-start(bf16[32,4,4608]{2,1,0:T(4,128)(2,1)} %sum_blocks.1), calls=%async_computation.3 | async-start | bytes 2359296 | tf_op jit(solution)/shard_map/all_to_all | solution.py:768
  208.4 6.8 %collective-permute-start.10 = (bf16[32,2560]{1,0:T(8,128)(2,1)S(1)}, bf16[32,2560]{1,0:T(8,128)(2,1)S(1)}, u32[]{:S(2)}, u32[]{:S(2)}) collective-permute-start(bf16[32,2560]{1,0:T(8,128)(2,1)S(1)} %copy-done.4), channel_id=1, source_target_pairs={{0,32},{32,64},{64,96},{96,0},{1,33},{33,65},{65,97},{97,1},{2,34}... | collective-permute-start | bytes 491528 | tf_op jit(solution)/shard_map/ppermute | solution.py:773
  208.5 6.8 %collective-permute-start.11 = (bf16[32,2560]{1,0:T(8,128)(2,1)S(1)}, bf16[32,2560]{1,0:T(8,128)(2,1)S(1)}, u32[]{:S(2)}, u32[]{:S(2)}) collective-permute-start(bf16[32,2560]{1,0:T(8,128)(2,1)S(1)} %get-tuple-element.97), channel_id=1, source_target_pairs={{0,96},{32,0},{64,32},{96,64},{1,97},{33,1},{65,33},{97,65},{2,98}... | collective-permute-start | bytes 491528 | tf_op jit(solution)/shard_map/ppermute | solution.py:773
  215.3 9.4 %collective-permute-start.12 = (bf16[64,2560]{1,0:T(8,128)(2,1)S(1)}, bf16[64,2560]{1,0:T(8,128)(2,1)S(1)}, u32[]{:S(2)}, u32[]{:S(2)}) collective-permute-start(bf16[64,2560]{1,0:T(8,128)(2,1)S(1)} %get-tuple-element.98), channel_id=1, source_target_pairs={{0,32},{32,64},{64,96},{96,0},{1,33},{33,65},{65,97},{97,1},{2,34}... | collective-permute-start | bytes 983048 | tf_op jit(solution)/shard_map/ppermute | solution.py:773
  216.2 8.5 %collective-permute-start.13 = (bf16[64,2560]{1,0:T(8,128)(2,1)S(1)}, bf16[64,2560]{1,0:T(8,128)(2,1)S(1)}, u32[]{:S(2)}, u32[]{:S(2)}) collective-permute-start(bf16[64,2560]{1,0:T(8,128)(2,1)S(1)} %get-tuple-element.99), channel_id=1, source_target_pairs={{0,96},{32,0},{64,32},{96,64},{1,97},{33,1},{65,33},{97,65},{2,98}... | collective-permute-start | bytes 983048 | tf_op jit(solution)/shard_map/ppermute | solution.py:773
  (7 other events, 25.7 us)

commit v10 on v9

--- a/solution.py
+++ b/solution.py
@@ -38,14 +38,18 @@
     )
 
 
-def dispatch_gradient_kernel(ids_ref, w_ref, g_ref, table_ref, pick_ref, share_ref, ring_ref, held, sem):
+def dispatch_kernel(ids_ref, w_ref, g_ref, t_ref, table_ref, ring_ref, out_ref, held, tokens, staged, sem):
     load = pltpu.make_async_copy(g_ref, held, sem.at[0])
     load.start()
+    load_tokens = pltpu.make_async_copy(t_ref, tokens, sem.at[1])
+    load_tokens.start()
     topk, tok = ids_ref.shape
     buf = table_ref.shape[0]
     unit = 2 * CAP
-    share = share_ref.shape[1]
+    experts = out_ref.shape[1]
     cols = ring_ref.shape[1]
+    half = tokens.shape[1] // 2
+    share = half - cols
 
     def tables(count, per_expert):
         slot_row = lax.broadcasted_iota(jnp.int32, (count, tok), 0)
@@ -67,87 +71,61 @@
     table_ref[...] = tables(buf, CAP)[0].astype(BF)
     table, weighted, slot_row = tables(2 * buf, unit)
     low = lax.rem(slot_row, unit) < CAP
-    pick_ref[0] = jnp.where(low, table, 0.0).astype(BF)
-    pick_ref[1] = jnp.where(low, 0.0, table).astype(BF)
+    pick = jnp.concatenate(
+        [jnp.where(low, table, 0.0).astype(BF), jnp.where(low, 0.0, table).astype(BF)], axis=1
+    )
     both = jnp.concatenate(
         [jnp.where(low, weighted, 0.0).astype(BF), jnp.where(low, 0.0, weighted).astype(BF)], axis=1
     )
     load.wait()
 
-    def rows(first, second, count):
+    def rows(left, source, first, second, count):
         parts = jnp.concatenate(
-            [held[:, first : first + count], held[:, second : second + count]], axis=0
+            [source[:, first : first + count], source[:, second : second + count]], axis=0
         )
-        return jnp.dot(both, parts, preferred_element_type=F32).astype(BF)
-
-    share_ref[...] = rows(0, share, share)
+        return jnp.dot(left, parts, preferred_element_type=F32).astype(BF)
+
+    staged[:, :, half:] = rows(both, held, 0, share, share).reshape(experts, unit, share)
     part = TILE // 2
     for first in range(0, cols, part):
         start = 2 * share + first
-        ring_ref[:, first : first + part] = rows(start, start + cols, part)
-
-
-def dispatch_gradient(ids, weights, grad_out, experts, share):
-    tok, width = grad_out.shape
-    buf = experts * CAP
-    small = lambda *shape: jax.ShapeDtypeStruct(shape, BF)
-    return call(
-        dispatch_gradient_kernel,
-        "dispatch_gradient",
-        4 * tok * buf * width,
-        2 * width * (tok + buf),
-        in_specs=[VMEM, VMEM, ANY],
-        out_specs=[VMEM] * 4,
-        out_shape=[
-            small(buf, tok),
-            small(2, 2 * buf, tok),
-            small(2 * buf, share),
-            small(2 * buf, width // 2 - share),
-        ],
-        scratch_shapes=[pltpu.VMEM((tok, width), BF), pltpu.SemaphoreType.DMA((1,))],
-    )(ids, weights, grad_out)
-
-
-def dispatch_token_kernel(pick_ref, share_ref, t_ref, out_ref, held, staged, sem):
-    load = pltpu.make_async_copy(t_ref, held, sem.at[0])
-    load.start()
-    _, experts, unit, cols = out_ref.shape
-    share = share_ref.shape[1]
-    half = cols - share
-    both = jnp.concatenate([pick_ref[0], pick_ref[1]], axis=1)
-    staged[:, :, half:] = share_ref[...].reshape(experts, unit, share)
-    load.wait()
+        ring_ref[:, first : first + part] = rows(both, held, start, start + cols, part)
+    load_tokens.wait()
     for first in range(0, half, TILE):
-        parts = jnp.concatenate(
-            [held[:, first : first + TILE], held[:, half + first : half + first + TILE]], axis=0
-        )
-        rows = jnp.dot(both, parts, preferred_element_type=F32).astype(BF)
-        staged[:, :, first : first + TILE] = rows.reshape(experts, unit, TILE)
-    stores = [pltpu.make_async_copy(staged, out_ref.at[h], sem.at[1 + h]) for h in range(2)]
+        value = rows(pick, tokens, first, half + first, TILE)
+        staged[:, :, first : first + TILE] = value.reshape(experts, unit, TILE)
+    stores = [pltpu.make_async_copy(staged, out_ref.at[h], sem.at[2 + h]) for h in range(2)]
     for store in stores:
         store.start()
     for store in stores:
         store.wait()
 
 
-def dispatch_token(pick, share, tokens, experts):
-    tok, width = tokens.shape
+def dispatch(ids, weights, grad_out, tokens, experts, share):
+    tok, width = grad_out.shape
+    buf = experts * CAP
     unit = 2 * CAP
-    cols = width // 2 + share.shape[1]
-    return call(
-        dispatch_token_kernel,
-        "dispatch_token",
-        4 * tok * experts * CAP * width,
-        2 * width * (tok + 2 * experts * CAP),
-        in_specs=[VMEM, VMEM, ANY],
-        out_specs=ANY,
-        out_shape=jax.ShapeDtypeStruct((2, experts, unit, cols), BF),
+    half = width // 2
+    small = lambda *shape: jax.ShapeDtypeStruct(shape, BF)
+    return call(
+        dispatch_kernel,
+        "dispatch",
+        8 * tok * buf * width,
+        2 * width * (2 * tok + 3 * buf),
+        in_specs=[VMEM, VMEM, ANY, ANY],
+        out_specs=[VMEM, VMEM, ANY],
+        out_shape=[
+            small(buf, tok),
+            small(2 * buf, half - share),
+            small(2, experts, unit, half + share),
+        ],
         scratch_shapes=[
             pltpu.VMEM((tok, width), BF),
-            pltpu.VMEM((experts, unit, cols), BF),
-            pltpu.SemaphoreType.DMA((3,)),
-        ],
-    )(pick, share, tokens)
+            pltpu.VMEM((tok, width), BF),
+            pltpu.VMEM((experts, unit, half + share), BF),
+            pltpu.SemaphoreType.DMA((4,)),
+        ],
+    )(ids, weights, grad_out, tokens)
 
 
 def regroup_kernel(own_ref, next_ref, top_ref, bottom_ref, prev_ref, out_ref, held, sem):
@@ -197,10 +175,8 @@
     )(*[b.reshape(b.shape[0] // unit, unit, cols) for b in blocks])
 
 
-def pre_kernel(count, *refs):
-    x_refs = refs[:count]
-    wg_ref, wu_ref, wd_ref, slope_ref, swish_ref, part_ref, outer_ref, x, w, d, acc, sem = refs[count:]
-    rows, cols = x.shape
+def pre_copies(x_refs, wg_ref, wu_ref, wd_ref, x, w, d, sem):
+    cols = x.shape[1]
     ff = w.shape[2] // 4
     share = d.shape[1]
     half = cols - share
@@ -229,40 +205,61 @@
             for h in range(2):
                 source = wd_ref.at[:, h * share : (h + 1) * share]
                 add(t, source, d.at[h * ff : (h + 1) * ff, :])
-    for group in copies:
-        for copy in group:
-            copy.start()
+    return copies
+
+
+def pre_values(copies, x, w, d, acc):
+    rows, cols = x.shape
+    ff = w.shape[2] // 4
+    half = cols - d.shape[1]
+    steps = half // TILE
     for t in range(steps):
-        for copy in copies[t]:
-            copy.wait()
+        wait_all(copies[t])
         value = jnp.dot(x[:, t * TILE : (t + 1) * TILE], w[t], preferred_element_type=F32)
         if t == 0:
             acc[...] = value
         else:
             acc[...] += value
-    for copy in copies[steps]:
-        copy.wait()
+    wait_all(copies[steps])
 
     def fold_halves(value):
         value = value.reshape(rows // (2 * CAP), 2 * CAP, 2 * ff)
         return (value[:, :CAP, :ff] + value[:, CAP:, ff:]).reshape(rows // 2, ff)
 
-    part_ref[...] = fold_halves(contract_cols(x[:, half:], d[...]))
+    part = fold_halves(contract_cols(x[:, half:], d[...]))
     gate = fold_halves(acc[:, : 2 * ff])
     up = fold_halves(acc[:, 2 * ff :])
     sig = 1.0 / (1.0 + jnp.exp(-gate))
     swish = gate * sig
-    slope_ref[...] = up * sig * (1.0 + gate * (1.0 - sig))
-    swish_ref[...] = swish
-    outer_ref[...] = swish * up
+    return up * sig * (1.0 + gate * (1.0 - sig)), swish, part, swish * up
+
+
+def pre_kernel(count, *refs):
+    wg_ref, wu_ref, wd_ref = refs[count : count + 3]
+    out_refs = refs[count + 3 : count + 7]
+    x, w, d, acc, sem = refs[count + 7 :]
+    copies = pre_copies(refs[:count], wg_ref, wu_ref, wd_ref, x, w, d, sem)
+    for group in copies:
+        start_all(group)
+    for ref, value in zip(out_refs, pre_values(copies, x, w, d, acc)):
+        ref[...] = value
+
+
+def pre_scratch(rows, cols, share, ff, blocks):
+    steps = (cols - share) // TILE
+    return [
+        pltpu.VMEM((rows, cols), BF),
+        pltpu.VMEM((steps, TILE, 4 * ff), BF),
+        pltpu.VMEM((2 * ff, share), BF),
+        pltpu.VMEM((rows, 4 * ff), F32),
+        pltpu.SemaphoreType.DMA(((blocks + 4) * steps + blocks + 2,)),
+    ]
 
 
 def pre(blocks, w_gate, w_up, w_down, share):
     cols = blocks[0].shape[1]
     rows = sum(b.shape[0] for b in blocks)
     ff = w_gate.shape[1]
-    steps = (cols - share) // TILE
-    copies = (len(blocks) + 4) * steps + len(blocks) + 2
     return call(
         functools.partial(pre_kernel, len(blocks)),
         "pre",
@@ -271,13 +268,7 @@
         in_specs=[ANY] * len(blocks) + [HBM] * 3,
         out_specs=[VMEM] * 4,
         out_shape=[jax.ShapeDtypeStruct((rows // 2, ff), F32)] * 4,
-        scratch_shapes=[
-            pltpu.VMEM((rows, cols), BF),
-            pltpu.VMEM((steps, TILE, 4 * ff), BF),
-            pltpu.VMEM((2 * ff, share), BF),
-            pltpu.VMEM((rows, 4 * ff), F32),
-            pltpu.SemaphoreType.DMA((copies,)),
-        ],
+        scratch_shapes=pre_scratch(rows, cols, share, ff, len(blocks)),
     )(*blocks, w_gate, w_up, w_down)
 
 
@@ -305,8 +296,9 @@
 def hidden_kernel(
     g_ref, wd_ref, wg_ref, wu_ref, *refs
 ):
-    own, side, far = refs[0:3], refs[3:6], refs[6:9]
-    gu_ref, near_ref, top_ref, bottom_ref, g, d, w, small, staged, sem = refs[9:]
+    own, side, far_rows = refs[0:3], refs[3:6], refs[6:8]
+    gu_ref, near_ref, top_ref, bottom_ref, outer_ref, g, d, w, small, staged, sem = refs[8:19]
+    far_x, far_w, far_d, far_acc, far_sem = refs[19:]
     groups, span, double = gu_ref.shape
     ff = double // 2
     locs = span // CAP
@@ -328,14 +320,18 @@
     more = []
     index = 3 * steps
     for k in range(3):
-        places = [(own[k], 0), (side[k].at[:span], 1), (far[k], 2), (side[k].at[span:], 3)]
+        places = [(own[k], 0), (side[k].at[:span], 1), (side[k].at[span:], 3)]
         for source, group in places:
             more.append(pltpu.make_async_copy(source, small.at[k, group], sem.at[index]))
             index += 1
     weights = load_weights(wg_ref, wu_ref, w, wg_ref.shape[0] - wide_cols, sem, index)
+    far_copies = pre_copies(far_rows, wg_ref, wu_ref, wd_ref, far_x, far_w, far_d, far_sem)
+    for group in far_copies:
+        start_all(group)
     start_all(loads)
     start_all(more)
     start_all(weights)
+    slope, swish, part, outer_ref[...] = pre_values(far_copies, far_x, far_w, far_d, far_acc)
     total = None
     for t, window in enumerate(windows):
         wait_all(loads[3 * t : 3 * t + 3])
@@ -347,9 +343,9 @@
         first = group * unit
         hidden = (
             halves[:, first : first + CAP, :ff] + halves[:, first + CAP : first + unit, ff:]
-        ).reshape(span, ff) + small[2, group]
-        gate = hidden * small[0, group]
-        up = hidden * small[1, group]
+        ).reshape(span, ff) + (part if group == 2 else small[2, group])
+        gate = hidden * (slope if group == 2 else small[0, group])
+        up = hidden * (swish if group == 2 else small[1, group])
         both = jnp.concatenate([gate, up], axis=1)
         gu_ref[group] = both.astype(BF)
         near_ref[:, group * CAP : (group + 1) * CAP, :] = both.reshape(locs, CAP, double).astype(BF)
@@ -363,7 +359,7 @@
     wait_all(stores)
 
 
-def hidden(g_rows, w_down, w_gate, w_up, own, side, far, wide_cols):
+def hidden(g_rows, w_down, w_gate, w_up, own, side, far, share, wide_cols):
     rows, cols = g_rows.shape
     span, ff = own[0].shape
     groups = rows // 2 // span
@@ -373,13 +369,14 @@
         "hidden",
         4 * rows * cols * ff + 4 * span * ff * wide_cols,
         2 * (rows * cols + 2 * wide_cols * ff + span * wide_cols),
-        in_specs=[ANY] + [HBM] * 3 + [ANY] * 9,
-        out_specs=[VMEM, VMEM, ANY, ANY],
+        in_specs=[ANY] + [HBM] * 3 + [ANY] * 8,
+        out_specs=[VMEM, VMEM, ANY, ANY, VMEM],
         out_shape=[
             small(groups, span, 2 * ff),
             small(span // CAP, groups * CAP, 2 * ff),
             small(span // 2, wide_cols),
             small(span // 2, wide_cols),
+            jax.ShapeDtypeStruct((span, ff), F32),
         ],
         scratch_shapes=[
             pltpu.VMEM((rows, cols), BF),
@@ -387,7 +384,8 @@
             pltpu.VMEM((wide_cols, 2 * ff), BF),
             pltpu.VMEM((3, groups, span, ff), F32),
             pltpu.VMEM((span, wide_cols), BF),
-            pltpu.SemaphoreType.DMA((3 * pl.cdiv(cols, 3 * TILE // 2) + 12 + 4,)),
+            pltpu.SemaphoreType.DMA((3 * pl.cdiv(cols, 3 * TILE // 2) + 9 + 4,)),
+            *pre_scratch(2 * span, far[0].shape[1], share, ff, 2),
         ],
     )(g_rows, w_down, w_gate, w_up, *own, *side, *far)
 
@@ -792,11 +790,10 @@
 
     w_gate, w_up, w_down = gate_weight[0], up_weight[0], down_weight[0]
 
-    table, pick, g_share, g_send = dispatch_gradient(
-        expert_ids.T, route_weight.T, grad_out, experts, share
+    table, g_send, xg_send = dispatch(
+        expert_ids.T, route_weight.T, grad_out, tokens, experts, share
     )
     g_blocks = ring_gather(g_send)
-    xg_send = dispatch_token(pick, g_share, tokens, experts)
     xg = over_loc(xg_send.reshape(locs, unit, xg_send.shape[3]))
     xg, *g_blocks = lax.optimization_barrier((xg, *g_blocks))
     blocks = ring_gather(xg.reshape(locs * unit, xg.shape[2]))
@@ -807,9 +804,8 @@
     own, after, top, bottom, before = blocks
     *pre_own, outer_own = pre([own], w_gate, w_up, w_down, share)
     *pre_side, outer_side = pre([after, before], w_gate, w_up, w_down, share)
-    *pre_far, outer_far = pre([top, bottom], w_gate, w_up, w_down, share)
-    gu, near, far_top, far_bottom = hidden(
-        g_rows, w_down, w_gate, w_up, pre_own, pre_side, pre_far, wide_cols
+    gu, near, far_top, far_bottom, outer_far = hidden(
+        g_rows, w_down, w_gate, w_up, pre_own, pre_side, [top, bottom], share, wide_cols
     )
 
     came_top, came_bottom = shift(far_top, 1), shift(far_bottom, -1)

time: 231 us -> 233 us (level)
  waiting for transfers between devices: 89.7 us -> 94.2 us
  Pallas kernels: 72.5 us -> 69.9 us
    pallas_call x3 -> x2, Pallas kernels: 14.3 us -> 9.91 us  [pre(): call(functools.partial(pre_kernel, len(blocks)), 'pre', 200 * (8 * rows *...]
    all_to_all x4, waiting for transfers between devices: 8.79 us -> 13.2 us  [over_loc(): return lax.all_to_all(a, 'loc', split_axis=0, concat_axis=0, tiled=True)]
    pallas_call x1, Pallas kernels: 8.44 us -> 12.6 us  [hidden(): call(hidden_kernel, 'hidden', 4 * rows * cols * ff + 4 * span * ff * wide...]
    pallas_call x2 -> x1, Pallas kernels: 7.79 us -> 5.45 us  [dispatch(): call(dispatch_kernel, 'dispatch', 8 * tok * buf * width, 2 * width * (2 *...]
  transfers between devices with their start and end apart: 20 -> 20, of which waited for: 11 -> 11; matrix products, arithmetic and copies ran while one was open for 2% -> 2% of each run, Pallas kernels for 22% -> 20%
where the time goes in v10:
time: 233 us; the launch traced here: 232 us
  waiting for transfers between devices  94.2 us (40%)
  Pallas kernels  69.9 us (30%)
  starting transfers between devices  60 us (26%)
  local copies, waits for them, and re-layouts  6.88 us (3%)
    ppermute x16, waiting for transfers between devices, shift(): lax.ppermute(a, 'grp', [(i, (i + step) % groups) for i in range(groups)])  80.9 us
    all_to_all x4, starting transfers between devices, over_loc(): return lax.all_to_all(a, 'loc', split_axis=0, concat_axis=0, tiled=True)  37.6 us
    ppermute x16, starting transfers between devices, shift(): lax.ppermute(a, 'grp', [(i, (i + step) % groups) for i in range(groups)])  22.3 us
    all_to_all x4, waiting for transfers between devices, over_loc(): return lax.all_to_all(a, 'loc', split_axis=0, concat_axis=0, tiled=True)  13.2 us
    pallas_call x1, Pallas kernels, hidden(): call(hidden_kernel, 'hidden', 4 * rows * cols * ff + 4 * span * ff * wide...  12.6 us
    pallas_call x1, Pallas kernels, down(): call(down_kernel, 'down', 4 * rows * (cols + share) * ff, 2 * (cols + sha...  11.8 us
    pallas_call x2, Pallas kernels, pre(): call(functools.partial(pre_kernel, len(blocks)), 'pre', 200 * (8 * rows *...  9.91 us
    pallas_call x1, Pallas kernels, row_grads(): call(row_grads_kernel, 'row_grads', 8 * rows * half * ff, 2 * half * (row...  9.47 us
  transfers between devices with their start and end apart: 20, of which 11 were waited for; matrix products, arithmetic and copies ran while one was open for 2% of the time, Pallas kernels for 20%

profile of v10, /device:TPU:1, one launch (start us, length us, event | category | flops | bytes accessed | tf_op | source)
XLA Modules:
  0.0 231.9 jit_solution(16265781529005946348)
XLA Ops:
  0.6 5.4 %dispatch.1 = (bf16[64,128]{1,0:T(8,128)(2,1)}, bf16[128,2816]{1,0:T(8,128)(2,1)}, bf16[2,16,8,4352]{3,2,1,0:T(8,128)(2,1)}) custom-call(s32[8,128]{1,0:T(8,128)} %bitcast.44, bf16[8,128]{1,0:T(8,128)(2,1)} %bitcast.45, bf16[128,7168]{1,0:T(8,128)(2,1)} %g_ref.1, bf16[128,7168]{1,0:T(8,128)(2,1)} %t_ref.1), custom_call_target="tpu_custom_call" | custom-call | flops 469762048 | bytes 6422528 | tf_op jit(solution)/shard_map/dispatch/pallas_call | solution.py:110
  6.1 9.6 %all-to-all-start = ((bf16[32,8,4352]{2,1,0:T(8,128)(2,1)}), bf16[32,8,4352]{2,1,0:T(8,128)(2,1)}, u32[]{:S(2)}, u32[]{:S(2)}) async-start(bf16[32,8,4352]{2,1,0:T(8,128)(2,1)} %bitcast.34), calls=%async_computation | async-start | bytes 4456448 | tf_op jit(solution)/shard_map/all_to_all | solution.py:766
  18.6 16.1 %collective-permute-done.1 = bf16[128,2816]{1,0:T(8,128)(2,1)S(1)} collective-permute-done((bf16[128,2816]{1,0:T(8,128)(2,1)S(1)}, bf16[128,2816]{1,0:T(8,128)(2,1)S(1)}, u32[]{:S(2)}, u32[]{:S(2)}) %collective-permute-start.1) | collective-permute-done | bytes 720928 | tf_op jit(solution)/shard_map/ppermute | solution.py:771
  37.6 7.4 %collective-permute-done.2 = bf16[64,2816]{1,0:T(8,128)(2,1)S(1)} collective-permute-done((bf16[64,2816]{1,0:T(8,128)(2,1)S(1)}, bf16[64,2816]{1,0:T(8,128)(2,1)S(1)}, u32[]{:S(2)}, u32[]{:S(2)}) %collective-permute-start.2) | collective-permute-done | bytes 360480 | tf_op jit(solution)/shard_map/ppermute | solution.py:771
  48.2 3.9 %regroup.1 = bf16[2,16,32,2816]{3,2,1,0:T(8,128)(2,1)} custom-call(bf16[16,8,2816]{2,1,0:T(8,128)(2,1)} %bitcast.41, bf16[16,8,2816]{2,1,0:T(8,128)(2,1)} %bitcast.40, bf16[8,8,2816]{2,1,0:T(8,128)(2,1)} %bitcast.42, bf16[8,8,2816]{2,1,0:T(8,128)(2,1)} %bitcast.43, bf16[16,8,2816]{2,1,0:T(8,128)(2,1)} %bitcast.39), custom_call_target="tpu_custom_call" | custom-call | bytes 8650752 | tf_op jit(solution)/shard_map/regroup/pallas_call | solution.py:163
  52.2 8.9 %all-to-all-start.1 = ((bf16[32,32,2816]{2,1,0:T(8,128)(2,1)}), bf16[32,32,2816]{2,1,0:T(8,128)(2,1)}, u32[]{:S(2)}, u32[]{:S(2)}) async-start(bf16[32,32,2816]{2,1,0:T(8,128)(2,1)} %bitcast.22), calls=%async_computation.1 | async-start | bytes 11534336 | tf_op jit(solution)/shard_map/all_to_all | solution.py:766
  61.1 4.3 %pre.2 = (f32[128,128]{1,0:T(8,128)}, f32[128,128]{1,0:T(8,128)}, f32[128,128]{1,0:T(8,128)}, f32[128,128]{1,0:T(8,128)}) custom-call(bf16[256,4352]{1,0:T(8,128)(2,1)} %bitcast.13.refs_0_.own_ref.refs_3_, bf16[7168,128]{1,0:T(8,128)(2,1)} %bitcast.24, bf16[7168,128]{1,0:T(8,128)(2,1)} %bitcast.29, bf16[128,7168]{1,0:T(8,128)(2,1)} %bitcast.35), custom_call_target="tpu_custom_call" | custom-call | flops 228170137600 | bytes 1336934400 | tf_op jit(solution)/shard_map/pre/pallas_call | solution.py:263
  65.4 30.3 %collective-permute-done.5.refs_1_.prev_ref.refs_7_ = bf16[256,4352]{1,0:T(8,128)(2,1)} collective-permute-done((bf16[256,4352]{1,0:T(8,128)(2,1)}, bf16[256,4352]{1,0:T(8,128)(2,1)}, u32[]{:S(2)}, u32[]{:S(2)}) %collective-permute-start.5) | collective-permute-done | bytes 2228256 | tf_op jit(solution)/shard_map/ppermute | solution.py:771
  103.0 5.6 %pre.3 = (f32[256,128]{1,0:T(8,128)}, f32[256,128]{1,0:T(8,128)}, f32[256,128]{1,0:T(8,128)}, f32[256,128]{1,0:T(8,128)}) custom-call(bf16[256,4352]{1,0:T(8,128)(2,1)} %collective-permute-done.4.refs_0_.next_ref.refs_4_, bf16[256,4352]{1,0:T(8,128)(2,1)} %collective-permute-done.5.refs_1_.prev_ref.refs_7_, bf16[7168,128]{1,0:T(8,128)(2,1)} %bitcast.25, ...), custom_call_target="tpu_custom_call" | custom-call | flops 456340275200 | bytes 1782579200 | tf_op jit(solution)/shard_map/pre/pallas_call | solution.py:263
  108.6 14.7 %collective-permute-done.6.refs_6_.top_ref.refs_5_ = bf16[128,4352]{1,0:T(8,128)(2,1)} collective-permute-done((bf16[128,4352]{1,0:T(8,128)(2,1)}, bf16[128,4352]{1,0:T(8,128)(2,1)}, u32[]{:S(2)}, u32[]{:S(2)}) %collective-permute-start.6) | collective-permute-done | bytes 1114144 | tf_op jit(solution)/shard_map/ppermute | solution.py:771
  125.1 7.0 %all-to-all-done.1 = bf16[32,32,2816]{2,1,0:T(8,128)(2,1)} async-done(((bf16[32,32,2816]{2,1,0:T(8,128)(2,1)}), bf16[32,32,2816]{2,1,0:T(8,128)(2,1)}, u32[]{:S(2)}, u32[]{:S(2)}) %all-to-all-start.1) | async-done | bytes 5767200 | tf_op jit(solution)/shard_map/all_to_all | solution.py:766
  132.1 12.6 %hidden.1 = (bf16[4,128,256]{2,1,0:T(8,128)(2,1)}, bf16[32,16,256]{2,1,0:T(8,128)(2,1)}, bf16[64,4608]{1,0:T(8,128)(2,1)}, bf16[64,4608]{1,0:T(8,128)(2,1)}, f32[128,128]{1,0:T(8,128)}) custom-call(bf16[1024,2816]{1,0:T(8,128)(2,1)} %bitcast.9.g_ref, bf16[128,7168]{1,0:T(8,128)(2,1)} %bitcast.37, bf16[7168,128]{1,0:T(8,128)(2,1)} %bitcast.26, ...), custom_call_target="tpu_custom_call" | custom-call | flops 1778384896 | bytes 9306112 | tf_op jit(solution)/shard_map/hidden/pallas_call | solution.py:367
  147.6 4.2 %ring_part.1 = bf16[512,2560]{1,0:T(8,128)(2,1)} custom-call(bf16[32,16,256]{2,1,0:T(8,128)(2,1)} %get-tuple-element.66.near_ref, bf16[7168,128]{1,0:T(8,128)(2,1)} %bitcast.27, bf16[7168,128]{1,0:T(8,128)(2,1)} %bitcast.32), custom_call_target="tpu_custom_call" | custom-call | flops 671088640 | bytes 3932160 | tf_op jit(solution)/shard_map/ring_part/pallas_call | solution.py:412
  151.7 11.9 %all-to-all-start.2 = ((bf16[32,16,2560]{2,1,0:T(8,128)(2,1)}), bf16[32,16,2560]{2,1,0:T(8,128)(2,1)S(1)}, u32[]{:S(2)}, u32[]{:S(2)}) async-start(bf16[32,16,2560]{2,1,0:T(8,128)(2,1)} %bitcast.23), calls=%async_computation.2 | async-start | bytes 5242880 | tf_op jit(solution)/shard_map/all_to_all | solution.py:766
  164.4 5.3 %side_part.1 = (bf16[128,4608]{1,0:T(8,128)(2,1)}, bf16[128,4608]{1,0:T(8,128)(2,1)}, bf16[128,4608]{1,0:T(8,128)(2,1)}) custom-call(bf16[4,128,256]{2,1,0:T(8,128)(2,1)} %get-tuple-element.79.gu_ref, bf16[7168,128]{1,0:T(8,128)(2,1)} %bitcast.28, bf16[7168,128]{1,0:T(8,128)(2,1)} %bitcast.33, bf16[64,4608]{1,0:T(8,128)(2,1)} %copy-done.10, ...), custom_call_target="tpu_custom_call" | custom-call | flops 36238786560 | bytes 283115520 | tf_op jit(solution)/shard_map/side_part/pallas_call | solution.py:465
  172.5 11.8 %down.1 = bf16[128,7168]{1,0:T(8,128)(2,1)} custom-call(bf16[1024,2816]{1,0:T(8,128)(2,1)} %bitcast.9.g_ref, f32[128,128]{1,0:T(8,128)} %get-tuple-element.82.refs_0_, f32[256,128]{1,0:T(8,128)} %get-tuple-element.83.refs_1_, f32[128,128]{1,0:T(8,128)} %get-tuple-element.84.refs_2_, bf16[256,4352]{1,0:T(8,128)(2,1)} %bitcast.13.refs_0_.own_ref.refs_3_, ...), custom_call_target="tpu_custom_call" | custom-call | flops 1879048192 | bytes 9175040 | tf_op jit(solution)/shard_map/down/pallas_call | solution.py:623
  184.3 9.5 %row_grads.1 = (bf16[2,3584,128]{2,1,0:T(8,128)(2,1)}, bf16[2,3584,128]{2,1,0:T(8,128)(2,1)}) custom-call(bf16[4,128,256]{2,1,0:T(8,128)(2,1)} %get-tuple-element.79.gu_ref, bf16[256,4352]{1,0:T(8,128)(2,1)} %bitcast.13.refs_0_.own_ref.refs_3_, bf16[256,4352]{1,0:T(8,128)(2,1)} %collective-permute-done.4.refs_0_.next_ref.refs_4_, ...), custom_call_target="tpu_custom_call" | custom-call | flops 3758096384 | bytes 11010048 | tf_op jit(solution)/shard_map/row_grads/pallas_call | solution.py:554
  193.8 3.7 %all-to-all-done.2 = bf16[32,16,2560]{2,1,0:T(8,128)(2,1)S(1)} async-done(((bf16[32,16,2560]{2,1,0:T(8,128)(2,1)}), bf16[32,16,2560]{2,1,0:T(8,128)(2,1)S(1)}, u32[]{:S(2)}, u32[]{:S(2)}) %all-to-all-start.2) | async-done | bytes 2621472 | tf_op jit(solution)/shard_map/all_to_all | solution.py:766
  199.7 3.2 %sum_blocks.1 = bf16[32,4,4608]{2,1,0:T(4,128)(2,1)} custom-call(bf16[128,4608]{1,0:T(8,128)(2,1)} %get-tuple-element.92.a_ref, bf16[128,4608]{1,0:T(8,128)(2,1)} %collective-permute-done.14.b_ref, bf16[128,4608]{1,0:T(8,128)(2,1)} %collective-permute-done.15.c_ref), custom_call_target="tpu_custom_call" | custom-call | flops 1179648 | bytes 4718592 | tf_op jit(solution)/shard_map/sum_blocks/pallas_call | solution.py:506
  202.9 7.2 %all-to-all-start.3 = ((bf16[32,4,4608]{2,1,0:T(4,128)(2,1)}), bf16[32,4,4608]{2,1,0:T(4,128)(2,1)S(1)}, u32[]{:S(2)}, u32[]{:S(2)}) async-start(bf16[32,4,4608]{2,1,0:T(4,128)(2,1)} %sum_blocks.1), calls=%async_computation.3 | async-start | bytes 2359296 | tf_op jit(solution)/shard_map/all_to_all | solution.py:766
  210.2 2.7 %collective-permute-start.11 = (bf16[32,2560]{1,0:T(8,128)(2,1)S(1)}, bf16[32,2560]{1,0:T(8,128)(2,1)S(1)}, u32[]{:S(2)}, u32[]{:S(2)}) collective-permute-start(bf16[32,2560]{1,0:T(8,128)(2,1)S(1)} %get-tuple-element.89), channel_id=1, source_target_pairs={{0,96},{32,0},{64,32},{96,64},{1,97},{33,1},{65,33},{97,65},{2,98}... | collective-permute-start | bytes 491528 | tf_op jit(solution)/shard_map/ppermute | solution.py:771
  212.9 4.0 %collective-permute-done.10.top_ref = bf16[32,2560]{1,0:T(8,128)(2,1)S(1)} collective-permute-done((bf16[32,2560]{1,0:T(8,128)(2,1)S(1)}, bf16[32,2560]{1,0:T(8,128)(2,1)S(1)}, u32[]{:S(2)}, u32[]{:S(2)}) %collective-permute-start.10) | collective-permute-done | bytes 163872 | tf_op jit(solution)/shard_map/ppermute | solution.py:771
  219.8 6.7 %collective-permute-done.12.left_ref = bf16[64,2560]{1,0:T(8,128)(2,1)S(1)} collective-permute-done((bf16[64,2560]{1,0:T(8,128)(2,1)S(1)}, bf16[64,2560]{1,0:T(8,128)(2,1)S(1)}, u32[]{:S(2)}, u32[]{:S(2)}) %collective-permute-start.12) | collective-permute-done | bytes 327712 | tf_op jit(solution)/shard_map/ppermute | solution.py:771
  228.5 3.3 %combine.1 = bf16[128,7168]{1,0:T(8,128)(2,1)} custom-call(bf16[64,128]{1,0:T(8,128)(2,1)S(1)} %copy-done.2, bf16[64,2560]{1,0:T(8,128)(2,1)S(1)} %copy-done.1, bf16[64,2560]{1,0:T(8,128)(2,1)S(1)} %collective-permute-done.12.left_ref, bf16[64,2560]{1,0:T(8,128)(2,1)S(1)} %collective-permute-done.13.right_ref, bf16[32,4,4608]{2,1,0:T(4,128)(2,1)S(1)} %all-to-all-done.3.wide_ref), custom_call_target="tpu_custom_call" | custom-call | flops 117440512 | bytes 3670016 | tf_op jit(solution)/shard_map/combine/pallas_call | solution.py:747
  (55 shorter events, 31.6 us)
Async XLA Ops:
  6.1 39.4 %all-to-all-start = ((bf16[32,8,4352]{2,1,0:T(8,128)(2,1)}), bf16[32,8,4352]{2,1,0:T(8,128)(2,1)}, u32[]{:S(2)}, u32[]{:S(2)}) async-start(bf16[32,8,4352]{2,1,0:T(8,128)(2,1)} %bitcast.34), calls=%async_computation | async-start | bytes 4456448 | tf_op jit(solution)/shard_map/all_to_all | solution.py:766
  15.7 19.0 %collective-permute-start.1 = (bf16[128,2816]{1,0:T(8,128)(2,1)S(1)}, bf16[128,2816]{1,0:T(8,128)(2,1)S(1)}, u32[]{:S(2)}, u32[]{:S(2)}) collective-permute-start(bf16[128,2816]{1,0:T(8,128)(2,1)S(1)} %copy-done.7), channel_id=1, source_target_pairs={{0,32},{32,64},{64,96},{96,0},{1,33},{33,65},{65,97},{97,1},{2,34}... | collective-permute-start | bytes 2162696 | tf_op jit(solution)/shard_map/ppermute | solution.py:771
  17.1 17.7 %collective-permute-start = (bf16[128,2816]{1,0:T(8,128)(2,1)S(1)}, bf16[128,2816]{1,0:T(8,128)(2,1)S(1)}, u32[]{:S(2)}, u32[]{:S(2)}) collective-permute-start(bf16[128,2816]{1,0:T(8,128)(2,1)S(1)} %copy-done.7), channel_id=1, source_target_pairs={{0,96},{32,0},{64,32},{96,64},{1,97},{33,1},{65,33},{97,65},{2,98}... | collective-permute-start | bytes 2162696 | tf_op jit(solution)/shard_map/ppermute | solution.py:771
  34.7 13.5 %copy-start.5 = (bf16[128,2816]{1,0:T(8,128)(2,1)}, bf16[128,2816]{1,0:T(8,128)(2,1)S(1)}, u32[]{:S(2)}) copy-start(bf16[128,2816]{1,0:T(8,128)(2,1)S(1)} %collective-permute-done.1) | copy-start | bytes 2162692
  34.7 10.3 %collective-permute-start.2 = (bf16[64,2816]{1,0:T(8,128)(2,1)S(1)}, bf16[64,2816]{1,0:T(8,128)(2,1)S(1)}, u32[]{:S(2)}, u32[]{:S(2)}) collective-permute-start(bf16[64,2816]{1,0:T(8,128)(2,1)S(1)} %slice.16), channel_id=1, source_target_pairs={{0,32},{32,64},{64,96},{96,0},{1,33},{33,65},{65,97},{97,1},{2,34}... | collective-permute-start | bytes 1081352 | tf_op jit(solution)/shard_map/ppermute | solution.py:771
  34.8 13.4 %copy-start.6 = (bf16[128,2816]{1,0:T(8,128)(2,1)}, bf16[128,2816]{1,0:T(8,128)(2,1)S(1)}, u32[]{:S(2)}) copy-start(bf16[128,2816]{1,0:T(8,128)(2,1)S(1)} %collective-permute-done) | copy-start | bytes 2162692
  34.9 10.1 %collective-permute-start.3 = (bf16[64,2816]{1,0:T(8,128)(2,1)S(1)}, bf16[64,2816]{1,0:T(8,128)(2,1)S(1)}, u32[]{:S(2)}, u32[]{:S(2)}) collective-permute-start(bf16[64,2816]{1,0:T(8,128)(2,1)S(1)} %slice.17), channel_id=1, source_target_pairs={{0,96},{32,0},{64,32},{96,64},{1,97},{33,1},{65,33},{97,65},{2,98}... | collective-permute-start | bytes 1081352 | tf_op jit(solution)/shard_map/ppermute | solution.py:771
  45.5 50.2 %collective-permute-start.5 = (bf16[256,4352]{1,0:T(8,128)(2,1)}, bf16[256,4352]{1,0:T(8,128)(2,1)}, u32[]{:S(2)}, u32[]{:S(2)}) collective-permute-start(bf16[256,4352]{1,0:T(8,128)(2,1)} %bitcast.13.refs_0_.own_ref.refs_3_), channel_id=1, source_target_pairs={{0,32},{32,64},{64,96},{96,0},{1,33},{33,65},{65,97},{97,1},{2,34}... | collective-permute-start | bytes 6684680 | tf_op jit(solution)/shard_map/ppermute | solution.py:771
  46.8 51.7 %collective-permute-start.4 = (bf16[256,4352]{1,0:T(8,128)(2,1)}, bf16[256,4352]{1,0:T(8,128)(2,1)}, u32[]{:S(2)}, u32[]{:S(2)}) collective-permute-start(bf16[256,4352]{1,0:T(8,128)(2,1)} %bitcast.13.refs_0_.own_ref.refs_3_), channel_id=1, source_target_pairs={{0,96},{32,0},{64,32},{96,64},{1,97},{33,1},{65,33},{97,65},{2,98}... | collective-permute-start | bytes 6684680 | tf_op jit(solution)/shard_map/ppermute | solution.py:771
  52.2 79.9 %all-to-all-start.1 = ((bf16[32,32,2816]{2,1,0:T(8,128)(2,1)}), bf16[32,32,2816]{2,1,0:T(8,128)(2,1)}, u32[]{:S(2)}, u32[]{:S(2)}) async-start(bf16[32,32,2816]{2,1,0:T(8,128)(2,1)} %bitcast.22), calls=%async_computation.1 | async-start | bytes 11534336 | tf_op jit(solution)/shard_map/all_to_all | solution.py:766
  98.0 25.3 %collective-permute-start.6 = (bf16[128,4352]{1,0:T(8,128)(2,1)}, bf16[128,4352]{1,0:T(8,128)(2,1)}, u32[]{:S(2)}, u32[]{:S(2)}) collective-permute-start(bf16[128,4352]{1,0:T(8,128)(2,1)} %slice.18), channel_id=1, source_target_pairs={{0,32},{32,64},{64,96},{96,0},{1,33},{33,65},{65,97},{97,1},{2,34}... | collective-permute-start | bytes 3342344 | tf_op jit(solution)/shard_map/ppermute | solution.py:771
  100.8 24.3 %collective-permute-start.7 = (bf16[128,4352]{1,0:T(8,128)(2,1)}, bf16[128,4352]{1,0:T(8,128)(2,1)}, u32[]{:S(2)}, u32[]{:S(2)}) collective-permute-start(bf16[128,4352]{1,0:T(8,128)(2,1)} %slice.19), channel_id=1, source_target_pairs={{0,96},{32,0},{64,32},{96,64},{1,97},{33,1},{65,33},{97,65},{2,98}... | collective-permute-start | bytes 3342344 | tf_op jit(solution)/shard_map/ppermute | solution.py:771
  144.6 19.0 %collective-permute-start.8 = (bf16[64,4608]{1,0:T(8,128)(2,1)}, bf16[64,4608]{1,0:T(8,128)(2,1)S(1)}, u32[]{:S(2)}, u32[]{:S(2)}) collective-permute-start(bf16[64,4608]{1,0:T(8,128)(2,1)} %get-tuple-element.72), channel_id=1, source_target_pairs={{0,32},{32,64},{64,96},{96,0},{1,33},{33,65},{65,97},{97,1},{2,34}... | collective-permute-start | bytes 1769480 | tf_op jit(solution)/shard_map/ppermute | solution.py:771
  144.9 18.7 %collective-permute-start.9 = (bf16[64,4608]{1,0:T(8,128)(2,1)}, bf16[64,4608]{1,0:T(8,128)(2,1)}, u32[]{:S(2)}, u32[]{:S(2)}) collective-permute-start(bf16[64,4608]{1,0:T(8,128)(2,1)} %get-tuple-element.73), channel_id=1, source_target_pairs={{0,96},{32,0},{64,32},{96,64},{1,97},{33,1},{65,33},{97,65},{2,98}... | collective-permute-start | bytes 1769480 | tf_op jit(solution)/shard_map/ppermute | solution.py:771
  151.7 45.8 %all-to-all-start.2 = ((bf16[32,16,2560]{2,1,0:T(8,128)(2,1)}), bf16[32,16,2560]{2,1,0:T(8,128)(2,1)S(1)}, u32[]{:S(2)}, u32[]{:S(2)}) async-start(bf16[32,16,2560]{2,1,0:T(8,128)(2,1)} %bitcast.23), calls=%async_computation.2 | async-start | bytes 5242880 | tf_op jit(solution)/shard_map/all_to_all | solution.py:766
  169.7 30.0 %collective-permute-start.14 = (bf16[128,4608]{1,0:T(8,128)(2,1)}, bf16[128,4608]{1,0:T(8,128)(2,1)}, u32[]{:S(2)}, u32[]{:S(2)}) collective-permute-start(bf16[128,4608]{1,0:T(8,128)(2,1)} %get-tuple-element.93), channel_id=1, source_target_pairs={{0,32},{32,64},{64,96},{96,0},{1,33},{33,65},{65,97},{97,1},{2,34}... | collective-permute-start | bytes 3538952 | tf_op jit(solution)/shard_map/ppermute | solution.py:771
  169.8 29.9 %collective-permute-start.15 = (bf16[128,4608]{1,0:T(8,128)(2,1)}, bf16[128,4608]{1,0:T(8,128)(2,1)}, u32[]{:S(2)}, u32[]{:S(2)}) collective-permute-start(bf16[128,4608]{1,0:T(8,128)(2,1)} %get-tuple-element.94), channel_id=1, source_target_pairs={{0,96},{32,0},{64,32},{96,64},{1,97},{33,1},{65,33},{97,65},{2,98}... | collective-permute-start | bytes 3538952 | tf_op jit(solution)/shard_map/ppermute | solution.py:771
  202.9 25.6 %copy-start.1 = (bf16[64,2560]{1,0:T(8,128)(2,1)S(1)}, bf16[64,2560]{1,0:T(8,128)(2,1)}, u32[]{:S(2)}) copy-start(bf16[64,2560]{1,0:T(8,128)(2,1)} %copy-done) | copy-start | bytes 983044
  202.9 25.6 %copy-start.2 = (bf16[64,128]{1,0:T(8,128)(2,1)S(1)}, bf16[64,128]{1,0:T(8,128)(2,1)}, u32[]{:S(2)}) copy-start(bf16[64,128]{1,0:T(8,128)(2,1)} %get-tuple-element.51.table_ref) | copy-start | bytes 49156
  202.9 25.6 %all-to-all-start.3 = ((bf16[32,4,4608]{2,1,0:T(4,128)(2,1)}), bf16[32,4,4608]{2,1,0:T(4,128)(2,1)S(1)}, u32[]{:S(2)}, u32[]{:S(2)}) async-start(bf16[32,4,4608]{2,1,0:T(4,128)(2,1)} %sum_blocks.1), calls=%async_computation.3 | async-start | bytes 2359296 | tf_op jit(solution)/shard_map/all_to_all | solution.py:766
  210.1 6.8 %collective-permute-start.10 = (bf16[32,2560]{1,0:T(8,128)(2,1)S(1)}, bf16[32,2560]{1,0:T(8,128)(2,1)S(1)}, u32[]{:S(2)}, u32[]{:S(2)}) collective-permute-start(bf16[32,2560]{1,0:T(8,128)(2,1)S(1)} %copy-done.4), channel_id=1, source_target_pairs={{0,32},{32,64},{64,96},{96,0},{1,33},{33,65},{65,97},{97,1},{2,34}... | collective-permute-start | bytes 491528 | tf_op jit(solution)/shard_map/ppermute | solution.py:771
  210.2 6.8 %collective-permute-start.11 = (bf16[32,2560]{1,0:T(8,128)(2,1)S(1)}, bf16[32,2560]{1,0:T(8,128)(2,1)S(1)}, u32[]{:S(2)}, u32[]{:S(2)}) collective-permute-start(bf16[32,2560]{1,0:T(8,128)(2,1)S(1)} %get-tuple-element.89), channel_id=1, source_target_pairs={{0,96},{32,0},{64,32},{96,64},{1,97},{33,1},{65,33},{97,65},{2,98}... | collective-permute-start | bytes 491528 | tf_op jit(solution)/shard_map/ppermute | solution.py:771
  217.1 9.4 %collective-permute-start.12 = (bf16[64,2560]{1,0:T(8,128)(2,1)S(1)}, bf16[64,2560]{1,0:T(8,128)(2,1)S(1)}, u32[]{:S(2)}, u32[]{:S(2)}) collective-permute-start(bf16[64,2560]{1,0:T(8,128)(2,1)S(1)} %get-tuple-element.90), channel_id=1, source_target_pairs={{0,32},{32,64},{64,96},{96,0},{1,33},{33,65},{65,97},{97,1},{2,34}... | collective-permute-start | bytes 983048 | tf_op jit(solution)/shard_map/ppermute | solution.py:771
  218.0 8.5 %collective-permute-start.13 = (bf16[64,2560]{1,0:T(8,128)(2,1)S(1)}, bf16[64,2560]{1,0:T(8,128)(2,1)S(1)}, u32[]{:S(2)}, u32[]{:S(2)}) collective-permute-start(bf16[64,2560]{1,0:T(8,128)(2,1)S(1)} %get-tuple-element.91), channel_id=1, source_target_pairs={{0,96},{32,0},{64,32},{96,64},{1,97},{33,1},{65,33},{97,65},{2,98}... | collective-permute-start | bytes 983048 | tf_op jit(solution)/shard_map/ppermute | solution.py:771
  (7 other events, 25.6 us)

commit v11 on v10

--- a/solution.py
+++ b/solution.py
@@ -175,8 +175,10 @@
     )(*[b.reshape(b.shape[0] // unit, unit, cols) for b in blocks])
 
 
-def pre_copies(x_refs, wg_ref, wu_ref, wd_ref, x, w, d, sem):
-    cols = x.shape[1]
+def pre_kernel(count, *refs):
+    x_refs = refs[:count]
+    wg_ref, wu_ref, wd_ref, slope_ref, swish_ref, part_ref, outer_ref, x, w, d, acc, sem = refs[count:]
+    rows, cols = x.shape
     ff = w.shape[2] // 4
     share = d.shape[1]
     half = cols - share
@@ -205,61 +207,40 @@
             for h in range(2):
                 source = wd_ref.at[:, h * share : (h + 1) * share]
                 add(t, source, d.at[h * ff : (h + 1) * ff, :])
-    return copies
-
-
-def pre_values(copies, x, w, d, acc):
-    rows, cols = x.shape
-    ff = w.shape[2] // 4
-    half = cols - d.shape[1]
-    steps = half // TILE
+    for group in copies:
+        for copy in group:
+            copy.start()
     for t in range(steps):
-        wait_all(copies[t])
+        for copy in copies[t]:
+            copy.wait()
         value = jnp.dot(x[:, t * TILE : (t + 1) * TILE], w[t], preferred_element_type=F32)
         if t == 0:
             acc[...] = value
         else:
             acc[...] += value
-    wait_all(copies[steps])
+    for copy in copies[steps]:
+        copy.wait()
 
     def fold_halves(value):
         value = value.reshape(rows // (2 * CAP), 2 * CAP, 2 * ff)
         return (value[:, :CAP, :ff] + value[:, CAP:, ff:]).reshape(rows // 2, ff)
 
-    part = fold_halves(contract_cols(x[:, half:], d[...]))
+    part_ref[...] = fold_halves(contract_cols(x[:, half:], d[...]))
     gate = fold_halves(acc[:, : 2 * ff])
     up = fold_halves(acc[:, 2 * ff :])
     sig = 1.0 / (1.0 + jnp.exp(-gate))
     swish = gate * sig
-    return up * sig * (1.0 + gate * (1.0 - sig)), swish, part, swish * up
-
-
-def pre_kernel(count, *refs):
-    wg_ref, wu_ref, wd_ref = refs[count : count + 3]
-    out_refs = refs[count + 3 : count + 7]
-    x, w, d, acc, sem = refs[count + 7 :]
-    copies = pre_copies(refs[:count], wg_ref, wu_ref, wd_ref, x, w, d, sem)
-    for group in copies:
-        start_all(group)
-    for ref, value in zip(out_refs, pre_values(copies, x, w, d, acc)):
-        ref[...] = value
-
-
-def pre_scratch(rows, cols, share, ff, blocks):
-    steps = (cols - share) // TILE
-    return [
-        pltpu.VMEM((rows, cols), BF),
-        pltpu.VMEM((steps, TILE, 4 * ff), BF),
-        pltpu.VMEM((2 * ff, share), BF),
-        pltpu.VMEM((rows, 4 * ff), F32),
-        pltpu.SemaphoreType.DMA(((blocks + 4) * steps + blocks + 2,)),
-    ]
+    slope_ref[...] = up * sig * (1.0 + gate * (1.0 - sig))
+    swish_ref[...] = swish
+    outer_ref[...] = swish * up
 
 
 def pre(blocks, w_gate, w_up, w_down, share):
     cols = blocks[0].shape[1]
     rows = sum(b.shape[0] for b in blocks)
     ff = w_gate.shape[1]
+    steps = (cols - share) // TILE
+    copies = (len(blocks) + 4) * steps + len(blocks) + 2
     return call(
         functools.partial(pre_kernel, len(blocks)),
         "pre",
@@ -268,7 +249,13 @@
         in_specs=[ANY] * len(blocks) + [HBM] * 3,
         out_specs=[VMEM] * 4,
         out_shape=[jax.ShapeDtypeStruct((rows // 2, ff), F32)] * 4,
-        scratch_shapes=pre_scratch(rows, cols, share, ff, len(blocks)),
+        scratch_shapes=[
+            pltpu.VMEM((rows, cols), BF),
+            pltpu.VMEM((steps, TILE, 4 * ff), BF),
+            pltpu.VMEM((2 * ff, share), BF),
+            pltpu.VMEM((rows, 4 * ff), F32),
+            pltpu.SemaphoreType.DMA((copies,)),
+        ],
     )(*blocks, w_gate, w_up, w_down)
 
 
@@ -296,9 +283,8 @@
 def hidden_kernel(
     g_ref, wd_ref, wg_ref, wu_ref, *refs
 ):
-    own, side, far_rows = refs[0:3], refs[3:6], refs[6:8]
-    gu_ref, near_ref, top_ref, bottom_ref, outer_ref, g, d, w, small, staged, sem = refs[8:19]
-    far_x, far_w, far_d, far_acc, far_sem = refs[19:]
+    own, side, far = refs[0:3], refs[3:6], refs[6:9]
+    gu_ref, near_ref, top_ref, bottom_ref, g, d, w, small, staged, sem = refs[9:]
     groups, span, double = gu_ref.shape
     ff = double // 2
     locs = span // CAP
@@ -320,18 +306,14 @@
     more = []
     index = 3 * steps
     for k in range(3):
-        places = [(own[k], 0), (side[k].at[:span], 1), (side[k].at[span:], 3)]
+        places = [(own[k], 0), (side[k].at[:span], 1), (far[k], 2), (side[k].at[span:], 3)]
         for source, group in places:
             more.append(pltpu.make_async_copy(source, small.at[k, group], sem.at[index]))
             index += 1
     weights = load_weights(wg_ref, wu_ref, w, wg_ref.shape[0] - wide_cols, sem, index)
-    far_copies = pre_copies(far_rows, wg_ref, wu_ref, wd_ref, far_x, far_w, far_d, far_sem)
-    for group in far_copies:
-        start_all(group)
     start_all(loads)
     start_all(more)
     start_all(weights)
-    slope, swish, part, outer_ref[...] = pre_values(far_copies, far_x, far_w, far_d, far_acc)
     total = None
     for t, window in enumerate(windows):
         wait_all(loads[3 * t : 3 * t + 3])
@@ -343,9 +325,9 @@
         first = group * unit
         hidden = (
             halves[:, first : first + CAP, :ff] + halves[:, first + CAP : first + unit, ff:]
-        ).reshape(span, ff) + (part if group == 2 else small[2, group])
-        gate = hidden * (slope if group == 2 else small[0, group])
-        up = hidden * (swish if group == 2 else small[1, group])
+        ).reshape(span, ff) + small[2, group]
+        gate = hidden * small[0, group]
+        up = hidden * small[1, group]
         both = jnp.concatenate([gate, up], axis=1)
         gu_ref[group] = both.astype(BF)
         near_ref[:, group * CAP : (group + 1) * CAP, :] = both.reshape(locs, CAP, double).astype(BF)
@@ -359,7 +341,7 @@
     wait_all(stores)
 
 
-def hidden(g_rows, w_down, w_gate, w_up, own, side, far, share, wide_cols):
+def hidden(g_rows, w_down, w_gate, w_up, own, side, far, wide_cols):
     rows, cols = g_rows.shape
     span, ff = own[0].shape
     groups = rows // 2 // span
@@ -369,14 +351,13 @@
         "hidden",
         4 * rows * cols * ff + 4 * span * ff * wide_cols,
         2 * (rows * cols + 2 * wide_cols * ff + span * wide_cols),
-        in_specs=[ANY] + [HBM] * 3 + [ANY] * 8,
-        out_specs=[VMEM, VMEM, ANY, ANY, VMEM],
+        in_specs=[ANY] + [HBM] * 3 + [ANY] * 9,
+        out_specs=[VMEM, VMEM, ANY, ANY],
         out_shape=[
             small(groups, span, 2 * ff),
             small(span // CAP, groups * CAP, 2 * ff),
             small(span // 2, wide_cols),
             small(span // 2, wide_cols),
-            jax.ShapeDtypeStruct((span, ff), F32),
         ],
         scratch_shapes=[
             pltpu.VMEM((rows, cols), BF),
@@ -384,8 +365,7 @@
             pltpu.VMEM((wide_cols, 2 * ff), BF),
             pltpu.VMEM((3, groups, span, ff), F32),
             pltpu.VMEM((span, wide_cols), BF),
-            pltpu.SemaphoreType.DMA((3 * pl.cdiv(cols, 3 * TILE // 2) + 9 + 4,)),
-            *pre_scratch(2 * span, far[0].shape[1], share, ff, 2),
+            pltpu.SemaphoreType.DMA((3 * pl.cdiv(cols, 3 * TILE // 2) + 12 + 4,)),
         ],
     )(g_rows, w_down, w_gate, w_up, *own, *side, *far)
 
@@ -804,8 +784,9 @@
     own, after, top, bottom, before = blocks
     *pre_own, outer_own = pre([own], w_gate, w_up, w_down, share)
     *pre_side, outer_side = pre([after, before], w_gate, w_up, w_down, share)
-    gu, near, far_top, far_bottom, outer_far = hidden(
-        g_rows, w_down, w_gate, w_up, pre_own, pre_side, [top, bottom], share, wide_cols
+    *pre_far, outer_far = pre([top, bottom], w_gate, w_up, w_down, share)
+    gu, near, far_top, far_bottom = hidden(
+        g_rows, w_down, w_gate, w_up, pre_own, pre_side, pre_far, wide_cols
     )
 
     came_top, came_bottom = shift(far_top, 1), shift(far_bottom, -1)

time: 233 us -> 229 us (0.983)
  waiting for transfers between devices: 94.2 us -> 89.7 us
    pallas_call x2 -> x3, Pallas kernels: 9.91 us -> 14.3 us  [pre(): call(functools.partial(pre_kernel, len(blocks)), 'pre', 200 * (8 * rows *...]
    all_to_all x4, waiting for transfers between devices: 13.2 us -> 8.79 us  [over_loc(): return lax.all_to_all(a, 'loc', split_axis=0, concat_axis=0, tiled=True)]
    pallas_call x1, Pallas kernels: 12.6 us -> 8.44 us  [hidden(): call(hidden_kernel, 'hidden', 4 * rows * cols * ff + 4 * span * ff * wide...]
  transfers between devices with their start and end apart: 20 -> 20, of which waited for: 11 -> 11; matrix products, arithmetic and copies ran while one was open for 2% -> 2% of each run, Pallas kernels for 20% -> 22%
where the time goes in v11:
time: 229 us; the launch traced here: 228 us
  waiting for transfers between devices  89.7 us (39%)
  Pallas kernels  70.2 us (31%)
  starting transfers between devices  60 us (26%)
  local copies, waits for them, and re-layouts  6.88 us (3%)
    ppermute x16, waiting for transfers between devices, shift(): lax.ppermute(a, 'grp', [(i, (i + step) % groups) for i in range(groups)])  80.9 us
    all_to_all x4, starting transfers between devices, over_loc(): return lax.all_to_all(a, 'loc', split_axis=0, concat_axis=0, tiled=True)  37.7 us
    ppermute x16, starting transfers between devices, shift(): lax.ppermute(a, 'grp', [(i, (i + step) % groups) for i in range(groups)])  22.3 us
    pallas_call x3, Pallas kernels, pre(): call(functools.partial(pre_kernel, len(blocks)), 'pre', 200 * (8 * rows *...  14.3 us
    pallas_call x1, Pallas kernels, down(): call(down_kernel, 'down', 4 * rows * (cols + share) * ff, 2 * (cols + sha...  11.8 us
    pallas_call x1, Pallas kernels, row_grads(): call(row_grads_kernel, 'row_grads', 8 * rows * half * ff, 2 * half * (row...  9.47 us
    all_to_all x4, waiting for transfers between devices, over_loc(): return lax.all_to_all(a, 'loc', split_axis=0, concat_axis=0, tiled=True)  8.79 us
    pallas_call x1, Pallas kernels, hidden(): call(hidden_kernel, 'hidden', 4 * rows * cols * ff + 4 * span * ff * wide...  8.44 us
  transfers between devices with their start and end apart: 20, of which 11 were waited for; matrix products, arithmetic and copies ran while one was open for 2% of the time, Pallas kernels for 22%

profile of v11, /device:TPU:1, one launch (start us, length us, event | category | flops | bytes accessed | tf_op | source)
XLA Modules:
  0.0 227.8 jit_solution(6542760373075229813)
XLA Ops:
  0.6 5.5 %dispatch.1 = (bf16[64,128]{1,0:T(8,128)(2,1)}, bf16[128,2816]{1,0:T(8,128)(2,1)}, bf16[2,16,8,4352]{3,2,1,0:T(8,128)(2,1)}) custom-call(s32[8,128]{1,0:T(8,128)} %bitcast.47, bf16[8,128]{1,0:T(8,128)(2,1)} %bitcast.48, bf16[128,7168]{1,0:T(8,128)(2,1)} %g_ref.1, bf16[128,7168]{1,0:T(8,128)(2,1)} %t_ref.1), custom_call_target="tpu_custom_call" | custom-call | flops 469762048 | bytes 6422528 | tf_op jit(solution)/shard_map/dispatch/pallas_call | solution.py:110
  6.1 9.6 %all-to-all-start = ((bf16[32,8,4352]{2,1,0:T(8,128)(2,1)}), bf16[32,8,4352]{2,1,0:T(8,128)(2,1)}, u32[]{:S(2)}, u32[]{:S(2)}) async-start(bf16[32,8,4352]{2,1,0:T(8,128)(2,1)} %bitcast.36), calls=%async_computation | async-start | bytes 4456448 | tf_op jit(solution)/shard_map/all_to_all | solution.py:746
  18.7 16.1 %collective-permute-done.1 = bf16[128,2816]{1,0:T(8,128)(2,1)S(1)} collective-permute-done((bf16[128,2816]{1,0:T(8,128)(2,1)S(1)}, bf16[128,2816]{1,0:T(8,128)(2,1)S(1)}, u32[]{:S(2)}, u32[]{:S(2)}) %collective-permute-start.1) | collective-permute-done | bytes 720928 | tf_op jit(solution)/shard_map/ppermute | solution.py:751
  37.6 7.4 %collective-permute-done.2 = bf16[64,2816]{1,0:T(8,128)(2,1)S(1)} collective-permute-done((bf16[64,2816]{1,0:T(8,128)(2,1)S(1)}, bf16[64,2816]{1,0:T(8,128)(2,1)S(1)}, u32[]{:S(2)}, u32[]{:S(2)}) %collective-permute-start.2) | collective-permute-done | bytes 360480 | tf_op jit(solution)/shard_map/ppermute | solution.py:751
  48.3 3.9 %regroup.1 = bf16[2,16,32,2816]{3,2,1,0:T(8,128)(2,1)} custom-call(bf16[16,8,2816]{2,1,0:T(8,128)(2,1)} %bitcast.44, bf16[16,8,2816]{2,1,0:T(8,128)(2,1)} %bitcast.43, bf16[8,8,2816]{2,1,0:T(8,128)(2,1)} %bitcast.45, bf16[8,8,2816]{2,1,0:T(8,128)(2,1)} %bitcast.46, bf16[16,8,2816]{2,1,0:T(8,128)(2,1)} %bitcast.42), custom_call_target="tpu_custom_call" | custom-call | bytes 8650752 | tf_op jit(solution)/shard_map/regroup/pallas_call | solution.py:163
  52.2 8.9 %all-to-all-start.1 = ((bf16[32,32,2816]{2,1,0:T(8,128)(2,1)}), bf16[32,32,2816]{2,1,0:T(8,128)(2,1)}, u32[]{:S(2)}, u32[]{:S(2)}) async-start(bf16[32,32,2816]{2,1,0:T(8,128)(2,1)} %bitcast.22), calls=%async_computation.1 | async-start | bytes 11534336 | tf_op jit(solution)/shard_map/all_to_all | solution.py:746
  61.1 4.3 %pre.3 = (f32[128,128]{1,0:T(8,128)}, f32[128,128]{1,0:T(8,128)}, f32[128,128]{1,0:T(8,128)}, f32[128,128]{1,0:T(8,128)}) custom-call(bf16[256,4352]{1,0:T(8,128)(2,1)} %bitcast.13.refs_0_.own_ref.refs_3_, bf16[7168,128]{1,0:T(8,128)(2,1)} %bitcast.24, bf16[7168,128]{1,0:T(8,128)(2,1)} %bitcast.30, bf16[128,7168]{1,0:T(8,128)(2,1)} %bitcast.37), custom_call_target="tpu_custom_call" | custom-call | flops 228170137600 | bytes 1336934400 | tf_op jit(solution)/shard_map/pre/pallas_call | solution.py:244
  65.4 30.3 %collective-permute-done.5.refs_1_.prev_ref.refs_7_ = bf16[256,4352]{1,0:T(8,128)(2,1)} collective-permute-done((bf16[256,4352]{1,0:T(8,128)(2,1)}, bf16[256,4352]{1,0:T(8,128)(2,1)}, u32[]{:S(2)}, u32[]{:S(2)}) %collective-permute-start.5) | collective-permute-done | bytes 2228256 | tf_op jit(solution)/shard_map/ppermute | solution.py:751
  103.0 5.6 %pre.4 = (f32[256,128]{1,0:T(8,128)}, f32[256,128]{1,0:T(8,128)}, f32[256,128]{1,0:T(8,128)}, f32[256,128]{1,0:T(8,128)}) custom-call(bf16[256,4352]{1,0:T(8,128)(2,1)} %collective-permute-done.4.refs_0_.next_ref.refs_4_, bf16[256,4352]{1,0:T(8,128)(2,1)} %collective-permute-done.5.refs_1_.prev_ref.refs_7_, bf16[7168,128]{1,0:T(8,128)(2,1)} %bitcast.25, ...), custom_call_target="tpu_custom_call" | custom-call | flops 456340275200 | bytes 1782579200 | tf_op jit(solution)/shard_map/pre/pallas_call | solution.py:244
  108.6 14.7 %collective-permute-done.6.refs_0_.top_ref.refs_5_ = bf16[128,4352]{1,0:T(8,128)(2,1)} collective-permute-done((bf16[128,4352]{1,0:T(8,128)(2,1)}, bf16[128,4352]{1,0:T(8,128)(2,1)}, u32[]{:S(2)}, u32[]{:S(2)}) %collective-permute-start.6) | collective-permute-done | bytes 1114144 | tf_op jit(solution)/shard_map/ppermute | solution.py:751
  125.1 4.4 %pre.5 = (f32[128,128]{1,0:T(8,128)}, f32[128,128]{1,0:T(8,128)}, f32[128,128]{1,0:T(8,128)}, f32[128,128]{1,0:T(8,128)}) custom-call(bf16[128,4352]{1,0:T(8,128)(2,1)} %collective-permute-done.6.refs_0_.top_ref.refs_5_, bf16[128,4352]{1,0:T(8,128)(2,1)} %collective-permute-done.7.refs_1_.bottom_ref.refs_6_, bf16[7168,128]{1,0:T(8,128)(2,1)} %bitcast.26, ...), custom_call_target="tpu_custom_call" | custom-call | flops 228170137600 | bytes 1336934400 | tf_op jit(solution)/shard_map/pre/pallas_call | solution.py:244
  132.1 8.4 %hidden.1 = (bf16[4,128,256]{2,1,0:T(8,128)(2,1)}, bf16[32,16,256]{2,1,0:T(8,128)(2,1)}, bf16[64,4608]{1,0:T(8,128)(2,1)}, bf16[64,4608]{1,0:T(8,128)(2,1)}) custom-call(bf16[1024,2816]{1,0:T(8,128)(2,1)} %bitcast.9.g_ref, bf16[128,7168]{1,0:T(8,128)(2,1)} %bitcast.40, bf16[7168,128]{1,0:T(8,128)(2,1)} %bitcast.27, bf16[7168,128]{1,0:T(8,128)(2,1)} %bitcast.33, ...), custom_call_target="tpu_custom_call" | custom-call | flops 1778384896 | bytes 9306112 | tf_op jit(solution)/shard_map/hidden/pallas_call | solution.py:349
  143.5 4.1 %ring_part.1 = bf16[512,2560]{1,0:T(8,128)(2,1)} custom-call(bf16[32,16,256]{2,1,0:T(8,128)(2,1)} %get-tuple-element.72.near_ref, bf16[7168,128]{1,0:T(8,128)(2,1)} %bitcast.28, bf16[7168,128]{1,0:T(8,128)(2,1)} %bitcast.34), custom_call_target="tpu_custom_call" | custom-call | flops 671088640 | bytes 3932160 | tf_op jit(solution)/shard_map/ring_part/pallas_call | solution.py:392
  147.6 11.9 %all-to-all-start.2 = ((bf16[32,16,2560]{2,1,0:T(8,128)(2,1)}), bf16[32,16,2560]{2,1,0:T(8,128)(2,1)S(1)}, u32[]{:S(2)}, u32[]{:S(2)}) async-start(bf16[32,16,2560]{2,1,0:T(8,128)(2,1)} %bitcast.23), calls=%async_computation.2 | async-start | bytes 5242880 | tf_op jit(solution)/shard_map/all_to_all | solution.py:746
  160.3 5.3 %side_part.1 = (bf16[128,4608]{1,0:T(8,128)(2,1)}, bf16[128,4608]{1,0:T(8,128)(2,1)}, bf16[128,4608]{1,0:T(8,128)(2,1)}) custom-call(bf16[4,128,256]{2,1,0:T(8,128)(2,1)} %get-tuple-element.85.gu_ref, bf16[7168,128]{1,0:T(8,128)(2,1)} %bitcast.29, bf16[7168,128]{1,0:T(8,128)(2,1)} %bitcast.35, bf16[64,4608]{1,0:T(8,128)(2,1)} %copy-done.10, ...), custom_call_target="tpu_custom_call" | custom-call | flops 36238786560 | bytes 283115520 | tf_op jit(solution)/shard_map/side_part/pallas_call | solution.py:445
  168.3 11.8 %down.1 = bf16[128,7168]{1,0:T(8,128)(2,1)} custom-call(bf16[1024,2816]{1,0:T(8,128)(2,1)} %bitcast.9.g_ref, f32[128,128]{1,0:T(8,128)} %get-tuple-element.88.refs_0_, f32[256,128]{1,0:T(8,128)} %get-tuple-element.89.refs_1_, f32[128,128]{1,0:T(8,128)} %get-tuple-element.90.refs_2_, bf16[256,4352]{1,0:T(8,128)(2,1)} %bitcast.13.refs_0_.own_ref.refs_3_, ...), custom_call_target="tpu_custom_call" | custom-call | flops 1879048192 | bytes 9175040 | tf_op jit(solution)/shard_map/down/pallas_call | solution.py:603
  180.2 9.5 %row_grads.1 = (bf16[2,3584,128]{2,1,0:T(8,128)(2,1)}, bf16[2,3584,128]{2,1,0:T(8,128)(2,1)}) custom-call(bf16[4,128,256]{2,1,0:T(8,128)(2,1)} %get-tuple-element.85.gu_ref, bf16[256,4352]{1,0:T(8,128)(2,1)} %bitcast.13.refs_0_.own_ref.refs_3_, bf16[256,4352]{1,0:T(8,128)(2,1)} %collective-permute-done.4.refs_0_.next_ref.refs_4_, ...), custom_call_target="tpu_custom_call" | custom-call | flops 3758096384 | bytes 11010048 | tf_op jit(solution)/shard_map/row_grads/pallas_call | solution.py:534
  189.7 3.7 %all-to-all-done.2 = bf16[32,16,2560]{2,1,0:T(8,128)(2,1)S(1)} async-done(((bf16[32,16,2560]{2,1,0:T(8,128)(2,1)}), bf16[32,16,2560]{2,1,0:T(8,128)(2,1)S(1)}, u32[]{:S(2)}, u32[]{:S(2)}) %all-to-all-start.2) | async-done | bytes 2621472 | tf_op jit(solution)/shard_map/all_to_all | solution.py:746
  195.6 3.2 %sum_blocks.1 = bf16[32,4,4608]{2,1,0:T(4,128)(2,1)} custom-call(bf16[128,4608]{1,0:T(8,128)(2,1)} %get-tuple-element.98.a_ref, bf16[128,4608]{1,0:T(8,128)(2,1)} %collective-permute-done.14.b_ref, bf16[128,4608]{1,0:T(8,128)(2,1)} %collective-permute-done.15.c_ref), custom_call_target="tpu_custom_call" | custom-call | flops 1179648 | bytes 4718592 | tf_op jit(solution)/shard_map/sum_blocks/pallas_call | solution.py:486
  198.7 7.3 %all-to-all-start.3 = ((bf16[32,4,4608]{2,1,0:T(4,128)(2,1)}), bf16[32,4,4608]{2,1,0:T(4,128)(2,1)S(1)}, u32[]{:S(2)}, u32[]{:S(2)}) async-start(bf16[32,4,4608]{2,1,0:T(4,128)(2,1)} %sum_blocks.1), calls=%async_computation.3 | async-start | bytes 2359296 | tf_op jit(solution)/shard_map/all_to_all | solution.py:746
  206.1 2.7 %collective-permute-start.11 = (bf16[32,2560]{1,0:T(8,128)(2,1)S(1)}, bf16[32,2560]{1,0:T(8,128)(2,1)S(1)}, u32[]{:S(2)}, u32[]{:S(2)}) collective-permute-start(bf16[32,2560]{1,0:T(8,128)(2,1)S(1)} %get-tuple-element.95), channel_id=1, source_target_pairs={{0,96},{32,0},{64,32},{96,64},{1,97},{33,1},{65,33},{97,65},{2,98}... | collective-permute-start | bytes 491528 | tf_op jit(solution)/shard_map/ppermute | solution.py:751
  208.9 4.0 %collective-permute-done.10.top_ref = bf16[32,2560]{1,0:T(8,128)(2,1)S(1)} collective-permute-done((bf16[32,2560]{1,0:T(8,128)(2,1)S(1)}, bf16[32,2560]{1,0:T(8,128)(2,1)S(1)}, u32[]{:S(2)}, u32[]{:S(2)}) %collective-permute-start.10) | collective-permute-done | bytes 163872 | tf_op jit(solution)/shard_map/ppermute | solution.py:751
  215.7 6.7 %collective-permute-done.12.left_ref = bf16[64,2560]{1,0:T(8,128)(2,1)S(1)} collective-permute-done((bf16[64,2560]{1,0:T(8,128)(2,1)S(1)}, bf16[64,2560]{1,0:T(8,128)(2,1)S(1)}, u32[]{:S(2)}, u32[]{:S(2)}) %collective-permute-start.12) | collective-permute-done | bytes 327712 | tf_op jit(solution)/shard_map/ppermute | solution.py:751
  224.4 3.3 %combine.1 = bf16[128,7168]{1,0:T(8,128)(2,1)} custom-call(bf16[64,128]{1,0:T(8,128)(2,1)S(1)} %copy-done.2, bf16[64,2560]{1,0:T(8,128)(2,1)S(1)} %copy-done.1, bf16[64,2560]{1,0:T(8,128)(2,1)S(1)} %collective-permute-done.12.left_ref, bf16[64,2560]{1,0:T(8,128)(2,1)S(1)} %collective-permute-done.13.right_ref, bf16[32,4,4608]{2,1,0:T(4,128)(2,1)S(1)} %all-to-all-done.3.wide_ref), custom_call_target="tpu_custom_call" | custom-call | flops 117440512 | bytes 3670016 | tf_op jit(solution)/shard_map/combine/pallas_call | solution.py:727
  (56 shorter events, 34.2 us)
Async XLA Ops:
  6.1 39.4 %all-to-all-start = ((bf16[32,8,4352]{2,1,0:T(8,128)(2,1)}), bf16[32,8,4352]{2,1,0:T(8,128)(2,1)}, u32[]{:S(2)}, u32[]{:S(2)}) async-start(bf16[32,8,4352]{2,1,0:T(8,128)(2,1)} %bitcast.36), calls=%async_computation | async-start | bytes 4456448 | tf_op jit(solution)/shard_map/all_to_all | solution.py:746
  15.8 19.0 %collective-permute-start.1 = (bf16[128,2816]{1,0:T(8,128)(2,1)S(1)}, bf16[128,2816]{1,0:T(8,128)(2,1)S(1)}, u32[]{:S(2)}, u32[]{:S(2)}) collective-permute-start(bf16[128,2816]{1,0:T(8,128)(2,1)S(1)} %copy-done.7), channel_id=1, source_target_pairs={{0,32},{32,64},{64,96},{96,0},{1,33},{33,65},{65,97},{97,1},{2,34}... | collective-permute-start | bytes 2162696 | tf_op jit(solution)/shard_map/ppermute | solution.py:751
  17.1 17.7 %collective-permute-start = (bf16[128,2816]{1,0:T(8,128)(2,1)S(1)}, bf16[128,2816]{1,0:T(8,128)(2,1)S(1)}, u32[]{:S(2)}, u32[]{:S(2)}) collective-permute-start(bf16[128,2816]{1,0:T(8,128)(2,1)S(1)} %copy-done.7), channel_id=1, source_target_pairs={{0,96},{32,0},{64,32},{96,64},{1,97},{33,1},{65,33},{97,65},{2,98}... | collective-permute-start | bytes 2162696 | tf_op jit(solution)/shard_map/ppermute | solution.py:751
  34.7 13.5 %copy-start.5 = (bf16[128,2816]{1,0:T(8,128)(2,1)}, bf16[128,2816]{1,0:T(8,128)(2,1)S(1)}, u32[]{:S(2)}) copy-start(bf16[128,2816]{1,0:T(8,128)(2,1)S(1)} %collective-permute-done.1) | copy-start | bytes 2162692
  34.8 10.3 %collective-permute-start.2 = (bf16[64,2816]{1,0:T(8,128)(2,1)S(1)}, bf16[64,2816]{1,0:T(8,128)(2,1)S(1)}, u32[]{:S(2)}, u32[]{:S(2)}) collective-permute-start(bf16[64,2816]{1,0:T(8,128)(2,1)S(1)} %slice.16), channel_id=1, source_target_pairs={{0,32},{32,64},{64,96},{96,0},{1,33},{33,65},{65,97},{97,1},{2,34}... | collective-permute-start | bytes 1081352 | tf_op jit(solution)/shard_map/ppermute | solution.py:751
  34.8 13.4 %copy-start.6 = (bf16[128,2816]{1,0:T(8,128)(2,1)}, bf16[128,2816]{1,0:T(8,128)(2,1)S(1)}, u32[]{:S(2)}) copy-start(bf16[128,2816]{1,0:T(8,128)(2,1)S(1)} %collective-permute-done) | copy-start | bytes 2162692
  34.9 10.1 %collective-permute-start.3 = (bf16[64,2816]{1,0:T(8,128)(2,1)S(1)}, bf16[64,2816]{1,0:T(8,128)(2,1)S(1)}, u32[]{:S(2)}, u32[]{:S(2)}) collective-permute-start(bf16[64,2816]{1,0:T(8,128)(2,1)S(1)} %slice.17), channel_id=1, source_target_pairs={{0,96},{32,0},{64,32},{96,64},{1,97},{33,1},{65,33},{97,65},{2,98}... | collective-permute-start | bytes 1081352 | tf_op jit(solution)/shard_map/ppermute | solution.py:751
  45.5 50.2 %collective-permute-start.5 = (bf16[256,4352]{1,0:T(8,128)(2,1)}, bf16[256,4352]{1,0:T(8,128)(2,1)}, u32[]{:S(2)}, u32[]{:S(2)}) collective-permute-start(bf16[256,4352]{1,0:T(8,128)(2,1)} %bitcast.13.refs_0_.own_ref.refs_3_), channel_id=1, source_target_pairs={{0,32},{32,64},{64,96},{96,0},{1,33},{33,65},{65,97},{97,1},{2,34}... | collective-permute-start | bytes 6684680 | tf_op jit(solution)/shard_map/ppermute | solution.py:751
  46.8 51.7 %collective-permute-start.4 = (bf16[256,4352]{1,0:T(8,128)(2,1)}, bf16[256,4352]{1,0:T(8,128)(2,1)}, u32[]{:S(2)}, u32[]{:S(2)}) collective-permute-start(bf16[256,4352]{1,0:T(8,128)(2,1)} %bitcast.13.refs_0_.own_ref.refs_3_), channel_id=1, source_target_pairs={{0,96},{32,0},{64,32},{96,64},{1,97},{33,1},{65,33},{97,65},{2,98}... | collective-permute-start | bytes 6684680 | tf_op jit(solution)/shard_map/ppermute | solution.py:751
  52.2 79.9 %all-to-all-start.1 = ((bf16[32,32,2816]{2,1,0:T(8,128)(2,1)}), bf16[32,32,2816]{2,1,0:T(8,128)(2,1)}, u32[]{:S(2)}, u32[]{:S(2)}) async-start(bf16[32,32,2816]{2,1,0:T(8,128)(2,1)} %bitcast.22), calls=%async_computation.1 | async-start | bytes 11534336 | tf_op jit(solution)/shard_map/all_to_all | solution.py:746
  98.0 25.3 %collective-permute-start.6 = (bf16[128,4352]{1,0:T(8,128)(2,1)}, bf16[128,4352]{1,0:T(8,128)(2,1)}, u32[]{:S(2)}, u32[]{:S(2)}) collective-permute-start(bf16[128,4352]{1,0:T(8,128)(2,1)} %slice.18), channel_id=1, source_target_pairs={{0,32},{32,64},{64,96},{96,0},{1,33},{33,65},{65,97},{97,1},{2,34}... | collective-permute-start | bytes 3342344 | tf_op jit(solution)/shard_map/ppermute | solution.py:751
  100.8 24.3 %collective-permute-start.7 = (bf16[128,4352]{1,0:T(8,128)(2,1)}, bf16[128,4352]{1,0:T(8,128)(2,1)}, u32[]{:S(2)}, u32[]{:S(2)}) collective-permute-start(bf16[128,4352]{1,0:T(8,128)(2,1)} %slice.19), channel_id=1, source_target_pairs={{0,96},{32,0},{64,32},{96,64},{1,97},{33,1},{65,33},{97,65},{2,98}... | collective-permute-start | bytes 3342344 | tf_op jit(solution)/shard_map/ppermute | solution.py:751
  140.6 18.9 %collective-permute-start.8 = (bf16[64,4608]{1,0:T(8,128)(2,1)}, bf16[64,4608]{1,0:T(8,128)(2,1)S(1)}, u32[]{:S(2)}, u32[]{:S(2)}) collective-permute-start(bf16[64,4608]{1,0:T(8,128)(2,1)} %get-tuple-element.78), channel_id=1, source_target_pairs={{0,32},{32,64},{64,96},{96,0},{1,33},{33,65},{65,97},{97,1},{2,34}... | collective-permute-start | bytes 1769480 | tf_op jit(solution)/shard_map/ppermute | solution.py:751
  140.8 18.7 %collective-permute-start.9 = (bf16[64,4608]{1,0:T(8,128)(2,1)}, bf16[64,4608]{1,0:T(8,128)(2,1)}, u32[]{:S(2)}, u32[]{:S(2)}) collective-permute-start(bf16[64,4608]{1,0:T(8,128)(2,1)} %get-tuple-element.79), channel_id=1, source_target_pairs={{0,96},{32,0},{64,32},{96,64},{1,97},{33,1},{65,33},{97,65},{2,98}... | collective-permute-start | bytes 1769480 | tf_op jit(solution)/shard_map/ppermute | solution.py:751
  147.6 45.8 %all-to-all-start.2 = ((bf16[32,16,2560]{2,1,0:T(8,128)(2,1)}), bf16[32,16,2560]{2,1,0:T(8,128)(2,1)S(1)}, u32[]{:S(2)}, u32[]{:S(2)}) async-start(bf16[32,16,2560]{2,1,0:T(8,128)(2,1)} %bitcast.23), calls=%async_computation.2 | async-start | bytes 5242880 | tf_op jit(solution)/shard_map/all_to_all | solution.py:746
  165.6 30.0 %collective-permute-start.14 = (bf16[128,4608]{1,0:T(8,128)(2,1)}, bf16[128,4608]{1,0:T(8,128)(2,1)}, u32[]{:S(2)}, u32[]{:S(2)}) collective-permute-start(bf16[128,4608]{1,0:T(8,128)(2,1)} %get-tuple-element.99), channel_id=1, source_target_pairs={{0,32},{32,64},{64,96},{96,0},{1,33},{33,65},{65,97},{97,1},{2,34}... | collective-permute-start | bytes 3538952 | tf_op jit(solution)/shard_map/ppermute | solution.py:751
  165.7 29.9 %collective-permute-start.15 = (bf16[128,4608]{1,0:T(8,128)(2,1)}, bf16[128,4608]{1,0:T(8,128)(2,1)}, u32[]{:S(2)}, u32[]{:S(2)}) collective-permute-start(bf16[128,4608]{1,0:T(8,128)(2,1)} %get-tuple-element.100), channel_id=1, source_target_pairs={{0,96},{32,0},{64,32},{96,64},{1,97},{33,1},{65,33},{97,65},{2,98}... | collective-permute-start | bytes 3538952 | tf_op jit(solution)/shard_map/ppermute | solution.py:751
  198.7 25.7 %copy-start.1 = (bf16[64,2560]{1,0:T(8,128)(2,1)S(1)}, bf16[64,2560]{1,0:T(8,128)(2,1)}, u32[]{:S(2)}) copy-start(bf16[64,2560]{1,0:T(8,128)(2,1)} %copy-done) | copy-start | bytes 983044
  198.7 25.7 %copy-start.2 = (bf16[64,128]{1,0:T(8,128)(2,1)S(1)}, bf16[64,128]{1,0:T(8,128)(2,1)}, u32[]{:S(2)}) copy-start(bf16[64,128]{1,0:T(8,128)(2,1)} %get-tuple-element.54.table_ref) | copy-start | bytes 49156
  198.7 25.6 %all-to-all-start.3 = ((bf16[32,4,4608]{2,1,0:T(4,128)(2,1)}), bf16[32,4,4608]{2,1,0:T(4,128)(2,1)S(1)}, u32[]{:S(2)}, u32[]{:S(2)}) async-start(bf16[32,4,4608]{2,1,0:T(4,128)(2,1)} %sum_blocks.1), calls=%async_computation.3 | async-start | bytes 2359296 | tf_op jit(solution)/shard_map/all_to_all | solution.py:746
  206.0 6.8 %collective-permute-start.10 = (bf16[32,2560]{1,0:T(8,128)(2,1)S(1)}, bf16[32,2560]{1,0:T(8,128)(2,1)S(1)}, u32[]{:S(2)}, u32[]{:S(2)}) collective-permute-start(bf16[32,2560]{1,0:T(8,128)(2,1)S(1)} %copy-done.4), channel_id=1, source_target_pairs={{0,32},{32,64},{64,96},{96,0},{1,33},{33,65},{65,97},{97,1},{2,34}... | collective-permute-start | bytes 491528 | tf_op jit(solution)/shard_map/ppermute | solution.py:751
  206.1 6.8 %collective-permute-start.11 = (bf16[32,2560]{1,0:T(8,128)(2,1)S(1)}, bf16[32,2560]{1,0:T(8,128)(2,1)S(1)}, u32[]{:S(2)}, u32[]{:S(2)}) collective-permute-start(bf16[32,2560]{1,0:T(8,128)(2,1)S(1)} %get-tuple-element.95), channel_id=1, source_target_pairs={{0,96},{32,0},{64,32},{96,64},{1,97},{33,1},{65,33},{97,65},{2,98}... | collective-permute-start | bytes 491528 | tf_op jit(solution)/shard_map/ppermute | solution.py:751
  213.0 9.4 %collective-permute-start.12 = (bf16[64,2560]{1,0:T(8,128)(2,1)S(1)}, bf16[64,2560]{1,0:T(8,128)(2,1)S(1)}, u32[]{:S(2)}, u32[]{:S(2)}) collective-permute-start(bf16[64,2560]{1,0:T(8,128)(2,1)S(1)} %get-tuple-element.96), channel_id=1, source_target_pairs={{0,32},{32,64},{64,96},{96,0},{1,33},{33,65},{65,97},{97,1},{2,34}... | collective-permute-start | bytes 983048 | tf_op jit(solution)/shard_map/ppermute | solution.py:751
  213.9 8.5 %collective-permute-start.13 = (bf16[64,2560]{1,0:T(8,128)(2,1)S(1)}, bf16[64,2560]{1,0:T(8,128)(2,1)S(1)}, u32[]{:S(2)}, u32[]{:S(2)}) collective-permute-start(bf16[64,2560]{1,0:T(8,128)(2,1)S(1)} %get-tuple-element.97), channel_id=1, source_target_pairs={{0,96},{32,0},{64,32},{96,64},{1,97},{33,1},{65,33},{97,65},{2,98}... | collective-permute-start | bytes 983048 | tf_op jit(solution)/shard_map/ppermute | solution.py:751
  (7 other events, 25.7 us)

commit v12 on v11

--- a/solution.py
+++ b/solution.py
@@ -488,6 +488,7 @@
         "sum_blocks",
         2 * rows * cols,
         8 * rows * cols,
+        mib=24,
         in_specs=[HBM, ANY, ANY],
         out_specs=ANY,
         out_shape=jax.ShapeDtypeStruct((rows // CAP, CAP, cols), BF),
@@ -806,7 +807,6 @@
     fold_own, fold_top, fold_bottom, fold_side = fold(
         home_ring.reshape(2, experts, groups * CAP, ring_cols)
     )
-    part_own, fold_top, fold_bottom = lax.optimization_barrier((part_own, fold_top, fold_bottom))
     home_wide = over_loc(sum_blocks(part_own, from_before, from_after))
     fold_next, fold_prev = add_far(fold_side, shift(fold_top, 1), shift(fold_bottom, -1))
     tokens_grad = combine(table, fold_own, shift(fold_next, 1), shift(fold_prev, -1), home_wide)

time: 229 us -> 229 us (level)
  transfers between devices with their start and end apart: 20 -> 20, of which waited for: 11 -> 10; matrix products, arithmetic and copies ran while one was open for 2% -> 2% of each run, Pallas kernels for 22% -> 23%
where the time goes in v12:
time: 229 us; the launch traced here: 228 us
  waiting for transfers between devices  90 us (39%)
  Pallas kernels  69.1 us (30%)
  starting transfers between devices  60.9 us (27%)
  local copies, waits for them, and re-layouts  6.51 us (3%)
    ppermute x16, waiting for transfers between devices, shift(): lax.ppermute(a, 'grp', [(i, (i + step) % groups) for i in range(groups)])  79 us
    all_to_all x4, starting transfers between devices, over_loc(): return lax.all_to_all(a, 'loc', split_axis=0, concat_axis=0, tiled=True)  38.6 us
    ppermute x16, starting transfers between devices, shift(): lax.ppermute(a, 'grp', [(i, (i + step) % groups) for i in range(groups)])  22.3 us
    pallas_call x3, Pallas kernels, pre(): call(functools.partial(pre_kernel, len(blocks)), 'pre', 200 * (8 * rows *...  14.3 us
    pallas_call x1, Pallas kernels, down(): call(down_kernel, 'down', 4 * rows * (cols + share) * ff, 2 * (cols + sha...  11.8 us
    all_to_all x4, waiting for transfers between devices, over_loc(): return lax.all_to_all(a, 'loc', split_axis=0, concat_axis=0, tiled=True)  11 us
    pallas_call x1, Pallas kernels, row_grads(): call(row_grads_kernel, 'row_grads', 8 * rows * half * ff, 2 * half * (row...  9.55 us
    pallas_call x1, Pallas kernels, hidden(): call(hidden_kernel, 'hidden', 4 * rows * cols * ff + 4 * span * ff * wide...  8.42 us
  transfers between devices with their start and end apart: 20, of which 10 were waited for; matrix products, arithmetic and copies ran while one was open for 2% of the time, Pallas kernels for 23%

profile of v12, /device:TPU:1, one launch (start us, length us, event | category | flops | bytes accessed | tf_op | source)
XLA Modules:
  0.0 227.5 jit_solution(10269393328443651892)
XLA Ops:
  0.6 5.4 %dispatch.1 = (bf16[64,128]{1,0:T(8,128)(2,1)}, bf16[128,2816]{1,0:T(8,128)(2,1)}, bf16[2,16,8,4352]{3,2,1,0:T(8,128)(2,1)}) custom-call(s32[8,128]{1,0:T(8,128)} %bitcast.47, bf16[8,128]{1,0:T(8,128)(2,1)} %bitcast.48, bf16[128,7168]{1,0:T(8,128)(2,1)} %g_ref.1, bf16[128,7168]{1,0:T(8,128)(2,1)} %t_ref.1), custom_call_target="tpu_custom_call" | custom-call | flops 469762048 | bytes 6422528 | tf_op jit(solution)/shard_map/dispatch/pallas_call | solution.py:110
  6.1 9.6 %all-to-all-start = ((bf16[32,8,4352]{2,1,0:T(8,128)(2,1)}), bf16[32,8,4352]{2,1,0:T(8,128)(2,1)}, u32[]{:S(2)}, u32[]{:S(2)}) async-start(bf16[32,8,4352]{2,1,0:T(8,128)(2,1)} %bitcast.36), calls=%async_computation | async-start | bytes 4456448 | tf_op jit(solution)/shard_map/all_to_all | solution.py:747
  18.6 16.1 %collective-permute-done.1 = bf16[128,2816]{1,0:T(8,128)(2,1)S(1)} collective-permute-done((bf16[128,2816]{1,0:T(8,128)(2,1)S(1)}, bf16[128,2816]{1,0:T(8,128)(2,1)S(1)}, u32[]{:S(2)}, u32[]{:S(2)}) %collective-permute-start.1) | collective-permute-done | bytes 720928 | tf_op jit(solution)/shard_map/ppermute | solution.py:752
  34.9 2.7 %collective-permute-start.3 = (bf16[64,2816]{1,0:T(8,128)(2,1)S(1)}, bf16[64,2816]{1,0:T(8,128)(2,1)S(1)}, u32[]{:S(2)}, u32[]{:S(2)}) collective-permute-start(bf16[64,2816]{1,0:T(8,128)(2,1)S(1)} %slice.17), channel_id=1, source_target_pairs={{0,96},{32,0},{64,32},{96,64},{1,97},{33,1},{65,33},{97,65},{2,98}... | collective-permute-start | bytes 1081352 | tf_op jit(solution)/shard_map/ppermute | solution.py:752
  37.6 7.4 %collective-permute-done.2 = bf16[64,2816]{1,0:T(8,128)(2,1)S(1)} collective-permute-done((bf16[64,2816]{1,0:T(8,128)(2,1)S(1)}, bf16[64,2816]{1,0:T(8,128)(2,1)S(1)}, u32[]{:S(2)}, u32[]{:S(2)}) %collective-permute-start.2) | collective-permute-done | bytes 360480 | tf_op jit(solution)/shard_map/ppermute | solution.py:752
  48.2 3.9 %regroup.1 = bf16[2,16,32,2816]{3,2,1,0:T(8,128)(2,1)} custom-call(bf16[16,8,2816]{2,1,0:T(8,128)(2,1)} %bitcast.44, bf16[16,8,2816]{2,1,0:T(8,128)(2,1)} %bitcast.43, bf16[8,8,2816]{2,1,0:T(8,128)(2,1)} %bitcast.45, bf16[8,8,2816]{2,1,0:T(8,128)(2,1)} %bitcast.46, bf16[16,8,2816]{2,1,0:T(8,128)(2,1)} %bitcast.42), custom_call_target="tpu_custom_call" | custom-call | bytes 8650752 | tf_op jit(solution)/shard_map/regroup/pallas_call | solution.py:163
  52.1 8.9 %all-to-all-start.1 = ((bf16[32,32,2816]{2,1,0:T(8,128)(2,1)}), bf16[32,32,2816]{2,1,0:T(8,128)(2,1)}, u32[]{:S(2)}, u32[]{:S(2)}) async-start(bf16[32,32,2816]{2,1,0:T(8,128)(2,1)} %bitcast.22), calls=%async_computation.1 | async-start | bytes 11534336 | tf_op jit(solution)/shard_map/all_to_all | solution.py:747
  61.1 4.3 %pre.3 = (f32[128,128]{1,0:T(8,128)}, f32[128,128]{1,0:T(8,128)}, f32[128,128]{1,0:T(8,128)}, f32[128,128]{1,0:T(8,128)}) custom-call(bf16[256,4352]{1,0:T(8,128)(2,1)} %bitcast.13.refs_0_.own_ref.refs_3_, bf16[7168,128]{1,0:T(8,128)(2,1)} %bitcast.24, bf16[7168,128]{1,0:T(8,128)(2,1)} %bitcast.30, bf16[128,7168]{1,0:T(8,128)(2,1)} %bitcast.37), custom_call_target="tpu_custom_call" | custom-call | flops 228170137600 | bytes 1336934400 | tf_op jit(solution)/shard_map/pre/pallas_call | solution.py:244
  65.4 30.3 %collective-permute-done.5.refs_1_.prev_ref.refs_7_ = bf16[256,4352]{1,0:T(8,128)(2,1)} collective-permute-done((bf16[256,4352]{1,0:T(8,128)(2,1)}, bf16[256,4352]{1,0:T(8,128)(2,1)}, u32[]{:S(2)}, u32[]{:S(2)}) %collective-permute-start.5) | collective-permute-done | bytes 2228256 | tf_op jit(solution)/shard_map/ppermute | solution.py:752
  102.9 5.6 %pre.4 = (f32[256,128]{1,0:T(8,128)}, f32[256,128]{1,0:T(8,128)}, f32[256,128]{1,0:T(8,128)}, f32[256,128]{1,0:T(8,128)}) custom-call(bf16[256,4352]{1,0:T(8,128)(2,1)} %collective-permute-done.4.refs_0_.next_ref.refs_4_, bf16[256,4352]{1,0:T(8,128)(2,1)} %collective-permute-done.5.refs_1_.prev_ref.refs_7_, bf16[7168,128]{1,0:T(8,128)(2,1)} %bitcast.25, ...), custom_call_target="tpu_custom_call" | custom-call | flops 456340275200 | bytes 1782579200 | tf_op jit(solution)/shard_map/pre/pallas_call | solution.py:244
  108.6 14.7 %collective-permute-done.6.refs_0_.top_ref.refs_5_ = bf16[128,4352]{1,0:T(8,128)(2,1)} collective-permute-done((bf16[128,4352]{1,0:T(8,128)(2,1)}, bf16[128,4352]{1,0:T(8,128)(2,1)}, u32[]{:S(2)}, u32[]{:S(2)}) %collective-permute-start.6) | collective-permute-done | bytes 1114144 | tf_op jit(solution)/shard_map/ppermute | solution.py:752
  125.0 4.4 %pre.5 = (f32[128,128]{1,0:T(8,128)}, f32[128,128]{1,0:T(8,128)}, f32[128,128]{1,0:T(8,128)}, f32[128,128]{1,0:T(8,128)}) custom-call(bf16[128,4352]{1,0:T(8,128)(2,1)} %collective-permute-done.6.refs_0_.top_ref.refs_5_, bf16[128,4352]{1,0:T(8,128)(2,1)} %collective-permute-done.7.refs_1_.bottom_ref.refs_6_, bf16[7168,128]{1,0:T(8,128)(2,1)} %bitcast.26, ...), custom_call_target="tpu_custom_call" | custom-call | flops 228170137600 | bytes 1336934400 | tf_op jit(solution)/shard_map/pre/pallas_call | solution.py:244
  132.1 8.4 %hidden.1 = (bf16[4,128,256]{2,1,0:T(8,128)(2,1)}, bf16[32,16,256]{2,1,0:T(8,128)(2,1)}, bf16[64,4608]{1,0:T(8,128)(2,1)}, bf16[64,4608]{1,0:T(8,128)(2,1)}) custom-call(bf16[1024,2816]{1,0:T(8,128)(2,1)} %bitcast.9.g_ref, bf16[128,7168]{1,0:T(8,128)(2,1)} %bitcast.40, bf16[7168,128]{1,0:T(8,128)(2,1)} %bitcast.27, bf16[7168,128]{1,0:T(8,128)(2,1)} %bitcast.33, ...), custom_call_target="tpu_custom_call" | custom-call | flops 1778384896 | bytes 9306112 | tf_op jit(solution)/shard_map/hidden/pallas_call | solution.py:349
  143.4 4.2 %ring_part.1 = bf16[512,2560]{1,0:T(8,128)(2,1)} custom-call(bf16[32,16,256]{2,1,0:T(8,128)(2,1)} %get-tuple-element.69.near_ref, bf16[7168,128]{1,0:T(8,128)(2,1)} %bitcast.28, bf16[7168,128]{1,0:T(8,128)(2,1)} %bitcast.34), custom_call_target="tpu_custom_call" | custom-call | flops 671088640 | bytes 3932160 | tf_op jit(solution)/shard_map/ring_part/pallas_call | solution.py:392
  147.6 11.9 %all-to-all-start.2 = ((bf16[32,16,2560]{2,1,0:T(8,128)(2,1)}), bf16[32,16,2560]{2,1,0:T(8,128)(2,1)S(1)}, u32[]{:S(2)}, u32[]{:S(2)}) async-start(bf16[32,16,2560]{2,1,0:T(8,128)(2,1)} %bitcast.23), calls=%async_computation.2 | async-start | bytes 5242880 | tf_op jit(solution)/shard_map/all_to_all | solution.py:747
  160.3 5.3 %side_part.1 = (bf16[128,4608]{1,0:T(8,128)(2,1)}, bf16[128,4608]{1,0:T(8,128)(2,1)}, bf16[128,4608]{1,0:T(8,128)(2,1)}) custom-call(bf16[4,128,256]{2,1,0:T(8,128)(2,1)} %get-tuple-element.86.gu_ref, bf16[7168,128]{1,0:T(8,128)(2,1)} %bitcast.29, bf16[7168,128]{1,0:T(8,128)(2,1)} %bitcast.35, bf16[64,4608]{1,0:T(8,128)(2,1)} %copy-done.8, ...), custom_call_target="tpu_custom_call" | custom-call | flops 36238786560 | bytes 283115520 | tf_op jit(solution)/shard_map/side_part/pallas_call | solution.py:445
  168.3 11.8 %down.1 = bf16[128,7168]{1,0:T(8,128)(2,1)} custom-call(bf16[1024,2816]{1,0:T(8,128)(2,1)} %bitcast.9.g_ref, f32[128,128]{1,0:T(8,128)} %get-tuple-element.89.refs_0_, f32[256,128]{1,0:T(8,128)} %get-tuple-element.90.refs_1_, f32[128,128]{1,0:T(8,128)} %get-tuple-element.91.refs_2_, bf16[256,4352]{1,0:T(8,128)(2,1)} %bitcast.13.refs_0_.own_ref.refs_3_, ...), custom_call_target="tpu_custom_call" | custom-call | flops 1879048192 | bytes 9175040 | tf_op jit(solution)/shard_map/down/pallas_call | solution.py:604
  180.2 9.5 %row_grads.1 = (bf16[2,3584,128]{2,1,0:T(8,128)(2,1)}, bf16[2,3584,128]{2,1,0:T(8,128)(2,1)}) custom-call(bf16[4,128,256]{2,1,0:T(8,128)(2,1)} %get-tuple-element.86.gu_ref, bf16[256,4352]{1,0:T(8,128)(2,1)} %bitcast.13.refs_0_.own_ref.refs_3_, bf16[256,4352]{1,0:T(8,128)(2,1)} %collective-permute-done.4.refs_0_.next_ref.refs_4_, ...), custom_call_target="tpu_custom_call" | custom-call | flops 3758096384 | bytes 11010048 | tf_op jit(solution)/shard_map/row_grads/pallas_call | solution.py:535
  189.7 4.7 %collective-permute-done.14.b_ref = bf16[128,4608]{1,0:T(8,128)(2,1)S(1)} collective-permute-done((bf16[128,4608]{1,0:T(8,128)(2,1)}, bf16[128,4608]{1,0:T(8,128)(2,1)S(1)}, u32[]{:S(2)}, u32[]{:S(2)}) %collective-permute-start.14) | collective-permute-done | bytes 1179680 | tf_op jit(solution)/shard_map/ppermute | solution.py:752
  197.0 8.2 %all-to-all-start.3 = ((bf16[32,4,4608]{2,1,0:T(4,128)(2,1)}), bf16[32,4,4608]{2,1,0:T(4,128)(2,1)}, u32[]{:S(2)}, u32[]{:S(2)}) async-start(bf16[32,4,4608]{2,1,0:T(4,128)(2,1)} %copy-done), calls=%async_computation.3 | async-start | bytes 2359296 | tf_op jit(solution)/shard_map/all_to_all | solution.py:747
  206.1 2.7 %collective-permute-start.9 = (bf16[32,2560]{1,0:T(8,128)(2,1)S(1)}, bf16[32,2560]{1,0:T(8,128)(2,1)S(1)}, u32[]{:S(2)}, u32[]{:S(2)}) collective-permute-start(bf16[32,2560]{1,0:T(8,128)(2,1)S(1)} %get-tuple-element.75), channel_id=1, source_target_pairs={{0,96},{32,0},{64,32},{96,64},{1,97},{33,1},{65,33},{97,65},{2,98}... | collective-permute-start | bytes 491528 | tf_op jit(solution)/shard_map/ppermute | solution.py:752
  208.8 4.1 %collective-permute-done.8.top_ref = bf16[32,2560]{1,0:T(8,128)(2,1)S(1)} collective-permute-done((bf16[32,2560]{1,0:T(8,128)(2,1)S(1)}, bf16[32,2560]{1,0:T(8,128)(2,1)S(1)}, u32[]{:S(2)}, u32[]{:S(2)}) %collective-permute-start.8) | collective-permute-done | bytes 163872 | tf_op jit(solution)/shard_map/ppermute | solution.py:752
  215.7 7.9 %all-to-all-done.3.wide_ref = bf16[32,4,4608]{2,1,0:T(4,128)(2,1)} async-done(((bf16[32,4,4608]{2,1,0:T(4,128)(2,1)}), bf16[32,4,4608]{2,1,0:T(4,128)(2,1)}, u32[]{:S(2)}, u32[]{:S(2)}) %all-to-all-start.3) | async-done | bytes 1179680 | tf_op jit(solution)/shard_map/all_to_all | solution.py:747
  223.6 3.8 %combine.1 = bf16[128,7168]{1,0:T(8,128)(2,1)} custom-call(bf16[64,128]{1,0:T(8,128)(2,1)S(1)} %copy-done.2, bf16[64,2560]{1,0:T(8,128)(2,1)S(1)} %get-tuple-element.72.own_ref, bf16[64,2560]{1,0:T(8,128)(2,1)S(1)} %collective-permute-done.10.left_ref, bf16[64,2560]{1,0:T(8,128)(2,1)S(1)} %collective-permute-done.11.right_ref, ...), custom_call_target="tpu_custom_call" | custom-call | flops 117440512 | bytes 3670016 | tf_op jit(solution)/shard_map/combine/pallas_call | solution.py:728
  (52 shorter events, 30.7 us)
Async XLA Ops:
  6.1 39.4 %all-to-all-start = ((bf16[32,8,4352]{2,1,0:T(8,128)(2,1)}), bf16[32,8,4352]{2,1,0:T(8,128)(2,1)}, u32[]{:S(2)}, u32[]{:S(2)}) async-start(bf16[32,8,4352]{2,1,0:T(8,128)(2,1)} %bitcast.36), calls=%async_computation | async-start | bytes 4456448 | tf_op jit(solution)/shard_map/all_to_all | solution.py:747
  15.7 19.0 %collective-permute-start.1 = (bf16[128,2816]{1,0:T(8,128)(2,1)S(1)}, bf16[128,2816]{1,0:T(8,128)(2,1)S(1)}, u32[]{:S(2)}, u32[]{:S(2)}) collective-permute-start(bf16[128,2816]{1,0:T(8,128)(2,1)S(1)} %copy-done.5), channel_id=1, source_target_pairs={{0,32},{32,64},{64,96},{96,0},{1,33},{33,65},{65,97},{97,1},{2,34}... | collective-permute-start | bytes 2162696 | tf_op jit(solution)/shard_map/ppermute | solution.py:752
  17.1 17.7 %collective-permute-start = (bf16[128,2816]{1,0:T(8,128)(2,1)S(1)}, bf16[128,2816]{1,0:T(8,128)(2,1)S(1)}, u32[]{:S(2)}, u32[]{:S(2)}) collective-permute-start(bf16[128,2816]{1,0:T(8,128)(2,1)S(1)} %copy-done.5), channel_id=1, source_target_pairs={{0,96},{32,0},{64,32},{96,64},{1,97},{33,1},{65,33},{97,65},{2,98}... | collective-permute-start | bytes 2162696 | tf_op jit(solution)/shard_map/ppermute | solution.py:752
  34.7 13.5 %copy-start.3 = (bf16[128,2816]{1,0:T(8,128)(2,1)}, bf16[128,2816]{1,0:T(8,128)(2,1)S(1)}, u32[]{:S(2)}) copy-start(bf16[128,2816]{1,0:T(8,128)(2,1)S(1)} %collective-permute-done.1) | copy-start | bytes 2162692
  34.7 10.3 %collective-permute-start.2 = (bf16[64,2816]{1,0:T(8,128)(2,1)S(1)}, bf16[64,2816]{1,0:T(8,128)(2,1)S(1)}, u32[]{:S(2)}, u32[]{:S(2)}) collective-permute-start(bf16[64,2816]{1,0:T(8,128)(2,1)S(1)} %slice.16), channel_id=1, source_target_pairs={{0,32},{32,64},{64,96},{96,0},{1,33},{33,65},{65,97},{97,1},{2,34}... | collective-permute-start | bytes 1081352 | tf_op jit(solution)/shard_map/ppermute | solution.py:752
  34.8 13.4 %copy-start.4 = (bf16[128,2816]{1,0:T(8,128)(2,1)}, bf16[128,2816]{1,0:T(8,128)(2,1)S(1)}, u32[]{:S(2)}) copy-start(bf16[128,2816]{1,0:T(8,128)(2,1)S(1)} %collective-permute-done) | copy-start | bytes 2162692
  34.9 10.1 %collective-permute-start.3 = (bf16[64,2816]{1,0:T(8,128)(2,1)S(1)}, bf16[64,2816]{1,0:T(8,128)(2,1)S(1)}, u32[]{:S(2)}, u32[]{:S(2)}) collective-permute-start(bf16[64,2816]{1,0:T(8,128)(2,1)S(1)} %slice.17), channel_id=1, source_target_pairs={{0,96},{32,0},{64,32},{96,64},{1,97},{33,1},{65,33},{97,65},{2,98}... | collective-permute-start | bytes 1081352 | tf_op jit(solution)/shard_map/ppermute | solution.py:752
  45.5 50.2 %collective-permute-start.5 = (bf16[256,4352]{1,0:T(8,128)(2,1)}, bf16[256,4352]{1,0:T(8,128)(2,1)}, u32[]{:S(2)}, u32[]{:S(2)}) collective-permute-start(bf16[256,4352]{1,0:T(8,128)(2,1)} %bitcast.13.refs_0_.own_ref.refs_3_), channel_id=1, source_target_pairs={{0,32},{32,64},{64,96},{96,0},{1,33},{33,65},{65,97},{97,1},{2,34}... | collective-permute-start | bytes 6684680 | tf_op jit(solution)/shard_map/ppermute | solution.py:752
  46.8 51.7 %collective-permute-start.4 = (bf16[256,4352]{1,0:T(8,128)(2,1)}, bf16[256,4352]{1,0:T(8,128)(2,1)}, u32[]{:S(2)}, u32[]{:S(2)}) collective-permute-start(bf16[256,4352]{1,0:T(8,128)(2,1)} %bitcast.13.refs_0_.own_ref.refs_3_), channel_id=1, source_target_pairs={{0,96},{32,0},{64,32},{96,64},{1,97},{33,1},{65,33},{97,65},{2,98}... | collective-permute-start | bytes 6684680 | tf_op jit(solution)/shard_map/ppermute | solution.py:752
  52.1 79.9 %all-to-all-start.1 = ((bf16[32,32,2816]{2,1,0:T(8,128)(2,1)}), bf16[32,32,2816]{2,1,0:T(8,128)(2,1)}, u32[]{:S(2)}, u32[]{:S(2)}) async-start(bf16[32,32,2816]{2,1,0:T(8,128)(2,1)} %bitcast.22), calls=%async_computation.1 | async-start | bytes 11534336 | tf_op jit(solution)/shard_map/all_to_all | solution.py:747
  98.0 25.3 %collective-permute-start.6 = (bf16[128,4352]{1,0:T(8,128)(2,1)}, bf16[128,4352]{1,0:T(8,128)(2,1)}, u32[]{:S(2)}, u32[]{:S(2)}) collective-permute-start(bf16[128,4352]{1,0:T(8,128)(2,1)} %slice.18), channel_id=1, source_target_pairs={{0,32},{32,64},{64,96},{96,0},{1,33},{33,65},{65,97},{97,1},{2,34}... | collective-permute-start | bytes 3342344 | tf_op jit(solution)/shard_map/ppermute | solution.py:752
  100.8 24.3 %collective-permute-start.7 = (bf16[128,4352]{1,0:T(8,128)(2,1)}, bf16[128,4352]{1,0:T(8,128)(2,1)}, u32[]{:S(2)}, u32[]{:S(2)}) collective-permute-start(bf16[128,4352]{1,0:T(8,128)(2,1)} %slice.19), channel_id=1, source_target_pairs={{0,96},{32,0},{64,32},{96,64},{1,97},{33,1},{65,33},{97,65},{2,98}... | collective-permute-start | bytes 3342344 | tf_op jit(solution)/shard_map/ppermute | solution.py:752
  140.5 19.0 %collective-permute-start.12 = (bf16[64,4608]{1,0:T(8,128)(2,1)}, bf16[64,4608]{1,0:T(8,128)(2,1)S(1)}, u32[]{:S(2)}, u32[]{:S(2)}) collective-permute-start(bf16[64,4608]{1,0:T(8,128)(2,1)} %get-tuple-element.79), channel_id=1, source_target_pairs={{0,32},{32,64},{64,96},{96,0},{1,33},{33,65},{65,97},{97,1},{2,34}... | collective-permute-start | bytes 1769480 | tf_op jit(solution)/shard_map/ppermute | solution.py:752
  140.8 18.7 %collective-permute-start.13 = (bf16[64,4608]{1,0:T(8,128)(2,1)}, bf16[64,4608]{1,0:T(8,128)(2,1)}, u32[]{:S(2)}, u32[]{:S(2)}) collective-permute-start(bf16[64,4608]{1,0:T(8,128)(2,1)} %get-tuple-element.80), channel_id=1, source_target_pairs={{0,96},{32,0},{64,32},{96,64},{1,97},{33,1},{65,33},{97,65},{2,98}... | collective-permute-start | bytes 1769480 | tf_op jit(solution)/shard_map/ppermute | solution.py:752
  147.6 49.4 %all-to-all-start.2 = ((bf16[32,16,2560]{2,1,0:T(8,128)(2,1)}), bf16[32,16,2560]{2,1,0:T(8,128)(2,1)S(1)}, u32[]{:S(2)}, u32[]{:S(2)}) async-start(bf16[32,16,2560]{2,1,0:T(8,128)(2,1)} %bitcast.23), calls=%async_computation.2 | async-start | bytes 5242880 | tf_op jit(solution)/shard_map/all_to_all | solution.py:747
  165.6 28.8 %collective-permute-start.14 = (bf16[128,4608]{1,0:T(8,128)(2,1)}, bf16[128,4608]{1,0:T(8,128)(2,1)S(1)}, u32[]{:S(2)}, u32[]{:S(2)}) collective-permute-start(bf16[128,4608]{1,0:T(8,128)(2,1)} %get-tuple-element.93), channel_id=1, source_target_pairs={{0,32},{32,64},{64,96},{96,0},{1,33},{33,65},{65,97},{97,1},{2,34}... | collective-permute-start | bytes 3538952 | tf_op jit(solution)/shard_map/ppermute | solution.py:752
  165.7 28.7 %collective-permute-start.15 = (bf16[128,4608]{1,0:T(8,128)(2,1)}, bf16[128,4608]{1,0:T(8,128)(2,1)S(1)}, u32[]{:S(2)}, u32[]{:S(2)}) collective-permute-start(bf16[128,4608]{1,0:T(8,128)(2,1)} %get-tuple-element.94), channel_id=1, source_target_pairs={{0,96},{32,0},{64,32},{96,64},{1,97},{33,1},{65,33},{97,65},{2,98}... | collective-permute-start | bytes 3538952 | tf_op jit(solution)/shard_map/ppermute | solution.py:752
  180.2 14.2 %copy-start.1 = (bf16[128,4608]{1,0:T(8,128)(2,1)S(1)}, bf16[128,4608]{1,0:T(8,128)(2,1)}, u32[]{:S(2)}) copy-start(bf16[128,4608]{1,0:T(8,128)(2,1)} %get-tuple-element.92.a_ref) | copy-start | bytes 3538948
  197.0 26.6 %all-to-all-start.3 = ((bf16[32,4,4608]{2,1,0:T(4,128)(2,1)}), bf16[32,4,4608]{2,1,0:T(4,128)(2,1)}, u32[]{:S(2)}, u32[]{:S(2)}) async-start(bf16[32,4,4608]{2,1,0:T(4,128)(2,1)} %copy-done), calls=%async_computation.3 | async-start | bytes 2359296 | tf_op jit(solution)/shard_map/all_to_all | solution.py:747
  205.2 18.4 %copy-start.2 = (bf16[64,128]{1,0:T(8,128)(2,1)S(1)}, bf16[64,128]{1,0:T(8,128)(2,1)}, u32[]{:S(2)}) copy-start(bf16[64,128]{1,0:T(8,128)(2,1)} %get-tuple-element.51.table_ref) | copy-start | bytes 49156
  206.0 6.9 %collective-permute-start.8 = (bf16[32,2560]{1,0:T(8,128)(2,1)S(1)}, bf16[32,2560]{1,0:T(8,128)(2,1)S(1)}, u32[]{:S(2)}, u32[]{:S(2)}) collective-permute-start(bf16[32,2560]{1,0:T(8,128)(2,1)S(1)} %get-tuple-element.74), channel_id=1, source_target_pairs={{0,32},{32,64},{64,96},{96,0},{1,33},{33,65},{65,97},{97,1},{2,34}... | collective-permute-start | bytes 491528 | tf_op jit(solution)/shard_map/ppermute | solution.py:752
  206.1 6.8 %collective-permute-start.9 = (bf16[32,2560]{1,0:T(8,128)(2,1)S(1)}, bf16[32,2560]{1,0:T(8,128)(2,1)S(1)}, u32[]{:S(2)}, u32[]{:S(2)}) collective-permute-start(bf16[32,2560]{1,0:T(8,128)(2,1)S(1)} %get-tuple-element.75), channel_id=1, source_target_pairs={{0,96},{32,0},{64,32},{96,64},{1,97},{33,1},{65,33},{97,65},{2,98}... | collective-permute-start | bytes 491528 | tf_op jit(solution)/shard_map/ppermute | solution.py:752
  213.0 10.6 %collective-permute-start.10 = (bf16[64,2560]{1,0:T(8,128)(2,1)S(1)}, bf16[64,2560]{1,0:T(8,128)(2,1)S(1)}, u32[]{:S(2)}, u32[]{:S(2)}) collective-permute-start(bf16[64,2560]{1,0:T(8,128)(2,1)S(1)} %get-tuple-element.76), channel_id=1, source_target_pairs={{0,32},{32,64},{64,96},{96,0},{1,33},{33,65},{65,97},{97,1},{2,34}... | collective-permute-start | bytes 983048 | tf_op jit(solution)/shard_map/ppermute | solution.py:752
  213.9 9.7 %collective-permute-start.11 = (bf16[64,2560]{1,0:T(8,128)(2,1)S(1)}, bf16[64,2560]{1,0:T(8,128)(2,1)S(1)}, u32[]{:S(2)}, u32[]{:S(2)}) collective-permute-start(bf16[64,2560]{1,0:T(8,128)(2,1)S(1)} %get-tuple-element.77), channel_id=1, source_target_pairs={{0,96},{32,0},{64,32},{96,64},{1,97},{33,1},{65,33},{97,65},{2,98}... | collective-permute-start | bytes 983048 | tf_op jit(solution)/shard_map/ppermute | solution.py:752
  (5 other events, 18.0 us)

commit v13 on v12

--- a/solution.py
+++ b/solution.py
@@ -766,7 +766,7 @@
     buf = experts * CAP
     unit = 2 * CAP
     share = 768
-    ring_cols = 2560
+    ring_cols = 3072
     wide_cols = width - ring_cols
 
     w_gate, w_up, w_down = gate_weight[0], up_weight[0], down_weight[0]

time: 229 us -> 230 us (level)
  waiting for transfers between devices: 90 us -> 94 us
  starting transfers between devices: 60.9 us -> 57.7 us
    all_to_all x4, waiting for transfers between devices: 11 us -> 14.6 us  [over_loc(): return lax.all_to_all(a, 'loc', split_axis=0, concat_axis=0, tiled=True)]
    all_to_all x4, starting transfers between devices: 38.6 us -> 35.4 us  [over_loc(): return lax.all_to_all(a, 'loc', split_axis=0, concat_axis=0, tiled=True)]
  transfers between devices with their start and end apart: 20 -> 20, of which waited for: 10 -> 12; matrix products, arithmetic and copies ran while one was open for 2% -> 2% of each run, Pallas kernels for 23% -> 23%
where the time goes in v13:
time: 230 us; the launch traced here: 228 us
  waiting for transfers between devices  94 us (41%)
  Pallas kernels  69.6 us (30%)
  starting transfers between devices  57.7 us (25%)
  local copies, waits for them, and re-layouts  5.67 us (2%)
    ppermute x16, waiting for transfers between devices, shift(): lax.ppermute(a, 'grp', [(i, (i + step) % groups) for i in range(groups)])  79.4 us
    all_to_all x4, starting transfers between devices, over_loc(): return lax.all_to_all(a, 'loc', split_axis=0, concat_axis=0, tiled=True)  35.4 us
    ppermute x16, starting transfers between devices, shift(): lax.ppermute(a, 'grp', [(i, (i + step) % groups) for i in range(groups)])  22.2 us
    all_to_all x4, waiting for transfers between devices, over_loc(): return lax.all_to_all(a, 'loc', split_axis=0, concat_axis=0, tiled=True)  14.6 us
    pallas_call x3, Pallas kernels, pre(): call(functools.partial(pre_kernel, len(blocks)), 'pre', 200 * (8 * rows *...  14.4 us
    pallas_call x1, Pallas kernels, down(): call(down_kernel, 'down', 4 * rows * (cols + share) * ff, 2 * (cols + sha...  11.8 us
    pallas_call x1, Pallas kernels, row_grads(): call(row_grads_kernel, 'row_grads', 8 * rows * half * ff, 2 * half * (row...  9.54 us
    pallas_call x1, Pallas kernels, hidden(): call(hidden_kernel, 'hidden', 4 * rows * cols * ff + 4 * span * ff * wide...  8.31 us
  transfers between devices with their start and end apart: 20, of which 12 were waited for; matrix products, arithmetic and copies ran while one was open for 2% of the time, Pallas kernels for 23%

profile of v13, /device:TPU:1, one launch (start us, length us, event | category | flops | bytes accessed | tf_op | source)
XLA Modules:
  0.0 227.9 jit_solution(9964221040215214475)
XLA Ops:
  0.6 5.4 %dispatch.1 = (bf16[64,128]{1,0:T(8,128)(2,1)}, bf16[128,2816]{1,0:T(8,128)(2,1)}, bf16[2,16,8,4352]{3,2,1,0:T(8,128)(2,1)}) custom-call(s32[8,128]{1,0:T(8,128)} %bitcast.47, bf16[8,128]{1,0:T(8,128)(2,1)} %bitcast.48, bf16[128,7168]{1,0:T(8,128)(2,1)} %g_ref.1, bf16[128,7168]{1,0:T(8,128)(2,1)} %t_ref.1), custom_call_target="tpu_custom_call" | custom-call | flops 469762048 | bytes 6422528 | tf_op jit(solution)/shard_map/dispatch/pallas_call | solution.py:110
  6.1 9.6 %all-to-all-start = ((bf16[32,8,4352]{2,1,0:T(8,128)(2,1)}), bf16[32,8,4352]{2,1,0:T(8,128)(2,1)}, u32[]{:S(2)}, u32[]{:S(2)}) async-start(bf16[32,8,4352]{2,1,0:T(8,128)(2,1)} %bitcast.36), calls=%async_computation | async-start | bytes 4456448 | tf_op jit(solution)/shard_map/all_to_all | solution.py:747
  18.6 16.1 %collective-permute-done.1 = bf16[128,2816]{1,0:T(8,128)(2,1)S(1)} collective-permute-done((bf16[128,2816]{1,0:T(8,128)(2,1)S(1)}, bf16[128,2816]{1,0:T(8,128)(2,1)S(1)}, u32[]{:S(2)}, u32[]{:S(2)}) %collective-permute-start.1) | collective-permute-done | bytes 720928 | tf_op jit(solution)/shard_map/ppermute | solution.py:752
  34.9 2.7 %collective-permute-start.3 = (bf16[64,2816]{1,0:T(8,128)(2,1)S(1)}, bf16[64,2816]{1,0:T(8,128)(2,1)S(1)}, u32[]{:S(2)}, u32[]{:S(2)}) collective-permute-start(bf16[64,2816]{1,0:T(8,128)(2,1)S(1)} %slice.17), channel_id=1, source_target_pairs={{0,96},{32,0},{64,32},{96,64},{1,97},{33,1},{65,33},{97,65},{2,98}... | collective-permute-start | bytes 1081352 | tf_op jit(solution)/shard_map/ppermute | solution.py:752
  37.6 7.4 %collective-permute-done.2 = bf16[64,2816]{1,0:T(8,128)(2,1)S(1)} collective-permute-done((bf16[64,2816]{1,0:T(8,128)(2,1)S(1)}, bf16[64,2816]{1,0:T(8,128)(2,1)S(1)}, u32[]{:S(2)}, u32[]{:S(2)}) %collective-permute-start.2) | collective-permute-done | bytes 360480 | tf_op jit(solution)/shard_map/ppermute | solution.py:752
  48.2 3.9 %regroup.1 = bf16[2,16,32,2816]{3,2,1,0:T(8,128)(2,1)} custom-call(bf16[16,8,2816]{2,1,0:T(8,128)(2,1)} %bitcast.44, bf16[16,8,2816]{2,1,0:T(8,128)(2,1)} %bitcast.43, bf16[8,8,2816]{2,1,0:T(8,128)(2,1)} %bitcast.45, bf16[8,8,2816]{2,1,0:T(8,128)(2,1)} %bitcast.46, bf16[16,8,2816]{2,1,0:T(8,128)(2,1)} %bitcast.42), custom_call_target="tpu_custom_call" | custom-call | bytes 8650752 | tf_op jit(solution)/shard_map/regroup/pallas_call | solution.py:163
  52.2 8.9 %all-to-all-start.1 = ((bf16[32,32,2816]{2,1,0:T(8,128)(2,1)}), bf16[32,32,2816]{2,1,0:T(8,128)(2,1)}, u32[]{:S(2)}, u32[]{:S(2)}) async-start(bf16[32,32,2816]{2,1,0:T(8,128)(2,1)} %bitcast.22), calls=%async_computation.1 | async-start | bytes 11534336 | tf_op jit(solution)/shard_map/all_to_all | solution.py:747
  61.1 4.3 %pre.3 = (f32[128,128]{1,0:T(8,128)}, f32[128,128]{1,0:T(8,128)}, f32[128,128]{1,0:T(8,128)}, f32[128,128]{1,0:T(8,128)}) custom-call(bf16[256,4352]{1,0:T(8,128)(2,1)} %bitcast.13.refs_0_.own_ref.refs_3_, bf16[7168,128]{1,0:T(8,128)(2,1)} %bitcast.24, bf16[7168,128]{1,0:T(8,128)(2,1)} %bitcast.30, bf16[128,7168]{1,0:T(8,128)(2,1)} %bitcast.37), custom_call_target="tpu_custom_call" | custom-call | flops 228170137600 | bytes 1336934400 | tf_op jit(solution)/shard_map/pre/pallas_call | solution.py:244
  65.4 30.2 %collective-permute-done.5.refs_1_.prev_ref.refs_7_ = bf16[256,4352]{1,0:T(8,128)(2,1)} collective-permute-done((bf16[256,4352]{1,0:T(8,128)(2,1)}, bf16[256,4352]{1,0:T(8,128)(2,1)}, u32[]{:S(2)}, u32[]{:S(2)}) %collective-permute-start.5) | collective-permute-done | bytes 2228256 | tf_op jit(solution)/shard_map/ppermute | solution.py:752
  102.9 5.6 %pre.4 = (f32[256,128]{1,0:T(8,128)}, f32[256,128]{1,0:T(8,128)}, f32[256,128]{1,0:T(8,128)}, f32[256,128]{1,0:T(8,128)}) custom-call(bf16[256,4352]{1,0:T(8,128)(2,1)} %collective-permute-done.4.refs_0_.next_ref.refs_4_, bf16[256,4352]{1,0:T(8,128)(2,1)} %collective-permute-done.5.refs_1_.prev_ref.refs_7_, bf16[7168,128]{1,0:T(8,128)(2,1)} %bitcast.25, ...), custom_call_target="tpu_custom_call" | custom-call | flops 456340275200 | bytes 1782579200 | tf_op jit(solution)/shard_map/pre/pallas_call | solution.py:244
  108.6 14.7 %collective-permute-done.6.refs_0_.top_ref.refs_5_ = bf16[128,4352]{1,0:T(8,128)(2,1)} collective-permute-done((bf16[128,4352]{1,0:T(8,128)(2,1)}, bf16[128,4352]{1,0:T(8,128)(2,1)}, u32[]{:S(2)}, u32[]{:S(2)}) %collective-permute-start.6) | collective-permute-done | bytes 1114144 | tf_op jit(solution)/shard_map/ppermute | solution.py:752
  125.0 4.4 %pre.5 = (f32[128,128]{1,0:T(8,128)}, f32[128,128]{1,0:T(8,128)}, f32[128,128]{1,0:T(8,128)}, f32[128,128]{1,0:T(8,128)}) custom-call(bf16[128,4352]{1,0:T(8,128)(2,1)} %collective-permute-done.6.refs_0_.top_ref.refs_5_, bf16[128,4352]{1,0:T(8,128)(2,1)} %collective-permute-done.7.refs_1_.bottom_ref.refs_6_, bf16[7168,128]{1,0:T(8,128)(2,1)} %bitcast.26, ...), custom_call_target="tpu_custom_call" | custom-call | flops 228170137600 | bytes 1336934400 | tf_op jit(solution)/shard_map/pre/pallas_call | solution.py:244
  132.1 8.3 %hidden.1 = (bf16[4,128,256]{2,1,0:T(8,128)(2,1)}, bf16[32,16,256]{2,1,0:T(8,128)(2,1)}, bf16[64,4096]{1,0:T(8,128)(2,1)}, bf16[64,4096]{1,0:T(8,128)(2,1)}) custom-call(bf16[1024,2816]{1,0:T(8,128)(2,1)} %bitcast.9.g_ref, bf16[128,7168]{1,0:T(8,128)(2,1)} %bitcast.40, bf16[7168,128]{1,0:T(8,128)(2,1)} %bitcast.27, bf16[7168,128]{1,0:T(8,128)(2,1)} %bitcast.33, ...), custom_call_target="tpu_custom_call" | custom-call | flops 1744830464 | bytes 8912896 | tf_op jit(solution)/shard_map/hidden/pallas_call | solution.py:349
  143.3 4.5 %ring_part.1 = bf16[512,3072]{1,0:T(8,128)(2,1)} custom-call(bf16[32,16,256]{2,1,0:T(8,128)(2,1)} %get-tuple-element.69.near_ref, bf16[7168,128]{1,0:T(8,128)(2,1)} %bitcast.28, bf16[7168,128]{1,0:T(8,128)(2,1)} %bitcast.34), custom_call_target="tpu_custom_call" | custom-call | flops 805306368 | bytes 4718592 | tf_op jit(solution)/shard_map/ring_part/pallas_call | solution.py:392
  147.8 11.9 %all-to-all-start.2 = ((bf16[32,16,3072]{2,1,0:T(8,128)(2,1)}), bf16[32,16,3072]{2,1,0:T(8,128)(2,1)S(1)}, u32[]{:S(2)}, u32[]{:S(2)}) async-start(bf16[32,16,3072]{2,1,0:T(8,128)(2,1)} %bitcast.23), calls=%async_computation.2 | async-start | bytes 6291456 | tf_op jit(solution)/shard_map/all_to_all | solution.py:747
  159.7 5.0 %side_part.1 = (bf16[128,4096]{1,0:T(8,128)(2,1)}, bf16[128,4096]{1,0:T(8,128)(2,1)}, bf16[128,4096]{1,0:T(8,128)(2,1)}) custom-call(bf16[4,128,256]{2,1,0:T(8,128)(2,1)} %get-tuple-element.86.gu_ref, bf16[7168,128]{1,0:T(8,128)(2,1)} %bitcast.29, bf16[7168,128]{1,0:T(8,128)(2,1)} %bitcast.35, bf16[64,4096]{1,0:T(8,128)(2,1)} %collective-permute-done.12.top_ref, ...), custom_call_target="tpu_custom_call" | custom-call | flops 32212254720 | bytes 251658240 | tf_op jit(solution)/shard_map/side_part/pallas_call | solution.py:445
  164.8 2.7 %collective-permute-start.15 = (bf16[128,4096]{1,0:T(8,128)(2,1)}, bf16[128,4096]{1,0:T(8,128)(2,1)S(1)}, u32[]{:S(2)}, u32[]{:S(2)}) collective-permute-start(bf16[128,4096]{1,0:T(8,128)(2,1)} %get-tuple-element.94), channel_id=1, source_target_pairs={{0,96},{32,0},{64,32},{96,64},{1,97},{33,1},{65,33},{97,65},{2,98}... | collective-permute-start | bytes 3145736 | tf_op jit(solution)/shard_map/ppermute | solution.py:752
  167.4 11.8 %down.1 = bf16[128,7168]{1,0:T(8,128)(2,1)} custom-call(bf16[1024,2816]{1,0:T(8,128)(2,1)} %bitcast.9.g_ref, f32[128,128]{1,0:T(8,128)} %get-tuple-element.89.refs_0_, f32[256,128]{1,0:T(8,128)} %get-tuple-element.90.refs_1_, f32[128,128]{1,0:T(8,128)} %get-tuple-element.91.refs_2_, bf16[256,4352]{1,0:T(8,128)(2,1)} %bitcast.13.refs_0_.own_ref.refs_3_, ...), custom_call_target="tpu_custom_call" | custom-call | flops 1879048192 | bytes 9175040 | tf_op jit(solution)/shard_map/down/pallas_call | solution.py:604
  179.3 9.5 %row_grads.1 = (bf16[2,3584,128]{2,1,0:T(8,128)(2,1)}, bf16[2,3584,128]{2,1,0:T(8,128)(2,1)}) custom-call(bf16[4,128,256]{2,1,0:T(8,128)(2,1)} %get-tuple-element.86.gu_ref, bf16[256,4352]{1,0:T(8,128)(2,1)} %bitcast.13.refs_0_.own_ref.refs_3_, bf16[256,4352]{1,0:T(8,128)(2,1)} %collective-permute-done.4.refs_0_.next_ref.refs_4_, ...), custom_call_target="tpu_custom_call" | custom-call | flops 3758096384 | bytes 11010048 | tf_op jit(solution)/shard_map/row_grads/pallas_call | solution.py:535
  193.5 5.9 %all-to-all-done.2 = bf16[32,16,3072]{2,1,0:T(8,128)(2,1)S(1)} async-done(((bf16[32,16,3072]{2,1,0:T(8,128)(2,1)}), bf16[32,16,3072]{2,1,0:T(8,128)(2,1)S(1)}, u32[]{:S(2)}, u32[]{:S(2)}) %all-to-all-start.2) | async-done | bytes 3145760 | tf_op jit(solution)/shard_map/all_to_all | solution.py:747
  199.4 5.0 %all-to-all-start.3 = ((bf16[32,4,4096]{2,1,0:T(4,128)(2,1)}), bf16[32,4,4096]{2,1,0:T(4,128)(2,1)}, u32[]{:S(2)}, u32[]{:S(2)}) async-start(bf16[32,4,4096]{2,1,0:T(4,128)(2,1)} %copy-done), calls=%async_computation.3 | async-start | bytes 2097152 | tf_op jit(solution)/shard_map/all_to_all | solution.py:747
  208.2 4.8 %collective-permute-done.8.top_ref = bf16[32,3072]{1,0:T(8,128)(2,1)S(1)} collective-permute-done((bf16[32,3072]{1,0:T(8,128)(2,1)S(1)}, bf16[32,3072]{1,0:T(8,128)(2,1)S(1)}, u32[]{:S(2)}, u32[]{:S(2)}) %collective-permute-start.8) | collective-permute-done | bytes 196640 | tf_op jit(solution)/shard_map/ppermute | solution.py:752
  215.8 5.6 %all-to-all-done.3.wide_ref = bf16[32,4,4096]{2,1,0:T(4,128)(2,1)} async-done(((bf16[32,4,4096]{2,1,0:T(4,128)(2,1)}), bf16[32,4,4096]{2,1,0:T(4,128)(2,1)}, u32[]{:S(2)}, u32[]{:S(2)}) %all-to-all-start.3) | async-done | bytes 1048608 | tf_op jit(solution)/shard_map/all_to_all | solution.py:747
  224.0 3.8 %combine.1 = bf16[128,7168]{1,0:T(8,128)(2,1)} custom-call(bf16[64,128]{1,0:T(8,128)(2,1)S(1)} %copy-done.2, bf16[64,3072]{1,0:T(8,128)(2,1)S(1)} %get-tuple-element.72.own_ref, bf16[64,3072]{1,0:T(8,128)(2,1)S(1)} %collective-permute-done.10.left_ref, bf16[64,3072]{1,0:T(8,128)(2,1)S(1)} %collective-permute-done.11.right_ref, ...), custom_call_target="tpu_custom_call" | custom-call | flops 117440512 | bytes 3670016 | tf_op jit(solution)/shard_map/combine/pallas_call | solution.py:728
  (50 shorter events, 34.7 us)
Async XLA Ops:
  6.1 39.4 %all-to-all-start = ((bf16[32,8,4352]{2,1,0:T(8,128)(2,1)}), bf16[32,8,4352]{2,1,0:T(8,128)(2,1)}, u32[]{:S(2)}, u32[]{:S(2)}) async-start(bf16[32,8,4352]{2,1,0:T(8,128)(2,1)} %bitcast.36), calls=%async_computation | async-start | bytes 4456448 | tf_op jit(solution)/shard_map/all_to_all | solution.py:747
  15.7 19.0 %collective-permute-start.1 = (bf16[128,2816]{1,0:T(8,128)(2,1)S(1)}, bf16[128,2816]{1,0:T(8,128)(2,1)S(1)}, u32[]{:S(2)}, u32[]{:S(2)}) collective-permute-start(bf16[128,2816]{1,0:T(8,128)(2,1)S(1)} %copy-done.5), channel_id=1, source_target_pairs={{0,32},{32,64},{64,96},{96,0},{1,33},{33,65},{65,97},{97,1},{2,34}... | collective-permute-start | bytes 2162696 | tf_op jit(solution)/shard_map/ppermute | solution.py:752
  17.1 17.7 %collective-permute-start = (bf16[128,2816]{1,0:T(8,128)(2,1)S(1)}, bf16[128,2816]{1,0:T(8,128)(2,1)S(1)}, u32[]{:S(2)}, u32[]{:S(2)}) collective-permute-start(bf16[128,2816]{1,0:T(8,128)(2,1)S(1)} %copy-done.5), channel_id=1, source_target_pairs={{0,96},{32,0},{64,32},{96,64},{1,97},{33,1},{65,33},{97,65},{2,98}... | collective-permute-start | bytes 2162696 | tf_op jit(solution)/shard_map/ppermute | solution.py:752
  34.7 13.5 %copy-start.3 = (bf16[128,2816]{1,0:T(8,128)(2,1)}, bf16[128,2816]{1,0:T(8,128)(2,1)S(1)}, u32[]{:S(2)}) copy-start(bf16[128,2816]{1,0:T(8,128)(2,1)S(1)} %collective-permute-done.1) | copy-start | bytes 2162692
  34.7 10.3 %collective-permute-start.2 = (bf16[64,2816]{1,0:T(8,128)(2,1)S(1)}, bf16[64,2816]{1,0:T(8,128)(2,1)S(1)}, u32[]{:S(2)}, u32[]{:S(2)}) collective-permute-start(bf16[64,2816]{1,0:T(8,128)(2,1)S(1)} %slice.16), channel_id=1, source_target_pairs={{0,32},{32,64},{64,96},{96,0},{1,33},{33,65},{65,97},{97,1},{2,34}... | collective-permute-start | bytes 1081352 | tf_op jit(solution)/shard_map/ppermute | solution.py:752
  34.8 13.4 %copy-start.4 = (bf16[128,2816]{1,0:T(8,128)(2,1)}, bf16[128,2816]{1,0:T(8,128)(2,1)S(1)}, u32[]{:S(2)}) copy-start(bf16[128,2816]{1,0:T(8,128)(2,1)S(1)} %collective-permute-done) | copy-start | bytes 2162692
  34.9 10.1 %collective-permute-start.3 = (bf16[64,2816]{1,0:T(8,128)(2,1)S(1)}, bf16[64,2816]{1,0:T(8,128)(2,1)S(1)}, u32[]{:S(2)}, u32[]{:S(2)}) collective-permute-start(bf16[64,2816]{1,0:T(8,128)(2,1)S(1)} %slice.17), channel_id=1, source_target_pairs={{0,96},{32,0},{64,32},{96,64},{1,97},{33,1},{65,33},{97,65},{2,98}... | collective-permute-start | bytes 1081352 | tf_op jit(solution)/shard_map/ppermute | solution.py:752
  45.5 50.2 %collective-permute-start.5 = (bf16[256,4352]{1,0:T(8,128)(2,1)}, bf16[256,4352]{1,0:T(8,128)(2,1)}, u32[]{:S(2)}, u32[]{:S(2)}) collective-permute-start(bf16[256,4352]{1,0:T(8,128)(2,1)} %bitcast.13.refs_0_.own_ref.refs_3_), channel_id=1, source_target_pairs={{0,32},{32,64},{64,96},{96,0},{1,33},{33,65},{65,97},{97,1},{2,34}... | collective-permute-start | bytes 6684680 | tf_op jit(solution)/shard_map/ppermute | solution.py:752
  46.8 51.7 %collective-permute-start.4 = (bf16[256,4352]{1,0:T(8,128)(2,1)}, bf16[256,4352]{1,0:T(8,128)(2,1)}, u32[]{:S(2)}, u32[]{:S(2)}) collective-permute-start(bf16[256,4352]{1,0:T(8,128)(2,1)} %bitcast.13.refs_0_.own_ref.refs_3_), channel_id=1, source_target_pairs={{0,96},{32,0},{64,32},{96,64},{1,97},{33,1},{65,33},{97,65},{2,98}... | collective-permute-start | bytes 6684680 | tf_op jit(solution)/shard_map/ppermute | solution.py:752
  52.2 79.9 %all-to-all-start.1 = ((bf16[32,32,2816]{2,1,0:T(8,128)(2,1)}), bf16[32,32,2816]{2,1,0:T(8,128)(2,1)}, u32[]{:S(2)}, u32[]{:S(2)}) async-start(bf16[32,32,2816]{2,1,0:T(8,128)(2,1)} %bitcast.22), calls=%async_computation.1 | async-start | bytes 11534336 | tf_op jit(solution)/shard_map/all_to_all | solution.py:747
  98.0 25.3 %collective-permute-start.6 = (bf16[128,4352]{1,0:T(8,128)(2,1)}, bf16[128,4352]{1,0:T(8,128)(2,1)}, u32[]{:S(2)}, u32[]{:S(2)}) collective-permute-start(bf16[128,4352]{1,0:T(8,128)(2,1)} %slice.18), channel_id=1, source_target_pairs={{0,32},{32,64},{64,96},{96,0},{1,33},{33,65},{65,97},{97,1},{2,34}... | collective-permute-start | bytes 3342344 | tf_op jit(solution)/shard_map/ppermute | solution.py:752
  100.8 24.3 %collective-permute-start.7 = (bf16[128,4352]{1,0:T(8,128)(2,1)}, bf16[128,4352]{1,0:T(8,128)(2,1)}, u32[]{:S(2)}, u32[]{:S(2)}) collective-permute-start(bf16[128,4352]{1,0:T(8,128)(2,1)} %slice.19), channel_id=1, source_target_pairs={{0,96},{32,0},{64,32},{96,64},{1,97},{33,1},{65,33},{97,65},{2,98}... | collective-permute-start | bytes 3342344 | tf_op jit(solution)/shard_map/ppermute | solution.py:752
  140.4 19.3 %collective-permute-start.12 = (bf16[64,4096]{1,0:T(8,128)(2,1)}, bf16[64,4096]{1,0:T(8,128)(2,1)}, u32[]{:S(2)}, u32[]{:S(2)}) collective-permute-start(bf16[64,4096]{1,0:T(8,128)(2,1)} %get-tuple-element.79), channel_id=1, source_target_pairs={{0,32},{32,64},{64,96},{96,0},{1,33},{33,65},{65,97},{97,1},{2,34}... | collective-permute-start | bytes 1572872 | tf_op jit(solution)/shard_map/ppermute | solution.py:752
  140.7 19.0 %collective-permute-start.13 = (bf16[64,4096]{1,0:T(8,128)(2,1)}, bf16[64,4096]{1,0:T(8,128)(2,1)}, u32[]{:S(2)}, u32[]{:S(2)}) collective-permute-start(bf16[64,4096]{1,0:T(8,128)(2,1)} %get-tuple-element.80), channel_id=1, source_target_pairs={{0,96},{32,0},{64,32},{96,64},{1,97},{33,1},{65,33},{97,65},{2,98}... | collective-permute-start | bytes 1572872 | tf_op jit(solution)/shard_map/ppermute | solution.py:752
  147.8 51.6 %all-to-all-start.2 = ((bf16[32,16,3072]{2,1,0:T(8,128)(2,1)}), bf16[32,16,3072]{2,1,0:T(8,128)(2,1)S(1)}, u32[]{:S(2)}, u32[]{:S(2)}) async-start(bf16[32,16,3072]{2,1,0:T(8,128)(2,1)} %bitcast.23), calls=%async_computation.2 | async-start | bytes 6291456 | tf_op jit(solution)/shard_map/all_to_all | solution.py:747
  164.7 26.0 %collective-permute-start.14 = (bf16[128,4096]{1,0:T(8,128)(2,1)}, bf16[128,4096]{1,0:T(8,128)(2,1)S(1)}, u32[]{:S(2)}, u32[]{:S(2)}) collective-permute-start(bf16[128,4096]{1,0:T(8,128)(2,1)} %get-tuple-element.93), channel_id=1, source_target_pairs={{0,32},{32,64},{64,96},{96,0},{1,33},{33,65},{65,97},{97,1},{2,34}... | collective-permute-start | bytes 3145736 | tf_op jit(solution)/shard_map/ppermute | solution.py:752
  164.8 25.9 %collective-permute-start.15 = (bf16[128,4096]{1,0:T(8,128)(2,1)}, bf16[128,4096]{1,0:T(8,128)(2,1)S(1)}, u32[]{:S(2)}, u32[]{:S(2)}) collective-permute-start(bf16[128,4096]{1,0:T(8,128)(2,1)} %get-tuple-element.94), channel_id=1, source_target_pairs={{0,96},{32,0},{64,32},{96,64},{1,97},{33,1},{65,33},{97,65},{2,98}... | collective-permute-start | bytes 3145736 | tf_op jit(solution)/shard_map/ppermute | solution.py:752
  179.3 11.4 %copy-start.1 = (bf16[128,4096]{1,0:T(8,128)(2,1)S(1)}, bf16[128,4096]{1,0:T(8,128)(2,1)}, u32[]{:S(2)}) copy-start(bf16[128,4096]{1,0:T(8,128)(2,1)} %get-tuple-element.92.a_ref) | copy-start | bytes 3145732
  199.4 22.0 %all-to-all-start.3 = ((bf16[32,4,4096]{2,1,0:T(4,128)(2,1)}), bf16[32,4,4096]{2,1,0:T(4,128)(2,1)}, u32[]{:S(2)}, u32[]{:S(2)}) async-start(bf16[32,4,4096]{2,1,0:T(4,128)(2,1)} %copy-done), calls=%async_computation.3 | async-start | bytes 2097152 | tf_op jit(solution)/shard_map/all_to_all | solution.py:747
  204.5 19.5 %copy-start.2 = (bf16[64,128]{1,0:T(8,128)(2,1)S(1)}, bf16[64,128]{1,0:T(8,128)(2,1)}, u32[]{:S(2)}) copy-start(bf16[64,128]{1,0:T(8,128)(2,1)} %get-tuple-element.51.table_ref) | copy-start | bytes 49156
  205.4 7.6 %collective-permute-start.8 = (bf16[32,3072]{1,0:T(8,128)(2,1)S(1)}, bf16[32,3072]{1,0:T(8,128)(2,1)S(1)}, u32[]{:S(2)}, u32[]{:S(2)}) collective-permute-start(bf16[32,3072]{1,0:T(8,128)(2,1)S(1)} %get-tuple-element.74), channel_id=1, source_target_pairs={{0,32},{32,64},{64,96},{96,0},{1,33},{33,65},{65,97},{97,1},{2,34}... | collective-permute-start | bytes 589832 | tf_op jit(solution)/shard_map/ppermute | solution.py:752
  205.5 7.5 %collective-permute-start.9 = (bf16[32,3072]{1,0:T(8,128)(2,1)S(1)}, bf16[32,3072]{1,0:T(8,128)(2,1)S(1)}, u32[]{:S(2)}, u32[]{:S(2)}) collective-permute-start(bf16[32,3072]{1,0:T(8,128)(2,1)S(1)} %get-tuple-element.75), channel_id=1, source_target_pairs={{0,96},{32,0},{64,32},{96,64},{1,97},{33,1},{65,33},{97,65},{2,98}... | collective-permute-start | bytes 589832 | tf_op jit(solution)/shard_map/ppermute | solution.py:752
  213.1 10.9 %collective-permute-start.10 = (bf16[64,3072]{1,0:T(8,128)(2,1)S(1)}, bf16[64,3072]{1,0:T(8,128)(2,1)S(1)}, u32[]{:S(2)}, u32[]{:S(2)}) collective-permute-start(bf16[64,3072]{1,0:T(8,128)(2,1)S(1)} %get-tuple-element.76), channel_id=1, source_target_pairs={{0,32},{32,64},{64,96},{96,0},{1,33},{33,65},{65,97},{97,1},{2,34}... | collective-permute-start | bytes 1179656 | tf_op jit(solution)/shard_map/ppermute | solution.py:752
  213.2 10.8 %collective-permute-start.11 = (bf16[64,3072]{1,0:T(8,128)(2,1)S(1)}, bf16[64,3072]{1,0:T(8,128)(2,1)S(1)}, u32[]{:S(2)}, u32[]{:S(2)}) collective-permute-start(bf16[64,3072]{1,0:T(8,128)(2,1)S(1)} %get-tuple-element.77), channel_id=1, source_target_pairs={{0,96},{32,0},{64,32},{96,64},{1,97},{33,1},{65,33},{97,65},{2,98}... | collective-permute-start | bytes 1179656 | tf_op jit(solution)/shard_map/ppermute | solution.py:752
  (4 other events, 17.1 us)
